TPU v7x, 32 devices: a whole 2x2x4 slice. The times are simulated.
32 devices in a mesh: dp: 8 (over z, y), mp: 4 (over x, core).
Axes of the slice: x: 2, y: 2, z: 4, core: 2. Of those that a mesh axis runs over, the one named last changes fastest.
Arguments:
- activations: bfloat16 [4096, 8192], P(('dp', 'mp')), may hold values from -6 to 6
- grad_out: bfloat16 [4096, 28672], P('dp', 'mp'), may hold values from -0.25 to 0.25
- basis: bfloat16 [8192, 256], P('dp'), may hold values from -0.0625 to 0.0625
- first_moment: float32 [28672, 256], P(('mp', 'dp')), may hold values from -3 to 3
- second_moment: float32 [28672, 256], P(('mp', 'dp')), may hold values from 0.01 to 0.5
Outputs:
- update: bfloat16 [8192, 28672], P('dp', 'mp')
- first_new: float32 [28672, 256], P(('mp', 'dp'))
- second_new: float32 [28672, 256], P(('mp', 'dp'))
All inputs are finite; a program needn't handle non-finite values.
Results may differ from a plain program's by a relative error of at most 0.0069.
Values may be sent and summed in bfloat16 or wider, within the bound.
No kernel may reach another device: no remote copies, remote signals or barrier semaphores. Data moves between devices by JAX's collectives and lax.ppermute only.
A program may use at most 128 MiB of HBM per device.

v0:
```python
import jax
import jax.numpy as jnp
from jax import lax
from jax.sharding import PartitionSpec as P

STEP = 1000


beta_first = 0.9
beta_second = 0.999
adam_eps = 1e-08


def on_device(activations, grad_out, basis, first_moment, second_moment):
    columns = activations
    own_coords = jnp.dot(
        columns, lax.all_gather(basis, "dp", axis=0, tiled=True), preferred_element_type=jnp.float32
    ).astype(jnp.bfloat16)
    coords = lax.all_gather(own_coords, "mp", axis=0, tiled=True)
    columns = grad_out
    projected = lax.psum_scatter(
        lax.dot_general(
            columns, coords, (((0,), (0,)), ((), ())), preferred_element_type=jnp.float32
        ),
        "dp",
        scatter_dimension=0,
        tiled=True,
    )
    first_new = beta_first * first_moment + (1.0 - beta_first) * projected
    second_new = beta_second * second_moment + (1.0 - beta_second) * projected * projected
    corr_first = 1.0 - beta_first**STEP
    corr_second = 1.0 - beta_second**STEP
    direction = (first_new / corr_first / (jnp.sqrt(second_new / corr_second) + adam_eps)).astype(
        jnp.bfloat16
    )
    update = lax.dot_general(
        basis,
        lax.all_gather(direction, "dp", axis=0, tiled=True),
        (((1,), (1,)), ((), ())),
        preferred_element_type=jnp.float32,
    ).astype(jnp.bfloat16)
    return (update, first_new, second_new)


def solution(mesh):
    placed = (
        P(("dp", "mp"), None),
        P("dp", "mp"),
        P("dp", None),
        P(("mp", "dp"), None),
        P(("mp", "dp"), None),
    )
    return jax.shard_map(
        on_device,
        mesh=mesh,
        in_specs=placed,
        out_specs=(P("dp", "mp"), P(("mp", "dp"), None), P(("mp", "dp"), None)),
        check_vma=False,
    )
```

profile of v0, /device:TPU:0, one launch (start us, length us, event | category | flops | bytes accessed | tf_op | source)
XLA Modules:
  0.0 339.1 jit_solution(13559171904034469441)
XLA Ops:
  7.2 0.0 copy-start
  7.2 0.0 all-gather.3.cloned.1.call-start
  7.2 0.7 all-gather.3.cloned.1.call-update
  7.9 0.0 reduce-scatter.2.cloned.1.call-start
  8.0 77.7 %all-gather.3.cloned.1.call-done = bf16[8192,256]{1,0:T(8,128)(2,1)} async-done(((bf16[1024,256]{1,0:T(8,128)(2,1)}), bf16[8192,256]{1,0:T(8,128)(2,1)}) %all-gather.3.cloned.1.call-update) | async-done | bytes 4194320 | tf_op jit(solution)/shard_map/all_gather | solution.py:17
  85.7 0.0 copy-done
  85.7 2.9 convolution_convert_fusion
  88.6 5.8 %all_gather.10 = bf16[512,256]{1,0:T(8,128)(2,1)S(1)} all-gather(bf16[128,256]{1,0:T(8,128)(2,1)S(1)} %convolution_convert_fusion), channel_id=1, replica_groups=mesh['dp'=8,'mp'=4] {'mp'}, dimensions={0}, use_global_device_ids=true | all-gather | bytes 327680 | tf_op jit(solution)/shard_map/all_gather | solution.py:19
  94.3 8.2 %convolution_bitcast_fusion = f32[7168,256]{0,1:T(8,128)} fusion(bf16[512,256]{1,0:T(8,128)(2,1)S(1)} %all_gather.10, bf16[512,7168]{1,0:T(8,128)(2,1)} %param.6), kind=kOutput, calls=%fused_computation.1 | convolution fusion | flops 1879048192 | bytes 14942208 | tf_op jit(solution)/shard_map/dot_general | solution.py:22
  102.6 0.0 copy-start.2
  102.6 0.0 reduce-scatter.2.cloned.1.call-update
  102.6 0.0 all-gather.5.cloned.1.call-start
  102.7 1.1 copy-done.2
  103.8 1.2 copy.8
  105.0 2.4 copy.9
  107.4 0.0 copy-start.1
  107.4 126.8 %reduce-scatter.2.cloned.1.call-done = f32[896,256]{0,1:T(8,128)} async-done(((f32[7168,256]{0,1:T(8,128)}), f32[896,256]{0,1:T(8,128)}) %reduce-scatter.2.cloned.1.call-update) | async-done | bytes 917520 | tf_op jit(solution)/shard_map/reduce_scatter | solution.py:21
  234.2 3.4 divide_convert_fusion
  237.5 0.0 all-gather.5.cloned.1.call-update
  237.5 2.4 copy.12
  239.9 1.2 copy.11
  241.2 62.0 %all-gather.5.cloned.1.call-done = bf16[7168,256]{0,1:T(8,128)(2,1)} async-done(((bf16[896,256]{0,1:T(8,128)(2,1)}), bf16[7168,256]{0,1:T(8,128)(2,1)}) %all-gather.5.cloned.1.call-update) | async-done | bytes 3670032 | tf_op jit(solution)/shard_map/all_gather | solution.py:38
  303.2 0.0 copy-done.1
  303.2 9.4 %convert_bitcast_fusion = bf16[1024,7168]{0,1:T(8,128)(2,1)} fusion(bf16[7168,256]{0,1:T(8,128)(2,1)} %all-gather.5.cloned.1.call-done, bf16[1024,256]{1,0:T(8,128)(2,1)S(1)} %copy-done.1), kind=kOutput, calls=%fused_computation | convolution fusion | flops 3765436416 | bytes 18874368 | tf_op jit(solution)/shard_map/dot_general | solution.py:36
  312.7 19.9 %copy.10 = bf16[1024,7168]{1,0:T(8,128)(2,1)} copy(bf16[1024,7168]{0,1:T(8,128)(2,1)} %convert_bitcast_fusion) | data formatting | bytes 29360128
Async XLA Ops:
  7.2 78.5 %copy-start = (bf16[128,8192]{1,0:T(8,128)(2,1)S(1)}, bf16[128,8192]{1,0:T(8,128)(2,1)}, u32[]{:S(2)}) copy-start(bf16[128,8192]{1,0:T(8,128)(2,1)} %param.5) | copy-start | bytes 6291460
  7.2 78.5 %all-gather.3.cloned.1.call-start = ((), (), s32[]{:S(2)}) async-start(), calls=%async_computation.1 | async-start | bytes 4718592 | tf_op jit(solution)/shard_map/all_gather | solution.py:17
  7.9 226.2 %reduce-scatter.2.cloned.1.call-start = ((), (), s32[]{:S(2)}) async-start(), calls=%async_computation.2 | async-start | bytes 8257536 | tf_op jit(solution)/shard_map/reduce_scatter | solution.py:21
  102.6 1.2 copy-start.2
  102.6 200.6 %all-gather.5.cloned.1.call-start = ((), (), s32[]{:S(2)}) async-start(), calls=%async_computation.3 | async-start | bytes 4128768 | tf_op jit(solution)/shard_map/all_gather | solution.py:38
  107.4 195.8 %copy-start.1 = (bf16[1024,256]{1,0:T(8,128)(2,1)S(1)}, bf16[1024,256]{1,0:T(8,128)(2,1)}, u32[]{:S(2)}) copy-start(bf16[1024,256]{1,0:T(8,128)(2,1)} %param.7) | copy-start | bytes 1572868
Sparse Core Ops, SparseCore 0:
  10.1 75.5 all-gather.2
  102.7 131.3 reduce-scatter.1
  237.7 65.5 all-gather.4
where the time goes:
time: 340 us; the launch traced here: 339 us
  waiting for transfers between devices  267 us (79%)
  local copies, waits for them, and re-layouts  28.3 us (8%)
  matrix products  20.6 us (6%)
  between operations  13.8 us (4%)
  blocking collectives  5.78 us (2%)
    reduce_scatter x1, waiting for transfers between devices, on_device(): lax.psum_scatter(lax.dot_general(columns, coords, (((0,), (0,)), ((), ())...  127 us
    all_gather x1, waiting for transfers between devices, on_device(): lax.all_gather(basis, 'dp', axis=0, tiled=True)  77.7 us
    all_gather x1, waiting for transfers between devices, on_device(): lax.all_gather(direction, 'dp', axis=0, tiled=True)  62 us
    unnamed x11, local copies, waits for them, and re-layouts  28.3 us
    dot_general x1, matrix products, on_device(): lax.dot_general(basis, lax.all_gather(direction, 'dp', axis=0, tiled=True...  9.44 us
    dot_general x1, matrix products, on_device(): lax.dot_general(columns, coords, (((0,), (0,)), ((), ())), preferred_elem...  8.24 us
  transfers between devices with their start and end apart: 3, of which 3 were waited for; matrix products, arithmetic and copies ran while one was open for 2% of the time, Pallas kernels for 0%

commit v1 on v0

v1 whole, which is shorter than its diff:
```python
import functools

import jax
import jax.numpy as jnp
import numpy as np
from jax import lax
from jax.experimental import pallas as pl
from jax.experimental.pallas import tpu as pltpu
from jax.sharding import PartitionSpec as P

STEP = 1000


beta_first = 0.9
beta_second = 0.999
adam_eps = 1e-08

STREAMS = 2
LONGEST_RING = 16


def adam(projected, first_moment, second_moment):
    first_new = beta_first * first_moment + (1.0 - beta_first) * projected
    second_new = beta_second * second_moment + (1.0 - beta_second) * projected * projected
    corr_first = 1.0 - beta_first**STEP
    corr_second = 1.0 - beta_second**STEP
    direction = (first_new / corr_first / (jnp.sqrt(second_new / corr_second) + adam_eps)).astype(
        jnp.bfloat16
    )
    return first_new, second_new, direction


def with_collectives(activations, grad_out, basis, first_moment, second_moment):
    own_coords = jnp.dot(
        activations, lax.all_gather(basis, "dp", axis=0, tiled=True), preferred_element_type=jnp.float32
    ).astype(jnp.bfloat16)
    coords = lax.all_gather(own_coords, "mp", axis=0, tiled=True)
    projected = lax.psum_scatter(
        lax.dot_general(
            grad_out, coords, (((0,), (0,)), ((), ())), preferred_element_type=jnp.float32
        ),
        "dp",
        scatter_dimension=0,
        tiled=True,
    )
    first_new, second_new, direction = adam(projected, first_moment, second_moment)
    update = lax.dot_general(
        basis,
        lax.all_gather(direction, "dp", axis=0, tiled=True),
        (((1,), (1,)), ((), ())),
        preferred_element_type=jnp.float32,
    ).astype(jnp.bfloat16)
    return (update, first_new, second_new)


def whole(shape):
    return pl.BlockSpec(shape, lambda *_: (0,) * len(shape))


def add_coords(offsets, activations, total, pieces, out_dtype):
    rows, width = activations.shape[0], pieces[0].shape[1]
    held = () if total is None else (total,)

    def kernel(at, act, *refs):
        out = refs[-1]
        acc = refs[0][...] if held else jnp.zeros((rows, width), jnp.float32)
        for k, piece in enumerate(refs[len(held) : -1]):
            depth = piece.shape[0]
            block = act[:, pl.ds(pl.multiple_of(at[k], 128), depth)]
            acc += jnp.dot(block, piece[...], preferred_element_type=jnp.float32)
        out[...] = acc.astype(out.dtype)

    return pl.pallas_call(
        kernel,
        out_shape=jax.ShapeDtypeStruct((rows, width), out_dtype),
        grid_spec=pltpu.PrefetchScalarGridSpec(
            num_scalar_prefetch=1,
            grid=(1,),
            in_specs=[whole(a.shape) for a in (activations, *held, *pieces)],
            out_specs=whole((rows, width)),
        ),
        name="add_coords",
    )(offsets, activations, *held, *pieces)


def contract_tokens(grad, coords):
    return lax.dot_general(grad, coords, (((0,), (0,)), ((), ())), preferred_element_type=jnp.float32)


def first_partials(ids, grad_out, coords, n, cols):
    tokens, width = coords.shape

    def kernel(ids_ref, grad, coord, top, bottom):
        part = contract_tokens(grad[...], coord[...]).astype(jnp.bfloat16)
        top[...] = part[: cols // 2]
        bottom[...] = part[cols // 2 :]

    half = jax.ShapeDtypeStruct((cols // 2, width), jnp.bfloat16)
    return pl.pallas_call(
        kernel,
        out_shape=(half, half),
        grid_spec=pltpu.PrefetchScalarGridSpec(
            num_scalar_prefetch=1,
            grid=(1,),
            in_specs=[
                pl.BlockSpec((tokens, cols), lambda g, ids: (0, ids[n // 2])),
                whole(coords.shape),
            ],
            out_specs=(whole(half.shape), whole(half.shape)),
        ),
        name="first_partials",
    )(ids, grad_out, coords)


def next_partials(ids, grad_out, coords, came_up, came_down, n, cols, away):
    tokens, width = coords.shape
    rows = came_up.shape[0]

    def kernel(ids_ref, grad, coord, in_up, in_down, up, down):
        part = contract_tokens(grad[...], coord[...])

        @pl.when(pl.program_id(0) == 0)
        def _():
            up[:rows] = (part[:rows] + in_up[...].astype(jnp.float32)).astype(jnp.bfloat16)
            if rows < cols:
                up[rows:] = part[rows:].astype(jnp.bfloat16)

        @pl.when(pl.program_id(0) == 1)
        def _():
            down[cols - rows :] = (
                part[cols - rows :] + in_down[...].astype(jnp.float32)
            ).astype(jnp.bfloat16)
            if rows < cols:
                down[: cols - rows] = part[: cols - rows].astype(jnp.bfloat16)

    full = jax.ShapeDtypeStruct((cols, width), jnp.bfloat16)
    return pl.pallas_call(
        kernel,
        out_shape=(full, full),
        grid_spec=pltpu.PrefetchScalarGridSpec(
            num_scalar_prefetch=1,
            grid=(2,),
            in_specs=[
                pl.BlockSpec(
                    (tokens, cols), lambda g, ids: (0, jnp.where(g == 0, ids[away], ids[n - away]))
                ),
                whole(coords.shape),
                whole(came_up.shape),
                whole(came_down.shape),
            ],
            out_specs=(whole(full.shape), whole(full.shape)),
        ),
        name="next_partials",
    )(ids, grad_out, coords, came_up, came_down)


def own_rows(ids, grad_out, coords, came_up, came_down, first_moment, second_moment, earlier, s, cols):
    tokens, width = coords.shape
    held = () if earlier is None else earlier

    def kernel(ids_ref, grad, coord, in_up, in_down, first, second, *refs):
        first_new, second_new, direction = refs[len(held) :]
        projected = (
            contract_tokens(grad[...], coord[...])
            + in_up[...].astype(jnp.float32)
            + in_down[...].astype(jnp.float32)
        )
        first_new[...], second_new[...], direction[...] = adam(projected, first[...], second[...])

    part = pl.BlockSpec((cols, width), lambda g, ids: (0, s))
    moment = jax.ShapeDtypeStruct(first_moment.shape, jnp.float32)
    return pl.pallas_call(
        kernel,
        out_shape=(moment, moment, jax.ShapeDtypeStruct((cols, width), jnp.bfloat16)),
        grid_spec=pltpu.PrefetchScalarGridSpec(
            num_scalar_prefetch=1,
            grid=(1,),
            in_specs=[
                pl.BlockSpec((tokens, cols), lambda g, ids: (0, ids[0])),
                whole(coords.shape),
                whole(came_up.shape),
                whole(came_down.shape),
                part,
                part,
                *[pl.BlockSpec(memory_space=pl.ANY)] * len(held),
            ],
            out_specs=(part, part, whole((cols, width))),
        ),
        input_output_aliases={7 + k: k for k in range(len(held))},
        name="own_rows",
    )(ids, grad_out, coords, came_up, came_down, first_moment, second_moment, *held)


def write_update(ids, basis, chunks, places, update, all_columns):
    depth, rank = basis.shape
    cols = sum(row[0].shape[0] for row in chunks[0])
    flat = [stream for chunk in chunks for row in chunk for stream in row]
    held = () if update is None else (update,)
    tile = depth // 2

    def kernel(ids_ref, base, *refs):
        out = refs[-1]
        left = list(refs[: len(flat)])
        for g, chunk in enumerate(chunks):
            rows = [[left.pop(0) for _ in row] for row in chunk]

            @pl.when(pl.program_id(0) == g)
            def _(rows=rows):
                at = 0
                for row in rows:
                    size, width = row[0].shape
                    total = None
                    for s, stream in enumerate(row):
                        product = lax.dot_general(
                            base[:, s * width : (s + 1) * width],
                            stream[...],
                            (((1,), (1,)), ((), ())),
                            preferred_element_type=jnp.float32,
                        )
                        total = product if total is None else total + product
                    out[:, at : at + size] = total.astype(out.dtype)
                    at += size

    def place(g, r, ids):
        at = ids[places[0]]
        for k in range(1, len(places)):
            at = jnp.where(g == k, ids[places[k]], at)
        return (r, at)

    return pl.pallas_call(
        kernel,
        out_shape=jax.ShapeDtypeStruct((depth, all_columns), jnp.bfloat16),
        grid_spec=pltpu.PrefetchScalarGridSpec(
            num_scalar_prefetch=1,
            grid=(len(chunks), depth // tile),
            in_specs=[
                pl.BlockSpec((tile, rank), lambda g, r, ids: (r, 0)),
                *[whole(a.shape) for a in flat],
                *[pl.BlockSpec(memory_space=pl.ANY)] * len(held),
            ],
            out_specs=pl.BlockSpec((tile, cols), place),
        ),
        input_output_aliases={2 + len(flat): 0} if held else {},
        name="write_update",
    )(ids, basis, *flat, *held)


def on_ring(n, m, activations, grad_out, basis, first_moment, second_moment):
    order = [*range(0, n, 2), *range(n - 1, 0, -2)]
    upward = [(order[k], order[(k + 1) % n]) for k in range(n)]
    downward = [(b, a) for a, b in upward]
    partner = [(k, k ^ 1) for k in range(m)]
    up = functools.partial(lax.ppermute, axis_name="dp", perm=upward)
    down = functools.partial(lax.ppermute, axis_name="dp", perm=downward)

    around = np.zeros((n, n), np.int32)
    for place, index in enumerate(order):
        around[index] = [order[(place + away) % n] for away in range(n)]
    ids = jnp.asarray(around)[lax.axis_index("dp")]
    mine = lax.axis_index("mp")
    side = mine % 2

    depth, rank = basis.shape
    tokens = activations.shape[0]
    width = rank // STREAMS
    all_columns = grad_out.shape[1]
    cols = all_columns // n
    half = n // 2
    streams = range(STREAMS)

    part = depth // 2
    sent_up = [None] * STREAMS
    sent_down = [None] * STREAMS
    total = [None] * STREAMS
    for s in streams:
        own = basis[:, s * width : (s + 1) * width]
        sent_up[s] = sent_down[s] = lax.dynamic_slice(own, (side * part, 0), (part, width))
        total[s] = add_coords(ids[:1] * depth, activations, None, [own], jnp.float32)
    for k in range(1, half + 1):
        for s in streams:
            if k == half:
                sent_up[s], sent_down[s] = sent_up[s][: part // 2], sent_down[s][part // 2 :]
            sent_up[s], sent_down[s] = up(sent_up[s]), down(sent_down[s])
            pieces = [sent_up[s], sent_down[s]]
            pieces += [lax.ppermute(a, "mp", partner) for a in pieces]
            low = part // 2 if k == half else 0
            at = jnp.stack(
                [
                    ids[n - k] * depth + side * part,
                    ids[k] * depth + side * part + low,
                    ids[n - k] * depth + (1 - side) * part,
                    ids[k] * depth + (1 - side) * part + low,
                ]
            )
            total[s] = add_coords(
                at, activations, total[s], pieces, jnp.bfloat16 if k == half else jnp.float32
            )

    coords = [None] * STREAMS
    for s in streams:
        parts = [total[s]]
        for k in range(1, m):
            parts.append(lax.ppermute(total[s], "mp", [(a, (a + k) % m) for a in range(m)]))
        turned = [parts[-k % m] for k in range(m)]
        coords[s] = lax.dynamic_slice(
            jnp.concatenate(turned + turned), ((m - mine) % m * tokens, 0), (m * tokens, width)
        )

    for s in streams:
        top, bottom = first_partials(ids, grad_out, coords[s], n, cols)
        sent_up[s], sent_down[s] = up(top), down(bottom)
    for away in range(half - 1, 0, -1):
        for s in streams:
            to_up, to_down = next_partials(
                ids, grad_out, coords[s], sent_up[s], sent_down[s], n, cols, away
            )
            sent_up[s], sent_down[s] = up(to_up), down(to_down)
    moments = None
    direction = [None] * STREAMS
    for s in streams:
        *moments, direction[s] = own_rows(
            ids, grad_out, coords[s], sent_up[s], sent_down[s], first_moment, second_moment, moments, s, cols
        )
    first_new, second_new = moments

    sent_up, sent_down = list(direction), list(direction)
    update = write_update(ids, basis, [[direction]], [0], None, all_columns)
    for k in range(1, half):
        for s in streams:
            sent_up[s], sent_down[s] = up(sent_up[s]), down(sent_down[s])
        update = write_update(
            ids, basis, [[list(sent_up)], [list(sent_down)]], [n - k, k], update, all_columns
        )
    for s in streams:
        sent_up[s], sent_down[s] = up(sent_up[s][: cols // 2]), down(sent_down[s][cols // 2 :])
    update = write_update(ids, basis, [[sent_up, sent_down]], [half], update, all_columns)
    return (update, first_new, second_new)


def solution(mesh):
    n, m = mesh.shape["dp"], mesh.shape["mp"]
    ring = 4 <= n <= LONGEST_RING and n % 2 == 0 and m % 2 == 0
    placed = (
        P(("dp", "mp"), None),
        P("dp", "mp"),
        P("dp", None),
        P(("mp", "dp"), None),
        P(("mp", "dp"), None),
    )
    return jax.shard_map(
        functools.partial(on_ring, n, m) if ring else with_collectives,
        mesh=mesh,
        in_specs=placed,
        out_specs=(P("dp", "mp"), P(("mp", "dp"), None), P(("mp", "dp"), None)),
        check_vma=False,
    )
```

time: 340 us -> 212 us (0.62)
  waiting for transfers between devices: 267 us -> 26.9 us
  Pallas kernels: 0 us -> 94.5 us
  starting transfers between devices: 0.12 us -> 57.1 us
  matrix products: 20.6 us -> 0 us
  between operations: 13.8 us -> 6.21 us
  blocking collectives: 5.78 us -> 0 us
  local copies, waits for them, and re-layouts: 28.3 us -> 23 us
    all_gather x2 -> x0, waiting for transfers between devices: 140 us -> none  [the longest x1 77.7 us: on_device(): lax.all_gather(basis, 'dp', axis=0, tiled=True)]
    reduce_scatter x1 -> x0, waiting for transfers between devices: 127 us -> none  [on_device(): lax.psum_scatter(lax.dot_general(columns, coords, (((0,), (0,)), ((), ())...]
    pallas_call x0 -> x25, Pallas kernels: none -> 94.5 us  [the longest x10 31 us: add_coords(): pl.pallas_call(kernel, out_shape=jax.ShapeDtypeStruct((rows, width), out_...]
    ppermute x0 -> x70, starting transfers between devices: none -> 57.1 us  [the longest x28 29.5 us: on_ring(): sent_up[s], sent_down[s] = (up(sent_up[s]), down(sent_down[s]))]
    ppermute x0 -> x70, waiting for transfers between devices: none -> 26.9 us  [the longest x28 23.7 us: on_ring(): sent_up[s], sent_down[s] = (up(sent_up[s]), down(sent_down[s]))]
    dot_general x3 -> x0, matrix products: 20.6 us -> none  [the longest x1 9.44 us: on_device(): lax.dot_general(basis, lax.all_gather(direction, 'dp', axis=0, tiled=True...]
    unnamed x11 -> x138, local copies, waits for them, and re-layouts: 28.3 us -> 17.2 us
    all_gather x1 -> x0, blocking collectives: 5.78 us -> none  [on_device(): coords = lax.all_gather(own_coords, 'mp', axis=0, tiled=True)]
  transfers between devices with their start and end apart: 3 -> 70, of which waited for: 3 -> 16; matrix products, arithmetic and copies ran while one was open for 2% -> 4% of each run, Pallas kernels for 0% -> 40%
where the time goes in v1:
time: 212 us; the launch traced here: 210 us
  Pallas kernels  94.5 us (45%)
  starting transfers between devices  57.1 us (27%)
  waiting for transfers between devices  26.9 us (13%)
  local copies, waits for them, and re-layouts  23 us (11%)
  between operations  6.21 us (3%)
  other arithmetic  2.45 us (1%)
    pallas_call x10, Pallas kernels, add_coords(): pl.pallas_call(kernel, out_shape=jax.ShapeDtypeStruct((rows, width), out_...  31 us
    ppermute x28, starting transfers between devices, on_ring(): sent_up[s], sent_down[s] = (up(sent_up[s]), down(sent_down[s]))  29.5 us
    pallas_call x5, Pallas kernels, write_update(): pl.pallas_call(kernel, out_shape=jax.ShapeDtypeStruct((depth, all_columns...  27 us
    ppermute x28, waiting for transfers between devices, on_ring(): sent_up[s], sent_down[s] = (up(sent_up[s]), down(sent_down[s]))  23.7 us
    pallas_call x6, Pallas kernels, next_partials(): pl.pallas_call(kernel, out_shape=(full, full), grid_spec=pltpu.PrefetchSc...  22.6 us
    unnamed x138, local copies, waits for them, and re-layouts  17.2 us
    ppermute x12, starting transfers between devices, on_ring(): sent_up[s], sent_down[s] = (up(to_up), down(to_down))  12.2 us
    pallas_call x2, Pallas kernels, own_rows(): pl.pallas_call(kernel, out_shape=(moment, moment, jax.ShapeDtypeStruct((c...  7.88 us
  transfers between devices with their start and end apart: 70, of which 16 were waited for; matrix products, arithmetic and copies ran while one was open for 4% of the time, Pallas kernels for 40%

profile of v1, /device:TPU:0, one launch (start us, length us, event | category | flops | bytes accessed | tf_op | source)
XLA Modules:
  0.0 210.1 jit_solution(7970050651047761222)
XLA Ops:
  0.6 1.1 fusion.1
  1.8 3.1 %collective-permute-start.31 = (bf16[512,128]{1,0:T(8,128)(2,1)S(1)}, bf16[512,128]{1,0:T(8,128)(2,1)S(1)}, u32[]{:S(2)}, u32[]{:S(2)}) collective-permute-start(bf16[512,128]{1,0:T(8,128)(2,1)S(1)} %constant_dynamic-slice_fusion.1), channel_id=1, source_target_pairs={{0,8},{8,16},{16,24},{24,28},{28,20},{20,12},{12,4},{4,0},{1,9},{9... | collective-permute-start | bytes 393224 | tf_op jit(solution)/shard_map/ppermute | solution.py:283
  4.9 2.1 collective-permute-start
  7.0 2.2 %collective-permute-done.31.refs_1_ = bf16[512,128]{1,0:T(8,128)(2,1)S(1)} collective-permute-done((bf16[512,128]{1,0:T(8,128)(2,1)S(1)}, bf16[512,128]{1,0:T(8,128)(2,1)S(1)}, u32[]{:S(2)}, u32[]{:S(2)}) %collective-permute-start.31) | collective-permute-done | bytes 131104 | tf_op jit(solution)/shard_map/ppermute | solution.py:283
  9.2 2.0 collective-permute-done.32.refs_2_
  11.1 1.6 collective-permute-start.35
  13.7 1.6 collective-permute-start.4
  15.3 2.2 %collective-permute-done.35.refs_1_ = bf16[512,128]{1,0:T(8,128)(2,1)S(1)} collective-permute-done((bf16[512,128]{1,0:T(8,128)(2,1)S(1)}, bf16[512,128]{1,0:T(8,128)(2,1)S(1)}, u32[]{:S(2)}, u32[]{:S(2)}) %collective-permute-start.35) | collective-permute-done | bytes 131104 | tf_op jit(solution)/shard_map/ppermute | solution.py:283
  18.4 1.6 collective-permute-start.39
  20.5 1.2 constant_dynamic-slice_fusion.4
  22.5 1.6 collective-permute-start.8
  28.8 1.4 collective-permute-start.43
  33.9 1.4 collective-permute-start.12
  37.8 2.4 %add_coords.15.refs_0_ = f32[128,128]{1,0:T(8,128)} custom-call(s32[1]{0:T(128)} %bitcast.24.at, bf16[128,8192]{1,0:T(8,128)(2,1)} %act.19, bf16[1024,128]{1,0:T(8,128)(2,1)} %copy-done.1), custom_call_target="tpu_custom_call" | custom-call | tf_op jit(solution)/shard_map/add_coords/pallas_call | solution.py:73
  40.2 2.4 %add_coords.10.refs_0_ = f32[128,128]{1,0:T(8,128)} custom-call(s32[1]{0:T(128)} %bitcast.24.at, bf16[128,8192]{1,0:T(8,128)(2,1)} %act.19, bf16[1024,128]{1,0:T(8,128)(2,1)} %copy-done), custom_call_target="tpu_custom_call" | custom-call | tf_op jit(solution)/shard_map/add_coords/pallas_call | solution.py:73
  44.5 3.3 %add_coords.16.refs_0_ = f32[128,128]{1,0:T(8,128)} custom-call(s32[4]{0:T(128)} %pad_add_fusion.3.at, bf16[128,8192]{1,0:T(8,128)(2,1)} %act.19, f32[128,128]{1,0:T(8,128)} %add_coords.15.refs_0_, bf16[512,128]{1,0:T(8,128)(2,1)} %copy-done.30, bf16[512,128]{1,0:T(8,128)(2,1)} %copy-done.31, bf16[512,128]{1,0:T(8,128)(2,1)} %copy-done.34, ...), custom_call_target="tpu_custom_call" | custom-call | tf_op jit(solution)/shard_map/add_coords/pallas_call | solution.py:73
  47.8 3.3 %add_coords.11.refs_0_ = f32[128,128]{1,0:T(8,128)} custom-call(s32[4]{0:T(128)} %pad_add_fusion.3.at, bf16[128,8192]{1,0:T(8,128)(2,1)} %act.19, f32[128,128]{1,0:T(8,128)} %add_coords.10.refs_0_, bf16[512,128]{1,0:T(8,128)(2,1)} %copy-done.32, bf16[512,128]{1,0:T(8,128)(2,1)} %copy-done.33, bf16[512,128]{1,0:T(8,128)(2,1)} %copy-done.38, ...), custom_call_target="tpu_custom_call" | custom-call | tf_op jit(solution)/shard_map/add_coords/pallas_call | solution.py:73
  51.1 3.3 %add_coords.17.refs_0_ = f32[128,128]{1,0:T(8,128)} custom-call(s32[4]{0:T(128)} %pad_add_fusion.2.at, bf16[128,8192]{1,0:T(8,128)(2,1)} %act.19, f32[128,128]{1,0:T(8,128)} %add_coords.16.refs_0_, bf16[512,128]{1,0:T(8,128)(2,1)} %copy-done.35, bf16[512,128]{1,0:T(8,128)(2,1)} %copy-done.37, bf16[512,128]{1,0:T(8,128)(2,1)} %copy-done.42, ...), custom_call_target="tpu_custom_call" | custom-call | tf_op jit(solution)/shard_map/add_coords/pallas_call | solution.py:73
  54.5 3.3 %add_coords.12.refs_0_ = f32[128,128]{1,0:T(8,128)} custom-call(s32[4]{0:T(128)} %pad_add_fusion.2.at, bf16[128,8192]{1,0:T(8,128)(2,1)} %act.19, f32[128,128]{1,0:T(8,128)} %add_coords.11.refs_0_, bf16[512,128]{1,0:T(8,128)(2,1)} %copy-done.39, bf16[512,128]{1,0:T(8,128)(2,1)} %copy-done.41, bf16[512,128]{1,0:T(8,128)(2,1)} %copy-done.44, ...), custom_call_target="tpu_custom_call" | custom-call | tf_op jit(solution)/shard_map/add_coords/pallas_call | solution.py:73
  57.8 3.3 %add_coords.18.refs_0_ = f32[128,128]{1,0:T(8,128)} custom-call(s32[4]{0:T(128)} %pad_add_fusion.1.at, bf16[128,8192]{1,0:T(8,128)(2,1)} %act.19, f32[128,128]{1,0:T(8,128)} %add_coords.17.refs_0_, bf16[512,128]{1,0:T(8,128)(2,1)} %copy-done.6, bf16[512,128]{1,0:T(8,128)(2,1)} %copy-done.8, bf16[512,128]{1,0:T(8,128)(2,1)} %copy-done.48, ...), custom_call_target="tpu_custom_call" | custom-call | tf_op jit(solution)/shard_map/add_coords/pallas_call | solution.py:73
  62.5 3.2 %add_coords.19 = bf16[128,128]{1,0:T(8,128)(2,1)} custom-call(s32[4]{0:T(128)} %pad_add_fusion.at, bf16[128,8192]{1,0:T(8,128)(2,1)} %act.19, f32[128,128]{1,0:T(8,128)} %add_coords.18.refs_0_, bf16[256,128]{1,0:T(8,128)(2,1)} %collective-permute-done.43.refs_1_, bf16[256,128]{1,0:T(8,128)(2,1)} %collective-permute-done.44.refs_2_, ...), custom_call_target="tpu_custom_call" | custom-call | tf_op jit(solution)/shard_map/add_coords/pallas_call | solution.py:73
  65.6 1.5 collective-permute-start.47
  68.3 3.3 %add_coords.13.refs_0_ = f32[128,128]{1,0:T(8,128)} custom-call(s32[4]{0:T(128)} %pad_add_fusion.1.at, bf16[128,8192]{1,0:T(8,128)(2,1)} %act.19, f32[128,128]{1,0:T(8,128)} %add_coords.12.refs_0_, bf16[512,128]{1,0:T(8,128)(2,1)} %copy-done.7, bf16[512,128]{1,0:T(8,128)(2,1)} %copy-done.9, bf16[512,128]{1,0:T(8,128)(2,1)} %copy-done.46, ...), custom_call_target="tpu_custom_call" | custom-call | tf_op jit(solution)/shard_map/add_coords/pallas_call | solution.py:73
  73.6 3.2 %add_coords.14 = bf16[128,128]{1,0:T(8,128)(2,1)} custom-call(s32[4]{0:T(128)} %pad_add_fusion.at, bf16[128,8192]{1,0:T(8,128)(2,1)} %act.19, f32[128,128]{1,0:T(8,128)} %add_coords.13.refs_0_, bf16[256,128]{1,0:T(8,128)(2,1)} %collective-permute-done.12.refs_1_, bf16[256,128]{1,0:T(8,128)(2,1)} %copy-done.57, bf16[256,128]{1,0:T(8,128)(2,1)} %copy-done.60, ...), custom_call_target="tpu_custom_call" | custom-call | tf_op jit(solution)/shard_map/add_coords/pallas_call | solution.py:73
  77.6 1.1 collective-permute-start.16
  78.7 1.5 collective-permute-start.17
  81.0 1.8 collective-permute-done.17
  82.8 0.9 collective-permute-done.18
  85.2 3.0 %first_partials.2 = (bf16[448,128]{1,0:T(8,128)(2,1)}, bf16[448,128]{1,0:T(8,128)(2,1)}) custom-call(s32[8]{0:T(128)} %get-tuple-element.50.ids_ref, bf16[512,7168]{1,0:T(8,128)(2,1)} %grad.19, bf16[512,128]{1,0:T(8,128)(2,1)} %constant_dynamic-slice_fusion.2.coord), custom_call_target="tpu_custom_call" | custom-call | tf_op jit(solution)/shard_map/first_partials/pallas_call | solution.py:99
  88.3 1.4 collective-permute-start.19
  91.0 3.0 %first_partials.3 = (bf16[448,128]{1,0:T(8,128)(2,1)}, bf16[448,128]{1,0:T(8,128)(2,1)}) custom-call(s32[8]{0:T(128)} %get-tuple-element.50.ids_ref, bf16[512,7168]{1,0:T(8,128)(2,1)} %grad.19, bf16[512,128]{1,0:T(8,128)(2,1)} %constant_dynamic-slice_fusion.coord), custom_call_target="tpu_custom_call" | custom-call | tf_op jit(solution)/shard_map/first_partials/pallas_call | solution.py:99
  94.0 1.4 collective-permute-start.50
  97.3 3.7 %next_partials.6 = (bf16[896,128]{1,0:T(8,128)(2,1)}, bf16[896,128]{1,0:T(8,128)(2,1)}) custom-call(s32[8]{0:T(128)} %get-tuple-element.50.ids_ref, bf16[512,7168]{1,0:T(8,128)(2,1)} %grad.19, bf16[512,128]{1,0:T(8,128)(2,1)} %constant_dynamic-slice_fusion.2.coord, bf16[448,128]{1,0:T(8,128)(2,1)} %copy-done.53, bf16[448,128]{1,0:T(8,128)(2,1)} %copy-done.55), custom_call_target="tpu_custom_call" | custom-call | tf_op jit(solution)/shard_map/next_partials/pallas_call | solution.py:137
  101.0 1.4 collective-permute-start.21
  104.3 3.7 %next_partials.9 = (bf16[896,128]{1,0:T(8,128)(2,1)}, bf16[896,128]{1,0:T(8,128)(2,1)}) custom-call(s32[8]{0:T(128)} %get-tuple-element.50.ids_ref, bf16[512,7168]{1,0:T(8,128)(2,1)} %grad.19, bf16[512,128]{1,0:T(8,128)(2,1)} %constant_dynamic-slice_fusion.coord, bf16[448,128]{1,0:T(8,128)(2,1)} %copy-done.54, bf16[448,128]{1,0:T(8,128)(2,1)} %copy-done.56), custom_call_target="tpu_custom_call" | custom-call | tf_op jit(solution)/shard_map/next_partials/pallas_call | solution.py:137
  108.0 1.4 collective-permute-start.52
  111.4 3.8 %next_partials.7 = (bf16[896,128]{1,0:T(8,128)(2,1)}, bf16[896,128]{1,0:T(8,128)(2,1)}) custom-call(s32[8]{0:T(128)} %get-tuple-element.50.ids_ref, bf16[512,7168]{1,0:T(8,128)(2,1)} %grad.19, bf16[512,128]{1,0:T(8,128)(2,1)} %constant_dynamic-slice_fusion.2.coord, bf16[896,128]{1,0:T(8,128)(2,1)} %copy-done.11, bf16[896,128]{1,0:T(8,128)(2,1)} %copy-done.16), custom_call_target="tpu_custom_call" | custom-call | tf_op jit(solution)/shard_map/next_partials/pallas_call | solution.py:137
  115.2 1.4 collective-permute-start.23
  118.6 3.8 %next_partials.10 = (bf16[896,128]{1,0:T(8,128)(2,1)}, bf16[896,128]{1,0:T(8,128)(2,1)}) custom-call(s32[8]{0:T(128)} %get-tuple-element.50.ids_ref, bf16[512,7168]{1,0:T(8,128)(2,1)} %grad.19, bf16[512,128]{1,0:T(8,128)(2,1)} %constant_dynamic-slice_fusion.coord, bf16[896,128]{1,0:T(8,128)(2,1)} %copy-done.12, bf16[896,128]{1,0:T(8,128)(2,1)} %copy-done.17), custom_call_target="tpu_custom_call" | custom-call | tf_op jit(solution)/shard_map/next_partials/pallas_call | solution.py:137
  122.4 1.4 collective-permute-start.54
  125.8 3.8 %next_partials.8 = (bf16[896,128]{1,0:T(8,128)(2,1)}, bf16[896,128]{1,0:T(8,128)(2,1)}) custom-call(s32[8]{0:T(128)} %get-tuple-element.50.ids_ref, bf16[512,7168]{1,0:T(8,128)(2,1)} %grad.19, bf16[512,128]{1,0:T(8,128)(2,1)} %constant_dynamic-slice_fusion.2.coord, bf16[896,128]{1,0:T(8,128)(2,1)} %copy-done.13, bf16[896,128]{1,0:T(8,128)(2,1)} %copy-done.18), custom_call_target="tpu_custom_call" | custom-call | tf_op jit(solution)/shard_map/next_partials/pallas_call | solution.py:137
  129.6 1.4 collective-permute-start.25
  133.0 3.8 %next_partials.11 = (bf16[896,128]{1,0:T(8,128)(2,1)}, bf16[896,128]{1,0:T(8,128)(2,1)}) custom-call(s32[8]{0:T(128)} %get-tuple-element.50.ids_ref, bf16[512,7168]{1,0:T(8,128)(2,1)} %grad.19, bf16[512,128]{1,0:T(8,128)(2,1)} %constant_dynamic-slice_fusion.coord, bf16[896,128]{1,0:T(8,128)(2,1)} %copy-done.14, bf16[896,128]{1,0:T(8,128)(2,1)} %copy-done.19), custom_call_target="tpu_custom_call" | custom-call | tf_op jit(solution)/shard_map/next_partials/pallas_call | solution.py:137
  136.8 1.4 collective-permute-start.56
  140.3 3.9 %own_rows.2 = (f32[896,256]{1,0:T(8,128)}, f32[896,256]{1,0:T(8,128)}, bf16[896,128]{1,0:T(8,128)(2,1)}) custom-call(s32[8]{0:T(128)} %get-tuple-element.50.ids_ref, bf16[512,7168]{1,0:T(8,128)(2,1)} %grad.19, bf16[512,128]{1,0:T(8,128)(2,1)} %constant_dynamic-slice_fusion.2.coord, bf16[896,128]{1,0:T(8,128)(2,1)} %copy-done.10, ...), custom_call_target="tpu_custom_call" | custom-call | tf_op jit(solution)/shard_map/own_rows/pallas_call | solution.py:172
  145.1 4.0 %own_rows.3 = (f32[896,256]{1,0:T(8,128)}, f32[896,256]{1,0:T(8,128)}, bf16[896,128]{1,0:T(8,128)(2,1)}) custom-call(s32[8]{0:T(128)} %get-tuple-element.50.ids_ref, bf16[512,7168]{1,0:T(8,128)(2,1)} %grad.19, bf16[512,128]{1,0:T(8,128)(2,1)} %constant_dynamic-slice_fusion.coord, ...), custom_call_target="tpu_custom_call", output_to_operand_aliasing={{0}: (7, {}), {1}: (8, {})} | custom-call | tf_op jit(solution)/shard_map/own_rows/pallas_call | solution.py:172
  149.1 1.7 collective-permute-start.58
  151.1 1.7 collective-permute-start.27
  153.2 4.6 %collective-permute-done.58.refs_1_ = bf16[896,128]{1,0:T(8,128)(2,1)S(1)} collective-permute-done((bf16[896,128]{1,0:T(8,128)(2,1)}, bf16[896,128]{1,0:T(8,128)(2,1)S(1)}, u32[]{:S(2)}, u32[]{:S(2)}) %collective-permute-start.58) | collective-permute-done | bytes 229408 | tf_op jit(solution)/shard_map/ppermute | solution.py:330
  157.8 1.7 collective-permute-start.59
  159.8 2.9 %collective-permute-done.27.refs_0_ = bf16[896,128]{1,0:T(8,128)(2,1)S(1)} collective-permute-done((bf16[896,128]{1,0:T(8,128)(2,1)}, bf16[896,128]{1,0:T(8,128)(2,1)S(1)}, u32[]{:S(2)}, u32[]{:S(2)}) %collective-permute-start.27) | collective-permute-done | bytes 229408 | tf_op jit(solution)/shard_map/ppermute | solution.py:330
  162.7 1.7 collective-permute-start.28
  164.7 2.9 %collective-permute-done.59.refs_1_ = bf16[896,128]{1,0:T(8,128)(2,1)S(1)} collective-permute-done((bf16[896,128]{1,0:T(8,128)(2,1)S(1)}, bf16[896,128]{1,0:T(8,128)(2,1)S(1)}, u32[]{:S(2)}, u32[]{:S(2)}) %collective-permute-start.59) | collective-permute-done | bytes 229408 | tf_op jit(solution)/shard_map/ppermute | solution.py:330
  167.6 1.7 collective-permute-start.60
  169.7 2.9 %collective-permute-done.28.refs_0_ = bf16[896,128]{1,0:T(8,128)(2,1)S(1)} collective-permute-done((bf16[896,128]{1,0:T(8,128)(2,1)S(1)}, bf16[896,128]{1,0:T(8,128)(2,1)S(1)}, u32[]{:S(2)}, u32[]{:S(2)}) %collective-permute-start.28) | collective-permute-done | bytes 229408 | tf_op jit(solution)/shard_map/ppermute | solution.py:330
  172.5 1.7 collective-permute-start.29
  174.6 1.9 collective-permute-done.60.refs_1_
  176.5 1.7 collective-permute-start.61
  178.9 1.7 collective-permute-start.30
  181.7 4.0 %write_update.5.refs_4_ = bf16[1024,7168]{1,0:T(8,128)(2,1)} custom-call(s32[8]{0:T(128)} %get-tuple-element.50.ids_ref, bf16[1024,256]{1,0:T(8,128)(2,1)} %base.9, bf16[896,128]{1,0:T(8,128)(2,1)} %get-tuple-element.33.refs_0_, bf16[896,128]{1,0:T(8,128)(2,1)} %get-tuple-element.44.refs_1_), custom_call_target="tpu_custom_call" | custom-call | tf_op jit(solution)/shard_map/write_update/pallas_call | solution.py:230
  185.8 6.2 %write_update.6.refs_4_ = bf16[1024,7168]{1,0:T(8,128)(2,1)} custom-call(s32[8]{0:T(128)} %get-tuple-element.50.ids_ref, bf16[1024,256]{1,0:T(8,128)(2,1)} %base.9, bf16[896,128]{1,0:T(8,128)(2,1)} %copy-done.24, bf16[896,128]{1,0:T(8,128)(2,1)} %copy-done.22, bf16[896,128]{1,0:T(8,128)(2,1)} %copy-done.25, ...), custom_call_target="tpu_custom_call", output_to_operand_aliasing={{}: (6, {})} | custom-call | tf_op jit(solution)/shard_map/write_update/pallas_call | solution.py:230
  192.0 6.2 %write_update.7.refs_4_ = bf16[1024,7168]{1,0:T(8,128)(2,1)} custom-call(s32[8]{0:T(128)} %get-tuple-element.50.ids_ref, bf16[1024,256]{1,0:T(8,128)(2,1)} %base.9, bf16[896,128]{1,0:T(8,128)(2,1)} %copy-done.28, bf16[896,128]{1,0:T(8,128)(2,1)} %copy-done.26, bf16[896,128]{1,0:T(8,128)(2,1)} %copy-done.29, ...), custom_call_target="tpu_custom_call", output_to_operand_aliasing={{}: (6, {})} | custom-call | tf_op jit(solution)/shard_map/write_update/pallas_call | solution.py:230
  198.2 6.2 %write_update.8.refs_4_ = bf16[1024,7168]{1,0:T(8,128)(2,1)} custom-call(s32[8]{0:T(128)} %get-tuple-element.50.ids_ref, bf16[1024,256]{1,0:T(8,128)(2,1)} %base.9, bf16[896,128]{1,0:T(8,128)(2,1)} %copy-done.4, bf16[896,128]{1,0:T(8,128)(2,1)} %copy-done.2, bf16[896,128]{1,0:T(8,128)(2,1)} %copy-done.5, ...), custom_call_target="tpu_custom_call", output_to_operand_aliasing={{}: (6, {})} | custom-call | tf_op jit(solution)/shard_map/write_update/pallas_call | solution.py:230
  205.8 4.3 %write_update.9 = bf16[1024,7168]{1,0:T(8,128)(2,1)} custom-call(s32[8]{0:T(128)} %get-tuple-element.50.ids_ref, bf16[1024,256]{1,0:T(8,128)(2,1)} %base.9, bf16[448,128]{1,0:T(8,128)(2,1)} %copy-done.51, bf16[448,128]{1,0:T(8,128)(2,1)} %copy-done.49, bf16[448,128]{1,0:T(8,128)(2,1)} %copy-done.52, ...), custom_call_target="tpu_custom_call", output_to_operand_aliasing={{}: (6, {})} | custom-call | tf_op jit(solution)/shard_map/write_update/pallas_call | solution.py:230
  (260 shorter events, 39.9 us)
Async XLA Ops:
  1.8 7.4 %collective-permute-start.31 = (bf16[512,128]{1,0:T(8,128)(2,1)S(1)}, bf16[512,128]{1,0:T(8,128)(2,1)S(1)}, u32[]{:S(2)}, u32[]{:S(2)}) collective-permute-start(bf16[512,128]{1,0:T(8,128)(2,1)S(1)} %constant_dynamic-slice_fusion.1), channel_id=1, source_target_pairs={{0,8},{8,16},{16,24},{24,28},{28,20},{20,12},{12,4},{4,0},{1,9},{9... | collective-permute-start | bytes 393224 | tf_op jit(solution)/shard_map/ppermute | solution.py:283
  4.9 6.3 %collective-permute-start.32 = (bf16[512,128]{1,0:T(8,128)(2,1)S(1)}, bf16[512,128]{1,0:T(8,128)(2,1)S(1)}, u32[]{:S(2)}, u32[]{:S(2)}) collective-permute-start(bf16[512,128]{1,0:T(8,128)(2,1)S(1)} %constant_dynamic-slice_fusion.1), channel_id=1, source_target_pairs={{8,0},{16,8},{24,16},{28,24},{20,28},{12,20},{4,12},{0,4},{9,1},{1... | collective-permute-start | bytes 393224 | tf_op jit(solution)/shard_map/ppermute | solution.py:283
  4.9 7.8 %collective-permute-start = (bf16[512,128]{1,0:T(8,128)(2,1)S(1)}, bf16[512,128]{1,0:T(8,128)(2,1)S(1)}, u32[]{:S(2)}, u32[]{:S(2)}) collective-permute-start(bf16[512,128]{1,0:T(8,128)(2,1)S(1)} %constant_dynamic-slice_fusion.3), channel_id=1, source_target_pairs={{0,8},{8,16},{16,24},{24,28},{28,20},{20,12},{12,4},{4,0},{1,9},{9... | collective-permute-start | bytes 393224 | tf_op jit(solution)/shard_map/ppermute | solution.py:283
  7.0 6.2 %collective-permute-start.1 = (bf16[512,128]{1,0:T(8,128)(2,1)S(1)}, bf16[512,128]{1,0:T(8,128)(2,1)S(1)}, u32[]{:S(2)}, u32[]{:S(2)}) collective-permute-start(bf16[512,128]{1,0:T(8,128)(2,1)S(1)} %constant_dynamic-slice_fusion.3), channel_id=1, source_target_pairs={{8,0},{16,8},{24,16},{28,24},{20,28},{12,20},{4,12},{0,4},{9,1},{1... | collective-permute-start | bytes 393224 | tf_op jit(solution)/shard_map/ppermute | solution.py:283
  11.1 6.4 %collective-permute-start.35 = (bf16[512,128]{1,0:T(8,128)(2,1)S(1)}, bf16[512,128]{1,0:T(8,128)(2,1)S(1)}, u32[]{:S(2)}, u32[]{:S(2)}) collective-permute-start(bf16[512,128]{1,0:T(8,128)(2,1)S(1)} %collective-permute-done.31.refs_1_), channel_id=1, source_target_pairs={{0,8},{8,16},{16,24},{24,28},{28,20},{20,12},{12,4},{4,0},{1,9},{9... | collective-permute-start | bytes 393224 | tf_op jit(solution)/shard_map/ppermute | solution.py:283
  12.7 5.6 %collective-permute-start.36 = (bf16[512,128]{1,0:T(8,128)(2,1)S(1)}, bf16[512,128]{1,0:T(8,128)(2,1)S(1)}, u32[]{:S(2)}, u32[]{:S(2)}) collective-permute-start(bf16[512,128]{1,0:T(8,128)(2,1)S(1)} %collective-permute-done.32.refs_2_), channel_id=1, source_target_pairs={{8,0},{16,8},{24,16},{28,24},{20,28},{12,20},{4,12},{0,4},{9,1},{1... | collective-permute-start | bytes 393224 | tf_op jit(solution)/shard_map/ppermute | solution.py:283
  13.2 5.2 %collective-permute-start.2 = (bf16[512,128]{1,0:T(8,128)(2,1)S(1)}, bf16[512,128]{1,0:T(8,128)(2,1)S(1)}, u32[]{:S(2)}, u32[]{:S(2)}) collective-permute-start(bf16[512,128]{1,0:T(8,128)(2,1)S(1)} %collective-permute-done.refs_1_), channel_id=1, source_target_pairs={{0,1},{1,0},{2,3},{3,2},{4,5},{5,4},{6,7},{7,6},{8,9},{9,8},{10,11... | collective-permute-start | bytes 393224 | tf_op jit(solution)/shard_map/ppermute | solution.py:285
  13.2 6.8 %collective-permute-start.3 = (bf16[512,128]{1,0:T(8,128)(2,1)S(1)}, bf16[512,128]{1,0:T(8,128)(2,1)S(1)}, u32[]{:S(2)}, u32[]{:S(2)}) collective-permute-start(bf16[512,128]{1,0:T(8,128)(2,1)S(1)} %collective-permute-done.1.refs_2_), channel_id=1, source_target_pairs={{0,1},{1,0},{2,3},{3,2},{4,5},{5,4},{6,7},{7,6},{8,9},{9,8},{10,11... | collective-permute-start | bytes 393224 | tf_op jit(solution)/shard_map/ppermute | solution.py:285
  13.7 8.0 %collective-permute-start.4 = (bf16[512,128]{1,0:T(8,128)(2,1)S(1)}, bf16[512,128]{1,0:T(8,128)(2,1)S(1)}, u32[]{:S(2)}, u32[]{:S(2)}) collective-permute-start(bf16[512,128]{1,0:T(8,128)(2,1)S(1)} %collective-permute-done.refs_1_), channel_id=1, source_target_pairs={{0,8},{8,16},{16,24},{24,28},{28,20},{20,12},{12,4},{4,0},{1,9},{9... | collective-permute-start | bytes 393224 | tf_op jit(solution)/shard_map/ppermute | solution.py:283
  17.5 5.0 %collective-permute-start.5 = (bf16[512,128]{1,0:T(8,128)(2,1)S(1)}, bf16[512,128]{1,0:T(8,128)(2,1)S(1)}, u32[]{:S(2)}, u32[]{:S(2)}) collective-permute-start(bf16[512,128]{1,0:T(8,128)(2,1)S(1)} %collective-permute-done.1.refs_2_), channel_id=1, source_target_pairs={{8,0},{16,8},{24,16},{28,24},{20,28},{12,20},{4,12},{0,4},{9,1},{1... | collective-permute-start | bytes 393224 | tf_op jit(solution)/shard_map/ppermute | solution.py:283
  18.4 5.9 %collective-permute-start.39 = (bf16[512,128]{1,0:T(8,128)(2,1)S(1)}, bf16[512,128]{1,0:T(8,128)(2,1)S(1)}, u32[]{:S(2)}, u32[]{:S(2)}) collective-permute-start(bf16[512,128]{1,0:T(8,128)(2,1)S(1)} %collective-permute-done.35.refs_1_), channel_id=1, source_target_pairs={{0,8},{8,16},{16,24},{24,28},{28,20},{20,12},{12,4},{4,0},{1,9},{9... | collective-permute-start | bytes 393224 | tf_op jit(solution)/shard_map/ppermute | solution.py:283
  20.0 6.2 %collective-permute-start.40 = (bf16[512,128]{1,0:T(8,128)(2,1)S(1)}, bf16[512,128]{1,0:T(8,128)(2,1)S(1)}, u32[]{:S(2)}, u32[]{:S(2)}) collective-permute-start(bf16[512,128]{1,0:T(8,128)(2,1)S(1)} %collective-permute-done.36.refs_2_), channel_id=1, source_target_pairs={{8,0},{16,8},{24,16},{28,24},{20,28},{12,20},{4,12},{0,4},{9,1},{1... | collective-permute-start | bytes 393224 | tf_op jit(solution)/shard_map/ppermute | solution.py:283
  21.7 7.1 %collective-permute-start.38 = (bf16[512,128]{1,0:T(8,128)(2,1)S(1)}, bf16[512,128]{1,0:T(8,128)(2,1)S(1)}, u32[]{:S(2)}, u32[]{:S(2)}) collective-permute-start(bf16[512,128]{1,0:T(8,128)(2,1)S(1)} %collective-permute-done.36.refs_2_), channel_id=1, source_target_pairs={{0,1},{1,0},{2,3},{3,2},{4,5},{5,4},{6,7},{7,6},{8,9},{9,8},{10,11... | collective-permute-start | bytes 393224 | tf_op jit(solution)/shard_map/ppermute | solution.py:285
  22.5 7.8 %collective-permute-start.6 = (bf16[512,128]{1,0:T(8,128)(2,1)S(1)}, bf16[512,128]{1,0:T(8,128)(2,1)S(1)}, u32[]{:S(2)}, u32[]{:S(2)}) collective-permute-start(bf16[512,128]{1,0:T(8,128)(2,1)S(1)} %collective-permute-done.4.refs_1_), channel_id=1, source_target_pairs={{0,1},{1,0},{2,3},{3,2},{4,5},{5,4},{6,7},{7,6},{8,9},{9,8},{10,11... | collective-permute-start | bytes 393224 | tf_op jit(solution)/shard_map/ppermute | solution.py:285
  22.5 8.4 %collective-permute-start.8 = (bf16[512,128]{1,0:T(8,128)(2,1)S(1)}, bf16[512,128]{1,0:T(8,128)(2,1)S(1)}, u32[]{:S(2)}, u32[]{:S(2)}) collective-permute-start(bf16[512,128]{1,0:T(8,128)(2,1)S(1)} %collective-permute-done.4.refs_1_), channel_id=1, source_target_pairs={{0,8},{8,16},{16,24},{24,28},{28,20},{20,12},{12,4},{4,0},{1,9},{9... | collective-permute-start | bytes 393224 | tf_op jit(solution)/shard_map/ppermute | solution.py:283
  24.3 6.6 %collective-permute-start.7 = (bf16[512,128]{1,0:T(8,128)(2,1)S(1)}, bf16[512,128]{1,0:T(8,128)(2,1)S(1)}, u32[]{:S(2)}, u32[]{:S(2)}) collective-permute-start(bf16[512,128]{1,0:T(8,128)(2,1)S(1)} %collective-permute-done.5.refs_2_), channel_id=1, source_target_pairs={{0,1},{1,0},{2,3},{3,2},{4,5},{5,4},{6,7},{7,6},{8,9},{9,8},{10,11... | collective-permute-start | bytes 393224 | tf_op jit(solution)/shard_map/ppermute | solution.py:285
  26.2 7.6 %collective-permute-start.9 = (bf16[512,128]{1,0:T(8,128)(2,1)S(1)}, bf16[512,128]{1,0:T(8,128)(2,1)S(1)}, u32[]{:S(2)}, u32[]{:S(2)}) collective-permute-start(bf16[512,128]{1,0:T(8,128)(2,1)S(1)} %collective-permute-done.5.refs_2_), channel_id=1, source_target_pairs={{8,0},{16,8},{24,16},{28,24},{20,28},{12,20},{4,12},{0,4},{9,1},{1... | collective-permute-start | bytes 393224 | tf_op jit(solution)/shard_map/ppermute | solution.py:283
  28.8 6.4 %collective-permute-start.43 = (bf16[256,128]{1,0:T(8,128)(2,1)S(1)}, bf16[256,128]{1,0:T(8,128)(2,1)}, u32[]{:S(2)}, u32[]{:S(2)}) collective-permute-start(bf16[256,128]{1,0:T(8,128)(2,1)S(1)} %slice.109), channel_id=1, source_target_pairs={{0,8},{8,16},{16,24},{24,28},{28,20},{20,12},{12,4},{4,0},{1,9},{9... | collective-permute-start | bytes 196616 | tf_op jit(solution)/shard_map/ppermute | solution.py:283
  30.3 5.0 %collective-permute-start.44 = (bf16[256,128]{1,0:T(8,128)(2,1)S(1)}, bf16[256,128]{1,0:T(8,128)(2,1)}, u32[]{:S(2)}, u32[]{:S(2)}) collective-permute-start(bf16[256,128]{1,0:T(8,128)(2,1)S(1)} %slice.110), channel_id=1, source_target_pairs={{8,0},{16,8},{24,16},{28,24},{20,28},{12,20},{4,12},{0,4},{9,1},{1... | collective-permute-start | bytes 196616 | tf_op jit(solution)/shard_map/ppermute | solution.py:283
  30.9 12.5 %collective-permute-start.41 = (bf16[512,128]{1,0:T(8,128)(2,1)S(1)}, bf16[512,128]{1,0:T(8,128)(2,1)S(1)}, u32[]{:S(2)}, u32[]{:S(2)}) collective-permute-start(bf16[512,128]{1,0:T(8,128)(2,1)S(1)} %collective-permute-done.39.refs_1_), channel_id=1, source_target_pairs={{0,1},{1,0},{2,3},{3,2},{4,5},{5,4},{6,7},{7,6},{8,9},{9,8},{10,11... | collective-permute-start | bytes 393224 | tf_op jit(solution)/shard_map/ppermute | solution.py:285
  30.9 12.4 %collective-permute-start.42 = (bf16[512,128]{1,0:T(8,128)(2,1)S(1)}, bf16[512,128]{1,0:T(8,128)(2,1)}, u32[]{:S(2)}, u32[]{:S(2)}) collective-permute-start(bf16[512,128]{1,0:T(8,128)(2,1)S(1)} %collective-permute-done.40.refs_2_), channel_id=1, source_target_pairs={{0,1},{1,0},{2,3},{3,2},{4,5},{5,4},{6,7},{7,6},{8,9},{9,8},{10,11... | collective-permute-start | bytes 393224 | tf_op jit(solution)/shard_map/ppermute | solution.py:285
  33.9 8.8 %collective-permute-start.12 = (bf16[256,128]{1,0:T(8,128)(2,1)}, bf16[256,128]{1,0:T(8,128)(2,1)}, u32[]{:S(2)}, u32[]{:S(2)}) collective-permute-start(bf16[256,128]{1,0:T(8,128)(2,1)} %slice.106), channel_id=1, source_target_pairs={{0,8},{8,16},{16,24},{24,28},{28,20},{20,12},{12,4},{4,0},{1,9},{9... | collective-permute-start | bytes 196616 | tf_op jit(solution)/shard_map/ppermute | solution.py:283
  35.2 31.9 %collective-permute-start.10 = (bf16[512,128]{1,0:T(8,128)(2,1)S(1)}, bf16[512,128]{1,0:T(8,128)(2,1)S(1)}, u32[]{:S(2)}, u32[]{:S(2)}) collective-permute-start(bf16[512,128]{1,0:T(8,128)(2,1)S(1)} %collective-permute-done.8.refs_1_), channel_id=1, source_target_pairs={{0,1},{1,0},{2,3},{3,2},{4,5},{5,4},{6,7},{7,6},{8,9},{9,8},{10,11... | collective-permute-start | bytes 393224 | tf_op jit(solution)/shard_map/ppermute | solution.py:285
  35.2 32.4 %collective-permute-start.11 = (bf16[512,128]{1,0:T(8,128)(2,1)S(1)}, bf16[512,128]{1,0:T(8,128)(2,1)S(1)}, u32[]{:S(2)}, u32[]{:S(2)}) collective-permute-start(bf16[512,128]{1,0:T(8,128)(2,1)S(1)} %collective-permute-done.9.refs_2_), channel_id=1, source_target_pairs={{0,1},{1,0},{2,3},{3,2},{4,5},{5,4},{6,7},{7,6},{8,9},{9,8},{10,11... | collective-permute-start | bytes 393224 | tf_op jit(solution)/shard_map/ppermute | solution.py:285
  42.7 18.4 %collective-permute-start.13 = (bf16[256,128]{1,0:T(8,128)(2,1)S(1)}, bf16[256,128]{1,0:T(8,128)(2,1)S(1)}, u32[]{:S(2)}, u32[]{:S(2)}) collective-permute-start(bf16[256,128]{1,0:T(8,128)(2,1)S(1)} %slice.107), channel_id=1, source_target_pairs={{8,0},{16,8},{24,16},{28,24},{20,28},{12,20},{4,12},{0,4},{9,1},{1... | collective-permute-start | bytes 196616 | tf_op jit(solution)/shard_map/ppermute | solution.py:283
  43.4 17.8 %collective-permute-start.45 = (bf16[256,128]{1,0:T(8,128)(2,1)}, bf16[256,128]{1,0:T(8,128)(2,1)S(1)}, u32[]{:S(2)}, u32[]{:S(2)}) collective-permute-start(bf16[256,128]{1,0:T(8,128)(2,1)} %collective-permute-done.43.refs_1_), channel_id=1, source_target_pairs={{0,1},{1,0},{2,3},{3,2},{4,5},{5,4},{6,7},{7,6},{8,9},{9,8},{10,11... | collective-permute-start | bytes 196616 | tf_op jit(solution)/shard_map/ppermute | solution.py:285
  43.4 18.2 %collective-permute-start.46 = (bf16[256,128]{1,0:T(8,128)(2,1)}, bf16[256,128]{1,0:T(8,128)(2,1)S(1)}, u32[]{:S(2)}, u32[]{:S(2)}) collective-permute-start(bf16[256,128]{1,0:T(8,128)(2,1)} %collective-permute-done.44.refs_2_), channel_id=1, source_target_pairs={{0,1},{1,0},{2,3},{3,2},{4,5},{5,4},{6,7},{7,6},{8,9},{9,8},{10,11... | collective-permute-start | bytes 196616 | tf_op jit(solution)/shard_map/ppermute | solution.py:285
  61.1 11.3 %collective-permute-start.14 = (bf16[256,128]{1,0:T(8,128)(2,1)}, bf16[256,128]{1,0:T(8,128)(2,1)S(1)}, u32[]{:S(2)}, u32[]{:S(2)}) collective-permute-start(bf16[256,128]{1,0:T(8,128)(2,1)} %collective-permute-done.12.refs_1_), channel_id=1, source_target_pairs={{0,1},{1,0},{2,3},{3,2},{4,5},{5,4},{6,7},{7,6},{8,9},{9,8},{10,11... | collective-permute-start | bytes 196616 | tf_op jit(solution)/shard_map/ppermute | solution.py:285
  61.2 11.2 %collective-permute-start.15 = (bf16[256,128]{1,0:T(8,128)(2,1)S(1)}, bf16[256,128]{1,0:T(8,128)(2,1)S(1)}, u32[]{:S(2)}, u32[]{:S(2)}) collective-permute-start(bf16[256,128]{1,0:T(8,128)(2,1)S(1)} %collective-permute-done.13.refs_2_), channel_id=1, source_target_pairs={{0,1},{1,0},{2,3},{3,2},{4,5},{5,4},{6,7},{7,6},{8,9},{9,8},{10,11... | collective-permute-start | bytes 196616 | tf_op jit(solution)/shard_map/ppermute | solution.py:285
  65.6 14.6 %collective-permute-start.47 = (bf16[128,128]{1,0:T(8,128)(2,1)}, bf16[128,128]{1,0:T(8,128)(2,1)S(1)}, u32[]{:S(2)}, u32[]{:S(2)}) collective-permute-start(bf16[128,128]{1,0:T(8,128)(2,1)} %add_coords.19), channel_id=1, source_target_pairs={{0,3},{1,0},{2,1},{3,2},{4,7},{5,4},{6,5},{7,6},{8,11},{9,8},{10,9... | collective-permute-start | bytes 98312 | tf_op jit(solution)/shard_map/ppermute | solution.py:303
  67.1 13.1 %collective-permute-start.48 = (bf16[128,128]{1,0:T(8,128)(2,1)}, bf16[128,128]{1,0:T(8,128)(2,1)S(1)}, u32[]{:S(2)}, u32[]{:S(2)}) collective-permute-start(bf16[128,128]{1,0:T(8,128)(2,1)} %add_coords.19), channel_id=1, source_target_pairs={{0,2},{1,3},{2,0},{3,1},{4,6},{5,7},{6,4},{7,5},{8,10},{9,11},{10,... | collective-permute-start | bytes 98312 | tf_op jit(solution)/shard_map/ppermute | solution.py:303
  67.7 12.6 %collective-permute-start.49 = (bf16[128,128]{1,0:T(8,128)(2,1)}, bf16[128,128]{1,0:T(8,128)(2,1)S(1)}, u32[]{:S(2)}, u32[]{:S(2)}) collective-permute-start(bf16[128,128]{1,0:T(8,128)(2,1)} %add_coords.19), channel_id=1, source_target_pairs={{0,1},{1,2},{2,3},{3,0},{4,5},{5,6},{6,7},{7,4},{8,9},{9,10},{10,1... | collective-permute-start | bytes 98312 | tf_op jit(solution)/shard_map/ppermute | solution.py:303
  88.3 7.8 %collective-permute-start.19 = (bf16[448,128]{1,0:T(8,128)(2,1)}, bf16[448,128]{1,0:T(8,128)(2,1)S(1)}, u32[]{:S(2)}, u32[]{:S(2)}) collective-permute-start(bf16[448,128]{1,0:T(8,128)(2,1)} %get-tuple-element.25), channel_id=1, source_target_pairs={{0,8},{8,16},{16,24},{24,28},{28,20},{20,12},{12,4},{4,0},{1,9},{9... | collective-permute-start | bytes 344072 | tf_op jit(solution)/shard_map/ppermute | solution.py:311
  89.6 6.4 %collective-permute-start.20 = (bf16[448,128]{1,0:T(8,128)(2,1)}, bf16[448,128]{1,0:T(8,128)(2,1)S(1)}, u32[]{:S(2)}, u32[]{:S(2)}) collective-permute-start(bf16[448,128]{1,0:T(8,128)(2,1)} %get-tuple-element.26), channel_id=1, source_target_pairs={{8,0},{16,8},{24,16},{28,24},{20,28},{12,20},{4,12},{0,4},{9,1},{1... | collective-permute-start | bytes 344072 | tf_op jit(solution)/shard_map/ppermute | solution.py:311
  94.0 9.0 %collective-permute-start.50 = (bf16[448,128]{1,0:T(8,128)(2,1)}, bf16[448,128]{1,0:T(8,128)(2,1)S(1)}, u32[]{:S(2)}, u32[]{:S(2)}) collective-permute-start(bf16[448,128]{1,0:T(8,128)(2,1)} %get-tuple-element.34), channel_id=1, source_target_pairs={{0,8},{8,16},{16,24},{24,28},{28,20},{20,12},{12,4},{4,0},{1,9},{9... | collective-permute-start | bytes 344072 | tf_op jit(solution)/shard_map/ppermute | solution.py:311
  95.4 7.7 %collective-permute-start.51 = (bf16[448,128]{1,0:T(8,128)(2,1)}, bf16[448,128]{1,0:T(8,128)(2,1)S(1)}, u32[]{:S(2)}, u32[]{:S(2)}) collective-permute-start(bf16[448,128]{1,0:T(8,128)(2,1)} %get-tuple-element.35), channel_id=1, source_target_pairs={{8,0},{16,8},{24,16},{28,24},{20,28},{12,20},{4,12},{0,4},{9,1},{1... | collective-permute-start | bytes 344072 | tf_op jit(solution)/shard_map/ppermute | solution.py:311
  101.0 9.0 %collective-permute-start.21 = (bf16[896,128]{1,0:T(8,128)(2,1)}, bf16[896,128]{1,0:T(8,128)(2,1)S(1)}, u32[]{:S(2)}, u32[]{:S(2)}) collective-permute-start(bf16[896,128]{1,0:T(8,128)(2,1)} %get-tuple-element.27), channel_id=1, source_target_pairs={{0,8},{8,16},{16,24},{24,28},{28,20},{20,12},{12,4},{4,0},{1,9},{9... | collective-permute-start | bytes 688136 | tf_op jit(solution)/shard_map/ppermute | solution.py:317
  102.4 7.7 %collective-permute-start.22 = (bf16[896,128]{1,0:T(8,128)(2,1)}, bf16[896,128]{1,0:T(8,128)(2,1)S(1)}, u32[]{:S(2)}, u32[]{:S(2)}) collective-permute-start(bf16[896,128]{1,0:T(8,128)(2,1)} %get-tuple-element.28), channel_id=1, source_target_pairs={{8,0},{16,8},{24,16},{28,24},{20,28},{12,20},{4,12},{0,4},{9,1},{1... | collective-permute-start | bytes 688136 | tf_op jit(solution)/shard_map/ppermute | solution.py:317
  108.0 9.2 %collective-permute-start.52 = (bf16[896,128]{1,0:T(8,128)(2,1)}, bf16[896,128]{1,0:T(8,128)(2,1)S(1)}, u32[]{:S(2)}, u32[]{:S(2)}) collective-permute-start(bf16[896,128]{1,0:T(8,128)(2,1)} %get-tuple-element.36), channel_id=1, source_target_pairs={{0,8},{8,16},{16,24},{24,28},{28,20},{20,12},{12,4},{4,0},{1,9},{9... | collective-permute-start | bytes 688136 | tf_op jit(solution)/shard_map/ppermute | solution.py:317
  109.4 7.9 %collective-permute-start.53 = (bf16[896,128]{1,0:T(8,128)(2,1)}, bf16[896,128]{1,0:T(8,128)(2,1)S(1)}, u32[]{:S(2)}, u32[]{:S(2)}) collective-permute-start(bf16[896,128]{1,0:T(8,128)(2,1)} %get-tuple-element.37), channel_id=1, source_target_pairs={{8,0},{16,8},{24,16},{28,24},{20,28},{12,20},{4,12},{0,4},{9,1},{1... | collective-permute-start | bytes 688136 | tf_op jit(solution)/shard_map/ppermute | solution.py:317
  115.2 9.2 %collective-permute-start.23 = (bf16[896,128]{1,0:T(8,128)(2,1)}, bf16[896,128]{1,0:T(8,128)(2,1)S(1)}, u32[]{:S(2)}, u32[]{:S(2)}) collective-permute-start(bf16[896,128]{1,0:T(8,128)(2,1)} %get-tuple-element.29), channel_id=1, source_target_pairs={{0,8},{8,16},{16,24},{24,28},{28,20},{20,12},{12,4},{4,0},{1,9},{9... | collective-permute-start | bytes 688136 | tf_op jit(solution)/shard_map/ppermute | solution.py:317
  116.6 7.9 %collective-permute-start.24 = (bf16[896,128]{1,0:T(8,128)(2,1)}, bf16[896,128]{1,0:T(8,128)(2,1)S(1)}, u32[]{:S(2)}, u32[]{:S(2)}) collective-permute-start(bf16[896,128]{1,0:T(8,128)(2,1)} %get-tuple-element.30), channel_id=1, source_target_pairs={{8,0},{16,8},{24,16},{28,24},{20,28},{12,20},{4,12},{0,4},{9,1},{1... | collective-permute-start | bytes 688136 | tf_op jit(solution)/shard_map/ppermute | solution.py:317
  122.4 9.2 %collective-permute-start.54 = (bf16[896,128]{1,0:T(8,128)(2,1)}, bf16[896,128]{1,0:T(8,128)(2,1)S(1)}, u32[]{:S(2)}, u32[]{:S(2)}) collective-permute-start(bf16[896,128]{1,0:T(8,128)(2,1)} %get-tuple-element.38), channel_id=1, source_target_pairs={{0,8},{8,16},{16,24},{24,28},{28,20},{20,12},{12,4},{4,0},{1,9},{9... | collective-permute-start | bytes 688136 | tf_op jit(solution)/shard_map/ppermute | solution.py:317
  123.8 7.9 %collective-permute-start.55 = (bf16[896,128]{1,0:T(8,128)(2,1)}, bf16[896,128]{1,0:T(8,128)(2,1)S(1)}, u32[]{:S(2)}, u32[]{:S(2)}) collective-permute-start(bf16[896,128]{1,0:T(8,128)(2,1)} %get-tuple-element.39), channel_id=1, source_target_pairs={{8,0},{16,8},{24,16},{28,24},{20,28},{12,20},{4,12},{0,4},{9,1},{1... | collective-permute-start | bytes 688136 | tf_op jit(solution)/shard_map/ppermute | solution.py:317
  129.6 9.2 %collective-permute-start.25 = (bf16[896,128]{1,0:T(8,128)(2,1)}, bf16[896,128]{1,0:T(8,128)(2,1)S(1)}, u32[]{:S(2)}, u32[]{:S(2)}) collective-permute-start(bf16[896,128]{1,0:T(8,128)(2,1)} %get-tuple-element.31), channel_id=1, source_target_pairs={{0,8},{8,16},{16,24},{24,28},{28,20},{20,12},{12,4},{4,0},{1,9},{9... | collective-permute-start | bytes 688136 | tf_op jit(solution)/shard_map/ppermute | solution.py:317
  131.0 8.1 %collective-permute-start.26 = (bf16[896,128]{1,0:T(8,128)(2,1)}, bf16[896,128]{1,0:T(8,128)(2,1)S(1)}, u32[]{:S(2)}, u32[]{:S(2)}) collective-permute-start(bf16[896,128]{1,0:T(8,128)(2,1)} %get-tuple-element.32), channel_id=1, source_target_pairs={{8,0},{16,8},{24,16},{28,24},{20,28},{12,20},{4,12},{0,4},{9,1},{1... | collective-permute-start | bytes 688136 | tf_op jit(solution)/shard_map/ppermute | solution.py:317
  136.8 7.3 %collective-permute-start.56 = (bf16[896,128]{1,0:T(8,128)(2,1)}, bf16[896,128]{1,0:T(8,128)(2,1)S(1)}, u32[]{:S(2)}, u32[]{:S(2)}) collective-permute-start(bf16[896,128]{1,0:T(8,128)(2,1)} %get-tuple-element.40), channel_id=1, source_target_pairs={{0,8},{8,16},{16,24},{24,28},{28,20},{20,12},{12,4},{4,0},{1,9},{9... | collective-permute-start | bytes 688136 | tf_op jit(solution)/shard_map/ppermute | solution.py:317
  138.2 6.2 %collective-permute-start.57 = (bf16[896,128]{1,0:T(8,128)(2,1)}, bf16[896,128]{1,0:T(8,128)(2,1)S(1)}, u32[]{:S(2)}, u32[]{:S(2)}) collective-permute-start(bf16[896,128]{1,0:T(8,128)(2,1)} %get-tuple-element.41), channel_id=1, source_target_pairs={{8,0},{16,8},{24,16},{28,24},{20,28},{12,20},{4,12},{0,4},{9,1},{1... | collective-permute-start | bytes 688136 | tf_op jit(solution)/shard_map/ppermute | solution.py:317
  149.1 8.7 %collective-permute-start.58 = (bf16[896,128]{1,0:T(8,128)(2,1)}, bf16[896,128]{1,0:T(8,128)(2,1)S(1)}, u32[]{:S(2)}, u32[]{:S(2)}) collective-permute-start(bf16[896,128]{1,0:T(8,128)(2,1)} %get-tuple-element.44.refs_1_), channel_id=1, source_target_pairs={{0,8},{8,16},{16,24},{24,28},{28,20},{20,12},{12,4},{4,0},{1,9},{9... | collective-permute-start | bytes 688136 | tf_op jit(solution)/shard_map/ppermute | solution.py:330
  150.8 8.7 %collective-permute-start.66 = (bf16[896,128]{1,0:T(8,128)(2,1)}, bf16[896,128]{1,0:T(8,128)(2,1)S(1)}, u32[]{:S(2)}, u32[]{:S(2)}) collective-permute-start(bf16[896,128]{1,0:T(8,128)(2,1)} %get-tuple-element.44.refs_1_), channel_id=1, source_target_pairs={{8,0},{16,8},{24,16},{28,24},{20,28},{12,20},{4,12},{0,4},{9,1},{1... | collective-permute-start | bytes 688136 | tf_op jit(solution)/shard_map/ppermute | solution.py:330
  151.1 11.6 %collective-permute-start.27 = (bf16[896,128]{1,0:T(8,128)(2,1)}, bf16[896,128]{1,0:T(8,128)(2,1)S(1)}, u32[]{:S(2)}, u32[]{:S(2)}) collective-permute-start(bf16[896,128]{1,0:T(8,128)(2,1)} %get-tuple-element.33.refs_0_), channel_id=1, source_target_pairs={{0,8},{8,16},{16,24},{24,28},{28,20},{20,12},{12,4},{4,0},{1,9},{9... | collective-permute-start | bytes 688136 | tf_op jit(solution)/shard_map/ppermute | solution.py:330
  152.8 11.6 %collective-permute-start.62 = (bf16[896,128]{1,0:T(8,128)(2,1)}, bf16[896,128]{1,0:T(8,128)(2,1)S(1)}, u32[]{:S(2)}, u32[]{:S(2)}) collective-permute-start(bf16[896,128]{1,0:T(8,128)(2,1)} %get-tuple-element.33.refs_0_), channel_id=1, source_target_pairs={{8,0},{16,8},{24,16},{28,24},{20,28},{12,20},{4,12},{0,4},{9,1},{1... | collective-permute-start | bytes 688136 | tf_op jit(solution)/shard_map/ppermute | solution.py:330
  157.8 9.8 %collective-permute-start.59 = (bf16[896,128]{1,0:T(8,128)(2,1)S(1)}, bf16[896,128]{1,0:T(8,128)(2,1)S(1)}, u32[]{:S(2)}, u32[]{:S(2)}) collective-permute-start(bf16[896,128]{1,0:T(8,128)(2,1)S(1)} %collective-permute-done.58.refs_1_), channel_id=1, source_target_pairs={{0,8},{8,16},{16,24},{24,28},{28,20},{20,12},{12,4},{4,0},{1,9},{9... | collective-permute-start | bytes 688136 | tf_op jit(solution)/shard_map/ppermute | solution.py:330
  159.5 9.8 %collective-permute-start.67 = (bf16[896,128]{1,0:T(8,128)(2,1)S(1)}, bf16[896,128]{1,0:T(8,128)(2,1)S(1)}, u32[]{:S(2)}, u32[]{:S(2)}) collective-permute-start(bf16[896,128]{1,0:T(8,128)(2,1)S(1)} %collective-permute-done.66.refs_3_), channel_id=1, source_target_pairs={{8,0},{16,8},{24,16},{28,24},{20,28},{12,20},{4,12},{0,4},{9,1},{1... | collective-permute-start | bytes 688136 | tf_op jit(solution)/shard_map/ppermute | solution.py:330
  162.7 9.8 %collective-permute-start.28 = (bf16[896,128]{1,0:T(8,128)(2,1)S(1)}, bf16[896,128]{1,0:T(8,128)(2,1)S(1)}, u32[]{:S(2)}, u32[]{:S(2)}) collective-permute-start(bf16[896,128]{1,0:T(8,128)(2,1)S(1)} %collective-permute-done.27.refs_0_), channel_id=1, source_target_pairs={{0,8},{8,16},{16,24},{24,28},{28,20},{20,12},{12,4},{4,0},{1,9},{9... | collective-permute-start | bytes 688136 | tf_op jit(solution)/shard_map/ppermute | solution.py:330
  164.4 9.8 %collective-permute-start.63 = (bf16[896,128]{1,0:T(8,128)(2,1)S(1)}, bf16[896,128]{1,0:T(8,128)(2,1)S(1)}, u32[]{:S(2)}, u32[]{:S(2)}) collective-permute-start(bf16[896,128]{1,0:T(8,128)(2,1)S(1)} %collective-permute-done.62.refs_2_), channel_id=1, source_target_pairs={{8,0},{16,8},{24,16},{28,24},{20,28},{12,20},{4,12},{0,4},{9,1},{1... | collective-permute-start | bytes 688136 | tf_op jit(solution)/shard_map/ppermute | solution.py:330
  167.6 8.8 %collective-permute-start.60 = (bf16[896,128]{1,0:T(8,128)(2,1)S(1)}, bf16[896,128]{1,0:T(8,128)(2,1)S(1)}, u32[]{:S(2)}, u32[]{:S(2)}) collective-permute-start(bf16[896,128]{1,0:T(8,128)(2,1)S(1)} %collective-permute-done.59.refs_1_), channel_id=1, source_target_pairs={{0,8},{8,16},{16,24},{24,28},{28,20},{20,12},{12,4},{4,0},{1,9},{9... | collective-permute-start | bytes 688136 | tf_op jit(solution)/shard_map/ppermute | solution.py:330
  169.3 8.9 %collective-permute-start.68 = (bf16[896,128]{1,0:T(8,128)(2,1)S(1)}, bf16[896,128]{1,0:T(8,128)(2,1)S(1)}, u32[]{:S(2)}, u32[]{:S(2)}) collective-permute-start(bf16[896,128]{1,0:T(8,128)(2,1)S(1)} %collective-permute-done.67.refs_3_), channel_id=1, source_target_pairs={{8,0},{16,8},{24,16},{28,24},{20,28},{12,20},{4,12},{0,4},{9,1},{1... | collective-permute-start | bytes 688136 | tf_op jit(solution)/shard_map/ppermute | solution.py:330
  172.5 6.4 %collective-permute-start.29 = (bf16[896,128]{1,0:T(8,128)(2,1)S(1)}, bf16[896,128]{1,0:T(8,128)(2,1)S(1)}, u32[]{:S(2)}, u32[]{:S(2)}) collective-permute-start(bf16[896,128]{1,0:T(8,128)(2,1)S(1)} %collective-permute-done.28.refs_0_), channel_id=1, source_target_pairs={{0,8},{8,16},{16,24},{24,28},{28,20},{20,12},{12,4},{4,0},{1,9},{9... | collective-permute-start | bytes 688136 | tf_op jit(solution)/shard_map/ppermute | solution.py:330
  174.2 6.5 %collective-permute-start.64 = (bf16[896,128]{1,0:T(8,128)(2,1)S(1)}, bf16[896,128]{1,0:T(8,128)(2,1)S(1)}, u32[]{:S(2)}, u32[]{:S(2)}) collective-permute-start(bf16[896,128]{1,0:T(8,128)(2,1)S(1)} %collective-permute-done.63.refs_2_), channel_id=1, source_target_pairs={{8,0},{16,8},{24,16},{28,24},{20,28},{12,20},{4,12},{0,4},{9,1},{1... | collective-permute-start | bytes 688136 | tf_op jit(solution)/shard_map/ppermute | solution.py:330
  176.5 27.9 %collective-permute-start.61 = (bf16[448,128]{1,0:T(8,128)(2,1)S(1)}, bf16[448,128]{1,0:T(8,128)(2,1)S(1)}, u32[]{:S(2)}, u32[]{:S(2)}) collective-permute-start(bf16[448,128]{1,0:T(8,128)(2,1)S(1)} %slice.111), channel_id=1, source_target_pairs={{0,8},{8,16},{16,24},{24,28},{28,20},{20,12},{12,4},{4,0},{1,9},{9... | collective-permute-start | bytes 344072 | tf_op jit(solution)/shard_map/ppermute | solution.py:335
  178.2 26.2 %collective-permute-start.69 = (bf16[448,128]{1,0:T(8,128)(2,1)S(1)}, bf16[448,128]{1,0:T(8,128)(2,1)S(1)}, u32[]{:S(2)}, u32[]{:S(2)}) collective-permute-start(bf16[448,128]{1,0:T(8,128)(2,1)S(1)} %slice.113), channel_id=1, source_target_pairs={{8,0},{16,8},{24,16},{28,24},{20,28},{12,20},{4,12},{0,4},{9,1},{1... | collective-permute-start | bytes 344072 | tf_op jit(solution)/shard_map/ppermute | solution.py:335
  178.9 25.5 %collective-permute-start.30 = (bf16[448,128]{1,0:T(8,128)(2,1)S(1)}, bf16[448,128]{1,0:T(8,128)(2,1)S(1)}, u32[]{:S(2)}, u32[]{:S(2)}) collective-permute-start(bf16[448,128]{1,0:T(8,128)(2,1)S(1)} %slice.108), channel_id=1, source_target_pairs={{0,8},{8,16},{16,24},{24,28},{28,20},{20,12},{12,4},{4,0},{1,9},{9... | collective-permute-start | bytes 344072 | tf_op jit(solution)/shard_map/ppermute | solution.py:335
  181.4 23.1 %collective-permute-start.65 = (bf16[448,128]{1,0:T(8,128)(2,1)}, bf16[448,128]{1,0:T(8,128)(2,1)S(1)}, u32[]{:S(2)}, u32[]{:S(2)}) collective-permute-start(bf16[448,128]{1,0:T(8,128)(2,1)} %slice.112), channel_id=1, source_target_pairs={{8,0},{16,8},{24,16},{28,24},{20,28},{12,20},{4,12},{0,4},{9,1},{1... | collective-permute-start | bytes 344072 | tf_op jit(solution)/shard_map/ppermute | solution.py:335
  (68 other events, 999.4 us)

commit v2 on v0

v2 whole, which is shorter than its diff:
```python
import functools

import jax
import jax.numpy as jnp
import numpy as np
from jax import lax
from jax.experimental import pallas as pl
from jax.experimental.pallas import tpu as pltpu
from jax.sharding import PartitionSpec as P

STEP = 1000


beta_first = 0.9
beta_second = 0.999
adam_eps = 1e-08

STREAMS = 2
LONGEST_RING = 16
SCRATCH_BYTES = 12 << 20


def adam(projected, first_moment, second_moment):
    first_new = beta_first * first_moment + (1.0 - beta_first) * projected
    second_new = beta_second * second_moment + (1.0 - beta_second) * projected * projected
    corr_first = 1.0 - beta_first**STEP
    corr_second = 1.0 - beta_second**STEP
    direction = (first_new / corr_first / (jnp.sqrt(second_new / corr_second) + adam_eps)).astype(
        jnp.bfloat16
    )
    return first_new, second_new, direction


def with_collectives(activations, grad_out, basis, first_moment, second_moment):
    own_coords = jnp.dot(
        activations, lax.all_gather(basis, "dp", axis=0, tiled=True), preferred_element_type=jnp.float32
    ).astype(jnp.bfloat16)
    coords = lax.all_gather(own_coords, "mp", axis=0, tiled=True)
    projected = lax.psum_scatter(
        lax.dot_general(
            grad_out, coords, (((0,), (0,)), ((), ())), preferred_element_type=jnp.float32
        ),
        "dp",
        scatter_dimension=0,
        tiled=True,
    )
    first_new, second_new, direction = adam(projected, first_moment, second_moment)
    update = lax.dot_general(
        basis,
        lax.all_gather(direction, "dp", axis=0, tiled=True),
        (((1,), (1,)), ((), ())),
        preferred_element_type=jnp.float32,
    ).astype(jnp.bfloat16)
    return (update, first_new, second_new)


def on_chip():
    return pl.BlockSpec(memory_space=pltpu.VMEM)


def scalars():
    return pl.BlockSpec(memory_space=pltpu.SMEM)


def kept_on_chip(arrays):
    return [pltpu.with_memory_space_constraint(a, pltpu.VMEM) for a in arrays]


def split_columns(me, activations, n):
    tokens, features = activations.shape
    part = features // n // 2

    def kernel(me_ref, own, other, kept, sent):
        kept[...] = own[...]
        sent[...] = other[...]

    half = jax.ShapeDtypeStruct((tokens, features // 2), activations.dtype)
    return pl.pallas_call(
        kernel,
        out_shape=(half, half),
        grid_spec=pltpu.PrefetchScalarGridSpec(
            num_scalar_prefetch=1,
            grid=(n,),
            in_specs=[
                pl.BlockSpec((tokens, part), lambda j, me: (0, 2 * j + me[0] % 2)),
                pl.BlockSpec((tokens, part), lambda j, me: (0, 2 * j + 1 - me[0] % 2)),
            ],
            out_specs=(pl.BlockSpec((tokens, part), lambda j, me: (0, j)),) * 2,
        ),
        compiler_params=pltpu.CompilerParams(vmem_limit_bytes=SCRATCH_BYTES),
        name="split_columns",
    )(me, activations, activations)


def add_coords(ids, me, kept, came, total, pieces, depth):
    tokens, width = kept.shape[0], pieces[0][0].shape[1]
    held = () if total is None else (total,)
    arrays = [piece for piece, _, _ in pieces]

    def kernel(ids_ref, me_ref, *refs):
        out = refs[-1]
        side = me_ref[0] % 2
        refs_of = refs[2 + len(held) : -1]
        for act, place in ((refs[0], side), (refs[1], 1 - side)):
            rows = pl.ds(pl.multiple_of(place * tokens, tokens), tokens)
            acc = refs[2][rows] if held else jnp.zeros((tokens, width), jnp.float32)
            for ref, (_, away, low) in zip(refs_of, pieces, strict=True):
                start = pl.multiple_of(ids_ref[away] * depth + low, 128)
                acc += jnp.dot(
                    act[:, pl.ds(start, ref.shape[0])], ref[...], preferred_element_type=jnp.float32
                )
            out[rows] = acc

    return pl.pallas_call(
        kernel,
        out_shape=pltpu.VMEM((2 * tokens, width), jnp.float32),
        in_specs=[scalars(), scalars(), *[on_chip()] * (2 + len(held) + len(arrays))],
        out_specs=on_chip(),
        cost_estimate=pl.CostEstimate(
            flops=4 * tokens * width * sum(a.shape[0] for a in arrays), transcendentals=0, bytes_accessed=4 << 20
        ),
        compiler_params=pltpu.CompilerParams(vmem_limit_bytes=SCRATCH_BYTES),
        name="add_coords",
    )(ids, me, *kept_on_chip([kept, came, *held, *arrays]))


def contract_tokens(grad, coords):
    return lax.dot_general(grad, coords, (((0,), (0,)), ((), ())), preferred_element_type=jnp.float32)


def first_partials(ids, me, grad_out, parts, n):
    group, width = parts[0].shape
    tokens, all_columns = grad_out.shape
    cols = all_columns // n
    groups = tokens // group

    def kernel(ids_ref, me_ref, grad, *refs):
        coords, top, bottom = refs[len(parts) :]
        for k, ref in enumerate(refs[: len(parts)]):
            at = lax.rem(me_ref[0] // 2 + groups - k, groups)
            coords[pl.ds(pl.multiple_of(at * group, group), group)] = ref[...]
        column = pl.multiple_of(ids_ref[n // 2] * cols, 128)
        part = contract_tokens(grad[:, pl.ds(column, cols)], coords[...]).astype(jnp.bfloat16)
        top[...] = part[: cols // 2]
        bottom[...] = part[cols // 2 :]

    half = pltpu.VMEM((cols // 2, width), jnp.bfloat16)
    return pl.pallas_call(
        kernel,
        out_shape=(pltpu.VMEM((tokens, width), jnp.bfloat16), half, half),
        in_specs=[scalars(), scalars(), *[on_chip()] * (1 + len(parts))],
        out_specs=(on_chip(),) * 3,
        cost_estimate=pl.CostEstimate(
            flops=2 * tokens * cols * width, transcendentals=0, bytes_accessed=4 << 20
        ),
        compiler_params=pltpu.CompilerParams(vmem_limit_bytes=SCRATCH_BYTES),
        name="first_partials",
    )(ids, me, *kept_on_chip([grad_out, *parts]))


def next_partials(ids, grad_out, coords, came_up, came_down, n, away):
    tokens, width = coords.shape
    cols = grad_out.shape[1] // n
    rows = came_up.shape[0]

    def kernel(ids_ref, grad, coord, in_up, in_down, up, down):
        column = pl.multiple_of(ids_ref[away] * cols, 128)
        part = contract_tokens(grad[:, pl.ds(column, cols)], coord[...])
        up[:rows] = (part[:rows] + in_up[...].astype(jnp.float32)).astype(jnp.bfloat16)
        if rows < cols:
            up[rows:] = part[rows:].astype(jnp.bfloat16)
        column = pl.multiple_of(ids_ref[n - away] * cols, 128)
        part = contract_tokens(grad[:, pl.ds(column, cols)], coord[...])
        rest = cols - rows
        down[rest:] = (part[rest:] + in_down[...].astype(jnp.float32)).astype(jnp.bfloat16)
        if rest:
            down[:rest] = part[:rest].astype(jnp.bfloat16)

    full = pltpu.VMEM((cols, width), jnp.bfloat16)
    return pl.pallas_call(
        kernel,
        out_shape=(full, full),
        in_specs=[scalars(), *[on_chip()] * 4],
        out_specs=(on_chip(),) * 2,
        cost_estimate=pl.CostEstimate(
            flops=4 * tokens * cols * width, transcendentals=0, bytes_accessed=4 << 20
        ),
        compiler_params=pltpu.CompilerParams(vmem_limit_bytes=SCRATCH_BYTES),
        name="next_partials",
    )(ids, *kept_on_chip([grad_out, coords, came_up, came_down]))


def own_direction(ids, grad_out, coords, came_up, came_down, first_moment, second_moment, s, n):
    tokens, width = coords.shape
    cols = grad_out.shape[1] // n

    def kernel(ids_ref, grad, coord, in_up, in_down, first, second, projected, direction):
        column = pl.multiple_of(ids_ref[0] * cols, 128)
        total = (
            contract_tokens(grad[:, pl.ds(column, cols)], coord[...])
            + in_up[...].astype(jnp.float32)
            + in_down[...].astype(jnp.float32)
        )
        projected[...] = total
        mine = slice(s * width, (s + 1) * width)
        direction[...] = adam(total, first[:, mine], second[:, mine])[2]

    return pl.pallas_call(
        kernel,
        out_shape=(
            pltpu.VMEM((cols, width), jnp.float32),
            pltpu.VMEM((cols, width), jnp.bfloat16),
        ),
        in_specs=[scalars(), *[on_chip()] * 6],
        out_specs=(on_chip(),) * 2,
        cost_estimate=pl.CostEstimate(
            flops=2 * tokens * cols * width, transcendentals=0, bytes_accessed=4 << 20
        ),
        compiler_params=pltpu.CompilerParams(vmem_limit_bytes=SCRATCH_BYTES),
        name="own_direction",
    )(ids, *kept_on_chip([grad_out, coords, came_up, came_down, first_moment, second_moment]))


def new_moments(projected, first_moment, second_moment):
    width = projected[0].shape[1]
    rows = first_moment.shape[0]
    tile = rows // 2
    block = pl.BlockSpec((tile, first_moment.shape[1]), lambda r: (r, 0))

    def kernel(*refs):
        first, second, first_new, second_new = refs[len(projected) :]
        for s, ref in enumerate(refs[: len(projected)]):
            mine = slice(s * width, (s + 1) * width)
            at = pl.ds(pl.multiple_of(pl.program_id(0) * tile, tile), tile)
            first_new[:, mine], second_new[:, mine], _ = adam(ref[at], first[at, mine], second[at, mine])

    return pl.pallas_call(
        kernel,
        out_shape=(jax.ShapeDtypeStruct(first_moment.shape, jnp.float32),) * 2,
        grid=(rows // tile,),
        in_specs=[on_chip()] * (len(projected) + 2),
        out_specs=(block, block),
        cost_estimate=pl.CostEstimate(flops=0, transcendentals=0, bytes_accessed=6 << 20),
        compiler_params=pltpu.CompilerParams(vmem_limit_bytes=SCRATCH_BYTES),
        name="new_moments",
    )(*kept_on_chip([*projected, first_moment, second_moment]))


def write_update(ids, basis, chunks, places, update, all_columns):
    depth, rank = basis.shape
    cols = sum(row[0].shape[0] for row in chunks[0])
    flat = [stream for chunk in chunks for row in chunk for stream in row]
    held = () if update is None else (update,)
    tile = depth // 2

    def kernel(ids_ref, base, *refs):
        out = refs[-1]
        left = list(refs[: len(flat)])
        lines = pl.ds(pl.multiple_of(pl.program_id(1) * tile, tile), tile)
        for g, chunk in enumerate(chunks):
            rows = [[left.pop(0) for _ in row] for row in chunk]

            @pl.when(pl.program_id(0) == g)
            def _(rows=rows):
                whole = jnp.concatenate(
                    [jnp.concatenate([stream[...] for stream in row], axis=1) for row in rows], axis=0
                )
                out[...] = lax.dot_general(
                    base[lines], whole, (((1,), (1,)), ((), ())), preferred_element_type=jnp.float32
                ).astype(out.dtype)

    def place(g, r, ids):
        at = ids[places[0]]
        for k in range(1, len(places)):
            at = jnp.where(g == k, ids[places[k]], at)
        return (r, at)

    return pl.pallas_call(
        kernel,
        out_shape=jax.ShapeDtypeStruct((depth, all_columns), jnp.bfloat16),
        grid_spec=pltpu.PrefetchScalarGridSpec(
            num_scalar_prefetch=1,
            grid=(len(chunks), depth // tile),
            in_specs=[
                *[on_chip()] * (1 + len(flat)),
                *[pl.BlockSpec(memory_space=pl.ANY)] * len(held),
            ],
            out_specs=pl.BlockSpec((tile, cols), place),
        ),
        input_output_aliases={2 + len(flat): 0} if held else {},
        cost_estimate=pl.CostEstimate(
            flops=2 * depth * cols * rank * len(chunks),
            transcendentals=0,
            bytes_accessed=2 * depth * cols * len(chunks),
        ),
        compiler_params=pltpu.CompilerParams(vmem_limit_bytes=SCRATCH_BYTES),
        name="write_update",
    )(ids, *kept_on_chip([basis, *flat]), *held)


def on_ring(n, m, activations, grad_out, basis, first_moment, second_moment):
    order = [*range(0, n, 2), *range(n - 1, 0, -2)]
    upward = [(order[k], order[(k + 1) % n]) for k in range(n)]
    downward = [(b, a) for a, b in upward]
    up = functools.partial(lax.ppermute, axis_name="dp", perm=upward)
    down = functools.partial(lax.ppermute, axis_name="dp", perm=downward)
    swap = functools.partial(lax.ppermute, axis_name="mp", perm=[(k, k ^ 1) for k in range(m)])

    around = np.zeros((n, n), np.int32)
    for place, index in enumerate(order):
        around[index] = [order[(place + away) % n] for away in range(n)]
    ids = jnp.asarray(around)[lax.axis_index("dp")]
    me = lax.axis_index("mp").reshape(1)

    depth, rank = basis.shape
    width = rank // STREAMS
    all_columns = grad_out.shape[1]
    cols = all_columns // n
    half = n // 2
    streams = range(STREAMS)

    part = depth // 2
    own = lax.dynamic_slice(basis, (me[0] % 2 * part, 0), (part, rank))
    own = [own[:, s * width : (s + 1) * width] for s in streams]
    sent_up, sent_down = list(own), list(own)
    pieces = [[(own[s], 0, 0)] for s in streams]
    kept, sent = split_columns(me, activations, n)
    came = swap(sent)
    total = [None] * STREAMS
    for k in range(1, half + 1):
        for s in streams:
            low = 0
            if k == half:
                low = part // 2
                sent_up[s], sent_down[s] = sent_up[s][:low], sent_down[s][low:]
            sent_up[s], sent_down[s] = up(sent_up[s]), down(sent_down[s])
            pieces[s] += [(sent_up[s], n - k, 0), (sent_down[s], k, low)]
            if k >= half - 1:
                total[s] = add_coords(ids, me, kept, came, total[s], pieces[s], part)
                pieces[s] = []

    parts = [None] * STREAMS
    for s in streams:
        pair = (total[s] + swap(total[s])).astype(jnp.bfloat16)
        parts[s] = [pair] + [
            lax.ppermute(pair, "mp", [(a, (a + k) % m) for a in range(m)]) for k in range(2, m, 2)
        ]

    coords = [None] * STREAMS
    for s in streams:
        coords[s], top, bottom = first_partials(ids, me, grad_out, parts[s], n)
        sent_up[s], sent_down[s] = up(top), down(bottom)
    for away in range(half - 1, 0, -1):
        for s in streams:
            to_up, to_down = next_partials(ids, grad_out, coords[s], sent_up[s], sent_down[s], n, away)
            sent_up[s], sent_down[s] = up(to_up), down(to_down)
    projected = [None] * STREAMS
    direction = [None] * STREAMS
    for s in streams:
        projected[s], direction[s] = own_direction(
            ids, grad_out, coords[s], sent_up[s], sent_down[s], first_moment, second_moment, s, n
        )

    sent_up, sent_down = list(direction), list(direction)
    update = write_update(ids, basis, [[direction]], [0], None, all_columns)
    first_new, second_new = new_moments(projected, first_moment, second_moment)
    for k in range(1, half):
        for s in streams:
            sent_up[s], sent_down[s] = up(sent_up[s]), down(sent_down[s])
        sent_up[0], update = lax.optimization_barrier((sent_up[0], update))
        update = write_update(
            ids, basis, [[list(sent_up)], [list(sent_down)]], [n - k, k], update, all_columns
        )
    for s in streams:
        sent_up[s], sent_down[s] = up(sent_up[s][: cols // 2]), down(sent_down[s][cols // 2 :])
    sent_up[0], update = lax.optimization_barrier((sent_up[0], update))
    update = write_update(ids, basis, [[sent_up, sent_down]], [half], update, all_columns)
    return (update, first_new, second_new)


def solution(mesh):
    n, m = mesh.shape["dp"], mesh.shape["mp"]
    ring = 4 <= n <= LONGEST_RING and n % 2 == 0 and m % 2 == 0
    placed = (
        P(("dp", "mp"), None),
        P("dp", "mp"),
        P("dp", None),
        P(("mp", "dp"), None),
        P(("mp", "dp"), None),
    )
    return jax.shard_map(
        functools.partial(on_ring, n, m) if ring else with_collectives,
        mesh=mesh,
        in_specs=placed,
        out_specs=(P("dp", "mp"), P(("mp", "dp"), None), P(("mp", "dp"), None)),
        check_vma=False,
    )
```

time: 340 us -> 137 us (0.40)
  waiting for transfers between devices: 267 us -> 30.8 us
  starting transfers between devices: 0.12 us -> 55.5 us
  Pallas kernels: 0 us -> 39.8 us
  matrix products: 20.6 us -> 0 us
  local copies, waits for them, and re-layouts: 28.3 us -> 9.64 us
  between operations: 13.8 us -> 0.92 us
  blocking collectives: 5.78 us -> 0 us
    all_gather x2 -> x0, waiting for transfers between devices: 140 us -> none  [the longest x1 77.7 us: on_device(): lax.all_gather(basis, 'dp', axis=0, tiled=True)]
    reduce_scatter x1 -> x0, waiting for transfers between devices: 127 us -> none  [on_device(): lax.psum_scatter(lax.dot_general(columns, coords, (((0,), (0,)), ((), ())...]
    ppermute x0 -> x53, starting transfers between devices: none -> 55.5 us  [the longest x28 31 us: on_ring(): sent_up[s], sent_down[s] = (up(sent_up[s]), down(sent_down[s]))]
    pallas_call x0 -> x21, Pallas kernels: none -> 39.8 us  [the longest x5 16.5 us: write_update(): pl.pallas_call(kernel, out_shape=jax.ShapeDtypeStruct((depth, all_columns...]
    ppermute x0 -> x53, waiting for transfers between devices: none -> 30.8 us  [the longest x28 14.3 us: on_ring(): sent_up[s], sent_down[s] = (up(sent_up[s]), down(sent_down[s]))]
    unnamed x11 -> x24, local copies, waits for them, and re-layouts: 28.3 us -> 7.07 us
    dot_general x3 -> x0, matrix products: 20.6 us -> none  [the longest x1 9.44 us: on_device(): lax.dot_general(basis, lax.all_gather(direction, 'dp', axis=0, tiled=True...]
    all_gather x1 -> x0, blocking collectives: 5.78 us -> none  [on_device(): coords = lax.all_gather(own_coords, 'mp', axis=0, tiled=True)]
  transfers between devices with their start and end apart: 3 -> 53, of which waited for: 3 -> 23; matrix products, arithmetic and copies ran while one was open for 2% -> 2% of each run, Pallas kernels for 0% -> 25%
where the time goes in v2:
time: 137 us
  starting transfers between devices  55.5 us (41%)
  Pallas kernels  39.8 us (29%)
  waiting for transfers between devices  30.8 us (22%)
  local copies, waits for them, and re-layouts  9.64 us (7%)
    ppermute x28, starting transfers between devices, on_ring(): sent_up[s], sent_down[s] = (up(sent_up[s]), down(sent_down[s]))  31 us
    pallas_call x5, Pallas kernels, write_update(): pl.pallas_call(kernel, out_shape=jax.ShapeDtypeStruct((depth, all_columns...  16.5 us
    ppermute x28, waiting for transfers between devices, on_ring(): sent_up[s], sent_down[s] = (up(sent_up[s]), down(sent_down[s]))  14.3 us
    ppermute x12, waiting for transfers between devices, on_ring(): sent_up[s], sent_down[s] = (up(to_up), down(to_down))  13 us
    ppermute x12, starting transfers between devices, on_ring(): sent_up[s], sent_down[s] = (up(to_up), down(to_down))  12.6 us
    pallas_call x6, Pallas kernels, next_partials(): pl.pallas_call(kernel, out_shape=(full, full), in_specs=[scalars(), *[on_...  7.57 us
    unnamed x24, local copies, waits for them, and re-layouts  7.07 us
    pallas_call x4, Pallas kernels, add_coords(): pl.pallas_call(kernel, out_shape=pltpu.VMEM((2 * tokens, width), jnp.floa...  7.07 us
  transfers between devices with their start and end apart: 53, of which 23 were waited for; matrix products, arithmetic and copies ran while one was open for 2% of the time, Pallas kernels for 25%

profile of v2, /device:TPU:0, one launch (start us, length us, event | category | flops | bytes accessed | tf_op | source)
XLA Modules:
  0.0 136.7 jit_solution(9052119679739251419)
XLA Ops:
  0.7 1.7 %copy-done.3 = bf16[128,8192]{1,0:T(8,128)(2,1)S(1)} copy-done((bf16[128,8192]{1,0:T(8,128)(2,1)S(1)}, bf16[128,8192]{1,0:T(8,128)(2,1)}, u32[]{:S(2)}) %copy-start.3) | copy-done | bytes 2097176
  2.4 3.0 %split_columns.1 = (bf16[128,4096]{1,0:T(8,128)(2,1)S(1)}, bf16[128,4096]{1,0:T(8,128)(2,1)}) custom-call(s32[1]{0:T(128)} %bitcast.1.me_ref, bf16[128,8192]{1,0:T(8,128)(2,1)S(1)} %copy-done.3, bf16[128,8192]{1,0:T(8,128)(2,1)S(1)} %copy-done.3), custom_call_target="tpu_custom_call" | custom-call | tf_op jit(solution)/shard_map/split_columns/pallas_call | solution.py:78
  7.8 2.6 %collective-permute-start.1 = (bf16[512,128]{1,0:T(8,128)(2,1)S(1)}, bf16[512,128]{1,0:T(8,128)(2,1)S(1)}, u32[]{:S(2)}, u32[]{:S(2)}) collective-permute-start(bf16[512,128]{1,0:T(8,128)(2,1)S(1)} %get-tuple-element.72.refs_2_), channel_id=1, source_target_pairs={{0,8},{8,16},{16,24},{24,28},{28,20},{20,12},{12,4},{4,0},{1,9},{9... | collective-permute-start | bytes 393224 | tf_op jit(solution)/shard_map/ppermute | solution.py:336
  10.4 2.0 %collective-permute-start.20 = (bf16[512,128]{1,0:T(8,128)(2,1)S(1)}, bf16[512,128]{1,0:T(8,128)(2,1)}, u32[]{:S(2)}, u32[]{:S(2)}) collective-permute-start(bf16[512,128]{1,0:T(8,128)(2,1)S(1)} %get-tuple-element.71.refs_2_), channel_id=1, source_target_pairs={{0,8},{8,16},{16,24},{24,28},{28,20},{20,12},{12,4},{4,0},{1,9},{9... | collective-permute-start | bytes 393224 | tf_op jit(solution)/shard_map/ppermute | solution.py:336
  12.5 2.3 %collective-permute-done.1.refs_3_ = bf16[512,128]{1,0:T(8,128)(2,1)S(1)} collective-permute-done((bf16[512,128]{1,0:T(8,128)(2,1)S(1)}, bf16[512,128]{1,0:T(8,128)(2,1)S(1)}, u32[]{:S(2)}, u32[]{:S(2)}) %collective-permute-start.1) | collective-permute-done | bytes 131104 | tf_op jit(solution)/shard_map/ppermute | solution.py:336
  14.7 2.1 %collective-permute-start.3 = (bf16[512,128]{1,0:T(8,128)(2,1)S(1)}, bf16[512,128]{1,0:T(8,128)(2,1)}, u32[]{:S(2)}, u32[]{:S(2)}) collective-permute-start(bf16[512,128]{1,0:T(8,128)(2,1)S(1)} %collective-permute-done.1.refs_3_), channel_id=1, source_target_pairs={{0,8},{8,16},{16,24},{24,28},{28,20},{20,12},{12,4},{4,0},{1,9},{9... | collective-permute-start | bytes 393224 | tf_op jit(solution)/shard_map/ppermute | solution.py:336
  18.1 2.0 %collective-permute-start.22 = (bf16[512,128]{1,0:T(8,128)(2,1)}, bf16[512,128]{1,0:T(8,128)(2,1)}, u32[]{:S(2)}, u32[]{:S(2)}) collective-permute-start(bf16[512,128]{1,0:T(8,128)(2,1)} %collective-permute-done.20.refs_3_), channel_id=1, source_target_pairs={{0,8},{8,16},{16,24},{24,28},{28,20},{20,12},{12,4},{4,0},{1,9},{9... | collective-permute-start | bytes 393224 | tf_op jit(solution)/shard_map/ppermute | solution.py:336
  20.3 2.0 %collective-permute-start.5 = (bf16[512,128]{1,0:T(8,128)(2,1)}, bf16[512,128]{1,0:T(8,128)(2,1)S(1)}, u32[]{:S(2)}, u32[]{:S(2)}) collective-permute-start(bf16[512,128]{1,0:T(8,128)(2,1)} %collective-permute-done.3.refs_5_), channel_id=1, source_target_pairs={{0,8},{8,16},{16,24},{24,28},{28,20},{20,12},{12,4},{4,0},{1,9},{9... | collective-permute-start | bytes 393224 | tf_op jit(solution)/shard_map/ppermute | solution.py:336
  22.3 1.2 collective-permute-done.4.refs_6_
  24.4 2.4 %collective-permute-start.24 = (bf16[512,128]{1,0:T(8,128)(2,1)}, bf16[512,128]{1,0:T(8,128)(2,1)S(1)}, u32[]{:S(2)}, u32[]{:S(2)}) collective-permute-start(bf16[512,128]{1,0:T(8,128)(2,1)} %collective-permute-done.22.refs_5_), channel_id=1, source_target_pairs={{0,8},{8,16},{16,24},{24,28},{28,20},{20,12},{12,4},{4,0},{1,9},{9... | collective-permute-start | bytes 393224 | tf_op jit(solution)/shard_map/ppermute | solution.py:336
  27.2 2.4 %collective-permute-start.7 = (bf16[256,128]{1,0:T(8,128)(2,1)S(1)}, bf16[256,128]{1,0:T(8,128)(2,1)S(1)}, u32[]{:S(2)}, u32[]{:S(2)}) collective-permute-start(bf16[256,128]{1,0:T(8,128)(2,1)S(1)} %slice.40), channel_id=1, source_target_pairs={{0,8},{8,16},{16,24},{24,28},{28,20},{20,12},{12,4},{4,0},{1,9},{9... | collective-permute-start | bytes 196616 | tf_op jit(solution)/shard_map/ppermute | solution.py:336
  31.6 1.2 copy-done.1
  34.6 2.0 %add_coords.4.refs_2_ = f32[256,128]{1,0:T(8,128)S(1)} custom-call(s32[8]{0:T(128)S(1)} %dynamic-slice_bitcast_fusion.ids_ref, s32[1]{0:T(128)} %bitcast.1.me_ref, bf16[128,4096]{1,0:T(8,128)(2,1)S(1)} %copy-done.1, bf16[128,4096]{1,0:T(8,128)(2,1)} %collective-permute-done.refs_1_, bf16[512,128]{1,0:T(8,128)(2,1)S(1)} %get-tuple-element.72.refs_2_, ...), custom_call_target="tpu_custom_call" | custom-call | flops 234881024 | bytes 4194304 | tf_op jit(solution)/shard_map/add_coords/pallas_call | solution.py:114
  36.6 1.6 %add_coords.5 = f32[256,128]{1,0:T(8,128)S(1)} custom-call(s32[8]{0:T(128)S(1)} %dynamic-slice_bitcast_fusion.ids_ref, s32[1]{0:T(128)} %bitcast.1.me_ref, bf16[128,4096]{1,0:T(8,128)(2,1)S(1)} %copy-done.1, bf16[128,4096]{1,0:T(8,128)(2,1)} %collective-permute-done.refs_1_, f32[256,128]{1,0:T(8,128)S(1)} %add_coords.4.refs_2_, ...), custom_call_target="tpu_custom_call" | custom-call | flops 33554432 | bytes 4194304 | tf_op jit(solution)/shard_map/add_coords/pallas_call | solution.py:114
  38.4 1.8 %collective-permute-start.26 = (bf16[256,128]{1,0:T(8,128)(2,1)S(1)}, bf16[256,128]{1,0:T(8,128)(2,1)S(1)}, u32[]{:S(2)}, u32[]{:S(2)}) collective-permute-start(bf16[256,128]{1,0:T(8,128)(2,1)S(1)} %slice.42), channel_id=1, source_target_pairs={{0,8},{8,16},{16,24},{24,28},{28,20},{20,12},{12,4},{4,0},{1,9},{9... | collective-permute-start | bytes 196616 | tf_op jit(solution)/shard_map/ppermute | solution.py:336
  40.5 2.0 %add_coords.6.refs_2_ = f32[256,128]{1,0:T(8,128)S(1)} custom-call(s32[8]{0:T(128)S(1)} %dynamic-slice_bitcast_fusion.ids_ref, s32[1]{0:T(128)} %bitcast.1.me_ref, bf16[128,4096]{1,0:T(8,128)(2,1)S(1)} %copy-done.1, bf16[128,4096]{1,0:T(8,128)(2,1)} %collective-permute-done.refs_1_, bf16[512,128]{1,0:T(8,128)(2,1)S(1)} %get-tuple-element.71.refs_2_, ...), custom_call_target="tpu_custom_call" | custom-call | flops 234881024 | bytes 4194304 | tf_op jit(solution)/shard_map/add_coords/pallas_call | solution.py:114
  42.9 1.6 %collective-permute-done.27.refs_4_ = bf16[256,128]{1,0:T(8,128)(2,1)S(1)} collective-permute-done((bf16[256,128]{1,0:T(8,128)(2,1)S(1)}, bf16[256,128]{1,0:T(8,128)(2,1)S(1)}, u32[]{:S(2)}, u32[]{:S(2)}) %collective-permute-start.27) | collective-permute-done | bytes 65568 | tf_op jit(solution)/shard_map/ppermute | solution.py:336
  44.5 1.4 %add_coords.7 = f32[256,128]{1,0:T(8,128)S(1)} custom-call(s32[8]{0:T(128)S(1)} %dynamic-slice_bitcast_fusion.ids_ref, s32[1]{0:T(128)} %bitcast.1.me_ref, bf16[128,4096]{1,0:T(8,128)(2,1)S(1)} %copy-done.1, bf16[128,4096]{1,0:T(8,128)(2,1)} %collective-permute-done.refs_1_, f32[256,128]{1,0:T(8,128)S(1)} %add_coords.6.refs_2_, ...), custom_call_target="tpu_custom_call" | custom-call | flops 33554432 | bytes 4194304 | tf_op jit(solution)/shard_map/add_coords/pallas_call | solution.py:114
  46.0 1.6 %collective-permute-start.10 = (bf16[256,128]{1,0:T(8,128)(2,1)S(1)}, bf16[256,128]{1,0:T(8,128)(2,1)S(1)}, u32[]{:S(2)}, u32[]{:S(2)}) collective-permute-start(bf16[256,128]{1,0:T(8,128)(2,1)S(1)} %add_convert_fusion.1.refs_0_), channel_id=1, source_target_pairs={{0,2},{1,3},{2,0},{3,1},{4,6},{5,7},{6,4},{7,5},{8,10},{9,11},{10,... | collective-permute-start | bytes 196616 | tf_op jit(solution)/shard_map/ppermute | solution.py:346
  47.6 1.3 collective-permute-start.29
  48.9 1.8 %collective-permute-done.10.refs_1_ = bf16[256,128]{1,0:T(8,128)(2,1)S(1)} collective-permute-done((bf16[256,128]{1,0:T(8,128)(2,1)S(1)}, bf16[256,128]{1,0:T(8,128)(2,1)S(1)}, u32[]{:S(2)}, u32[]{:S(2)}) %collective-permute-start.10) | collective-permute-done | bytes 65568 | tf_op jit(solution)/shard_map/ppermute | solution.py:346
  51.7 1.6 %collective-permute-start.11 = (bf16[448,128]{1,0:T(8,128)(2,1)S(1)}, bf16[448,128]{1,0:T(8,128)(2,1)S(1)}, u32[]{:S(2)}, u32[]{:S(2)}) collective-permute-start(bf16[448,128]{1,0:T(8,128)(2,1)S(1)} %get-tuple-element.40), channel_id=1, source_target_pairs={{0,8},{8,16},{16,24},{24,28},{28,20},{20,12},{12,4},{4,0},{1,9},{9... | collective-permute-start | bytes 344072 | tf_op jit(solution)/shard_map/ppermute | solution.py:352
  53.8 1.0 first_partials.3
  54.9 1.6 %collective-permute-start.30 = (bf16[448,128]{1,0:T(8,128)(2,1)S(1)}, bf16[448,128]{1,0:T(8,128)(2,1)S(1)}, u32[]{:S(2)}, u32[]{:S(2)}) collective-permute-start(bf16[448,128]{1,0:T(8,128)(2,1)S(1)} %get-tuple-element.50), channel_id=1, source_target_pairs={{0,8},{8,16},{16,24},{24,28},{28,20},{20,12},{12,4},{4,0},{1,9},{9... | collective-permute-start | bytes 344072 | tf_op jit(solution)/shard_map/ppermute | solution.py:352
  56.9 1.6 %collective-permute-done.12.in_down = bf16[448,128]{1,0:T(8,128)(2,1)S(1)} collective-permute-done((bf16[448,128]{1,0:T(8,128)(2,1)S(1)}, bf16[448,128]{1,0:T(8,128)(2,1)S(1)}, u32[]{:S(2)}, u32[]{:S(2)}) %collective-permute-start.12) | collective-permute-done | bytes 114720 | tf_op jit(solution)/shard_map/ppermute | solution.py:352
  58.6 1.3 next_partials.6
  59.8 1.6 %collective-permute-start.13 = (bf16[896,128]{1,0:T(8,128)(2,1)S(1)}, bf16[896,128]{1,0:T(8,128)(2,1)S(1)}, u32[]{:S(2)}, u32[]{:S(2)}) collective-permute-start(bf16[896,128]{1,0:T(8,128)(2,1)S(1)} %get-tuple-element.42), channel_id=1, source_target_pairs={{0,8},{8,16},{16,24},{24,28},{28,20},{20,12},{12,4},{4,0},{1,9},{9... | collective-permute-start | bytes 688136 | tf_op jit(solution)/shard_map/ppermute | solution.py:356
  61.9 1.3 next_partials.9
  63.2 1.6 %collective-permute-start.32 = (bf16[896,128]{1,0:T(8,128)(2,1)S(1)}, bf16[896,128]{1,0:T(8,128)(2,1)S(1)}, u32[]{:S(2)}, u32[]{:S(2)}) collective-permute-start(bf16[896,128]{1,0:T(8,128)(2,1)S(1)} %get-tuple-element.52), channel_id=1, source_target_pairs={{0,8},{8,16},{16,24},{24,28},{28,20},{20,12},{12,4},{4,0},{1,9},{9... | collective-permute-start | bytes 688136 | tf_op jit(solution)/shard_map/ppermute | solution.py:356
  65.3 3.1 %collective-permute-done.13.in_up = bf16[896,128]{1,0:T(8,128)(2,1)S(1)} collective-permute-done((bf16[896,128]{1,0:T(8,128)(2,1)S(1)}, bf16[896,128]{1,0:T(8,128)(2,1)S(1)}, u32[]{:S(2)}, u32[]{:S(2)}) %collective-permute-start.13) | collective-permute-done | bytes 229408 | tf_op jit(solution)/shard_map/ppermute | solution.py:356
  68.4 1.4 %collective-permute-done.14.in_down = bf16[896,128]{1,0:T(8,128)(2,1)S(1)} collective-permute-done((bf16[896,128]{1,0:T(8,128)(2,1)S(1)}, bf16[896,128]{1,0:T(8,128)(2,1)S(1)}, u32[]{:S(2)}, u32[]{:S(2)}) %collective-permute-start.14) | collective-permute-done | bytes 229408 | tf_op jit(solution)/shard_map/ppermute | solution.py:356
  69.8 1.3 next_partials.7
  71.0 1.7 %collective-permute-start.15 = (bf16[896,128]{1,0:T(8,128)(2,1)S(1)}, bf16[896,128]{1,0:T(8,128)(2,1)S(1)}, u32[]{:S(2)}, u32[]{:S(2)}) collective-permute-start(bf16[896,128]{1,0:T(8,128)(2,1)S(1)} %get-tuple-element.44), channel_id=1, source_target_pairs={{0,8},{8,16},{16,24},{24,28},{28,20},{20,12},{12,4},{4,0},{1,9},{9... | collective-permute-start | bytes 688136 | tf_op jit(solution)/shard_map/ppermute | solution.py:356
  73.3 1.3 collective-permute-done.33.in_down
  74.6 1.3 next_partials.10
  75.8 1.9 %collective-permute-start.34 = (bf16[896,128]{1,0:T(8,128)(2,1)S(1)}, bf16[896,128]{1,0:T(8,128)(2,1)S(1)}, u32[]{:S(2)}, u32[]{:S(2)}) collective-permute-start(bf16[896,128]{1,0:T(8,128)(2,1)S(1)} %get-tuple-element.54), channel_id=1, source_target_pairs={{0,8},{8,16},{16,24},{24,28},{28,20},{20,12},{12,4},{4,0},{1,9},{9... | collective-permute-start | bytes 688136 | tf_op jit(solution)/shard_map/ppermute | solution.py:356
  78.3 1.2 collective-permute-done.16.in_down
  79.5 1.3 next_partials.8
  80.8 2.2 %collective-permute-start.17 = (bf16[896,128]{1,0:T(8,128)(2,1)S(1)}, bf16[896,128]{1,0:T(8,128)(2,1)S(1)}, u32[]{:S(2)}, u32[]{:S(2)}) collective-permute-start(bf16[896,128]{1,0:T(8,128)(2,1)S(1)} %get-tuple-element.46), channel_id=1, source_target_pairs={{0,8},{8,16},{16,24},{24,28},{28,20},{20,12},{12,4},{4,0},{1,9},{9... | collective-permute-start | bytes 688136 | tf_op jit(solution)/shard_map/ppermute | solution.py:356
  83.0 1.4 %collective-permute-done.34.in_up = bf16[896,128]{1,0:T(8,128)(2,1)S(1)} collective-permute-done((bf16[896,128]{1,0:T(8,128)(2,1)S(1)}, bf16[896,128]{1,0:T(8,128)(2,1)S(1)}, u32[]{:S(2)}, u32[]{:S(2)}) %collective-permute-start.34) | collective-permute-done | bytes 229408 | tf_op jit(solution)/shard_map/ppermute | solution.py:356
  84.8 1.3 next_partials.11
  86.1 1.8 %collective-permute-start.36 = (bf16[896,128]{1,0:T(8,128)(2,1)S(1)}, bf16[896,128]{1,0:T(8,128)(2,1)S(1)}, u32[]{:S(2)}, u32[]{:S(2)}) collective-permute-start(bf16[896,128]{1,0:T(8,128)(2,1)S(1)} %get-tuple-element.56), channel_id=1, source_target_pairs={{0,8},{8,16},{16,24},{24,28},{28,20},{20,12},{12,4},{4,0},{1,9},{9... | collective-permute-start | bytes 688136 | tf_op jit(solution)/shard_map/ppermute | solution.py:356
  88.2 1.2 collective-permute-done.17.in_up
  89.4 1.2 own_direction.2
  90.6 1.7 %collective-permute-start.19 = (bf16[896,128]{1,0:T(8,128)(2,1)S(1)}, bf16[896,128]{1,0:T(8,128)(2,1)S(1)}, u32[]{:S(2)}, u32[]{:S(2)}) collective-permute-start(bf16[896,128]{1,0:T(8,128)(2,1)S(1)} %get-tuple-element.48.refs_0_), channel_id=1, source_target_pairs={{0,8},{8,16},{16,24},{24,28},{28,20},{20,12},{12,4},{4,0},{1,9},{9... | collective-permute-start | bytes 688136 | tf_op jit(solution)/shard_map/ppermute | solution.py:369
  92.3 2.4 %collective-permute-done.36.in_up = bf16[896,128]{1,0:T(8,128)(2,1)S(1)} collective-permute-done((bf16[896,128]{1,0:T(8,128)(2,1)S(1)}, bf16[896,128]{1,0:T(8,128)(2,1)S(1)}, u32[]{:S(2)}, u32[]{:S(2)}) %collective-permute-start.36) | collective-permute-done | bytes 229408 | tf_op jit(solution)/shard_map/ppermute | solution.py:356
  94.6 1.2 own_direction.3
  96.8 1.2 collective-permute-start.41
  98.2 2.4 %write_update.5.refs_4_ = bf16[1024,7168]{1,0:T(8,128)(2,1)} custom-call(s32[8]{0:T(128)S(1)} %dynamic-slice_bitcast_fusion.ids_ref, bf16[1024,256]{1,0:T(8,128)(2,1)S(1)} %copy-done.2, bf16[896,128]{1,0:T(8,128)(2,1)S(1)} %get-tuple-element.48.refs_0_, bf16[896,128]{1,0:T(8,128)(2,1)S(1)} %get-tuple-element.58.refs_1_), custom_call_target="tpu_custom_call" | custom-call | flops 469762048 | bytes 1835008 | tf_op jit(solution)/shard_map/write_update/pallas_call | solution.py:278
  100.6 1.8 %collective-permute-start.38 = (bf16[896,128]{1,0:T(8,128)(2,1)S(1)}, bf16[896,128]{1,0:T(8,128)(2,1)S(1)}, u32[]{:S(2)}, u32[]{:S(2)}) collective-permute-start(bf16[896,128]{1,0:T(8,128)(2,1)S(1)} %collective-permute-done.19.refs_0_), channel_id=1, source_target_pairs={{0,8},{8,16},{16,24},{24,28},{28,20},{20,12},{12,4},{4,0},{1,9},{9... | collective-permute-start | bytes 688136 | tf_op jit(solution)/shard_map/ppermute | solution.py:369
  102.4 2.1 %collective-permute-done.39.refs_1_ = bf16[896,128]{1,0:T(8,128)(2,1)S(1)} collective-permute-done((bf16[896,128]{1,0:T(8,128)(2,1)S(1)}, bf16[896,128]{1,0:T(8,128)(2,1)S(1)}, u32[]{:S(2)}, u32[]{:S(2)}) %collective-permute-start.39) | collective-permute-done | bytes 229408 | tf_op jit(solution)/shard_map/ppermute | solution.py:369
  104.5 1.2 collective-permute-start.43
  106.5 3.3 %collective-permute-done.40.refs_2_ = bf16[896,128]{1,0:T(8,128)(2,1)S(1)} collective-permute-done((bf16[896,128]{1,0:T(8,128)(2,1)S(1)}, bf16[896,128]{1,0:T(8,128)(2,1)S(1)}, u32[]{:S(2)}, u32[]{:S(2)}) %collective-permute-start.40) | collective-permute-done | bytes 229408 | tf_op jit(solution)/shard_map/ppermute | solution.py:369
  109.8 1.2 collective-permute-start.44
  111.0 3.9 %write_update.6.refs_4_ = bf16[1024,7168]{1,0:T(8,128)(2,1)} custom-call(s32[8]{0:T(128)S(1)} %dynamic-slice_bitcast_fusion.ids_ref, bf16[1024,256]{1,0:T(8,128)(2,1)S(1)} %copy-done.2, bf16[896,128]{1,0:T(8,128)(2,1)S(1)} %collective-permute-done.19.refs_0_, bf16[896,128]{1,0:T(8,128)(2,1)S(1)} %collective-permute-done.39.refs_1_, ...), custom_call_target="tpu_custom_call", output_to_operand_aliasing={{}: (6, {})} | custom-call | flops 939524096 | bytes 3670016 | tf_op jit(solution)/shard_map/write_update/pallas_call | solution.py:278
  117.7 1.9 %collective-permute-done.44.refs_2_ = bf16[896,128]{1,0:T(8,128)(2,1)S(1)} collective-permute-done((bf16[896,128]{1,0:T(8,128)(2,1)S(1)}, bf16[896,128]{1,0:T(8,128)(2,1)S(1)}, u32[]{:S(2)}, u32[]{:S(2)}) %collective-permute-start.44) | collective-permute-done | bytes 229408 | tf_op jit(solution)/shard_map/ppermute | solution.py:369
  119.6 1.2 collective-permute-start.48
  120.8 3.9 %write_update.7.refs_4_ = bf16[1024,7168]{1,0:T(8,128)(2,1)} custom-call(s32[8]{0:T(128)S(1)} %dynamic-slice_bitcast_fusion.ids_ref, bf16[1024,256]{1,0:T(8,128)(2,1)S(1)} %copy-done.2, bf16[896,128]{1,0:T(8,128)(2,1)S(1)} %collective-permute-done.38.refs_0_, bf16[896,128]{1,0:T(8,128)(2,1)S(1)} %collective-permute-done.43.refs_1_, ...), custom_call_target="tpu_custom_call", output_to_operand_aliasing={{}: (6, {})} | custom-call | flops 939524096 | bytes 3670016 | tf_op jit(solution)/shard_map/write_update/pallas_call | solution.py:278
  125.6 1.1 collective-permute-start.50
  126.7 1.0 collective-permute-start.52
  127.8 1.2 collective-permute-start.51
  129.0 1.4 new_moments.1
  130.3 3.9 %write_update.8.refs_4_ = bf16[1024,7168]{1,0:T(8,128)(2,1)} custom-call(s32[8]{0:T(128)S(1)} %dynamic-slice_bitcast_fusion.ids_ref, bf16[1024,256]{1,0:T(8,128)(2,1)S(1)} %copy-done.2, bf16[896,128]{1,0:T(8,128)(2,1)S(1)} %collective-permute-done.42.refs_0_, bf16[896,128]{1,0:T(8,128)(2,1)S(1)} %collective-permute-done.47.refs_1_, ...), custom_call_target="tpu_custom_call", output_to_operand_aliasing={{}: (6, {})} | custom-call | flops 939524096 | bytes 3670016 | tf_op jit(solution)/shard_map/write_update/pallas_call | solution.py:278
  134.2 2.4 %write_update.9 = bf16[1024,7168]{1,0:T(8,128)(2,1)} custom-call(s32[8]{0:T(128)S(1)} %dynamic-slice_bitcast_fusion.ids_ref, bf16[1024,256]{1,0:T(8,128)(2,1)S(1)} %copy-done.2, bf16[448,128]{1,0:T(8,128)(2,1)S(1)} %collective-permute-done.46.refs_0_, bf16[448,128]{1,0:T(8,128)(2,1)S(1)} %collective-permute-done.50.refs_1_, ...), custom_call_target="tpu_custom_call", output_to_operand_aliasing={{}: (6, {})} | custom-call | flops 469762048 | bytes 1835008 | tf_op jit(solution)/shard_map/write_update/pallas_call | solution.py:278
  (100 shorter events, 20.6 us)
Async XLA Ops:
  0.6 50.1 %slice-start = ((s8[7340032]{0:T(1024)(128)(4,1)}), s8[3145728]{0:T(1024)(128)(4,1)S(1)}, s32[]{:S(2)}) async-start(s8[7340032]{0:T(1024)(128)(4,1)} %bitcast.3), calls=%async_computation | async-start | bytes 6291456
  0.6 1.7 %copy-start.3 = (bf16[128,8192]{1,0:T(8,128)(2,1)S(1)}, bf16[128,8192]{1,0:T(8,128)(2,1)}, u32[]{:S(2)}) copy-start(bf16[128,8192]{1,0:T(8,128)(2,1)} %other.1) | copy-start | bytes 6291460
  5.4 1.0 copy-start
  6.3 25.3 %collective-permute-start = (bf16[128,4096]{1,0:T(8,128)(2,1)}, bf16[128,4096]{1,0:T(8,128)(2,1)}, u32[]{:S(2)}, u32[]{:S(2)}) collective-permute-start(bf16[128,4096]{1,0:T(8,128)(2,1)} %get-tuple-element.38), channel_id=1, source_target_pairs={{0,1},{1,0},{2,3},{3,2},{4,5},{5,4},{6,7},{7,6},{8,9},{9,8},{10,11... | collective-permute-start | bytes 3145736 | tf_op jit(solution)/shard_map/ppermute | solution.py:328
  7.8 6.9 %collective-permute-start.1 = (bf16[512,128]{1,0:T(8,128)(2,1)S(1)}, bf16[512,128]{1,0:T(8,128)(2,1)S(1)}, u32[]{:S(2)}, u32[]{:S(2)}) collective-permute-start(bf16[512,128]{1,0:T(8,128)(2,1)S(1)} %get-tuple-element.72.refs_2_), channel_id=1, source_target_pairs={{0,8},{8,16},{16,24},{24,28},{28,20},{20,12},{12,4},{4,0},{1,9},{9... | collective-permute-start | bytes 393224 | tf_op jit(solution)/shard_map/ppermute | solution.py:336
  10.4 7.0 %collective-permute-start.2 = (bf16[512,128]{1,0:T(8,128)(2,1)S(1)}, bf16[512,128]{1,0:T(8,128)(2,1)S(1)}, u32[]{:S(2)}, u32[]{:S(2)}) collective-permute-start(bf16[512,128]{1,0:T(8,128)(2,1)S(1)} %get-tuple-element.72.refs_2_), channel_id=1, source_target_pairs={{8,0},{16,8},{24,16},{28,24},{20,28},{12,20},{4,12},{0,4},{9,1},{1... | collective-permute-start | bytes 393224 | tf_op jit(solution)/shard_map/ppermute | solution.py:336
  10.4 7.7 %collective-permute-start.20 = (bf16[512,128]{1,0:T(8,128)(2,1)S(1)}, bf16[512,128]{1,0:T(8,128)(2,1)}, u32[]{:S(2)}, u32[]{:S(2)}) collective-permute-start(bf16[512,128]{1,0:T(8,128)(2,1)S(1)} %get-tuple-element.71.refs_2_), channel_id=1, source_target_pairs={{0,8},{8,16},{16,24},{24,28},{28,20},{20,12},{12,4},{4,0},{1,9},{9... | collective-permute-start | bytes 393224 | tf_op jit(solution)/shard_map/ppermute | solution.py:336
  12.4 7.7 %collective-permute-start.21 = (bf16[512,128]{1,0:T(8,128)(2,1)S(1)}, bf16[512,128]{1,0:T(8,128)(2,1)}, u32[]{:S(2)}, u32[]{:S(2)}) collective-permute-start(bf16[512,128]{1,0:T(8,128)(2,1)S(1)} %get-tuple-element.71.refs_2_), channel_id=1, source_target_pairs={{8,0},{16,8},{24,16},{28,24},{20,28},{12,20},{4,12},{0,4},{9,1},{1... | collective-permute-start | bytes 393224 | tf_op jit(solution)/shard_map/ppermute | solution.py:336
  14.7 5.5 %collective-permute-start.3 = (bf16[512,128]{1,0:T(8,128)(2,1)S(1)}, bf16[512,128]{1,0:T(8,128)(2,1)}, u32[]{:S(2)}, u32[]{:S(2)}) collective-permute-start(bf16[512,128]{1,0:T(8,128)(2,1)S(1)} %collective-permute-done.1.refs_3_), channel_id=1, source_target_pairs={{0,8},{8,16},{16,24},{24,28},{28,20},{20,12},{12,4},{4,0},{1,9},{9... | collective-permute-start | bytes 393224 | tf_op jit(solution)/shard_map/ppermute | solution.py:336
  17.4 6.1 %collective-permute-start.4 = (bf16[512,128]{1,0:T(8,128)(2,1)S(1)}, bf16[512,128]{1,0:T(8,128)(2,1)}, u32[]{:S(2)}, u32[]{:S(2)}) collective-permute-start(bf16[512,128]{1,0:T(8,128)(2,1)S(1)} %collective-permute-done.2.refs_4_), channel_id=1, source_target_pairs={{8,0},{16,8},{24,16},{28,24},{20,28},{12,20},{4,12},{0,4},{9,1},{1... | collective-permute-start | bytes 393224 | tf_op jit(solution)/shard_map/ppermute | solution.py:336
  17.5 0.7 copy-start.8
  18.1 6.3 %collective-permute-start.22 = (bf16[512,128]{1,0:T(8,128)(2,1)}, bf16[512,128]{1,0:T(8,128)(2,1)}, u32[]{:S(2)}, u32[]{:S(2)}) collective-permute-start(bf16[512,128]{1,0:T(8,128)(2,1)} %collective-permute-done.20.refs_3_), channel_id=1, source_target_pairs={{0,8},{8,16},{16,24},{24,28},{28,20},{20,12},{12,4},{4,0},{1,9},{9... | collective-permute-start | bytes 393224 | tf_op jit(solution)/shard_map/ppermute | solution.py:336
  20.1 6.7 %collective-permute-start.23 = (bf16[512,128]{1,0:T(8,128)(2,1)}, bf16[512,128]{1,0:T(8,128)(2,1)}, u32[]{:S(2)}, u32[]{:S(2)}) collective-permute-start(bf16[512,128]{1,0:T(8,128)(2,1)} %collective-permute-done.21.refs_4_), channel_id=1, source_target_pairs={{8,0},{16,8},{24,16},{28,24},{20,28},{12,20},{4,12},{0,4},{9,1},{1... | collective-permute-start | bytes 393224 | tf_op jit(solution)/shard_map/ppermute | solution.py:336
  20.3 6.9 %collective-permute-start.5 = (bf16[512,128]{1,0:T(8,128)(2,1)}, bf16[512,128]{1,0:T(8,128)(2,1)S(1)}, u32[]{:S(2)}, u32[]{:S(2)}) collective-permute-start(bf16[512,128]{1,0:T(8,128)(2,1)} %collective-permute-done.3.refs_5_), channel_id=1, source_target_pairs={{0,8},{8,16},{16,24},{24,28},{28,20},{20,12},{12,4},{4,0},{1,9},{9... | collective-permute-start | bytes 393224 | tf_op jit(solution)/shard_map/ppermute | solution.py:336
  23.5 6.2 %collective-permute-start.6 = (bf16[512,128]{1,0:T(8,128)(2,1)}, bf16[512,128]{1,0:T(8,128)(2,1)}, u32[]{:S(2)}, u32[]{:S(2)}) collective-permute-start(bf16[512,128]{1,0:T(8,128)(2,1)} %collective-permute-done.4.refs_6_), channel_id=1, source_target_pairs={{8,0},{16,8},{24,16},{28,24},{20,28},{12,20},{4,12},{0,4},{9,1},{1... | collective-permute-start | bytes 393224 | tf_op jit(solution)/shard_map/ppermute | solution.py:336
  24.4 13.9 %collective-permute-start.24 = (bf16[512,128]{1,0:T(8,128)(2,1)}, bf16[512,128]{1,0:T(8,128)(2,1)S(1)}, u32[]{:S(2)}, u32[]{:S(2)}) collective-permute-start(bf16[512,128]{1,0:T(8,128)(2,1)} %collective-permute-done.22.refs_5_), channel_id=1, source_target_pairs={{0,8},{8,16},{16,24},{24,28},{28,20},{20,12},{12,4},{4,0},{1,9},{9... | collective-permute-start | bytes 393224 | tf_op jit(solution)/shard_map/ppermute | solution.py:336
  26.8 13.3 %collective-permute-start.25 = (bf16[512,128]{1,0:T(8,128)(2,1)}, bf16[512,128]{1,0:T(8,128)(2,1)S(1)}, u32[]{:S(2)}, u32[]{:S(2)}) collective-permute-start(bf16[512,128]{1,0:T(8,128)(2,1)} %collective-permute-done.23.refs_6_), channel_id=1, source_target_pairs={{8,0},{16,8},{24,16},{28,24},{20,28},{12,20},{4,12},{0,4},{9,1},{1... | collective-permute-start | bytes 393224 | tf_op jit(solution)/shard_map/ppermute | solution.py:336
  27.2 9.5 %collective-permute-start.7 = (bf16[256,128]{1,0:T(8,128)(2,1)S(1)}, bf16[256,128]{1,0:T(8,128)(2,1)S(1)}, u32[]{:S(2)}, u32[]{:S(2)}) collective-permute-start(bf16[256,128]{1,0:T(8,128)(2,1)S(1)} %slice.40), channel_id=1, source_target_pairs={{0,8},{8,16},{16,24},{24,28},{28,20},{20,12},{12,4},{4,0},{1,9},{9... | collective-permute-start | bytes 196616 | tf_op jit(solution)/shard_map/ppermute | solution.py:336
  30.6 6.0 %collective-permute-start.8 = (bf16[256,128]{1,0:T(8,128)(2,1)S(1)}, bf16[256,128]{1,0:T(8,128)(2,1)S(1)}, u32[]{:S(2)}, u32[]{:S(2)}) collective-permute-start(bf16[256,128]{1,0:T(8,128)(2,1)S(1)} %slice.41), channel_id=1, source_target_pairs={{8,0},{16,8},{24,16},{28,24},{20,28},{12,20},{4,12},{0,4},{9,1},{1... | collective-permute-start | bytes 196616 | tf_op jit(solution)/shard_map/ppermute | solution.py:336
  31.6 1.2 copy-start.1
  32.8 0.9 copy-start.7
  33.7 0.9 copy-start.9
  36.6 14.1 %slice-start.1 = ((s8[7340032]{0:T(1024)(128)(4,1)}), s8[4194304]{0:T(1024)(128)(4,1)S(1)}, s32[]{:S(2)}) async-start(s8[7340032]{0:T(1024)(128)(4,1)} %bitcast.3), calls=%async_computation.1 | async-start | bytes 8388608
  38.2 7.8 %collective-permute-start.9 = (f32[256,128]{1,0:T(8,128)S(1)}, f32[256,128]{1,0:T(8,128)S(1)}, u32[]{:S(2)}, u32[]{:S(2)}) collective-permute-start(f32[256,128]{1,0:T(8,128)S(1)} %add_coords.5), channel_id=1, source_target_pairs={{0,1},{1,0},{2,3},{3,2},{4,5},{5,4},{6,7},{7,6},{8,9},{9,8},{10,11... | collective-permute-start | bytes 393224 | tf_op jit(solution)/shard_map/ppermute | solution.py:344
  38.4 4.5 %collective-permute-start.26 = (bf16[256,128]{1,0:T(8,128)(2,1)S(1)}, bf16[256,128]{1,0:T(8,128)(2,1)S(1)}, u32[]{:S(2)}, u32[]{:S(2)}) collective-permute-start(bf16[256,128]{1,0:T(8,128)(2,1)S(1)} %slice.42), channel_id=1, source_target_pairs={{0,8},{8,16},{16,24},{24,28},{28,20},{20,12},{12,4},{4,0},{1,9},{9... | collective-permute-start | bytes 196616 | tf_op jit(solution)/shard_map/ppermute | solution.py:336
  40.2 4.3 %collective-permute-start.27 = (bf16[256,128]{1,0:T(8,128)(2,1)S(1)}, bf16[256,128]{1,0:T(8,128)(2,1)S(1)}, u32[]{:S(2)}, u32[]{:S(2)}) collective-permute-start(bf16[256,128]{1,0:T(8,128)(2,1)S(1)} %slice.43), channel_id=1, source_target_pairs={{8,0},{16,8},{24,16},{28,24},{20,28},{12,20},{4,12},{0,4},{9,1},{1... | collective-permute-start | bytes 196616 | tf_op jit(solution)/shard_map/ppermute | solution.py:336
  45.9 1.7 %collective-permute-start.28 = (f32[256,128]{1,0:T(8,128)S(1)}, f32[256,128]{1,0:T(8,128)S(1)}, u32[]{:S(2)}, u32[]{:S(2)}) collective-permute-start(f32[256,128]{1,0:T(8,128)S(1)} %add_coords.7), channel_id=1, source_target_pairs={{0,1},{1,0},{2,3},{3,2},{4,5},{5,4},{6,7},{7,6},{8,9},{9,8},{10,11... | collective-permute-start | bytes 393224 | tf_op jit(solution)/shard_map/ppermute | solution.py:344
  46.0 4.6 %collective-permute-start.10 = (bf16[256,128]{1,0:T(8,128)(2,1)S(1)}, bf16[256,128]{1,0:T(8,128)(2,1)S(1)}, u32[]{:S(2)}, u32[]{:S(2)}) collective-permute-start(bf16[256,128]{1,0:T(8,128)(2,1)S(1)} %add_convert_fusion.1.refs_0_), channel_id=1, source_target_pairs={{0,2},{1,3},{2,0},{3,1},{4,6},{5,7},{6,4},{7,5},{8,10},{9,11},{10,... | collective-permute-start | bytes 196616 | tf_op jit(solution)/shard_map/ppermute | solution.py:346
  47.6 6.2 %collective-permute-start.29 = (bf16[256,128]{1,0:T(8,128)(2,1)S(1)}, bf16[256,128]{1,0:T(8,128)(2,1)S(1)}, u32[]{:S(2)}, u32[]{:S(2)}) collective-permute-start(bf16[256,128]{1,0:T(8,128)(2,1)S(1)} %add_convert_fusion.refs_0_), channel_id=1, source_target_pairs={{0,2},{1,3},{2,0},{3,1},{4,6},{5,7},{6,4},{7,5},{8,10},{9,11},{10,... | collective-permute-start | bytes 196616 | tf_op jit(solution)/shard_map/ppermute | solution.py:346
  51.7 5.2 %collective-permute-start.11 = (bf16[448,128]{1,0:T(8,128)(2,1)S(1)}, bf16[448,128]{1,0:T(8,128)(2,1)S(1)}, u32[]{:S(2)}, u32[]{:S(2)}) collective-permute-start(bf16[448,128]{1,0:T(8,128)(2,1)S(1)} %get-tuple-element.40), channel_id=1, source_target_pairs={{0,8},{8,16},{16,24},{24,28},{28,20},{20,12},{12,4},{4,0},{1,9},{9... | collective-permute-start | bytes 344072 | tf_op jit(solution)/shard_map/ppermute | solution.py:352
  53.4 5.2 %collective-permute-start.12 = (bf16[448,128]{1,0:T(8,128)(2,1)S(1)}, bf16[448,128]{1,0:T(8,128)(2,1)S(1)}, u32[]{:S(2)}, u32[]{:S(2)}) collective-permute-start(bf16[448,128]{1,0:T(8,128)(2,1)S(1)} %get-tuple-element.41), channel_id=1, source_target_pairs={{8,0},{16,8},{24,16},{28,24},{20,28},{12,20},{4,12},{0,4},{9,1},{1... | collective-permute-start | bytes 344072 | tf_op jit(solution)/shard_map/ppermute | solution.py:352
  54.9 7.0 %collective-permute-start.30 = (bf16[448,128]{1,0:T(8,128)(2,1)S(1)}, bf16[448,128]{1,0:T(8,128)(2,1)S(1)}, u32[]{:S(2)}, u32[]{:S(2)}) collective-permute-start(bf16[448,128]{1,0:T(8,128)(2,1)S(1)} %get-tuple-element.50), channel_id=1, source_target_pairs={{0,8},{8,16},{16,24},{24,28},{28,20},{20,12},{12,4},{4,0},{1,9},{9... | collective-permute-start | bytes 344072 | tf_op jit(solution)/shard_map/ppermute | solution.py:352
  56.5 5.4 %collective-permute-start.31 = (bf16[448,128]{1,0:T(8,128)(2,1)S(1)}, bf16[448,128]{1,0:T(8,128)(2,1)S(1)}, u32[]{:S(2)}, u32[]{:S(2)}) collective-permute-start(bf16[448,128]{1,0:T(8,128)(2,1)S(1)} %get-tuple-element.51), channel_id=1, source_target_pairs={{8,0},{16,8},{24,16},{28,24},{20,28},{12,20},{4,12},{0,4},{9,1},{1... | collective-permute-start | bytes 344072 | tf_op jit(solution)/shard_map/ppermute | solution.py:352
  59.8 8.5 %collective-permute-start.13 = (bf16[896,128]{1,0:T(8,128)(2,1)S(1)}, bf16[896,128]{1,0:T(8,128)(2,1)S(1)}, u32[]{:S(2)}, u32[]{:S(2)}) collective-permute-start(bf16[896,128]{1,0:T(8,128)(2,1)S(1)} %get-tuple-element.42), channel_id=1, source_target_pairs={{0,8},{8,16},{16,24},{24,28},{28,20},{20,12},{12,4},{4,0},{1,9},{9... | collective-permute-start | bytes 688136 | tf_op jit(solution)/shard_map/ppermute | solution.py:356
  61.4 8.3 %collective-permute-start.14 = (bf16[896,128]{1,0:T(8,128)(2,1)S(1)}, bf16[896,128]{1,0:T(8,128)(2,1)S(1)}, u32[]{:S(2)}, u32[]{:S(2)}) collective-permute-start(bf16[896,128]{1,0:T(8,128)(2,1)S(1)} %get-tuple-element.43), channel_id=1, source_target_pairs={{8,0},{16,8},{24,16},{28,24},{20,28},{12,20},{4,12},{0,4},{9,1},{1... | collective-permute-start | bytes 688136 | tf_op jit(solution)/shard_map/ppermute | solution.py:356
  63.2 10.1 %collective-permute-start.32 = (bf16[896,128]{1,0:T(8,128)(2,1)S(1)}, bf16[896,128]{1,0:T(8,128)(2,1)S(1)}, u32[]{:S(2)}, u32[]{:S(2)}) collective-permute-start(bf16[896,128]{1,0:T(8,128)(2,1)S(1)} %get-tuple-element.52), channel_id=1, source_target_pairs={{0,8},{8,16},{16,24},{24,28},{28,20},{20,12},{12,4},{4,0},{1,9},{9... | collective-permute-start | bytes 688136 | tf_op jit(solution)/shard_map/ppermute | solution.py:356
  64.8 24.6 %copy-start.4 = (f32[896,256]{1,0:T(8,128)S(1)}, f32[896,256]{1,0:T(8,128)}, u32[]{:S(2)}) copy-start(f32[896,256]{1,0:T(8,128)} %refs_2_.1) | copy-start | bytes 2752516
  64.8 24.6 %copy-start.5 = (f32[896,256]{1,0:T(8,128)S(1)}, f32[896,256]{1,0:T(8,128)}, u32[]{:S(2)}) copy-start(f32[896,256]{1,0:T(8,128)} %refs_3_.1) | copy-start | bytes 2752516
  64.8 9.8 %collective-permute-start.33 = (bf16[896,128]{1,0:T(8,128)(2,1)S(1)}, bf16[896,128]{1,0:T(8,128)(2,1)S(1)}, u32[]{:S(2)}, u32[]{:S(2)}) collective-permute-start(bf16[896,128]{1,0:T(8,128)(2,1)S(1)} %get-tuple-element.53), channel_id=1, source_target_pairs={{8,0},{16,8},{24,16},{28,24},{20,28},{12,20},{4,12},{0,4},{9,1},{1... | collective-permute-start | bytes 688136 | tf_op jit(solution)/shard_map/ppermute | solution.py:356
  71.0 7.3 %collective-permute-start.15 = (bf16[896,128]{1,0:T(8,128)(2,1)S(1)}, bf16[896,128]{1,0:T(8,128)(2,1)S(1)}, u32[]{:S(2)}, u32[]{:S(2)}) collective-permute-start(bf16[896,128]{1,0:T(8,128)(2,1)S(1)} %get-tuple-element.44), channel_id=1, source_target_pairs={{0,8},{8,16},{16,24},{24,28},{28,20},{20,12},{12,4},{4,0},{1,9},{9... | collective-permute-start | bytes 688136 | tf_op jit(solution)/shard_map/ppermute | solution.py:356
  72.8 6.8 %collective-permute-start.16 = (bf16[896,128]{1,0:T(8,128)(2,1)S(1)}, bf16[896,128]{1,0:T(8,128)(2,1)S(1)}, u32[]{:S(2)}, u32[]{:S(2)}) collective-permute-start(bf16[896,128]{1,0:T(8,128)(2,1)S(1)} %get-tuple-element.45), channel_id=1, source_target_pairs={{8,0},{16,8},{24,16},{28,24},{20,28},{12,20},{4,12},{0,4},{9,1},{1... | collective-permute-start | bytes 688136 | tf_op jit(solution)/shard_map/ppermute | solution.py:356
  75.8 8.5 %collective-permute-start.34 = (bf16[896,128]{1,0:T(8,128)(2,1)S(1)}, bf16[896,128]{1,0:T(8,128)(2,1)S(1)}, u32[]{:S(2)}, u32[]{:S(2)}) collective-permute-start(bf16[896,128]{1,0:T(8,128)(2,1)S(1)} %get-tuple-element.54), channel_id=1, source_target_pairs={{0,8},{8,16},{16,24},{24,28},{28,20},{20,12},{12,4},{4,0},{1,9},{9... | collective-permute-start | bytes 688136 | tf_op jit(solution)/shard_map/ppermute | solution.py:356
  77.7 7.2 %collective-permute-start.35 = (bf16[896,128]{1,0:T(8,128)(2,1)S(1)}, bf16[896,128]{1,0:T(8,128)(2,1)S(1)}, u32[]{:S(2)}, u32[]{:S(2)}) collective-permute-start(bf16[896,128]{1,0:T(8,128)(2,1)S(1)} %get-tuple-element.55), channel_id=1, source_target_pairs={{8,0},{16,8},{24,16},{28,24},{20,28},{12,20},{4,12},{0,4},{9,1},{1... | collective-permute-start | bytes 688136 | tf_op jit(solution)/shard_map/ppermute | solution.py:356
  80.8 17.4 %copy-start.2 = (bf16[1024,256]{1,0:T(8,128)(2,1)S(1)}, bf16[1024,256]{1,0:T(8,128)(2,1)}, u32[]{:S(2)}) copy-start(bf16[1024,256]{1,0:T(8,128)(2,1)} %base.9) | copy-start | bytes 1572868
  80.8 8.5 %collective-permute-start.17 = (bf16[896,128]{1,0:T(8,128)(2,1)S(1)}, bf16[896,128]{1,0:T(8,128)(2,1)S(1)}, u32[]{:S(2)}, u32[]{:S(2)}) collective-permute-start(bf16[896,128]{1,0:T(8,128)(2,1)S(1)} %get-tuple-element.46), channel_id=1, source_target_pairs={{0,8},{8,16},{16,24},{24,28},{28,20},{20,12},{12,4},{4,0},{1,9},{9... | collective-permute-start | bytes 688136 | tf_op jit(solution)/shard_map/ppermute | solution.py:356
  83.0 6.4 %collective-permute-start.18 = (bf16[896,128]{1,0:T(8,128)(2,1)S(1)}, bf16[896,128]{1,0:T(8,128)(2,1)S(1)}, u32[]{:S(2)}, u32[]{:S(2)}) collective-permute-start(bf16[896,128]{1,0:T(8,128)(2,1)S(1)} %get-tuple-element.47), channel_id=1, source_target_pairs={{8,0},{16,8},{24,16},{28,24},{20,28},{12,20},{4,12},{0,4},{9,1},{1... | collective-permute-start | bytes 688136 | tf_op jit(solution)/shard_map/ppermute | solution.py:356
  86.1 8.5 %collective-permute-start.36 = (bf16[896,128]{1,0:T(8,128)(2,1)S(1)}, bf16[896,128]{1,0:T(8,128)(2,1)S(1)}, u32[]{:S(2)}, u32[]{:S(2)}) collective-permute-start(bf16[896,128]{1,0:T(8,128)(2,1)S(1)} %get-tuple-element.56), channel_id=1, source_target_pairs={{0,8},{8,16},{16,24},{24,28},{28,20},{20,12},{12,4},{4,0},{1,9},{9... | collective-permute-start | bytes 688136 | tf_op jit(solution)/shard_map/ppermute | solution.py:356
  87.9 6.8 %collective-permute-start.37 = (bf16[896,128]{1,0:T(8,128)(2,1)S(1)}, bf16[896,128]{1,0:T(8,128)(2,1)S(1)}, u32[]{:S(2)}, u32[]{:S(2)}) collective-permute-start(bf16[896,128]{1,0:T(8,128)(2,1)S(1)} %get-tuple-element.57), channel_id=1, source_target_pairs={{8,0},{16,8},{24,16},{28,24},{20,28},{12,20},{4,12},{0,4},{9,1},{1... | collective-permute-start | bytes 688136 | tf_op jit(solution)/shard_map/ppermute | solution.py:356
  90.6 10.0 %collective-permute-start.19 = (bf16[896,128]{1,0:T(8,128)(2,1)S(1)}, bf16[896,128]{1,0:T(8,128)(2,1)S(1)}, u32[]{:S(2)}, u32[]{:S(2)}) collective-permute-start(bf16[896,128]{1,0:T(8,128)(2,1)S(1)} %get-tuple-element.48.refs_0_), channel_id=1, source_target_pairs={{0,8},{8,16},{16,24},{24,28},{28,20},{20,12},{12,4},{4,0},{1,9},{9... | collective-permute-start | bytes 688136 | tf_op jit(solution)/shard_map/ppermute | solution.py:369
  95.8 8.6 %collective-permute-start.39 = (bf16[896,128]{1,0:T(8,128)(2,1)S(1)}, bf16[896,128]{1,0:T(8,128)(2,1)S(1)}, u32[]{:S(2)}, u32[]{:S(2)}) collective-permute-start(bf16[896,128]{1,0:T(8,128)(2,1)S(1)} %get-tuple-element.58.refs_1_), channel_id=1, source_target_pairs={{0,8},{8,16},{16,24},{24,28},{28,20},{20,12},{12,4},{4,0},{1,9},{9... | collective-permute-start | bytes 688136 | tf_op jit(solution)/shard_map/ppermute | solution.py:369
  96.8 8.9 %collective-permute-start.41 = (bf16[896,128]{1,0:T(8,128)(2,1)S(1)}, bf16[896,128]{1,0:T(8,128)(2,1)S(1)}, u32[]{:S(2)}, u32[]{:S(2)}) collective-permute-start(bf16[896,128]{1,0:T(8,128)(2,1)S(1)} %get-tuple-element.58.refs_1_), channel_id=1, source_target_pairs={{8,0},{16,8},{24,16},{28,24},{20,28},{12,20},{4,12},{0,4},{9,1},{1... | collective-permute-start | bytes 688136 | tf_op jit(solution)/shard_map/ppermute | solution.py:369
  97.9 11.9 %collective-permute-start.40 = (bf16[896,128]{1,0:T(8,128)(2,1)S(1)}, bf16[896,128]{1,0:T(8,128)(2,1)S(1)}, u32[]{:S(2)}, u32[]{:S(2)}) collective-permute-start(bf16[896,128]{1,0:T(8,128)(2,1)S(1)} %get-tuple-element.48.refs_0_), channel_id=1, source_target_pairs={{8,0},{16,8},{24,16},{28,24},{20,28},{12,20},{4,12},{0,4},{9,1},{1... | collective-permute-start | bytes 688136 | tf_op jit(solution)/shard_map/ppermute | solution.py:369
  100.6 14.2 %collective-permute-start.38 = (bf16[896,128]{1,0:T(8,128)(2,1)S(1)}, bf16[896,128]{1,0:T(8,128)(2,1)S(1)}, u32[]{:S(2)}, u32[]{:S(2)}) collective-permute-start(bf16[896,128]{1,0:T(8,128)(2,1)S(1)} %collective-permute-done.19.refs_0_), channel_id=1, source_target_pairs={{0,8},{8,16},{16,24},{24,28},{28,20},{20,12},{12,4},{4,0},{1,9},{9... | collective-permute-start | bytes 688136 | tf_op jit(solution)/shard_map/ppermute | solution.py:369
  104.5 11.2 %collective-permute-start.43 = (bf16[896,128]{1,0:T(8,128)(2,1)S(1)}, bf16[896,128]{1,0:T(8,128)(2,1)S(1)}, u32[]{:S(2)}, u32[]{:S(2)}) collective-permute-start(bf16[896,128]{1,0:T(8,128)(2,1)S(1)} %collective-permute-done.39.refs_1_), channel_id=1, source_target_pairs={{0,8},{8,16},{16,24},{24,28},{28,20},{20,12},{12,4},{4,0},{1,9},{9... | collective-permute-start | bytes 688136 | tf_op jit(solution)/shard_map/ppermute | solution.py:369
  105.7 11.1 %collective-permute-start.45 = (bf16[896,128]{1,0:T(8,128)(2,1)S(1)}, bf16[896,128]{1,0:T(8,128)(2,1)S(1)}, u32[]{:S(2)}, u32[]{:S(2)}) collective-permute-start(bf16[896,128]{1,0:T(8,128)(2,1)S(1)} %collective-permute-done.41.refs_3_), channel_id=1, source_target_pairs={{8,0},{16,8},{24,16},{28,24},{20,28},{12,20},{4,12},{0,4},{9,1},{1... | collective-permute-start | bytes 688136 | tf_op jit(solution)/shard_map/ppermute | solution.py:369
  109.8 9.8 %collective-permute-start.44 = (bf16[896,128]{1,0:T(8,128)(2,1)S(1)}, bf16[896,128]{1,0:T(8,128)(2,1)S(1)}, u32[]{:S(2)}, u32[]{:S(2)}) collective-permute-start(bf16[896,128]{1,0:T(8,128)(2,1)S(1)} %collective-permute-done.40.refs_2_), channel_id=1, source_target_pairs={{8,0},{16,8},{24,16},{28,24},{20,28},{12,20},{4,12},{0,4},{9,1},{1... | collective-permute-start | bytes 688136 | tf_op jit(solution)/shard_map/ppermute | solution.py:369
  114.8 9.8 %collective-permute-start.42 = (bf16[896,128]{1,0:T(8,128)(2,1)S(1)}, bf16[896,128]{1,0:T(8,128)(2,1)S(1)}, u32[]{:S(2)}, u32[]{:S(2)}) collective-permute-start(bf16[896,128]{1,0:T(8,128)(2,1)S(1)} %collective-permute-done.38.refs_0_), channel_id=1, source_target_pairs={{0,8},{8,16},{16,24},{24,28},{28,20},{20,12},{12,4},{4,0},{1,9},{9... | collective-permute-start | bytes 688136 | tf_op jit(solution)/shard_map/ppermute | solution.py:369
  115.7 9.9 %collective-permute-start.47 = (bf16[896,128]{1,0:T(8,128)(2,1)S(1)}, bf16[896,128]{1,0:T(8,128)(2,1)S(1)}, u32[]{:S(2)}, u32[]{:S(2)}) collective-permute-start(bf16[896,128]{1,0:T(8,128)(2,1)S(1)} %collective-permute-done.43.refs_1_), channel_id=1, source_target_pairs={{0,8},{8,16},{16,24},{24,28},{28,20},{20,12},{12,4},{4,0},{1,9},{9... | collective-permute-start | bytes 688136 | tf_op jit(solution)/shard_map/ppermute | solution.py:369
  116.7 10.0 %collective-permute-start.49 = (bf16[896,128]{1,0:T(8,128)(2,1)S(1)}, bf16[896,128]{1,0:T(8,128)(2,1)S(1)}, u32[]{:S(2)}, u32[]{:S(2)}) collective-permute-start(bf16[896,128]{1,0:T(8,128)(2,1)S(1)} %collective-permute-done.45.refs_3_), channel_id=1, source_target_pairs={{8,0},{16,8},{24,16},{28,24},{20,28},{12,20},{4,12},{0,4},{9,1},{1... | collective-permute-start | bytes 688136 | tf_op jit(solution)/shard_map/ppermute | solution.py:369
  119.6 8.1 %collective-permute-start.48 = (bf16[896,128]{1,0:T(8,128)(2,1)S(1)}, bf16[896,128]{1,0:T(8,128)(2,1)S(1)}, u32[]{:S(2)}, u32[]{:S(2)}) collective-permute-start(bf16[896,128]{1,0:T(8,128)(2,1)S(1)} %collective-permute-done.44.refs_2_), channel_id=1, source_target_pairs={{8,0},{16,8},{24,16},{28,24},{20,28},{12,20},{4,12},{0,4},{9,1},{1... | collective-permute-start | bytes 688136 | tf_op jit(solution)/shard_map/ppermute | solution.py:369
  124.7 9.5 %collective-permute-start.46 = (bf16[448,128]{1,0:T(8,128)(2,1)S(1)}, bf16[448,128]{1,0:T(8,128)(2,1)S(1)}, u32[]{:S(2)}, u32[]{:S(2)}) collective-permute-start(bf16[448,128]{1,0:T(8,128)(2,1)S(1)} %slice.36), channel_id=1, source_target_pairs={{0,8},{8,16},{16,24},{24,28},{28,20},{20,12},{12,4},{4,0},{1,9},{9... | collective-permute-start | bytes 344072 | tf_op jit(solution)/shard_map/ppermute | solution.py:375
  125.6 8.6 %collective-permute-start.50 = (bf16[448,128]{1,0:T(8,128)(2,1)S(1)}, bf16[448,128]{1,0:T(8,128)(2,1)S(1)}, u32[]{:S(2)}, u32[]{:S(2)}) collective-permute-start(bf16[448,128]{1,0:T(8,128)(2,1)S(1)} %slice.44), channel_id=1, source_target_pairs={{0,8},{8,16},{16,24},{24,28},{28,20},{20,12},{12,4},{4,0},{1,9},{9... | collective-permute-start | bytes 344072 | tf_op jit(solution)/shard_map/ppermute | solution.py:375
  126.7 7.5 %collective-permute-start.52 = (bf16[448,128]{1,0:T(8,128)(2,1)S(1)}, bf16[448,128]{1,0:T(8,128)(2,1)S(1)}, u32[]{:S(2)}, u32[]{:S(2)}) collective-permute-start(bf16[448,128]{1,0:T(8,128)(2,1)S(1)} %slice.46), channel_id=1, source_target_pairs={{8,0},{16,8},{24,16},{28,24},{20,28},{12,20},{4,12},{0,4},{9,1},{1... | collective-permute-start | bytes 344072 | tf_op jit(solution)/shard_map/ppermute | solution.py:375
  127.8 6.5 %collective-permute-start.51 = (bf16[448,128]{1,0:T(8,128)(2,1)S(1)}, bf16[448,128]{1,0:T(8,128)(2,1)S(1)}, u32[]{:S(2)}, u32[]{:S(2)}) collective-permute-start(bf16[448,128]{1,0:T(8,128)(2,1)S(1)} %slice.45), channel_id=1, source_target_pairs={{8,0},{16,8},{24,16},{28,24},{20,28},{12,20},{4,12},{0,4},{9,1},{1... | collective-permute-start | bytes 344072 | tf_op jit(solution)/shard_map/ppermute | solution.py:375
  (1 other events, 0.7 us)

commit v3 on v2

--- a/solution.py
+++ b/solution.py
@@ -2,7 +2,6 @@
 
 import jax
 import jax.numpy as jnp
-import numpy as np
 from jax import lax
 from jax.experimental import pallas as pl
 from jax.experimental.pallas import tpu as pltpu
@@ -62,6 +61,18 @@
     return pl.BlockSpec(memory_space=pltpu.SMEM)
 
 
+def ring_order(n):
+    return [*range(0, n, 2), *range(n - 1, 0, -2)]
+
+
+def chunk_at(here, away, n):
+    index = here[0]
+    step = lax.shift_right_logical(index, 1)
+    place = lax.select(lax.bitwise_and(index, 1) == 0, step, n - 1 - step)
+    there = lax.rem(place + away, n)
+    return lax.select(there < n // 2, 2 * there, 2 * (n - 1 - there) + 1)
+
+
 def kept_on_chip(arrays):
     return [pltpu.with_memory_space_constraint(a, pltpu.VMEM) for a in arrays]
 
@@ -74,7 +85,7 @@
         kept[...] = own[...]
         sent[...] = other[...]
 
-    half = jax.ShapeDtypeStruct((tokens, features // 2), activations.dtype)
+    half = pltpu.VMEM((tokens, features // 2), activations.dtype)
     return pl.pallas_call(
         kernel,
         out_shape=(half, half),
@@ -82,8 +93,8 @@
             num_scalar_prefetch=1,
             grid=(n,),
             in_specs=[
-                pl.BlockSpec((tokens, part), lambda j, me: (0, 2 * j + me[0] % 2)),
-                pl.BlockSpec((tokens, part), lambda j, me: (0, 2 * j + 1 - me[0] % 2)),
+                pl.BlockSpec((tokens, part), lambda j, me: (0, 2 * j + lax.bitwise_and(me[0], 1))),
+                pl.BlockSpec((tokens, part), lambda j, me: (0, 2 * j + 1 - lax.bitwise_and(me[0], 1))),
             ],
             out_specs=(pl.BlockSpec((tokens, part), lambda j, me: (0, j)),) * 2,
         ),
@@ -92,20 +103,20 @@
     )(me, activations, activations)
 
 
-def add_coords(ids, me, kept, came, total, pieces, depth):
+def add_coords(here, me, kept, came, total, pieces, depth, n):
     tokens, width = kept.shape[0], pieces[0][0].shape[1]
     held = () if total is None else (total,)
     arrays = [piece for piece, _, _ in pieces]
 
-    def kernel(ids_ref, me_ref, *refs):
+    def kernel(here_ref, me_ref, *refs):
         out = refs[-1]
-        side = me_ref[0] % 2
+        side = lax.bitwise_and(me_ref[0], 1)
         refs_of = refs[2 + len(held) : -1]
         for act, place in ((refs[0], side), (refs[1], 1 - side)):
             rows = pl.ds(pl.multiple_of(place * tokens, tokens), tokens)
             acc = refs[2][rows] if held else jnp.zeros((tokens, width), jnp.float32)
             for ref, (_, away, low) in zip(refs_of, pieces, strict=True):
-                start = pl.multiple_of(ids_ref[away] * depth + low, 128)
+                start = pl.multiple_of(chunk_at(here_ref, away, n) * depth + low, 128)
                 acc += jnp.dot(
                     act[:, pl.ds(start, ref.shape[0])], ref[...], preferred_element_type=jnp.float32
                 )
@@ -121,25 +132,25 @@
         ),
         compiler_params=pltpu.CompilerParams(vmem_limit_bytes=SCRATCH_BYTES),
         name="add_coords",
-    )(ids, me, *kept_on_chip([kept, came, *held, *arrays]))
+    )(here, me, *kept_on_chip([kept, came, *held, *arrays]))
 
 
 def contract_tokens(grad, coords):
     return lax.dot_general(grad, coords, (((0,), (0,)), ((), ())), preferred_element_type=jnp.float32)
 
 
-def first_partials(ids, me, grad_out, parts, n):
+def first_partials(here, me, grad_out, parts, n):
     group, width = parts[0].shape
     tokens, all_columns = grad_out.shape
     cols = all_columns // n
     groups = tokens // group
 
-    def kernel(ids_ref, me_ref, grad, *refs):
+    def kernel(here_ref, me_ref, grad, *refs):
         coords, top, bottom = refs[len(parts) :]
         for k, ref in enumerate(refs[: len(parts)]):
-            at = lax.rem(me_ref[0] // 2 + groups - k, groups)
+            at = lax.rem(lax.shift_right_logical(me_ref[0], 1) + groups - k, groups)
             coords[pl.ds(pl.multiple_of(at * group, group), group)] = ref[...]
-        column = pl.multiple_of(ids_ref[n // 2] * cols, 128)
+        column = pl.multiple_of(chunk_at(here_ref, n // 2, n) * cols, 128)
         part = contract_tokens(grad[:, pl.ds(column, cols)], coords[...]).astype(jnp.bfloat16)
         top[...] = part[: cols // 2]
         bottom[...] = part[cols // 2 :]
@@ -155,21 +166,21 @@
         ),
         compiler_params=pltpu.CompilerParams(vmem_limit_bytes=SCRATCH_BYTES),
         name="first_partials",
-    )(ids, me, *kept_on_chip([grad_out, *parts]))
-
-
-def next_partials(ids, grad_out, coords, came_up, came_down, n, away):
+    )(here, me, *kept_on_chip([grad_out, *parts]))
+
+
+def next_partials(here, grad_out, coords, came_up, came_down, n, away):
     tokens, width = coords.shape
     cols = grad_out.shape[1] // n
     rows = came_up.shape[0]
 
-    def kernel(ids_ref, grad, coord, in_up, in_down, up, down):
-        column = pl.multiple_of(ids_ref[away] * cols, 128)
+    def kernel(here_ref, grad, coord, in_up, in_down, up, down):
+        column = pl.multiple_of(chunk_at(here_ref, away, n) * cols, 128)
         part = contract_tokens(grad[:, pl.ds(column, cols)], coord[...])
         up[:rows] = (part[:rows] + in_up[...].astype(jnp.float32)).astype(jnp.bfloat16)
         if rows < cols:
             up[rows:] = part[rows:].astype(jnp.bfloat16)
-        column = pl.multiple_of(ids_ref[n - away] * cols, 128)
+        column = pl.multiple_of(chunk_at(here_ref, n - away, n) * cols, 128)
         part = contract_tokens(grad[:, pl.ds(column, cols)], coord[...])
         rest = cols - rows
         down[rest:] = (part[rest:] + in_down[...].astype(jnp.float32)).astype(jnp.bfloat16)
@@ -187,15 +198,15 @@
         ),
         compiler_params=pltpu.CompilerParams(vmem_limit_bytes=SCRATCH_BYTES),
         name="next_partials",
-    )(ids, *kept_on_chip([grad_out, coords, came_up, came_down]))
-
-
-def own_direction(ids, grad_out, coords, came_up, came_down, first_moment, second_moment, s, n):
+    )(here, *kept_on_chip([grad_out, coords, came_up, came_down]))
+
+
+def own_direction(here, grad_out, coords, came_up, came_down, first_moment, second_moment, s, n):
     tokens, width = coords.shape
     cols = grad_out.shape[1] // n
 
-    def kernel(ids_ref, grad, coord, in_up, in_down, first, second, projected, direction):
-        column = pl.multiple_of(ids_ref[0] * cols, 128)
+    def kernel(here_ref, grad, coord, in_up, in_down, first, second, projected, direction):
+        column = pl.multiple_of(here_ref[0] * cols, 128)
         total = (
             contract_tokens(grad[:, pl.ds(column, cols)], coord[...])
             + in_up[...].astype(jnp.float32)
@@ -218,7 +229,7 @@
         ),
         compiler_params=pltpu.CompilerParams(vmem_limit_bytes=SCRATCH_BYTES),
         name="own_direction",
-    )(ids, *kept_on_chip([grad_out, coords, came_up, came_down, first_moment, second_moment]))
+    )(here, *kept_on_chip([grad_out, coords, came_up, came_down, first_moment, second_moment]))
 
 
 def new_moments(projected, first_moment, second_moment):
@@ -246,14 +257,14 @@
     )(*kept_on_chip([*projected, first_moment, second_moment]))
 
 
-def write_update(ids, basis, chunks, places, update, all_columns):
+def write_update(here, basis, chunks, places, update, all_columns):
     depth, rank = basis.shape
     cols = sum(row[0].shape[0] for row in chunks[0])
     flat = [stream for chunk in chunks for row in chunk for stream in row]
     held = () if update is None else (update,)
     tile = depth // 2
 
-    def kernel(ids_ref, base, *refs):
+    def kernel(here_ref, base, *refs):
         out = refs[-1]
         left = list(refs[: len(flat)])
         lines = pl.ds(pl.multiple_of(pl.program_id(1) * tile, tile), tile)
@@ -269,10 +280,12 @@
                     base[lines], whole, (((1,), (1,)), ((), ())), preferred_element_type=jnp.float32
                 ).astype(out.dtype)
 
-    def place(g, r, ids):
-        at = ids[places[0]]
+    n = all_columns // cols
+
+    def place(g, r, here):
+        at = chunk_at(here, places[0], n)
         for k in range(1, len(places)):
-            at = jnp.where(g == k, ids[places[k]], at)
+            at = jnp.where(g == k, chunk_at(here, places[k], n), at)
         return (r, at)
 
     return pl.pallas_call(
@@ -295,22 +308,22 @@
         ),
         compiler_params=pltpu.CompilerParams(vmem_limit_bytes=SCRATCH_BYTES),
         name="write_update",
-    )(ids, *kept_on_chip([basis, *flat]), *held)
+    )(here, *kept_on_chip([basis, *flat]), *held)
 
 
 def on_ring(n, m, activations, grad_out, basis, first_moment, second_moment):
-    order = [*range(0, n, 2), *range(n - 1, 0, -2)]
+    order = ring_order(n)
     upward = [(order[k], order[(k + 1) % n]) for k in range(n)]
     downward = [(b, a) for a, b in upward]
-    up = functools.partial(lax.ppermute, axis_name="dp", perm=upward)
-    down = functools.partial(lax.ppermute, axis_name="dp", perm=downward)
-    swap = functools.partial(lax.ppermute, axis_name="mp", perm=[(k, k ^ 1) for k in range(m)])
-
-    around = np.zeros((n, n), np.int32)
-    for place, index in enumerate(order):
-        around[index] = [order[(place + away) % n] for away in range(n)]
-    ids = jnp.asarray(around)[lax.axis_index("dp")]
-    me = lax.axis_index("mp").reshape(1)
+    partners = [(k, k ^ 1) for k in range(m)]
+
+    def hop(to_up, to_down):
+        return (lax.ppermute(to_up, "dp", upward), lax.ppermute(to_down, "dp", downward))
+
+    me = lax.axis_index("mp")
+    here, me, side, activations, basis = lax.optimization_barrier(
+        (lax.axis_index("dp").reshape(1), me.reshape(1), lax.bitwise_and(me, 1), activations, basis)
+    )
 
     depth, rank = basis.shape
     width = rank // STREAMS
@@ -320,61 +333,57 @@
     streams = range(STREAMS)
 
     part = depth // 2
-    own = lax.dynamic_slice(basis, (me[0] % 2 * part, 0), (part, rank))
+    own = lax.dynamic_slice(basis, (side * part, 0), (part, rank))
     own = [own[:, s * width : (s + 1) * width] for s in streams]
-    sent_up, sent_down = list(own), list(own)
+    ups, downs = list(own), list(own)
     pieces = [[(own[s], 0, 0)] for s in streams]
     kept, sent = split_columns(me, activations, n)
-    came = swap(sent)
+    came = lax.ppermute(sent, "mp", partners)
     total = [None] * STREAMS
     for k in range(1, half + 1):
         for s in streams:
             low = 0
             if k == half:
                 low = part // 2
-                sent_up[s], sent_down[s] = sent_up[s][:low], sent_down[s][low:]
-            sent_up[s], sent_down[s] = up(sent_up[s]), down(sent_down[s])
-            pieces[s] += [(sent_up[s], n - k, 0), (sent_down[s], k, low)]
-            if k >= half - 1:
-                total[s] = add_coords(ids, me, kept, came, total[s], pieces[s], part)
+                ups[s], downs[s] = ups[s][:low], downs[s][low:]
+                total[s] = add_coords(here, me, kept, came, None, pieces[s], part, n)
                 pieces[s] = []
+            ups[s], downs[s] = hop(ups[s], downs[s])
+            pieces[s] += [(ups[s], n - k, 0), (downs[s], k, low)]
+    for s in streams:
+        total[s] = add_coords(here, me, kept, came, total[s], pieces[s], part, n)
 
     parts = [None] * STREAMS
     for s in streams:
-        pair = (total[s] + swap(total[s])).astype(jnp.bfloat16)
-        parts[s] = [pair] + [
-            lax.ppermute(pair, "mp", [(a, (a + k) % m) for a in range(m)]) for k in range(2, m, 2)
-        ]
+        other = lax.ppermute(total[s], "mp", partners)
+        pair = (total[s] + other).astype(jnp.bfloat16)
+        parts[s] = [pair] + [lax.ppermute(pair, "mp", [(a, (a + k) % m) for a in range(m)]) for k in range(2, m, 2)]
 
     coords = [None] * STREAMS
     for s in streams:
-        coords[s], top, bottom = first_partials(ids, me, grad_out, parts[s], n)
-        sent_up[s], sent_down[s] = up(top), down(bottom)
-    for away in range(half - 1, 0, -1):
+        coords[s], ups[s], downs[s] = first_partials(here, me, grad_out, parts[s], n)
+        ups[s], downs[s] = hop(ups[s], downs[s])
+    for k in range(2, half + 1):
         for s in streams:
-            to_up, to_down = next_partials(ids, grad_out, coords[s], sent_up[s], sent_down[s], n, away)
-            sent_up[s], sent_down[s] = up(to_up), down(to_down)
+            ups[s], downs[s] = next_partials(here, grad_out, coords[s], ups[s], downs[s], n, half + 1 - k)
+            ups[s], downs[s] = hop(ups[s], downs[s])
     projected = [None] * STREAMS
     direction = [None] * STREAMS
     for s in streams:
         projected[s], direction[s] = own_direction(
-            ids, grad_out, coords[s], sent_up[s], sent_down[s], first_moment, second_moment, s, n
+            here, grad_out, coords[s], ups[s], downs[s], first_moment, second_moment, s, n,
         )
 
-    sent_up, sent_down = list(direction), list(direction)
-    update = write_update(ids, basis, [[direction]], [0], None, all_columns)
+    ups, downs = list(direction), list(direction)
+    update = write_update(here, basis, [[direction]], [0], None, all_columns)
     first_new, second_new = new_moments(projected, first_moment, second_moment)
     for k in range(1, half):
         for s in streams:
-            sent_up[s], sent_down[s] = up(sent_up[s]), down(sent_down[s])
-        sent_up[0], update = lax.optimization_barrier((sent_up[0], update))
-        update = write_update(
-            ids, basis, [[list(sent_up)], [list(sent_down)]], [n - k, k], update, all_columns
-        )
+            ups[s], downs[s] = hop(ups[s], downs[s])
+        update = write_update(here, basis, [[list(ups)], [list(downs)]], [n - k, k], update, all_columns)
     for s in streams:
-        sent_up[s], sent_down[s] = up(sent_up[s][: cols // 2]), down(sent_down[s][cols // 2 :])
-    sent_up[0], update = lax.optimization_barrier((sent_up[0], update))
-    update = write_update(ids, basis, [[sent_up, sent_down]], [half], update, all_columns)
+        ups[s], downs[s] = hop(ups[s][: cols // 2], downs[s][cols // 2 :])
+    update = write_update(here, basis, [[ups, downs]], [half], update, all_columns)
     return (update, first_new, second_new)
 
 

time: 137 us -> 131 us (0.956)
  waiting for transfers between devices: 30.8 us -> 39.9 us
  Pallas kernels: 39.8 us -> 31.3 us
  local copies, waits for them, and re-layouts: 9.64 us -> 5.02 us
  starting transfers between devices: 55.5 us -> 53.9 us
    ppermute x51, waiting for transfers between devices: 29 us -> 38.2 us  [the longest x24 25 us: hop(): lax.ppermute(to_up, 'dp', upward)]
    pallas_call x6, Pallas kernels: 7.57 us -> 4.33 us  [next_partials(): pl.pallas_call(kernel, out_shape=(full, full), in_specs=[scalars(), *[on_...]
    unnamed x24 -> x16, local copies, waits for them, and re-layouts: 7.07 us -> 3.98 us
    pallas_call x5, Pallas kernels: 16.5 us -> 13.7 us  [write_update(): pl.pallas_call(kernel, out_shape=jax.ShapeDtypeStruct((depth, all_columns...]
    ppermute x51, starting transfers between devices: 52.6 us -> 51 us  [the longest x24 31.2 us: hop(): lax.ppermute(to_up, 'dp', upward)]
  transfers between devices with their start and end apart: 53 -> 53, of which waited for: 23 -> 27; matrix products, arithmetic and copies ran while one was open for 2% -> 1% of each run, Pallas kernels for 25% -> 20%
where the time goes in v3:
time: 131 us
  starting transfers between devices  53.9 us (41%)
  waiting for transfers between devices  39.9 us (30%)
  Pallas kernels  31.3 us (24%)
  local copies, waits for them, and re-layouts  5.02 us (4%)
    ppermute x24, starting transfers between devices, hop(): lax.ppermute(to_up, 'dp', upward)  31.2 us
    ppermute x24, waiting for transfers between devices, hop(): lax.ppermute(to_up, 'dp', upward)  25 us
    ppermute x24, starting transfers between devices, hop(): lax.ppermute(to_down, 'dp', downward)  19.2 us
    pallas_call x5, Pallas kernels, write_update(): pl.pallas_call(kernel, out_shape=jax.ShapeDtypeStruct((depth, all_columns...  13.7 us
    ppermute x24, waiting for transfers between devices, hop(): lax.ppermute(to_down, 'dp', downward)  13.1 us
    pallas_call x4, Pallas kernels, add_coords(): pl.pallas_call(kernel, out_shape=pltpu.VMEM((2 * tokens, width), jnp.floa...  6.7 us
    pallas_call x6, Pallas kernels, next_partials(): pl.pallas_call(kernel, out_shape=(full, full), in_specs=[scalars(), *[on_...  4.33 us
    unnamed x16, local copies, waits for them, and re-layouts  3.98 us
  transfers between devices with their start and end apart: 53, of which 27 were waited for; matrix products, arithmetic and copies ran while one was open for 1% of the time, Pallas kernels for 20%

profile of v3, /device:TPU:0, one launch (start us, length us, event | category | flops | bytes accessed | tf_op | source)
XLA Modules:
  0.0 131.1 jit_solution(18402371371963110743)
XLA Ops:
  0.7 1.7 %copy-done.3 = bf16[128,8192]{1,0:T(8,128)(2,1)S(1)} copy-done((bf16[128,8192]{1,0:T(8,128)(2,1)S(1)}, bf16[128,8192]{1,0:T(8,128)(2,1)}, u32[]{:S(2)}) %copy-start.3) | copy-done | bytes 2097176
  2.4 2.9 %split_columns.1 = (bf16[128,4096]{1,0:T(8,128)(2,1)S(1)}, bf16[128,4096]{1,0:T(8,128)(2,1)}) custom-call(s32[1]{0:T(128)} %bitcast.1.me_ref, bf16[128,8192]{1,0:T(8,128)(2,1)S(1)} %copy-done.3, bf16[128,8192]{1,0:T(8,128)(2,1)S(1)} %copy-done.3), custom_call_target="tpu_custom_call" | custom-call | tf_op jit(solution)/shard_map/split_columns/pallas_call | solution.py:89
  5.3 1.0 copy-done
  6.8 1.0 fusion
  7.8 2.6 %collective-permute-start.23 = (bf16[512,128]{1,0:T(8,128)(2,1)S(1)}, bf16[512,128]{1,0:T(8,128)(2,1)S(1)}, u32[]{:S(2)}, u32[]{:S(2)}) collective-permute-start(bf16[512,128]{1,0:T(8,128)(2,1)S(1)} %get-tuple-element.65.refs_2_), channel_id=1, source_target_pairs={{0,8},{8,16},{16,24},{24,28},{28,20},{20,12},{12,4},{4,0},{1,9},{9... | collective-permute-start | bytes 393224 | tf_op jit(solution)/shard_map/ppermute | solution.py:321
  10.4 2.0 %collective-permute-start.1 = (bf16[512,128]{1,0:T(8,128)(2,1)S(1)}, bf16[512,128]{1,0:T(8,128)(2,1)S(1)}, u32[]{:S(2)}, u32[]{:S(2)}) collective-permute-start(bf16[512,128]{1,0:T(8,128)(2,1)S(1)} %get-tuple-element.66.refs_2_), channel_id=1, source_target_pairs={{0,8},{8,16},{16,24},{24,28},{28,20},{20,12},{12,4},{4,0},{1,9},{9... | collective-permute-start | bytes 393224 | tf_op jit(solution)/shard_map/ppermute | solution.py:321
  12.5 2.3 %collective-permute-done.23.refs_3_ = bf16[512,128]{1,0:T(8,128)(2,1)S(1)} collective-permute-done((bf16[512,128]{1,0:T(8,128)(2,1)S(1)}, bf16[512,128]{1,0:T(8,128)(2,1)S(1)}, u32[]{:S(2)}, u32[]{:S(2)}) %collective-permute-start.23) | collective-permute-done | bytes 131104 | tf_op jit(solution)/shard_map/ppermute | solution.py:321
  14.7 2.1 %collective-permute-start.25 = (bf16[512,128]{1,0:T(8,128)(2,1)S(1)}, bf16[512,128]{1,0:T(8,128)(2,1)S(1)}, u32[]{:S(2)}, u32[]{:S(2)}) collective-permute-start(bf16[512,128]{1,0:T(8,128)(2,1)S(1)} %collective-permute-done.23.refs_3_), channel_id=1, source_target_pairs={{0,8},{8,16},{16,24},{24,28},{28,20},{20,12},{12,4},{4,0},{1,9},{9... | collective-permute-start | bytes 393224 | tf_op jit(solution)/shard_map/ppermute | solution.py:321
  17.5 2.1 %collective-permute-start.3 = (bf16[512,128]{1,0:T(8,128)(2,1)S(1)}, bf16[512,128]{1,0:T(8,128)(2,1)S(1)}, u32[]{:S(2)}, u32[]{:S(2)}) collective-permute-start(bf16[512,128]{1,0:T(8,128)(2,1)S(1)} %collective-permute-done.1.refs_3_), channel_id=1, source_target_pairs={{0,8},{8,16},{16,24},{24,28},{28,20},{20,12},{12,4},{4,0},{1,9},{9... | collective-permute-start | bytes 393224 | tf_op jit(solution)/shard_map/ppermute | solution.py:321
  19.6 0.8 collective-permute-done.25.refs_5_
  20.4 2.1 %collective-permute-start.27 = (bf16[512,128]{1,0:T(8,128)(2,1)S(1)}, bf16[512,128]{1,0:T(8,128)(2,1)S(1)}, u32[]{:S(2)}, u32[]{:S(2)}) collective-permute-start(bf16[512,128]{1,0:T(8,128)(2,1)S(1)} %collective-permute-done.25.refs_5_), channel_id=1, source_target_pairs={{0,8},{8,16},{16,24},{24,28},{28,20},{20,12},{12,4},{4,0},{1,9},{9... | collective-permute-start | bytes 393224 | tf_op jit(solution)/shard_map/ppermute | solution.py:321
  22.5 1.4 %collective-permute-done.3.refs_5_ = bf16[512,128]{1,0:T(8,128)(2,1)S(1)} collective-permute-done((bf16[512,128]{1,0:T(8,128)(2,1)S(1)}, bf16[512,128]{1,0:T(8,128)(2,1)S(1)}, u32[]{:S(2)}, u32[]{:S(2)}) %collective-permute-start.3) | collective-permute-done | bytes 131104 | tf_op jit(solution)/shard_map/ppermute | solution.py:321
  23.9 2.1 %collective-permute-start.5 = (bf16[512,128]{1,0:T(8,128)(2,1)S(1)}, bf16[512,128]{1,0:T(8,128)(2,1)S(1)}, u32[]{:S(2)}, u32[]{:S(2)}) collective-permute-start(bf16[512,128]{1,0:T(8,128)(2,1)S(1)} %collective-permute-done.3.refs_5_), channel_id=1, source_target_pairs={{0,8},{8,16},{16,24},{24,28},{28,20},{20,12},{12,4},{4,0},{1,9},{9... | collective-permute-start | bytes 393224 | tf_op jit(solution)/shard_map/ppermute | solution.py:321
  26.8 2.1 %collective-permute-start.29 = (bf16[256,128]{1,0:T(8,128)(2,1)S(1)}, bf16[256,128]{1,0:T(8,128)(2,1)S(1)}, u32[]{:S(2)}, u32[]{:S(2)}) collective-permute-start(bf16[256,128]{1,0:T(8,128)(2,1)S(1)} %slice.43), channel_id=1, source_target_pairs={{0,8},{8,16},{16,24},{24,28},{28,20},{20,12},{12,4},{4,0},{1,9},{9... | collective-permute-start | bytes 196616 | tf_op jit(solution)/shard_map/ppermute | solution.py:321
  29.0 1.2 copy-done.1
  30.2 1.9 %add_coords.6.refs_2_ = f32[256,128]{1,0:T(8,128)S(1)} custom-call(s32[1]{0:T(128)} %bitcast.here_ref, s32[1]{0:T(128)} %bitcast.1.me_ref, bf16[128,4096]{1,0:T(8,128)(2,1)S(1)} %copy-done.1, bf16[128,4096]{1,0:T(8,128)(2,1)} %collective-permute-done.refs_1_, bf16[512,128]{1,0:T(8,128)(2,1)S(1)} %get-tuple-element.65.refs_2_, ...), custom_call_target="tpu_custom_call" | custom-call | flops 234881024 | bytes 4194304 | tf_op jit(solution)/shard_map/add_coords/pallas_call | solution.py:125
  32.1 1.1 collective-permute-done.30.refs_4_
  33.2 1.6 %add_coords.7 = f32[256,128]{1,0:T(8,128)S(1)} custom-call(s32[1]{0:T(128)} %bitcast.here_ref, s32[1]{0:T(128)} %bitcast.1.me_ref, bf16[128,4096]{1,0:T(8,128)(2,1)S(1)} %copy-done.1, bf16[128,4096]{1,0:T(8,128)(2,1)} %collective-permute-done.refs_1_, f32[256,128]{1,0:T(8,128)S(1)} %add_coords.6.refs_2_, ...), custom_call_target="tpu_custom_call" | custom-call | flops 33554432 | bytes 4194304 | tf_op jit(solution)/shard_map/add_coords/pallas_call | solution.py:125
  34.9 1.9 %collective-permute-start.7 = (bf16[256,128]{1,0:T(8,128)(2,1)S(1)}, bf16[256,128]{1,0:T(8,128)(2,1)S(1)}, u32[]{:S(2)}, u32[]{:S(2)}) collective-permute-start(bf16[256,128]{1,0:T(8,128)(2,1)S(1)} %slice.40), channel_id=1, source_target_pairs={{0,8},{8,16},{16,24},{24,28},{28,20},{20,12},{12,4},{4,0},{1,9},{9... | collective-permute-start | bytes 196616 | tf_op jit(solution)/shard_map/ppermute | solution.py:321
  37.0 1.9 %add_coords.4.refs_2_ = f32[256,128]{1,0:T(8,128)S(1)} custom-call(s32[1]{0:T(128)} %bitcast.here_ref, s32[1]{0:T(128)} %bitcast.1.me_ref, bf16[128,4096]{1,0:T(8,128)(2,1)S(1)} %copy-done.1, bf16[128,4096]{1,0:T(8,128)(2,1)} %collective-permute-done.refs_1_, bf16[512,128]{1,0:T(8,128)(2,1)S(1)} %get-tuple-element.66.refs_2_, ...), custom_call_target="tpu_custom_call" | custom-call | flops 234881024 | bytes 4194304 | tf_op jit(solution)/shard_map/add_coords/pallas_call | solution.py:125
  39.4 1.7 %collective-permute-done.8.refs_4_ = bf16[256,128]{1,0:T(8,128)(2,1)S(1)} collective-permute-done((bf16[256,128]{1,0:T(8,128)(2,1)S(1)}, bf16[256,128]{1,0:T(8,128)(2,1)S(1)}, u32[]{:S(2)}, u32[]{:S(2)}) %collective-permute-start.8) | collective-permute-done | bytes 65568 | tf_op jit(solution)/shard_map/ppermute | solution.py:321
  41.1 1.4 %add_coords.5 = f32[256,128]{1,0:T(8,128)S(1)} custom-call(s32[1]{0:T(128)} %bitcast.here_ref, s32[1]{0:T(128)} %bitcast.1.me_ref, bf16[128,4096]{1,0:T(8,128)(2,1)S(1)} %copy-done.1, bf16[128,4096]{1,0:T(8,128)(2,1)} %collective-permute-done.refs_1_, f32[256,128]{1,0:T(8,128)S(1)} %add_coords.4.refs_2_, ...), custom_call_target="tpu_custom_call" | custom-call | flops 33554432 | bytes 4194304 | tf_op jit(solution)/shard_map/add_coords/pallas_call | solution.py:125
  42.7 1.6 %collective-permute-start.32 = (bf16[256,128]{1,0:T(8,128)(2,1)S(1)}, bf16[256,128]{1,0:T(8,128)(2,1)S(1)}, u32[]{:S(2)}, u32[]{:S(2)}) collective-permute-start(bf16[256,128]{1,0:T(8,128)(2,1)S(1)} %add_convert_fusion.refs_0_), channel_id=1, source_target_pairs={{0,2},{1,3},{2,0},{3,1},{4,6},{5,7},{6,4},{7,5},{8,10},{9,11},{10,... | collective-permute-start | bytes 196616 | tf_op jit(solution)/shard_map/ppermute | solution.py:360
  44.2 1.3 collective-permute-start.10
  45.5 1.8 %collective-permute-done.32.refs_1_ = bf16[256,128]{1,0:T(8,128)(2,1)S(1)} collective-permute-done((bf16[256,128]{1,0:T(8,128)(2,1)S(1)}, bf16[256,128]{1,0:T(8,128)(2,1)S(1)}, u32[]{:S(2)}, u32[]{:S(2)}) %collective-permute-start.32) | collective-permute-done | bytes 65568 | tf_op jit(solution)/shard_map/ppermute | solution.py:360
  47.8 1.6 %collective-permute-start.33 = (bf16[448,128]{1,0:T(8,128)(2,1)S(1)}, bf16[448,128]{1,0:T(8,128)(2,1)S(1)}, u32[]{:S(2)}, u32[]{:S(2)}) collective-permute-start(bf16[448,128]{1,0:T(8,128)(2,1)S(1)} %get-tuple-element.52), channel_id=1, source_target_pairs={{0,8},{8,16},{16,24},{24,28},{28,20},{20,12},{12,4},{4,0},{1,9},{9... | collective-permute-start | bytes 344072 | tf_op jit(solution)/shard_map/ppermute | solution.py:321
  50.4 1.6 %collective-permute-start.11 = (bf16[448,128]{1,0:T(8,128)(2,1)S(1)}, bf16[448,128]{1,0:T(8,128)(2,1)S(1)}, u32[]{:S(2)}, u32[]{:S(2)}) collective-permute-start(bf16[448,128]{1,0:T(8,128)(2,1)S(1)} %get-tuple-element.42), channel_id=1, source_target_pairs={{0,8},{8,16},{16,24},{24,28},{28,20},{20,12},{12,4},{4,0},{1,9},{9... | collective-permute-start | bytes 344072 | tf_op jit(solution)/shard_map/ppermute | solution.py:321
  52.5 0.8 collective-permute-done.33.in_up
  53.3 1.9 %collective-permute-done.34.in_down = bf16[448,128]{1,0:T(8,128)(2,1)S(1)} collective-permute-done((bf16[448,128]{1,0:T(8,128)(2,1)S(1)}, bf16[448,128]{1,0:T(8,128)(2,1)S(1)}, u32[]{:S(2)}, u32[]{:S(2)}) %collective-permute-start.34) | collective-permute-done | bytes 114720 | tf_op jit(solution)/shard_map/ppermute | solution.py:321
  55.9 1.5 %collective-permute-start.35 = (bf16[896,128]{1,0:T(8,128)(2,1)S(1)}, bf16[896,128]{1,0:T(8,128)(2,1)S(1)}, u32[]{:S(2)}, u32[]{:S(2)}) collective-permute-start(bf16[896,128]{1,0:T(8,128)(2,1)S(1)} %get-tuple-element.54), channel_id=1, source_target_pairs={{0,8},{8,16},{16,24},{24,28},{28,20},{20,12},{12,4},{4,0},{1,9},{9... | collective-permute-start | bytes 688136 | tf_op jit(solution)/shard_map/ppermute | solution.py:321
  58.7 1.5 %collective-permute-start.13 = (bf16[896,128]{1,0:T(8,128)(2,1)S(1)}, bf16[896,128]{1,0:T(8,128)(2,1)S(1)}, u32[]{:S(2)}, u32[]{:S(2)}) collective-permute-start(bf16[896,128]{1,0:T(8,128)(2,1)S(1)} %get-tuple-element.44), channel_id=1, source_target_pairs={{0,8},{8,16},{16,24},{24,28},{28,20},{20,12},{12,4},{4,0},{1,9},{9... | collective-permute-start | bytes 688136 | tf_op jit(solution)/shard_map/ppermute | solution.py:321
  60.8 3.3 %collective-permute-done.35.in_up = bf16[896,128]{1,0:T(8,128)(2,1)S(1)} collective-permute-done((bf16[896,128]{1,0:T(8,128)(2,1)S(1)}, bf16[896,128]{1,0:T(8,128)(2,1)S(1)}, u32[]{:S(2)}, u32[]{:S(2)}) %collective-permute-start.35) | collective-permute-done | bytes 229408 | tf_op jit(solution)/shard_map/ppermute | solution.py:321
  64.1 1.8 %collective-permute-done.36.in_down = bf16[896,128]{1,0:T(8,128)(2,1)S(1)} collective-permute-done((bf16[896,128]{1,0:T(8,128)(2,1)S(1)}, bf16[896,128]{1,0:T(8,128)(2,1)S(1)}, u32[]{:S(2)}, u32[]{:S(2)}) %collective-permute-start.36) | collective-permute-done | bytes 229408 | tf_op jit(solution)/shard_map/ppermute | solution.py:321
  67.4 1.3 collective-permute-start.38
  69.0 1.8 %collective-permute-done.14.in_down = bf16[896,128]{1,0:T(8,128)(2,1)S(1)} collective-permute-done((bf16[896,128]{1,0:T(8,128)(2,1)S(1)}, bf16[896,128]{1,0:T(8,128)(2,1)S(1)}, u32[]{:S(2)}, u32[]{:S(2)}) %collective-permute-start.14) | collective-permute-done | bytes 229408 | tf_op jit(solution)/shard_map/ppermute | solution.py:321
  72.3 1.3 collective-permute-start.16
  73.6 0.9 collective-permute-done.37.in_up
  74.5 1.4 %collective-permute-done.38.in_down = bf16[896,128]{1,0:T(8,128)(2,1)S(1)} collective-permute-done((bf16[896,128]{1,0:T(8,128)(2,1)S(1)}, bf16[896,128]{1,0:T(8,128)(2,1)S(1)}, u32[]{:S(2)}, u32[]{:S(2)}) %collective-permute-start.38) | collective-permute-done | bytes 229408 | tf_op jit(solution)/shard_map/ppermute | solution.py:321
  77.2 1.5 %collective-permute-start.40 = (bf16[896,128]{1,0:T(8,128)(2,1)S(1)}, bf16[896,128]{1,0:T(8,128)(2,1)S(1)}, u32[]{:S(2)}, u32[]{:S(2)}) collective-permute-start(bf16[896,128]{1,0:T(8,128)(2,1)S(1)} %get-tuple-element.59), channel_id=1, source_target_pairs={{8,0},{16,8},{24,16},{28,24},{20,28},{12,20},{4,12},{0,4},{9,1},{1... | collective-permute-start | bytes 688136 | tf_op jit(solution)/shard_map/ppermute | solution.py:321
  78.7 0.9 collective-permute-done.15.in_up
  79.6 1.2 collective-permute-done.16.in_down
  82.1 1.5 %collective-permute-start.18 = (bf16[896,128]{1,0:T(8,128)(2,1)S(1)}, bf16[896,128]{1,0:T(8,128)(2,1)S(1)}, u32[]{:S(2)}, u32[]{:S(2)}) collective-permute-start(bf16[896,128]{1,0:T(8,128)(2,1)S(1)} %get-tuple-element.49), channel_id=1, source_target_pairs={{8,0},{16,8},{24,16},{28,24},{20,28},{12,20},{4,12},{0,4},{9,1},{1... | collective-permute-start | bytes 688136 | tf_op jit(solution)/shard_map/ppermute | solution.py:321
  83.6 1.0 collective-permute-done.39.in_up
  84.6 1.1 collective-permute-done.40.in_down
  87.0 1.5 %collective-permute-start.49 = (bf16[896,128]{1,0:T(8,128)(2,1)S(1)}, bf16[896,128]{1,0:T(8,128)(2,1)S(1)}, u32[]{:S(2)}, u32[]{:S(2)}) collective-permute-start(bf16[896,128]{1,0:T(8,128)(2,1)S(1)} %get-tuple-element.60.refs_1_), channel_id=1, source_target_pairs={{8,0},{16,8},{24,16},{28,24},{20,28},{12,20},{4,12},{0,4},{9,1},{1... | collective-permute-start | bytes 688136 | tf_op jit(solution)/shard_map/ppermute | solution.py:321
  88.5 1.0 collective-permute-done.17.in_up
  89.5 1.1 collective-permute-done.18.in_down
  91.9 1.5 %collective-permute-start.45 = (bf16[896,128]{1,0:T(8,128)(2,1)S(1)}, bf16[896,128]{1,0:T(8,128)(2,1)S(1)}, u32[]{:S(2)}, u32[]{:S(2)}) collective-permute-start(bf16[896,128]{1,0:T(8,128)(2,1)S(1)} %get-tuple-element.50.refs_0_), channel_id=1, source_target_pairs={{8,0},{16,8},{24,16},{28,24},{20,28},{12,20},{4,12},{0,4},{9,1},{1... | collective-permute-start | bytes 688136 | tf_op jit(solution)/shard_map/ppermute | solution.py:321
  93.4 1.5 %collective-permute-done.41.refs_1_ = bf16[896,128]{1,0:T(8,128)(2,1)S(1)} collective-permute-done((bf16[896,128]{1,0:T(8,128)(2,1)S(1)}, bf16[896,128]{1,0:T(8,128)(2,1)S(1)}, u32[]{:S(2)}, u32[]{:S(2)}) %collective-permute-start.41) | collective-permute-done | bytes 229408 | tf_op jit(solution)/shard_map/ppermute | solution.py:321
  95.5 1.4 %collective-permute-start.50 = (bf16[896,128]{1,0:T(8,128)(2,1)S(1)}, bf16[896,128]{1,0:T(8,128)(2,1)S(1)}, u32[]{:S(2)}, u32[]{:S(2)}) collective-permute-start(bf16[896,128]{1,0:T(8,128)(2,1)S(1)} %collective-permute-done.49.refs_3_), channel_id=1, source_target_pairs={{8,0},{16,8},{24,16},{28,24},{20,28},{12,20},{4,12},{0,4},{9,1},{1... | collective-permute-start | bytes 688136 | tf_op jit(solution)/shard_map/ppermute | solution.py:321
  96.9 2.9 %collective-permute-done.19.refs_0_ = bf16[896,128]{1,0:T(8,128)(2,1)S(1)} collective-permute-done((bf16[896,128]{1,0:T(8,128)(2,1)S(1)}, bf16[896,128]{1,0:T(8,128)(2,1)S(1)}, u32[]{:S(2)}, u32[]{:S(2)}) %collective-permute-start.19) | collective-permute-done | bytes 229408 | tf_op jit(solution)/shard_map/ppermute | solution.py:321
  100.5 1.4 %collective-permute-start.46 = (bf16[896,128]{1,0:T(8,128)(2,1)S(1)}, bf16[896,128]{1,0:T(8,128)(2,1)S(1)}, u32[]{:S(2)}, u32[]{:S(2)}) collective-permute-start(bf16[896,128]{1,0:T(8,128)(2,1)S(1)} %collective-permute-done.45.refs_2_), channel_id=1, source_target_pairs={{8,0},{16,8},{24,16},{28,24},{20,28},{12,20},{4,12},{0,4},{9,1},{1... | collective-permute-start | bytes 688136 | tf_op jit(solution)/shard_map/ppermute | solution.py:321
  101.8 2.9 %collective-permute-done.42.refs_1_ = bf16[896,128]{1,0:T(8,128)(2,1)S(1)} collective-permute-done((bf16[896,128]{1,0:T(8,128)(2,1)S(1)}, bf16[896,128]{1,0:T(8,128)(2,1)S(1)}, u32[]{:S(2)}, u32[]{:S(2)}) %collective-permute-start.42) | collective-permute-done | bytes 229408 | tf_op jit(solution)/shard_map/ppermute | solution.py:321
  105.4 1.4 %collective-permute-start.51 = (bf16[896,128]{1,0:T(8,128)(2,1)S(1)}, bf16[896,128]{1,0:T(8,128)(2,1)S(1)}, u32[]{:S(2)}, u32[]{:S(2)}) collective-permute-start(bf16[896,128]{1,0:T(8,128)(2,1)S(1)} %collective-permute-done.50.refs_3_), channel_id=1, source_target_pairs={{8,0},{16,8},{24,16},{28,24},{20,28},{12,20},{4,12},{0,4},{9,1},{1... | collective-permute-start | bytes 688136 | tf_op jit(solution)/shard_map/ppermute | solution.py:321
  106.8 2.9 %collective-permute-done.20.refs_0_ = bf16[896,128]{1,0:T(8,128)(2,1)S(1)} collective-permute-done((bf16[896,128]{1,0:T(8,128)(2,1)S(1)}, bf16[896,128]{1,0:T(8,128)(2,1)S(1)}, u32[]{:S(2)}, u32[]{:S(2)}) %collective-permute-start.20) | collective-permute-done | bytes 229408 | tf_op jit(solution)/shard_map/ppermute | solution.py:321
  110.3 1.4 %collective-permute-start.47 = (bf16[896,128]{1,0:T(8,128)(2,1)S(1)}, bf16[896,128]{1,0:T(8,128)(2,1)S(1)}, u32[]{:S(2)}, u32[]{:S(2)}) collective-permute-start(bf16[896,128]{1,0:T(8,128)(2,1)S(1)} %collective-permute-done.46.refs_2_), channel_id=1, source_target_pairs={{8,0},{16,8},{24,16},{28,24},{20,28},{12,20},{4,12},{0,4},{9,1},{1... | collective-permute-start | bytes 688136 | tf_op jit(solution)/shard_map/ppermute | solution.py:321
  111.7 1.4 %new_moments.1 = (f32[896,256]{1,0:T(8,128)}, f32[896,256]{1,0:T(8,128)}) custom-call(f32[896,128]{1,0:T(8,128)S(1)} %get-tuple-element.61.refs_0_, f32[896,128]{1,0:T(8,128)S(1)} %get-tuple-element.62.refs_1_, f32[896,256]{1,0:T(8,128)S(1)} %copy-done.4, f32[896,256]{1,0:T(8,128)S(1)} %copy-done.5), custom_call_target="tpu_custom_call" | custom-call | bytes 6291456 | tf_op jit(solution)/shard_map/new_moments/pallas_call | solution.py:248
  113.0 1.9 %write_update.5.refs_4_ = bf16[1024,7168]{1,0:T(8,128)(2,1)} custom-call(s32[1]{0:T(128)} %bitcast.here_ref, bf16[1024,256]{1,0:T(8,128)(2,1)S(1)} %copy-done.2, bf16[896,128]{1,0:T(8,128)(2,1)S(1)} %get-tuple-element.50.refs_0_, bf16[896,128]{1,0:T(8,128)(2,1)S(1)} %get-tuple-element.60.refs_1_), custom_call_target="tpu_custom_call" | custom-call | flops 469762048 | bytes 1835008 | tf_op jit(solution)/shard_map/write_update/pallas_call | solution.py:291
  114.9 3.3 %write_update.6.refs_4_ = bf16[1024,7168]{1,0:T(8,128)(2,1)} custom-call(s32[1]{0:T(128)} %bitcast.here_ref, bf16[1024,256]{1,0:T(8,128)(2,1)S(1)} %copy-done.2, bf16[896,128]{1,0:T(8,128)(2,1)S(1)} %collective-permute-done.19.refs_0_, bf16[896,128]{1,0:T(8,128)(2,1)S(1)} %collective-permute-done.41.refs_1_, ...), custom_call_target="tpu_custom_call", output_to_operand_aliasing={{}: (6, {})} | custom-call | flops 939524096 | bytes 3670016 | tf_op jit(solution)/shard_map/write_update/pallas_call | solution.py:291
  118.9 1.4 %collective-permute-start.52 = (bf16[448,128]{1,0:T(8,128)(2,1)S(1)}, bf16[448,128]{1,0:T(8,128)(2,1)S(1)}, u32[]{:S(2)}, u32[]{:S(2)}) collective-permute-start(bf16[448,128]{1,0:T(8,128)(2,1)S(1)} %slice.47), channel_id=1, source_target_pairs={{8,0},{16,8},{24,16},{28,24},{20,28},{12,20},{4,12},{0,4},{9,1},{1... | collective-permute-start | bytes 344072 | tf_op jit(solution)/shard_map/ppermute | solution.py:321
  121.1 1.4 %collective-permute-start.48 = (bf16[448,128]{1,0:T(8,128)(2,1)S(1)}, bf16[448,128]{1,0:T(8,128)(2,1)S(1)}, u32[]{:S(2)}, u32[]{:S(2)}) collective-permute-start(bf16[448,128]{1,0:T(8,128)(2,1)S(1)} %slice.46), channel_id=1, source_target_pairs={{8,0},{16,8},{24,16},{28,24},{20,28},{12,20},{4,12},{0,4},{9,1},{1... | collective-permute-start | bytes 344072 | tf_op jit(solution)/shard_map/ppermute | solution.py:321
  122.5 3.3 %write_update.7.refs_4_ = bf16[1024,7168]{1,0:T(8,128)(2,1)} custom-call(s32[1]{0:T(128)} %bitcast.here_ref, bf16[1024,256]{1,0:T(8,128)(2,1)S(1)} %copy-done.2, bf16[896,128]{1,0:T(8,128)(2,1)S(1)} %collective-permute-done.20.refs_0_, bf16[896,128]{1,0:T(8,128)(2,1)S(1)} %collective-permute-done.42.refs_1_, ...), custom_call_target="tpu_custom_call", output_to_operand_aliasing={{}: (6, {})} | custom-call | flops 939524096 | bytes 3670016 | tf_op jit(solution)/shard_map/write_update/pallas_call | solution.py:291
  125.9 3.3 %write_update.8.refs_4_ = bf16[1024,7168]{1,0:T(8,128)(2,1)} custom-call(s32[1]{0:T(128)} %bitcast.here_ref, bf16[1024,256]{1,0:T(8,128)(2,1)S(1)} %copy-done.2, bf16[896,128]{1,0:T(8,128)(2,1)S(1)} %collective-permute-done.21.refs_0_, bf16[896,128]{1,0:T(8,128)(2,1)S(1)} %collective-permute-done.43.refs_1_, ...), custom_call_target="tpu_custom_call", output_to_operand_aliasing={{}: (6, {})} | custom-call | flops 939524096 | bytes 3670016 | tf_op jit(solution)/shard_map/write_update/pallas_call | solution.py:291
  129.2 1.9 %write_update.9 = bf16[1024,7168]{1,0:T(8,128)(2,1)} custom-call(s32[1]{0:T(128)} %bitcast.here_ref, bf16[1024,256]{1,0:T(8,128)(2,1)S(1)} %copy-done.2, bf16[448,128]{1,0:T(8,128)(2,1)S(1)} %collective-permute-done.22.refs_0_, bf16[448,128]{1,0:T(8,128)(2,1)S(1)} %collective-permute-done.44.refs_1_, ...), custom_call_target="tpu_custom_call", output_to_operand_aliasing={{}: (6, {})} | custom-call | flops 469762048 | bytes 1835008 | tf_op jit(solution)/shard_map/write_update/pallas_call | solution.py:291
  (91 shorter events, 20.2 us)
Async XLA Ops:
  0.6 46.7 %slice-start = ((s8[7340032]{0:T(1024)(128)(4,1)}), s8[3145728]{0:T(1024)(128)(4,1)S(1)}, s32[]{:S(2)}) async-start(s8[7340032]{0:T(1024)(128)(4,1)} %bitcast.2), calls=%async_computation | async-start | bytes 6291456
  0.6 1.7 %copy-start.3 = (bf16[128,8192]{1,0:T(8,128)(2,1)S(1)}, bf16[128,8192]{1,0:T(8,128)(2,1)}, u32[]{:S(2)}) copy-start(bf16[128,8192]{1,0:T(8,128)(2,1)} %other) | copy-start | bytes 6291460
  5.3 1.0 copy-start
  6.3 22.6 %collective-permute-start = (bf16[128,4096]{1,0:T(8,128)(2,1)}, bf16[128,4096]{1,0:T(8,128)(2,1)}, u32[]{:S(2)}, u32[]{:S(2)}) collective-permute-start(bf16[128,4096]{1,0:T(8,128)(2,1)} %get-tuple-element.39), channel_id=1, source_target_pairs={{0,1},{1,0},{2,3},{3,2},{4,5},{5,4},{6,7},{7,6},{8,9},{9,8},{10,11... | collective-permute-start | bytes 3145736 | tf_op jit(solution)/shard_map/ppermute | solution.py:341
  7.8 6.9 %collective-permute-start.23 = (bf16[512,128]{1,0:T(8,128)(2,1)S(1)}, bf16[512,128]{1,0:T(8,128)(2,1)S(1)}, u32[]{:S(2)}, u32[]{:S(2)}) collective-permute-start(bf16[512,128]{1,0:T(8,128)(2,1)S(1)} %get-tuple-element.65.refs_2_), channel_id=1, source_target_pairs={{0,8},{8,16},{16,24},{24,28},{28,20},{20,12},{12,4},{4,0},{1,9},{9... | collective-permute-start | bytes 393224 | tf_op jit(solution)/shard_map/ppermute | solution.py:321
  10.4 6.4 %collective-permute-start.24 = (bf16[512,128]{1,0:T(8,128)(2,1)S(1)}, bf16[512,128]{1,0:T(8,128)(2,1)S(1)}, u32[]{:S(2)}, u32[]{:S(2)}) collective-permute-start(bf16[512,128]{1,0:T(8,128)(2,1)S(1)} %get-tuple-element.65.refs_2_), channel_id=1, source_target_pairs={{8,0},{16,8},{24,16},{28,24},{20,28},{12,20},{4,12},{0,4},{9,1},{1... | collective-permute-start | bytes 393224 | tf_op jit(solution)/shard_map/ppermute | solution.py:321
  10.4 7.1 %collective-permute-start.1 = (bf16[512,128]{1,0:T(8,128)(2,1)S(1)}, bf16[512,128]{1,0:T(8,128)(2,1)S(1)}, u32[]{:S(2)}, u32[]{:S(2)}) collective-permute-start(bf16[512,128]{1,0:T(8,128)(2,1)S(1)} %get-tuple-element.66.refs_2_), channel_id=1, source_target_pairs={{0,8},{8,16},{16,24},{24,28},{28,20},{20,12},{12,4},{4,0},{1,9},{9... | collective-permute-start | bytes 393224 | tf_op jit(solution)/shard_map/ppermute | solution.py:321
  12.5 7.2 %collective-permute-start.2 = (bf16[512,128]{1,0:T(8,128)(2,1)S(1)}, bf16[512,128]{1,0:T(8,128)(2,1)S(1)}, u32[]{:S(2)}, u32[]{:S(2)}) collective-permute-start(bf16[512,128]{1,0:T(8,128)(2,1)S(1)} %get-tuple-element.66.refs_2_), channel_id=1, source_target_pairs={{8,0},{16,8},{24,16},{28,24},{20,28},{12,20},{4,12},{0,4},{9,1},{1... | collective-permute-start | bytes 393224 | tf_op jit(solution)/shard_map/ppermute | solution.py:321
  14.7 5.7 %collective-permute-start.25 = (bf16[512,128]{1,0:T(8,128)(2,1)S(1)}, bf16[512,128]{1,0:T(8,128)(2,1)S(1)}, u32[]{:S(2)}, u32[]{:S(2)}) collective-permute-start(bf16[512,128]{1,0:T(8,128)(2,1)S(1)} %collective-permute-done.23.refs_3_), channel_id=1, source_target_pairs={{0,8},{8,16},{16,24},{24,28},{28,20},{20,12},{12,4},{4,0},{1,9},{9... | collective-permute-start | bytes 393224 | tf_op jit(solution)/shard_map/ppermute | solution.py:321
  16.8 5.7 %collective-permute-start.26 = (bf16[512,128]{1,0:T(8,128)(2,1)S(1)}, bf16[512,128]{1,0:T(8,128)(2,1)S(1)}, u32[]{:S(2)}, u32[]{:S(2)}) collective-permute-start(bf16[512,128]{1,0:T(8,128)(2,1)S(1)} %collective-permute-done.24.refs_4_), channel_id=1, source_target_pairs={{8,0},{16,8},{24,16},{28,24},{20,28},{12,20},{4,12},{0,4},{9,1},{1... | collective-permute-start | bytes 393224 | tf_op jit(solution)/shard_map/ppermute | solution.py:321
  17.5 6.4 %collective-permute-start.3 = (bf16[512,128]{1,0:T(8,128)(2,1)S(1)}, bf16[512,128]{1,0:T(8,128)(2,1)S(1)}, u32[]{:S(2)}, u32[]{:S(2)}) collective-permute-start(bf16[512,128]{1,0:T(8,128)(2,1)S(1)} %collective-permute-done.1.refs_3_), channel_id=1, source_target_pairs={{0,8},{8,16},{16,24},{24,28},{28,20},{20,12},{12,4},{4,0},{1,9},{9... | collective-permute-start | bytes 393224 | tf_op jit(solution)/shard_map/ppermute | solution.py:321
  19.6 6.4 %collective-permute-start.4 = (bf16[512,128]{1,0:T(8,128)(2,1)S(1)}, bf16[512,128]{1,0:T(8,128)(2,1)S(1)}, u32[]{:S(2)}, u32[]{:S(2)}) collective-permute-start(bf16[512,128]{1,0:T(8,128)(2,1)S(1)} %collective-permute-done.2.refs_4_), channel_id=1, source_target_pairs={{8,0},{16,8},{24,16},{28,24},{20,28},{12,20},{4,12},{0,4},{9,1},{1... | collective-permute-start | bytes 393224 | tf_op jit(solution)/shard_map/ppermute | solution.py:321
  20.4 6.4 %collective-permute-start.27 = (bf16[512,128]{1,0:T(8,128)(2,1)S(1)}, bf16[512,128]{1,0:T(8,128)(2,1)S(1)}, u32[]{:S(2)}, u32[]{:S(2)}) collective-permute-start(bf16[512,128]{1,0:T(8,128)(2,1)S(1)} %collective-permute-done.25.refs_5_), channel_id=1, source_target_pairs={{0,8},{8,16},{16,24},{24,28},{28,20},{20,12},{12,4},{4,0},{1,9},{9... | collective-permute-start | bytes 393224 | tf_op jit(solution)/shard_map/ppermute | solution.py:321
  22.5 6.4 %collective-permute-start.28 = (bf16[512,128]{1,0:T(8,128)(2,1)S(1)}, bf16[512,128]{1,0:T(8,128)(2,1)S(1)}, u32[]{:S(2)}, u32[]{:S(2)}) collective-permute-start(bf16[512,128]{1,0:T(8,128)(2,1)S(1)} %collective-permute-done.26.refs_6_), channel_id=1, source_target_pairs={{8,0},{16,8},{24,16},{28,24},{20,28},{12,20},{4,12},{0,4},{9,1},{1... | collective-permute-start | bytes 393224 | tf_op jit(solution)/shard_map/ppermute | solution.py:321
  23.9 11.0 %collective-permute-start.5 = (bf16[512,128]{1,0:T(8,128)(2,1)S(1)}, bf16[512,128]{1,0:T(8,128)(2,1)S(1)}, u32[]{:S(2)}, u32[]{:S(2)}) collective-permute-start(bf16[512,128]{1,0:T(8,128)(2,1)S(1)} %collective-permute-done.3.refs_5_), channel_id=1, source_target_pairs={{0,8},{8,16},{16,24},{24,28},{28,20},{20,12},{12,4},{4,0},{1,9},{9... | collective-permute-start | bytes 393224 | tf_op jit(solution)/shard_map/ppermute | solution.py:321
  26.0 10.8 %collective-permute-start.6 = (bf16[512,128]{1,0:T(8,128)(2,1)S(1)}, bf16[512,128]{1,0:T(8,128)(2,1)S(1)}, u32[]{:S(2)}, u32[]{:S(2)}) collective-permute-start(bf16[512,128]{1,0:T(8,128)(2,1)S(1)} %collective-permute-done.4.refs_6_), channel_id=1, source_target_pairs={{8,0},{16,8},{24,16},{28,24},{20,28},{12,20},{4,12},{0,4},{9,1},{1... | collective-permute-start | bytes 393224 | tf_op jit(solution)/shard_map/ppermute | solution.py:321
  26.8 5.3 %collective-permute-start.29 = (bf16[256,128]{1,0:T(8,128)(2,1)S(1)}, bf16[256,128]{1,0:T(8,128)(2,1)S(1)}, u32[]{:S(2)}, u32[]{:S(2)}) collective-permute-start(bf16[256,128]{1,0:T(8,128)(2,1)S(1)} %slice.43), channel_id=1, source_target_pairs={{0,8},{8,16},{16,24},{24,28},{28,20},{20,12},{12,4},{4,0},{1,9},{9... | collective-permute-start | bytes 196616 | tf_op jit(solution)/shard_map/ppermute | solution.py:321
  28.9 4.3 %collective-permute-start.30 = (bf16[256,128]{1,0:T(8,128)(2,1)S(1)}, bf16[256,128]{1,0:T(8,128)(2,1)S(1)}, u32[]{:S(2)}, u32[]{:S(2)}) collective-permute-start(bf16[256,128]{1,0:T(8,128)(2,1)S(1)} %slice.44), channel_id=1, source_target_pairs={{8,0},{16,8},{24,16},{28,24},{20,28},{12,20},{4,12},{0,4},{9,1},{1... | collective-permute-start | bytes 196616 | tf_op jit(solution)/shard_map/ppermute | solution.py:321
  29.0 1.2 copy-start.1
  32.1 15.2 %slice-start.1 = ((s8[7340032]{0:T(1024)(128)(4,1)}), s8[4194304]{0:T(1024)(128)(4,1)S(1)}, s32[]{:S(2)}) async-start(s8[7340032]{0:T(1024)(128)(4,1)} %bitcast.2), calls=%async_computation.1 | async-start | bytes 8388608
  34.8 7.8 %collective-permute-start.31 = (f32[256,128]{1,0:T(8,128)S(1)}, f32[256,128]{1,0:T(8,128)S(1)}, u32[]{:S(2)}, u32[]{:S(2)}) collective-permute-start(f32[256,128]{1,0:T(8,128)S(1)} %add_coords.7), channel_id=1, source_target_pairs={{0,1},{1,0},{2,3},{3,2},{4,5},{5,4},{6,7},{7,6},{8,9},{9,8},{10,11... | collective-permute-start | bytes 393224 | tf_op jit(solution)/shard_map/ppermute | solution.py:358
  34.9 4.5 %collective-permute-start.7 = (bf16[256,128]{1,0:T(8,128)(2,1)S(1)}, bf16[256,128]{1,0:T(8,128)(2,1)S(1)}, u32[]{:S(2)}, u32[]{:S(2)}) collective-permute-start(bf16[256,128]{1,0:T(8,128)(2,1)S(1)} %slice.40), channel_id=1, source_target_pairs={{0,8},{8,16},{16,24},{24,28},{28,20},{20,12},{12,4},{4,0},{1,9},{9... | collective-permute-start | bytes 196616 | tf_op jit(solution)/shard_map/ppermute | solution.py:321
  36.8 4.3 %collective-permute-start.8 = (bf16[256,128]{1,0:T(8,128)(2,1)S(1)}, bf16[256,128]{1,0:T(8,128)(2,1)S(1)}, u32[]{:S(2)}, u32[]{:S(2)}) collective-permute-start(bf16[256,128]{1,0:T(8,128)(2,1)S(1)} %slice.41), channel_id=1, source_target_pairs={{8,0},{16,8},{24,16},{28,24},{20,28},{12,20},{4,12},{0,4},{9,1},{1... | collective-permute-start | bytes 196616 | tf_op jit(solution)/shard_map/ppermute | solution.py:321
  42.5 1.7 %collective-permute-start.9 = (f32[256,128]{1,0:T(8,128)S(1)}, f32[256,128]{1,0:T(8,128)S(1)}, u32[]{:S(2)}, u32[]{:S(2)}) collective-permute-start(f32[256,128]{1,0:T(8,128)S(1)} %add_coords.5), channel_id=1, source_target_pairs={{0,1},{1,0},{2,3},{3,2},{4,5},{5,4},{6,7},{7,6},{8,9},{9,8},{10,11... | collective-permute-start | bytes 393224 | tf_op jit(solution)/shard_map/ppermute | solution.py:358
  42.7 4.7 %collective-permute-start.32 = (bf16[256,128]{1,0:T(8,128)(2,1)S(1)}, bf16[256,128]{1,0:T(8,128)(2,1)S(1)}, u32[]{:S(2)}, u32[]{:S(2)}) collective-permute-start(bf16[256,128]{1,0:T(8,128)(2,1)S(1)} %add_convert_fusion.refs_0_), channel_id=1, source_target_pairs={{0,2},{1,3},{2,0},{3,1},{4,6},{5,7},{6,4},{7,5},{8,10},{9,11},{10,... | collective-permute-start | bytes 196616 | tf_op jit(solution)/shard_map/ppermute | solution.py:360
  44.2 5.7 %collective-permute-start.10 = (bf16[256,128]{1,0:T(8,128)(2,1)S(1)}, bf16[256,128]{1,0:T(8,128)(2,1)S(1)}, u32[]{:S(2)}, u32[]{:S(2)}) collective-permute-start(bf16[256,128]{1,0:T(8,128)(2,1)S(1)} %add_convert_fusion.1.refs_0_), channel_id=1, source_target_pairs={{0,2},{1,3},{2,0},{3,1},{4,6},{5,7},{6,4},{7,5},{8,10},{9,11},{10,... | collective-permute-start | bytes 196616 | tf_op jit(solution)/shard_map/ppermute | solution.py:360
  47.8 5.5 %collective-permute-start.33 = (bf16[448,128]{1,0:T(8,128)(2,1)S(1)}, bf16[448,128]{1,0:T(8,128)(2,1)S(1)}, u32[]{:S(2)}, u32[]{:S(2)}) collective-permute-start(bf16[448,128]{1,0:T(8,128)(2,1)S(1)} %get-tuple-element.52), channel_id=1, source_target_pairs={{0,8},{8,16},{16,24},{24,28},{28,20},{20,12},{12,4},{4,0},{1,9},{9... | collective-permute-start | bytes 344072 | tf_op jit(solution)/shard_map/ppermute | solution.py:321
  49.5 5.7 %collective-permute-start.34 = (bf16[448,128]{1,0:T(8,128)(2,1)S(1)}, bf16[448,128]{1,0:T(8,128)(2,1)S(1)}, u32[]{:S(2)}, u32[]{:S(2)}) collective-permute-start(bf16[448,128]{1,0:T(8,128)(2,1)S(1)} %get-tuple-element.53), channel_id=1, source_target_pairs={{8,0},{16,8},{24,16},{28,24},{20,28},{12,20},{4,12},{0,4},{9,1},{1... | collective-permute-start | bytes 344072 | tf_op jit(solution)/shard_map/ppermute | solution.py:321
  50.4 7.6 %collective-permute-start.11 = (bf16[448,128]{1,0:T(8,128)(2,1)S(1)}, bf16[448,128]{1,0:T(8,128)(2,1)S(1)}, u32[]{:S(2)}, u32[]{:S(2)}) collective-permute-start(bf16[448,128]{1,0:T(8,128)(2,1)S(1)} %get-tuple-element.42), channel_id=1, source_target_pairs={{0,8},{8,16},{16,24},{24,28},{28,20},{20,12},{12,4},{4,0},{1,9},{9... | collective-permute-start | bytes 344072 | tf_op jit(solution)/shard_map/ppermute | solution.py:321
  52.0 5.9 %collective-permute-start.12 = (bf16[448,128]{1,0:T(8,128)(2,1)S(1)}, bf16[448,128]{1,0:T(8,128)(2,1)S(1)}, u32[]{:S(2)}, u32[]{:S(2)}) collective-permute-start(bf16[448,128]{1,0:T(8,128)(2,1)S(1)} %get-tuple-element.43), channel_id=1, source_target_pairs={{8,0},{16,8},{24,16},{28,24},{20,28},{12,20},{4,12},{0,4},{9,1},{1... | collective-permute-start | bytes 344072 | tf_op jit(solution)/shard_map/ppermute | solution.py:321
  55.9 8.2 %collective-permute-start.35 = (bf16[896,128]{1,0:T(8,128)(2,1)S(1)}, bf16[896,128]{1,0:T(8,128)(2,1)S(1)}, u32[]{:S(2)}, u32[]{:S(2)}) collective-permute-start(bf16[896,128]{1,0:T(8,128)(2,1)S(1)} %get-tuple-element.54), channel_id=1, source_target_pairs={{0,8},{8,16},{16,24},{24,28},{28,20},{20,12},{12,4},{4,0},{1,9},{9... | collective-permute-start | bytes 688136 | tf_op jit(solution)/shard_map/ppermute | solution.py:321
  57.4 8.5 %collective-permute-start.36 = (bf16[896,128]{1,0:T(8,128)(2,1)S(1)}, bf16[896,128]{1,0:T(8,128)(2,1)S(1)}, u32[]{:S(2)}, u32[]{:S(2)}) collective-permute-start(bf16[896,128]{1,0:T(8,128)(2,1)S(1)} %get-tuple-element.55), channel_id=1, source_target_pairs={{8,0},{16,8},{24,16},{28,24},{20,28},{12,20},{4,12},{0,4},{9,1},{1... | collective-permute-start | bytes 688136 | tf_op jit(solution)/shard_map/ppermute | solution.py:321
  58.7 10.3 %collective-permute-start.13 = (bf16[896,128]{1,0:T(8,128)(2,1)S(1)}, bf16[896,128]{1,0:T(8,128)(2,1)S(1)}, u32[]{:S(2)}, u32[]{:S(2)}) collective-permute-start(bf16[896,128]{1,0:T(8,128)(2,1)S(1)} %get-tuple-element.44), channel_id=1, source_target_pairs={{0,8},{8,16},{16,24},{24,28},{28,20},{20,12},{12,4},{4,0},{1,9},{9... | collective-permute-start | bytes 688136 | tf_op jit(solution)/shard_map/ppermute | solution.py:321
  60.2 25.5 %copy-start.4 = (f32[896,256]{1,0:T(8,128)S(1)}, f32[896,256]{1,0:T(8,128)}, u32[]{:S(2)}) copy-start(f32[896,256]{1,0:T(8,128)} %refs_2_.1) | copy-start | bytes 2752516
  60.2 25.5 %copy-start.5 = (f32[896,256]{1,0:T(8,128)S(1)}, f32[896,256]{1,0:T(8,128)}, u32[]{:S(2)}) copy-start(f32[896,256]{1,0:T(8,128)} %refs_3_.1) | copy-start | bytes 2752516
  60.2 10.6 %collective-permute-start.14 = (bf16[896,128]{1,0:T(8,128)(2,1)S(1)}, bf16[896,128]{1,0:T(8,128)(2,1)S(1)}, u32[]{:S(2)}, u32[]{:S(2)}) collective-permute-start(bf16[896,128]{1,0:T(8,128)(2,1)S(1)} %get-tuple-element.45), channel_id=1, source_target_pairs={{8,0},{16,8},{24,16},{28,24},{20,28},{12,20},{4,12},{0,4},{9,1},{1... | collective-permute-start | bytes 688136 | tf_op jit(solution)/shard_map/ppermute | solution.py:321
  66.6 7.9 %collective-permute-start.37 = (bf16[896,128]{1,0:T(8,128)(2,1)S(1)}, bf16[896,128]{1,0:T(8,128)(2,1)S(1)}, u32[]{:S(2)}, u32[]{:S(2)}) collective-permute-start(bf16[896,128]{1,0:T(8,128)(2,1)S(1)} %get-tuple-element.56), channel_id=1, source_target_pairs={{0,8},{8,16},{16,24},{24,28},{28,20},{20,12},{12,4},{4,0},{1,9},{9... | collective-permute-start | bytes 688136 | tf_op jit(solution)/shard_map/ppermute | solution.py:321
  67.4 8.5 %collective-permute-start.38 = (bf16[896,128]{1,0:T(8,128)(2,1)S(1)}, bf16[896,128]{1,0:T(8,128)(2,1)S(1)}, u32[]{:S(2)}, u32[]{:S(2)}) collective-permute-start(bf16[896,128]{1,0:T(8,128)(2,1)S(1)} %get-tuple-element.57), channel_id=1, source_target_pairs={{8,0},{16,8},{24,16},{28,24},{20,28},{12,20},{4,12},{0,4},{9,1},{1... | collective-permute-start | bytes 688136 | tf_op jit(solution)/shard_map/ppermute | solution.py:321
  71.5 8.1 %collective-permute-start.15 = (bf16[896,128]{1,0:T(8,128)(2,1)S(1)}, bf16[896,128]{1,0:T(8,128)(2,1)S(1)}, u32[]{:S(2)}, u32[]{:S(2)}) collective-permute-start(bf16[896,128]{1,0:T(8,128)(2,1)S(1)} %get-tuple-element.46), channel_id=1, source_target_pairs={{0,8},{8,16},{16,24},{24,28},{28,20},{20,12},{12,4},{4,0},{1,9},{9... | collective-permute-start | bytes 688136 | tf_op jit(solution)/shard_map/ppermute | solution.py:321
  72.3 8.5 %collective-permute-start.16 = (bf16[896,128]{1,0:T(8,128)(2,1)S(1)}, bf16[896,128]{1,0:T(8,128)(2,1)S(1)}, u32[]{:S(2)}, u32[]{:S(2)}) collective-permute-start(bf16[896,128]{1,0:T(8,128)(2,1)S(1)} %get-tuple-element.47), channel_id=1, source_target_pairs={{8,0},{16,8},{24,16},{28,24},{20,28},{12,20},{4,12},{0,4},{9,1},{1... | collective-permute-start | bytes 688136 | tf_op jit(solution)/shard_map/ppermute | solution.py:321
  76.6 8.0 %collective-permute-start.39 = (bf16[896,128]{1,0:T(8,128)(2,1)S(1)}, bf16[896,128]{1,0:T(8,128)(2,1)S(1)}, u32[]{:S(2)}, u32[]{:S(2)}) collective-permute-start(bf16[896,128]{1,0:T(8,128)(2,1)S(1)} %get-tuple-element.58), channel_id=1, source_target_pairs={{0,8},{8,16},{16,24},{24,28},{28,20},{20,12},{12,4},{4,0},{1,9},{9... | collective-permute-start | bytes 688136 | tf_op jit(solution)/shard_map/ppermute | solution.py:321
  77.2 35.8 %copy-start.2 = (bf16[1024,256]{1,0:T(8,128)(2,1)S(1)}, bf16[1024,256]{1,0:T(8,128)(2,1)}, u32[]{:S(2)}) copy-start(bf16[1024,256]{1,0:T(8,128)(2,1)} %base.4) | copy-start | bytes 1572868
  77.2 8.5 %collective-permute-start.40 = (bf16[896,128]{1,0:T(8,128)(2,1)S(1)}, bf16[896,128]{1,0:T(8,128)(2,1)S(1)}, u32[]{:S(2)}, u32[]{:S(2)}) collective-permute-start(bf16[896,128]{1,0:T(8,128)(2,1)S(1)} %get-tuple-element.59), channel_id=1, source_target_pairs={{8,0},{16,8},{24,16},{28,24},{20,28},{12,20},{4,12},{0,4},{9,1},{1... | collective-permute-start | bytes 688136 | tf_op jit(solution)/shard_map/ppermute | solution.py:321
  81.5 8.0 %collective-permute-start.17 = (bf16[896,128]{1,0:T(8,128)(2,1)S(1)}, bf16[896,128]{1,0:T(8,128)(2,1)S(1)}, u32[]{:S(2)}, u32[]{:S(2)}) collective-permute-start(bf16[896,128]{1,0:T(8,128)(2,1)S(1)} %get-tuple-element.48), channel_id=1, source_target_pairs={{0,8},{8,16},{16,24},{24,28},{28,20},{20,12},{12,4},{4,0},{1,9},{9... | collective-permute-start | bytes 688136 | tf_op jit(solution)/shard_map/ppermute | solution.py:321
  82.1 8.5 %collective-permute-start.18 = (bf16[896,128]{1,0:T(8,128)(2,1)S(1)}, bf16[896,128]{1,0:T(8,128)(2,1)S(1)}, u32[]{:S(2)}, u32[]{:S(2)}) collective-permute-start(bf16[896,128]{1,0:T(8,128)(2,1)S(1)} %get-tuple-element.49), channel_id=1, source_target_pairs={{8,0},{16,8},{24,16},{28,24},{20,28},{12,20},{4,12},{0,4},{9,1},{1... | collective-permute-start | bytes 688136 | tf_op jit(solution)/shard_map/ppermute | solution.py:321
  86.4 8.5 %collective-permute-start.41 = (bf16[896,128]{1,0:T(8,128)(2,1)S(1)}, bf16[896,128]{1,0:T(8,128)(2,1)S(1)}, u32[]{:S(2)}, u32[]{:S(2)}) collective-permute-start(bf16[896,128]{1,0:T(8,128)(2,1)S(1)} %get-tuple-element.60.refs_1_), channel_id=1, source_target_pairs={{0,8},{8,16},{16,24},{24,28},{28,20},{20,12},{12,4},{4,0},{1,9},{9... | collective-permute-start | bytes 688136 | tf_op jit(solution)/shard_map/ppermute | solution.py:321
  87.0 8.6 %collective-permute-start.49 = (bf16[896,128]{1,0:T(8,128)(2,1)S(1)}, bf16[896,128]{1,0:T(8,128)(2,1)S(1)}, u32[]{:S(2)}, u32[]{:S(2)}) collective-permute-start(bf16[896,128]{1,0:T(8,128)(2,1)S(1)} %get-tuple-element.60.refs_1_), channel_id=1, source_target_pairs={{8,0},{16,8},{24,16},{28,24},{20,28},{12,20},{4,12},{0,4},{9,1},{1... | collective-permute-start | bytes 688136 | tf_op jit(solution)/shard_map/ppermute | solution.py:321
  91.3 8.5 %collective-permute-start.19 = (bf16[896,128]{1,0:T(8,128)(2,1)S(1)}, bf16[896,128]{1,0:T(8,128)(2,1)S(1)}, u32[]{:S(2)}, u32[]{:S(2)}) collective-permute-start(bf16[896,128]{1,0:T(8,128)(2,1)S(1)} %get-tuple-element.50.refs_0_), channel_id=1, source_target_pairs={{0,8},{8,16},{16,24},{24,28},{28,20},{20,12},{12,4},{4,0},{1,9},{9... | collective-permute-start | bytes 688136 | tf_op jit(solution)/shard_map/ppermute | solution.py:321
  91.9 8.6 %collective-permute-start.45 = (bf16[896,128]{1,0:T(8,128)(2,1)S(1)}, bf16[896,128]{1,0:T(8,128)(2,1)S(1)}, u32[]{:S(2)}, u32[]{:S(2)}) collective-permute-start(bf16[896,128]{1,0:T(8,128)(2,1)S(1)} %get-tuple-element.50.refs_0_), channel_id=1, source_target_pairs={{8,0},{16,8},{24,16},{28,24},{20,28},{12,20},{4,12},{0,4},{9,1},{1... | collective-permute-start | bytes 688136 | tf_op jit(solution)/shard_map/ppermute | solution.py:321
  94.9 9.8 %collective-permute-start.42 = (bf16[896,128]{1,0:T(8,128)(2,1)S(1)}, bf16[896,128]{1,0:T(8,128)(2,1)S(1)}, u32[]{:S(2)}, u32[]{:S(2)}) collective-permute-start(bf16[896,128]{1,0:T(8,128)(2,1)S(1)} %collective-permute-done.41.refs_1_), channel_id=1, source_target_pairs={{0,8},{8,16},{16,24},{24,28},{28,20},{20,12},{12,4},{4,0},{1,9},{9... | collective-permute-start | bytes 688136 | tf_op jit(solution)/shard_map/ppermute | solution.py:321
  95.5 9.8 %collective-permute-start.50 = (bf16[896,128]{1,0:T(8,128)(2,1)S(1)}, bf16[896,128]{1,0:T(8,128)(2,1)S(1)}, u32[]{:S(2)}, u32[]{:S(2)}) collective-permute-start(bf16[896,128]{1,0:T(8,128)(2,1)S(1)} %collective-permute-done.49.refs_3_), channel_id=1, source_target_pairs={{8,0},{16,8},{24,16},{28,24},{20,28},{12,20},{4,12},{0,4},{9,1},{1... | collective-permute-start | bytes 688136 | tf_op jit(solution)/shard_map/ppermute | solution.py:321
  99.8 9.8 %collective-permute-start.20 = (bf16[896,128]{1,0:T(8,128)(2,1)S(1)}, bf16[896,128]{1,0:T(8,128)(2,1)S(1)}, u32[]{:S(2)}, u32[]{:S(2)}) collective-permute-start(bf16[896,128]{1,0:T(8,128)(2,1)S(1)} %collective-permute-done.19.refs_0_), channel_id=1, source_target_pairs={{0,8},{8,16},{16,24},{24,28},{28,20},{20,12},{12,4},{4,0},{1,9},{9... | collective-permute-start | bytes 688136 | tf_op jit(solution)/shard_map/ppermute | solution.py:321
  100.5 9.8 %collective-permute-start.46 = (bf16[896,128]{1,0:T(8,128)(2,1)S(1)}, bf16[896,128]{1,0:T(8,128)(2,1)S(1)}, u32[]{:S(2)}, u32[]{:S(2)}) collective-permute-start(bf16[896,128]{1,0:T(8,128)(2,1)S(1)} %collective-permute-done.45.refs_2_), channel_id=1, source_target_pairs={{8,0},{16,8},{24,16},{28,24},{20,28},{12,20},{4,12},{0,4},{9,1},{1... | collective-permute-start | bytes 688136 | tf_op jit(solution)/shard_map/ppermute | solution.py:321
  104.7 13.5 %collective-permute-start.43 = (bf16[896,128]{1,0:T(8,128)(2,1)S(1)}, bf16[896,128]{1,0:T(8,128)(2,1)S(1)}, u32[]{:S(2)}, u32[]{:S(2)}) collective-permute-start(bf16[896,128]{1,0:T(8,128)(2,1)S(1)} %collective-permute-done.42.refs_1_), channel_id=1, source_target_pairs={{0,8},{8,16},{16,24},{24,28},{28,20},{20,12},{12,4},{4,0},{1,9},{9... | collective-permute-start | bytes 688136 | tf_op jit(solution)/shard_map/ppermute | solution.py:321
  105.4 13.6 %collective-permute-start.51 = (bf16[896,128]{1,0:T(8,128)(2,1)S(1)}, bf16[896,128]{1,0:T(8,128)(2,1)S(1)}, u32[]{:S(2)}, u32[]{:S(2)}) collective-permute-start(bf16[896,128]{1,0:T(8,128)(2,1)S(1)} %collective-permute-done.50.refs_3_), channel_id=1, source_target_pairs={{8,0},{16,8},{24,16},{28,24},{20,28},{12,20},{4,12},{0,4},{9,1},{1... | collective-permute-start | bytes 688136 | tf_op jit(solution)/shard_map/ppermute | solution.py:321
  109.6 10.7 %collective-permute-start.21 = (bf16[896,128]{1,0:T(8,128)(2,1)S(1)}, bf16[896,128]{1,0:T(8,128)(2,1)S(1)}, u32[]{:S(2)}, u32[]{:S(2)}) collective-permute-start(bf16[896,128]{1,0:T(8,128)(2,1)S(1)} %collective-permute-done.20.refs_0_), channel_id=1, source_target_pairs={{0,8},{8,16},{16,24},{24,28},{28,20},{20,12},{12,4},{4,0},{1,9},{9... | collective-permute-start | bytes 688136 | tf_op jit(solution)/shard_map/ppermute | solution.py:321
  110.3 10.8 %collective-permute-start.47 = (bf16[896,128]{1,0:T(8,128)(2,1)S(1)}, bf16[896,128]{1,0:T(8,128)(2,1)S(1)}, u32[]{:S(2)}, u32[]{:S(2)}) collective-permute-start(bf16[896,128]{1,0:T(8,128)(2,1)S(1)} %collective-permute-done.46.refs_2_), channel_id=1, source_target_pairs={{8,0},{16,8},{24,16},{28,24},{20,28},{12,20},{4,12},{0,4},{9,1},{1... | collective-permute-start | bytes 688136 | tf_op jit(solution)/shard_map/ppermute | solution.py:321
  118.2 11.0 %collective-permute-start.44 = (bf16[448,128]{1,0:T(8,128)(2,1)S(1)}, bf16[448,128]{1,0:T(8,128)(2,1)S(1)}, u32[]{:S(2)}, u32[]{:S(2)}) collective-permute-start(bf16[448,128]{1,0:T(8,128)(2,1)S(1)} %slice.45), channel_id=1, source_target_pairs={{0,8},{8,16},{16,24},{24,28},{28,20},{20,12},{12,4},{4,0},{1,9},{9... | collective-permute-start | bytes 344072 | tf_op jit(solution)/shard_map/ppermute | solution.py:321
  118.9 10.2 %collective-permute-start.52 = (bf16[448,128]{1,0:T(8,128)(2,1)S(1)}, bf16[448,128]{1,0:T(8,128)(2,1)S(1)}, u32[]{:S(2)}, u32[]{:S(2)}) collective-permute-start(bf16[448,128]{1,0:T(8,128)(2,1)S(1)} %slice.47), channel_id=1, source_target_pairs={{8,0},{16,8},{24,16},{28,24},{20,28},{12,20},{4,12},{0,4},{9,1},{1... | collective-permute-start | bytes 344072 | tf_op jit(solution)/shard_map/ppermute | solution.py:321
  120.4 8.8 %collective-permute-start.22 = (bf16[448,128]{1,0:T(8,128)(2,1)S(1)}, bf16[448,128]{1,0:T(8,128)(2,1)S(1)}, u32[]{:S(2)}, u32[]{:S(2)}) collective-permute-start(bf16[448,128]{1,0:T(8,128)(2,1)S(1)} %slice.42), channel_id=1, source_target_pairs={{0,8},{8,16},{16,24},{24,28},{28,20},{20,12},{12,4},{4,0},{1,9},{9... | collective-permute-start | bytes 344072 | tf_op jit(solution)/shard_map/ppermute | solution.py:321
  121.1 8.1 %collective-permute-start.48 = (bf16[448,128]{1,0:T(8,128)(2,1)S(1)}, bf16[448,128]{1,0:T(8,128)(2,1)S(1)}, u32[]{:S(2)}, u32[]{:S(2)}) collective-permute-start(bf16[448,128]{1,0:T(8,128)(2,1)S(1)} %slice.46), channel_id=1, source_target_pairs={{8,0},{16,8},{24,16},{28,24},{20,28},{12,20},{4,12},{0,4},{9,1},{1... | collective-permute-start | bytes 344072 | tf_op jit(solution)/shard_map/ppermute | solution.py:321

commit v4 on v3

--- a/solution.py
+++ b/solution.py
@@ -61,6 +61,10 @@
     return pl.BlockSpec(memory_space=pltpu.SMEM)
 
 
+def left_in_hbm(array):
+    return pltpu.with_memory_space_constraint(array, pltpu.HBM)
+
+
 def ring_order(n):
     return [*range(0, n, 2), *range(n - 1, 0, -2)]
 
@@ -80,27 +84,60 @@
 def split_columns(me, activations, n):
     tokens, features = activations.shape
     part = features // n // 2
-
-    def kernel(me_ref, own, other, kept, sent):
-        kept[...] = own[...]
-        sent[...] = other[...]
-
     half = pltpu.VMEM((tokens, features // 2), activations.dtype)
+
+    def kernel(me_ref, source, kept, sent, sems):
+        side = lax.bitwise_and(me_ref[0], 1)
+        copies = []
+        for way, (out, which) in enumerate(((sent, 1 - side), (kept, side))):
+            for j in range(n):
+                columns = pl.ds(pl.multiple_of((2 * j + which) * part, 128), part)
+                copies.append(
+                    pltpu.make_async_copy(
+                        source.at[:, columns], out.at[:, pl.ds(j * part, part)], sems.at[way, j]
+                    )
+                )
+        for copy in copies:
+            copy.start()
+        for copy in copies:
+            copy.wait()
+
     return pl.pallas_call(
         kernel,
         out_shape=(half, half),
-        grid_spec=pltpu.PrefetchScalarGridSpec(
-            num_scalar_prefetch=1,
-            grid=(n,),
-            in_specs=[
-                pl.BlockSpec((tokens, part), lambda j, me: (0, 2 * j + lax.bitwise_and(me[0], 1))),
-                pl.BlockSpec((tokens, part), lambda j, me: (0, 2 * j + 1 - lax.bitwise_and(me[0], 1))),
-            ],
-            out_specs=(pl.BlockSpec((tokens, part), lambda j, me: (0, j)),) * 2,
-        ),
+        in_specs=[scalars(), pl.BlockSpec(memory_space=pltpu.HBM)],
+        out_specs=(on_chip(),) * 2,
+        scratch_shapes=[pltpu.SemaphoreType.DMA((2, n))],
         compiler_params=pltpu.CompilerParams(vmem_limit_bytes=SCRATCH_BYTES),
         name="split_columns",
-    )(me, activations, activations)
+    )(me, left_in_hbm(activations))
+
+
+def own_pieces(me, basis):
+    depth, rank = basis.shape
+    piece = pltpu.VMEM((depth // 2, rank // STREAMS), basis.dtype)
+
+    def kernel(me_ref, source, *refs):
+        rows = pl.ds(pl.multiple_of(lax.bitwise_and(me_ref[0], 1) * (depth // 2), depth // 2), depth // 2)
+        width = rank // STREAMS
+        copies = [
+            pltpu.make_async_copy(source.at[rows, pl.ds(s * width, width)], refs[s], refs[-1].at[s])
+            for s in range(STREAMS)
+        ]
+        for copy in copies:
+            copy.start()
+        for copy in copies:
+            copy.wait()
+
+    return pl.pallas_call(
+        kernel,
+        out_shape=(piece,) * STREAMS,
+        in_specs=[scalars(), pl.BlockSpec(memory_space=pltpu.HBM)],
+        out_specs=(on_chip(),) * STREAMS,
+        scratch_shapes=[pltpu.SemaphoreType.DMA((STREAMS,))],
+        compiler_params=pltpu.CompilerParams(vmem_limit_bytes=SCRATCH_BYTES),
+        name="own_pieces",
+    )(me, left_in_hbm(basis))
 
 
 def add_coords(here, me, kept, came, total, pieces, depth, n):
@@ -169,36 +206,31 @@
     )(here, me, *kept_on_chip([grad_out, *parts]))
 
 
-def next_partials(here, grad_out, coords, came_up, came_down, n, away):
+def next_partials(here, grad_out, coords, came, n, away, upward):
     tokens, width = coords.shape
     cols = grad_out.shape[1] // n
-    rows = came_up.shape[0]
-
-    def kernel(here_ref, grad, coord, in_up, in_down, up, down):
-        column = pl.multiple_of(chunk_at(here_ref, away, n) * cols, 128)
+    rows = came.shape[0]
+    added = slice(0, rows) if upward else slice(cols - rows, cols)
+    rest = slice(rows, cols) if upward else slice(0, cols - rows)
+
+    def kernel(here_ref, grad, coord, arrived, out):
+        column = pl.multiple_of(chunk_at(here_ref, away if upward else n - away, n) * cols, 128)
         part = contract_tokens(grad[:, pl.ds(column, cols)], coord[...])
-        up[:rows] = (part[:rows] + in_up[...].astype(jnp.float32)).astype(jnp.bfloat16)
+        out[added] = (part[added] + arrived[...].astype(jnp.float32)).astype(jnp.bfloat16)
         if rows < cols:
-            up[rows:] = part[rows:].astype(jnp.bfloat16)
-        column = pl.multiple_of(chunk_at(here_ref, n - away, n) * cols, 128)
-        part = contract_tokens(grad[:, pl.ds(column, cols)], coord[...])
-        rest = cols - rows
-        down[rest:] = (part[rest:] + in_down[...].astype(jnp.float32)).astype(jnp.bfloat16)
-        if rest:
-            down[:rest] = part[:rest].astype(jnp.bfloat16)
-
-    full = pltpu.VMEM((cols, width), jnp.bfloat16)
-    return pl.pallas_call(
-        kernel,
-        out_shape=(full, full),
-        in_specs=[scalars(), *[on_chip()] * 4],
-        out_specs=(on_chip(),) * 2,
+            out[rest] = part[rest].astype(jnp.bfloat16)
+
+    return pl.pallas_call(
+        kernel,
+        out_shape=pltpu.VMEM((cols, width), jnp.bfloat16),
+        in_specs=[scalars(), *[on_chip()] * 3],
+        out_specs=on_chip(),
         cost_estimate=pl.CostEstimate(
-            flops=4 * tokens * cols * width, transcendentals=0, bytes_accessed=4 << 20
+            flops=2 * tokens * cols * width, transcendentals=0, bytes_accessed=2 << 20
         ),
         compiler_params=pltpu.CompilerParams(vmem_limit_bytes=SCRATCH_BYTES),
         name="next_partials",
-    )(here, *kept_on_chip([grad_out, coords, came_up, came_down]))
+    )(here, *kept_on_chip([grad_out, coords, came]))
 
 
 def own_direction(here, grad_out, coords, came_up, came_down, first_moment, second_moment, s, n):
@@ -262,44 +294,49 @@
     cols = sum(row[0].shape[0] for row in chunks[0])
     flat = [stream for chunk in chunks for row in chunk for stream in row]
     held = () if update is None else (update,)
-    tile = depth // 2
+    n = all_columns // cols
+    starts = range(0, cols, 256)
+    blocks = [(low, min(256, cols - low)) for low in starts]
 
     def kernel(here_ref, base, *refs):
-        out = refs[-1]
+        out, made, sems = refs[-3:]
         left = list(refs[: len(flat)])
-        lines = pl.ds(pl.multiple_of(pl.program_id(1) * tile, tile), tile)
+        copies = []
         for g, chunk in enumerate(chunks):
             rows = [[left.pop(0) for _ in row] for row in chunk]
-
-            @pl.when(pl.program_id(0) == g)
-            def _(rows=rows):
-                whole = jnp.concatenate(
-                    [jnp.concatenate([stream[...] for stream in row], axis=1) for row in rows], axis=0
+            whole = jnp.concatenate(
+                [jnp.concatenate([stream[...] for stream in row], axis=1) for row in rows], axis=0
+            )
+            column = chunk_at(here_ref, places[g], n) * cols
+            for b, (low, size) in enumerate(blocks):
+                made[g, :, low : low + size] = lax.dot_general(
+                    base[...],
+                    whole[low : low + size],
+                    (((1,), (1,)), ((), ())),
+                    preferred_element_type=jnp.float32,
+                ).astype(made.dtype)
+                columns = pl.ds(pl.multiple_of(column + low, 128), size)
+                copy = pltpu.make_async_copy(
+                    made.at[g, :, pl.ds(low, size)], out.at[:, columns], sems.at[g, b]
                 )
-                out[...] = lax.dot_general(
-                    base[lines], whole, (((1,), (1,)), ((), ())), preferred_element_type=jnp.float32
-                ).astype(out.dtype)
-
-    n = all_columns // cols
-
-    def place(g, r, here):
-        at = chunk_at(here, places[0], n)
-        for k in range(1, len(places)):
-            at = jnp.where(g == k, chunk_at(here, places[k], n), at)
-        return (r, at)
+                copy.start()
+                copies.append(copy)
+        for copy in copies:
+            copy.wait()
 
     return pl.pallas_call(
         kernel,
         out_shape=jax.ShapeDtypeStruct((depth, all_columns), jnp.bfloat16),
-        grid_spec=pltpu.PrefetchScalarGridSpec(
-            num_scalar_prefetch=1,
-            grid=(len(chunks), depth // tile),
-            in_specs=[
-                *[on_chip()] * (1 + len(flat)),
-                *[pl.BlockSpec(memory_space=pl.ANY)] * len(held),
-            ],
-            out_specs=pl.BlockSpec((tile, cols), place),
-        ),
+        in_specs=[
+            scalars(),
+            *[on_chip()] * (1 + len(flat)),
+            *[pl.BlockSpec(memory_space=pl.ANY)] * len(held),
+        ],
+        out_specs=pl.BlockSpec(memory_space=pl.ANY),
+        scratch_shapes=[
+            pltpu.VMEM((len(chunks), depth, cols), jnp.bfloat16),
+            pltpu.SemaphoreType.DMA((len(chunks), len(blocks))),
+        ],
         input_output_aliases={2 + len(flat): 0} if held else {},
         cost_estimate=pl.CostEstimate(
             flops=2 * depth * cols * rank * len(chunks),
@@ -321,24 +358,22 @@
         return (lax.ppermute(to_up, "dp", upward), lax.ppermute(to_down, "dp", downward))
 
     me = lax.axis_index("mp")
-    here, me, side, activations, basis = lax.optimization_barrier(
-        (lax.axis_index("dp").reshape(1), me.reshape(1), lax.bitwise_and(me, 1), activations, basis)
+    here, me, activations, basis = lax.optimization_barrier(
+        (lax.axis_index("dp").reshape(1), me.reshape(1), activations, basis)
     )
 
-    depth, rank = basis.shape
-    width = rank // STREAMS
+    depth, _ = basis.shape
     all_columns = grad_out.shape[1]
     cols = all_columns // n
     half = n // 2
     streams = range(STREAMS)
 
     part = depth // 2
-    own = lax.dynamic_slice(basis, (side * part, 0), (part, rank))
-    own = [own[:, s * width : (s + 1) * width] for s in streams]
+    own = own_pieces(me, basis)
     ups, downs = list(own), list(own)
     pieces = [[(own[s], 0, 0)] for s in streams]
     kept, sent = split_columns(me, activations, n)
-    came = lax.ppermute(sent, "mp", partners)
+    swapped = lax.ppermute(sent, "mp", partners)
     total = [None] * STREAMS
     for k in range(1, half + 1):
         for s in streams:
@@ -346,12 +381,12 @@
             if k == half:
                 low = part // 2
                 ups[s], downs[s] = ups[s][:low], downs[s][low:]
-                total[s] = add_coords(here, me, kept, came, None, pieces[s], part, n)
+                total[s] = add_coords(here, me, kept, swapped, None, pieces[s], part, n)
                 pieces[s] = []
             ups[s], downs[s] = hop(ups[s], downs[s])
             pieces[s] += [(ups[s], n - k, 0), (downs[s], k, low)]
     for s in streams:
-        total[s] = add_coords(here, me, kept, came, total[s], pieces[s], part, n)
+        total[s] = add_coords(here, me, kept, swapped, total[s], pieces[s], part, n)
 
     parts = [None] * STREAMS
     for s in streams:
@@ -365,7 +400,10 @@
         ups[s], downs[s] = hop(ups[s], downs[s])
     for k in range(2, half + 1):
         for s in streams:
-            ups[s], downs[s] = next_partials(here, grad_out, coords[s], ups[s], downs[s], n, half + 1 - k)
+            ups[s], downs[s] = [
+                next_partials(here, grad_out, coords[s], came, n, half + 1 - k, way == "up")
+                for way, came in (("up", ups[s]), ("down", downs[s]))
+            ]
             ups[s], downs[s] = hop(ups[s], downs[s])
     projected = [None] * STREAMS
     direction = [None] * STREAMS

time: 131 us -> 120 us (0.916)
  Pallas kernels: 31.3 us -> 24.6 us
  local copies, waits for them, and re-layouts: 5.02 us -> 0.09 us
    ppermute x24, starting transfers between devices: 31.2 us -> 42.3 us  [hop(): lax.ppermute(to_up, 'dp', upward)]
    ppermute x24, starting transfers between devices: 19.2 us -> 8.59 us  [hop(): lax.ppermute(to_down, 'dp', downward)]
    pallas_call x4, Pallas kernels: 6.7 us -> 1.72 us  [add_coords(): pl.pallas_call(kernel, out_shape=pltpu.VMEM((2 * tokens, width), jnp.floa...]
    unnamed x16 -> x10, local copies, waits for them, and re-layouts: 3.98 us -> 0.03 us
    pallas_call x5, Pallas kernels: 13.7 us -> 10.7 us  [write_update(): pl.pallas_call(kernel, out_shape=jax.ShapeDtypeStruct((depth, all_columns...]
    ppermute x24, waiting for transfers between devices: 25 us -> 22.3 us  [hop(): lax.ppermute(to_up, 'dp', upward)]
    ppermute x24, waiting for transfers between devices: 13.1 us -> 15.4 us  [hop(): lax.ppermute(to_down, 'dp', downward)]
    pallas_call x7 -> x14, Pallas kernels: 7.27 us -> 8.55 us  [the longest x12 5.67 us: next_partials(): pl.pallas_call(kernel, out_shape=pltpu.VMEM((cols, width), jnp.bfloat16),...]
  transfers between devices with their start and end apart: 53 -> 53, of which waited for: 27 -> 23; matrix products, arithmetic and copies ran while one was open for 1% -> 0% of each run, Pallas kernels for 20% -> 18%
where the time goes in v4:
time: 120 us
  starting transfers between devices  54.4 us (45%)
  waiting for transfers between devices  39.4 us (33%)
  Pallas kernels  24.6 us (20%)
    ppermute x24, starting transfers between devices, hop(): lax.ppermute(to_up, 'dp', upward)  42.3 us
    ppermute x24, waiting for transfers between devices, hop(): lax.ppermute(to_up, 'dp', upward)  22.3 us
    ppermute x24, waiting for transfers between devices, hop(): lax.ppermute(to_down, 'dp', downward)  15.4 us
    pallas_call x5, Pallas kernels, write_update(): pl.pallas_call(kernel, out_shape=jax.ShapeDtypeStruct((depth, all_columns...  10.7 us
    ppermute x24, starting transfers between devices, hop(): lax.ppermute(to_down, 'dp', downward)  8.59 us
    pallas_call x12, Pallas kernels, next_partials(): pl.pallas_call(kernel, out_shape=pltpu.VMEM((cols, width), jnp.bfloat16),...  5.67 us
    ppermute x2, starting transfers between devices, on_ring(): lax.ppermute(pair, 'mp', [(a, (a + k) % m) for a in range(m)])  2.86 us
  transfers between devices with their start and end apart: 53, of which 23 were waited for; matrix products, arithmetic and copies ran while one was open for 0% of the time, Pallas kernels for 18%

profile of v4, /device:TPU:0, one launch (start us, length us, event | category | flops | bytes accessed | tf_op | source)
XLA Modules:
  0.0 119.7 jit_solution(9393807717003696910)
XLA Ops:
  0.6 1.9 %split_columns.1 = (bf16[128,4096]{1,0:T(8,128)(2,1)S(1)}, bf16[128,4096]{1,0:T(8,128)(2,1)S(1)}) custom-call(s32[1]{0:T(128)} %bitcast.1.me_ref, bf16[128,8192]{1,0:T(8,128)(2,1)} %source), custom_call_target="tpu_custom_call" | custom-call | tf_op jit(solution)/shard_map/split_columns/pallas_call | solution.py:105
  2.6 0.6 collective-permute-start
  3.1 1.0 own_pieces.1
  4.1 2.6 %collective-permute-start.23 = (bf16[512,128]{1,0:T(8,128)(2,1)S(1)}, bf16[512,128]{1,0:T(8,128)(2,1)S(1)}, u32[]{:S(2)}, u32[]{:S(2)}) collective-permute-start(bf16[512,128]{1,0:T(8,128)(2,1)S(1)} %get-tuple-element.34.refs_2_), channel_id=1, source_target_pairs={{0,8},{8,16},{16,24},{24,28},{28,20},{20,12},{12,4},{4,0},{1,9},{9... | collective-permute-start | bytes 393224 | tf_op jit(solution)/shard_map/ppermute | solution.py:358
  6.7 2.0 %collective-permute-start.1 = (bf16[512,128]{1,0:T(8,128)(2,1)S(1)}, bf16[512,128]{1,0:T(8,128)(2,1)S(1)}, u32[]{:S(2)}, u32[]{:S(2)}) collective-permute-start(bf16[512,128]{1,0:T(8,128)(2,1)S(1)} %get-tuple-element.29.refs_2_), channel_id=1, source_target_pairs={{0,8},{8,16},{16,24},{24,28},{28,20},{20,12},{12,4},{4,0},{1,9},{9... | collective-permute-start | bytes 393224 | tf_op jit(solution)/shard_map/ppermute | solution.py:358
  8.8 2.3 %collective-permute-done.23.refs_3_ = bf16[512,128]{1,0:T(8,128)(2,1)S(1)} collective-permute-done((bf16[512,128]{1,0:T(8,128)(2,1)S(1)}, bf16[512,128]{1,0:T(8,128)(2,1)S(1)}, u32[]{:S(2)}, u32[]{:S(2)}) %collective-permute-start.23) | collective-permute-done | bytes 131104 | tf_op jit(solution)/shard_map/ppermute | solution.py:358
  11.0 2.1 %collective-permute-start.25 = (bf16[512,128]{1,0:T(8,128)(2,1)S(1)}, bf16[512,128]{1,0:T(8,128)(2,1)S(1)}, u32[]{:S(2)}, u32[]{:S(2)}) collective-permute-start(bf16[512,128]{1,0:T(8,128)(2,1)S(1)} %collective-permute-done.23.refs_3_), channel_id=1, source_target_pairs={{0,8},{8,16},{16,24},{24,28},{28,20},{20,12},{12,4},{4,0},{1,9},{9... | collective-permute-start | bytes 393224 | tf_op jit(solution)/shard_map/ppermute | solution.py:358
  13.1 0.7 collective-permute-done.1.refs_3_
  13.8 2.1 %collective-permute-start.3 = (bf16[512,128]{1,0:T(8,128)(2,1)S(1)}, bf16[512,128]{1,0:T(8,128)(2,1)S(1)}, u32[]{:S(2)}, u32[]{:S(2)}) collective-permute-start(bf16[512,128]{1,0:T(8,128)(2,1)S(1)} %collective-permute-done.1.refs_3_), channel_id=1, source_target_pairs={{0,8},{8,16},{16,24},{24,28},{28,20},{20,12},{12,4},{4,0},{1,9},{9... | collective-permute-start | bytes 393224 | tf_op jit(solution)/shard_map/ppermute | solution.py:358
  15.9 0.8 collective-permute-done.25.refs_5_
  16.7 2.1 %collective-permute-start.27 = (bf16[512,128]{1,0:T(8,128)(2,1)S(1)}, bf16[512,128]{1,0:T(8,128)(2,1)S(1)}, u32[]{:S(2)}, u32[]{:S(2)}) collective-permute-start(bf16[512,128]{1,0:T(8,128)(2,1)S(1)} %collective-permute-done.25.refs_5_), channel_id=1, source_target_pairs={{0,8},{8,16},{16,24},{24,28},{28,20},{20,12},{12,4},{4,0},{1,9},{9... | collective-permute-start | bytes 393224 | tf_op jit(solution)/shard_map/ppermute | solution.py:358
  18.8 1.4 %collective-permute-done.3.refs_5_ = bf16[512,128]{1,0:T(8,128)(2,1)S(1)} collective-permute-done((bf16[512,128]{1,0:T(8,128)(2,1)S(1)}, bf16[512,128]{1,0:T(8,128)(2,1)S(1)}, u32[]{:S(2)}, u32[]{:S(2)}) %collective-permute-start.3) | collective-permute-done | bytes 131104 | tf_op jit(solution)/shard_map/ppermute | solution.py:358
  20.2 2.1 %collective-permute-start.5 = (bf16[512,128]{1,0:T(8,128)(2,1)S(1)}, bf16[512,128]{1,0:T(8,128)(2,1)S(1)}, u32[]{:S(2)}, u32[]{:S(2)}) collective-permute-start(bf16[512,128]{1,0:T(8,128)(2,1)S(1)} %collective-permute-done.3.refs_5_), channel_id=1, source_target_pairs={{0,8},{8,16},{16,24},{24,28},{28,20},{20,12},{12,4},{4,0},{1,9},{9... | collective-permute-start | bytes 393224 | tf_op jit(solution)/shard_map/ppermute | solution.py:358
  22.3 0.8 collective-permute-done.27.refs_7_
  23.1 2.1 %collective-permute-start.29 = (bf16[256,128]{1,0:T(8,128)(2,1)S(1)}, bf16[256,128]{1,0:T(8,128)(2,1)S(1)}, u32[]{:S(2)}, u32[]{:S(2)}) collective-permute-start(bf16[256,128]{1,0:T(8,128)(2,1)S(1)} %slice.35), channel_id=1, source_target_pairs={{0,8},{8,16},{16,24},{24,28},{28,20},{20,12},{12,4},{4,0},{1,9},{9... | collective-permute-start | bytes 196616 | tf_op jit(solution)/shard_map/ppermute | solution.py:358
  25.3 0.6 add_coords.6.refs_2_
  25.9 1.4 %collective-permute-done.29.refs_3_ = bf16[256,128]{1,0:T(8,128)(2,1)S(1)} collective-permute-done((bf16[256,128]{1,0:T(8,128)(2,1)S(1)}, bf16[256,128]{1,0:T(8,128)(2,1)S(1)}, u32[]{:S(2)}, u32[]{:S(2)}) %collective-permute-start.29) | collective-permute-done | bytes 65568 | tf_op jit(solution)/shard_map/ppermute | solution.py:358
  27.4 2.1 %collective-permute-done.30.refs_4_ = bf16[256,128]{1,0:T(8,128)(2,1)S(1)} collective-permute-done((bf16[256,128]{1,0:T(8,128)(2,1)S(1)}, bf16[256,128]{1,0:T(8,128)(2,1)S(1)}, u32[]{:S(2)}, u32[]{:S(2)}) %collective-permute-start.30) | collective-permute-done | bytes 65568 | tf_op jit(solution)/shard_map/ppermute | solution.py:358
  29.9 1.6 %collective-permute-start.7 = (bf16[256,128]{1,0:T(8,128)(2,1)S(1)}, bf16[256,128]{1,0:T(8,128)(2,1)S(1)}, u32[]{:S(2)}, u32[]{:S(2)}) collective-permute-start(bf16[256,128]{1,0:T(8,128)(2,1)S(1)} %slice.32), channel_id=1, source_target_pairs={{0,8},{8,16},{16,24},{24,28},{28,20},{20,12},{12,4},{4,0},{1,9},{9... | collective-permute-start | bytes 196616 | tf_op jit(solution)/shard_map/ppermute | solution.py:358
  32.0 0.6 add_coords.4.refs_2_
  32.6 1.7 %collective-permute-done.7.refs_3_ = bf16[256,128]{1,0:T(8,128)(2,1)S(1)} collective-permute-done((bf16[256,128]{1,0:T(8,128)(2,1)S(1)}, bf16[256,128]{1,0:T(8,128)(2,1)S(1)}, u32[]{:S(2)}, u32[]{:S(2)}) %collective-permute-start.7) | collective-permute-done | bytes 65568 | tf_op jit(solution)/shard_map/ppermute | solution.py:358
  34.4 1.4 %collective-permute-done.8.refs_4_ = bf16[256,128]{1,0:T(8,128)(2,1)S(1)} collective-permute-done((bf16[256,128]{1,0:T(8,128)(2,1)S(1)}, bf16[256,128]{1,0:T(8,128)(2,1)S(1)}, u32[]{:S(2)}, u32[]{:S(2)}) %collective-permute-start.8) | collective-permute-done | bytes 65568 | tf_op jit(solution)/shard_map/ppermute | solution.py:358
  36.1 1.6 %collective-permute-start.32 = (bf16[256,128]{1,0:T(8,128)(2,1)S(1)}, bf16[256,128]{1,0:T(8,128)(2,1)S(1)}, u32[]{:S(2)}, u32[]{:S(2)}) collective-permute-start(bf16[256,128]{1,0:T(8,128)(2,1)S(1)} %add_convert_fusion.refs_0_), channel_id=1, source_target_pairs={{0,2},{1,3},{2,0},{3,1},{4,6},{5,7},{6,4},{7,5},{8,10},{9,11},{10,... | collective-permute-start | bytes 196616 | tf_op jit(solution)/shard_map/ppermute | solution.py:395
  37.7 1.3 %collective-permute-start.10 = (bf16[256,128]{1,0:T(8,128)(2,1)S(1)}, bf16[256,128]{1,0:T(8,128)(2,1)S(1)}, u32[]{:S(2)}, u32[]{:S(2)}) collective-permute-start(bf16[256,128]{1,0:T(8,128)(2,1)S(1)} %add_convert_fusion.1.refs_0_), channel_id=1, source_target_pairs={{0,2},{1,3},{2,0},{3,1},{4,6},{5,7},{6,4},{7,5},{8,10},{9,11},{10,... | collective-permute-start | bytes 196616 | tf_op jit(solution)/shard_map/ppermute | solution.py:395
  39.0 1.8 %collective-permute-done.32.refs_1_ = bf16[256,128]{1,0:T(8,128)(2,1)S(1)} collective-permute-done((bf16[256,128]{1,0:T(8,128)(2,1)S(1)}, bf16[256,128]{1,0:T(8,128)(2,1)S(1)}, u32[]{:S(2)}, u32[]{:S(2)}) %collective-permute-start.32) | collective-permute-done | bytes 65568 | tf_op jit(solution)/shard_map/ppermute | solution.py:395
  41.8 1.6 %collective-permute-start.33 = (bf16[448,128]{1,0:T(8,128)(2,1)S(1)}, bf16[448,128]{1,0:T(8,128)(2,1)S(1)}, u32[]{:S(2)}, u32[]{:S(2)}) collective-permute-start(bf16[448,128]{1,0:T(8,128)(2,1)S(1)} %get-tuple-element.36), channel_id=1, source_target_pairs={{0,8},{8,16},{16,24},{24,28},{28,20},{20,12},{12,4},{4,0},{1,9},{9... | collective-permute-start | bytes 344072 | tf_op jit(solution)/shard_map/ppermute | solution.py:358
  44.4 1.6 %collective-permute-start.11 = (bf16[448,128]{1,0:T(8,128)(2,1)S(1)}, bf16[448,128]{1,0:T(8,128)(2,1)S(1)}, u32[]{:S(2)}, u32[]{:S(2)}) collective-permute-start(bf16[448,128]{1,0:T(8,128)(2,1)S(1)} %get-tuple-element.31), channel_id=1, source_target_pairs={{0,8},{8,16},{16,24},{24,28},{28,20},{20,12},{12,4},{4,0},{1,9},{9... | collective-permute-start | bytes 344072 | tf_op jit(solution)/shard_map/ppermute | solution.py:358
  46.0 0.8 collective-permute-done.37.arrived
  48.3 1.6 %collective-permute-start.34 = (bf16[896,128]{1,0:T(8,128)(2,1)S(1)}, bf16[896,128]{1,0:T(8,128)(2,1)S(1)}, u32[]{:S(2)}, u32[]{:S(2)}) collective-permute-start(bf16[896,128]{1,0:T(8,128)(2,1)S(1)} %next_partials.18), channel_id=1, source_target_pairs={{0,8},{8,16},{16,24},{24,28},{28,20},{20,12},{12,4},{4,0},{1,9},{9... | collective-permute-start | bytes 688136 | tf_op jit(solution)/shard_map/ppermute | solution.py:358
  50.4 0.5 collective-permute-start.16
  51.5 1.6 %collective-permute-start.12 = (bf16[896,128]{1,0:T(8,128)(2,1)S(1)}, bf16[896,128]{1,0:T(8,128)(2,1)S(1)}, u32[]{:S(2)}, u32[]{:S(2)}) collective-permute-start(bf16[896,128]{1,0:T(8,128)(2,1)S(1)} %next_partials.12), channel_id=1, source_target_pairs={{0,8},{8,16},{16,24},{24,28},{28,20},{20,12},{12,4},{4,0},{1,9},{9... | collective-permute-start | bytes 688136 | tf_op jit(solution)/shard_map/ppermute | solution.py:358
  53.1 2.7 %collective-permute-done.38.arrived = bf16[896,128]{1,0:T(8,128)(2,1)S(1)} collective-permute-done((bf16[896,128]{1,0:T(8,128)(2,1)S(1)}, bf16[896,128]{1,0:T(8,128)(2,1)S(1)}, u32[]{:S(2)}, u32[]{:S(2)}) %collective-permute-start.38) | collective-permute-done | bytes 229408 | tf_op jit(solution)/shard_map/ppermute | solution.py:358
  57.3 1.6 %collective-permute-start.35 = (bf16[896,128]{1,0:T(8,128)(2,1)S(1)}, bf16[896,128]{1,0:T(8,128)(2,1)S(1)}, u32[]{:S(2)}, u32[]{:S(2)}) collective-permute-start(bf16[896,128]{1,0:T(8,128)(2,1)S(1)} %next_partials.19), channel_id=1, source_target_pairs={{0,8},{8,16},{16,24},{24,28},{28,20},{20,12},{12,4},{4,0},{1,9},{9... | collective-permute-start | bytes 688136 | tf_op jit(solution)/shard_map/ppermute | solution.py:358
  58.9 1.8 %collective-permute-done.16.arrived = bf16[896,128]{1,0:T(8,128)(2,1)S(1)} collective-permute-done((bf16[896,128]{1,0:T(8,128)(2,1)S(1)}, bf16[896,128]{1,0:T(8,128)(2,1)S(1)}, u32[]{:S(2)}, u32[]{:S(2)}) %collective-permute-start.16) | collective-permute-done | bytes 229408 | tf_op jit(solution)/shard_map/ppermute | solution.py:358
  62.2 1.6 %collective-permute-start.13 = (bf16[896,128]{1,0:T(8,128)(2,1)S(1)}, bf16[896,128]{1,0:T(8,128)(2,1)S(1)}, u32[]{:S(2)}, u32[]{:S(2)}) collective-permute-start(bf16[896,128]{1,0:T(8,128)(2,1)S(1)} %next_partials.13), channel_id=1, source_target_pairs={{0,8},{8,16},{16,24},{24,28},{28,20},{20,12},{12,4},{4,0},{1,9},{9... | collective-permute-start | bytes 688136 | tf_op jit(solution)/shard_map/ppermute | solution.py:358
  63.9 1.8 %collective-permute-done.39.arrived = bf16[896,128]{1,0:T(8,128)(2,1)S(1)} collective-permute-done((bf16[896,128]{1,0:T(8,128)(2,1)S(1)}, bf16[896,128]{1,0:T(8,128)(2,1)S(1)}, u32[]{:S(2)}, u32[]{:S(2)}) %collective-permute-start.39) | collective-permute-done | bytes 229408 | tf_op jit(solution)/shard_map/ppermute | solution.py:358
  67.1 1.6 %collective-permute-start.36 = (bf16[896,128]{1,0:T(8,128)(2,1)S(1)}, bf16[896,128]{1,0:T(8,128)(2,1)S(1)}, u32[]{:S(2)}, u32[]{:S(2)}) collective-permute-start(bf16[896,128]{1,0:T(8,128)(2,1)S(1)} %next_partials.20), channel_id=1, source_target_pairs={{0,8},{8,16},{16,24},{24,28},{28,20},{20,12},{12,4},{4,0},{1,9},{9... | collective-permute-start | bytes 688136 | tf_op jit(solution)/shard_map/ppermute | solution.py:358
  68.7 1.8 %collective-permute-done.17.arrived = bf16[896,128]{1,0:T(8,128)(2,1)S(1)} collective-permute-done((bf16[896,128]{1,0:T(8,128)(2,1)S(1)}, bf16[896,128]{1,0:T(8,128)(2,1)S(1)}, u32[]{:S(2)}, u32[]{:S(2)}) %collective-permute-start.17) | collective-permute-done | bytes 229408 | tf_op jit(solution)/shard_map/ppermute | solution.py:358
  72.1 1.8 %collective-permute-start.14 = (bf16[896,128]{1,0:T(8,128)(2,1)S(1)}, bf16[896,128]{1,0:T(8,128)(2,1)S(1)}, u32[]{:S(2)}, u32[]{:S(2)}) collective-permute-start(bf16[896,128]{1,0:T(8,128)(2,1)S(1)} %next_partials.14), channel_id=1, source_target_pairs={{0,8},{8,16},{16,24},{24,28},{28,20},{20,12},{12,4},{4,0},{1,9},{9... | collective-permute-start | bytes 688136 | tf_op jit(solution)/shard_map/ppermute | solution.py:358
  73.8 1.6 %collective-permute-done.40.in_down = bf16[896,128]{1,0:T(8,128)(2,1)S(1)} collective-permute-done((bf16[896,128]{1,0:T(8,128)(2,1)S(1)}, bf16[896,128]{1,0:T(8,128)(2,1)S(1)}, u32[]{:S(2)}, u32[]{:S(2)}) %collective-permute-start.40) | collective-permute-done | bytes 229408 | tf_op jit(solution)/shard_map/ppermute | solution.py:358
  75.5 1.0 collective-permute-done.36.in_up
  76.5 0.7 own_direction.3
  77.2 1.6 %collective-permute-start.41 = (bf16[896,128]{1,0:T(8,128)(2,1)S(1)}, bf16[896,128]{1,0:T(8,128)(2,1)S(1)}, u32[]{:S(2)}, u32[]{:S(2)}) collective-permute-start(bf16[896,128]{1,0:T(8,128)(2,1)S(1)} %get-tuple-element.38.refs_1_), channel_id=1, source_target_pairs={{0,8},{8,16},{16,24},{24,28},{28,20},{20,12},{12,4},{4,0},{1,9},{9... | collective-permute-start | bytes 688136 | tf_op jit(solution)/shard_map/ppermute | solution.py:358
  79.2 1.1 collective-permute-done.18.in_down
  80.4 1.0 collective-permute-done.14.in_up
  81.4 0.6 own_direction.2
  82.1 1.6 %collective-permute-start.19 = (bf16[896,128]{1,0:T(8,128)(2,1)S(1)}, bf16[896,128]{1,0:T(8,128)(2,1)S(1)}, u32[]{:S(2)}, u32[]{:S(2)}) collective-permute-start(bf16[896,128]{1,0:T(8,128)(2,1)S(1)} %get-tuple-element.33.refs_0_), channel_id=1, source_target_pairs={{0,8},{8,16},{16,24},{24,28},{28,20},{20,12},{12,4},{4,0},{1,9},{9... | collective-permute-start | bytes 688136 | tf_op jit(solution)/shard_map/ppermute | solution.py:358
  84.1 2.2 %collective-permute-done.41.refs_1_ = bf16[896,128]{1,0:T(8,128)(2,1)S(1)} collective-permute-done((bf16[896,128]{1,0:T(8,128)(2,1)S(1)}, bf16[896,128]{1,0:T(8,128)(2,1)S(1)}, u32[]{:S(2)}, u32[]{:S(2)}) %collective-permute-start.41) | collective-permute-done | bytes 229408 | tf_op jit(solution)/shard_map/ppermute | solution.py:358
  86.3 1.6 %collective-permute-start.42 = (bf16[896,128]{1,0:T(8,128)(2,1)S(1)}, bf16[896,128]{1,0:T(8,128)(2,1)S(1)}, u32[]{:S(2)}, u32[]{:S(2)}) collective-permute-start(bf16[896,128]{1,0:T(8,128)(2,1)S(1)} %collective-permute-done.41.refs_1_), channel_id=1, source_target_pairs={{0,8},{8,16},{16,24},{24,28},{28,20},{20,12},{12,4},{4,0},{1,9},{9... | collective-permute-start | bytes 688136 | tf_op jit(solution)/shard_map/ppermute | solution.py:358
  88.4 2.9 %collective-permute-done.19.refs_0_ = bf16[896,128]{1,0:T(8,128)(2,1)S(1)} collective-permute-done((bf16[896,128]{1,0:T(8,128)(2,1)S(1)}, bf16[896,128]{1,0:T(8,128)(2,1)S(1)}, u32[]{:S(2)}, u32[]{:S(2)}) %collective-permute-start.19) | collective-permute-done | bytes 229408 | tf_op jit(solution)/shard_map/ppermute | solution.py:358
  91.2 1.6 %collective-permute-start.20 = (bf16[896,128]{1,0:T(8,128)(2,1)S(1)}, bf16[896,128]{1,0:T(8,128)(2,1)S(1)}, u32[]{:S(2)}, u32[]{:S(2)}) collective-permute-start(bf16[896,128]{1,0:T(8,128)(2,1)S(1)} %collective-permute-done.19.refs_0_), channel_id=1, source_target_pairs={{0,8},{8,16},{16,24},{24,28},{28,20},{20,12},{12,4},{4,0},{1,9},{9... | collective-permute-start | bytes 688136 | tf_op jit(solution)/shard_map/ppermute | solution.py:358
  93.3 2.9 %collective-permute-done.42.refs_1_ = bf16[896,128]{1,0:T(8,128)(2,1)S(1)} collective-permute-done((bf16[896,128]{1,0:T(8,128)(2,1)S(1)}, bf16[896,128]{1,0:T(8,128)(2,1)S(1)}, u32[]{:S(2)}, u32[]{:S(2)}) %collective-permute-start.42) | collective-permute-done | bytes 229408 | tf_op jit(solution)/shard_map/ppermute | solution.py:358
  96.2 1.6 %collective-permute-start.43 = (bf16[896,128]{1,0:T(8,128)(2,1)S(1)}, bf16[896,128]{1,0:T(8,128)(2,1)S(1)}, u32[]{:S(2)}, u32[]{:S(2)}) collective-permute-start(bf16[896,128]{1,0:T(8,128)(2,1)S(1)} %collective-permute-done.42.refs_1_), channel_id=1, source_target_pairs={{0,8},{8,16},{16,24},{24,28},{28,20},{20,12},{12,4},{4,0},{1,9},{9... | collective-permute-start | bytes 688136 | tf_op jit(solution)/shard_map/ppermute | solution.py:358
  98.2 2.9 %collective-permute-done.20.refs_0_ = bf16[896,128]{1,0:T(8,128)(2,1)S(1)} collective-permute-done((bf16[896,128]{1,0:T(8,128)(2,1)S(1)}, bf16[896,128]{1,0:T(8,128)(2,1)S(1)}, u32[]{:S(2)}, u32[]{:S(2)}) %collective-permute-start.20) | collective-permute-done | bytes 229408 | tf_op jit(solution)/shard_map/ppermute | solution.py:358
  101.1 1.6 %collective-permute-start.21 = (bf16[896,128]{1,0:T(8,128)(2,1)S(1)}, bf16[896,128]{1,0:T(8,128)(2,1)S(1)}, u32[]{:S(2)}, u32[]{:S(2)}) collective-permute-start(bf16[896,128]{1,0:T(8,128)(2,1)S(1)} %collective-permute-done.20.refs_0_), channel_id=1, source_target_pairs={{0,8},{8,16},{16,24},{24,28},{28,20},{20,12},{12,4},{4,0},{1,9},{9... | collective-permute-start | bytes 688136 | tf_op jit(solution)/shard_map/ppermute | solution.py:358
  103.1 1.4 %new_moments.1 = (f32[896,256]{1,0:T(8,128)}, f32[896,256]{1,0:T(8,128)}) custom-call(f32[896,128]{1,0:T(8,128)S(1)} %get-tuple-element.39.refs_0_, f32[896,128]{1,0:T(8,128)S(1)} %get-tuple-element.40.refs_1_, f32[896,256]{1,0:T(8,128)S(1)} %copy-done.1, f32[896,256]{1,0:T(8,128)S(1)} %copy-done.2), custom_call_target="tpu_custom_call" | custom-call | bytes 6291456 | tf_op jit(solution)/shard_map/new_moments/pallas_call | solution.py:280
  104.5 1.7 %write_update.5.refs_4_ = bf16[1024,7168]{1,0:T(8,128)(2,1)} custom-call(s32[1]{0:T(128)} %bitcast.here_ref, bf16[1024,256]{1,0:T(8,128)(2,1)S(1)} %copy-done, bf16[896,128]{1,0:T(8,128)(2,1)S(1)} %get-tuple-element.33.refs_0_, bf16[896,128]{1,0:T(8,128)(2,1)S(1)} %get-tuple-element.38.refs_1_), custom_call_target="tpu_custom_call" | custom-call | flops 469762048 | bytes 1835008 | tf_op jit(solution)/shard_map/write_update/pallas_call | solution.py:327
  106.2 2.4 %write_update.6.refs_4_ = bf16[1024,7168]{1,0:T(8,128)(2,1)} custom-call(s32[1]{0:T(128)} %bitcast.here_ref, bf16[1024,256]{1,0:T(8,128)(2,1)S(1)} %copy-done, bf16[896,128]{1,0:T(8,128)(2,1)S(1)} %collective-permute-done.19.refs_0_, bf16[896,128]{1,0:T(8,128)(2,1)S(1)} %collective-permute-done.41.refs_1_, ...), custom_call_target="tpu_custom_call", output_to_operand_aliasing={{}: (6, {})} | custom-call | flops 939524096 | bytes 3670016 | tf_op jit(solution)/shard_map/write_update/pallas_call | solution.py:327
  108.7 1.6 %collective-permute-start.44 = (bf16[448,128]{1,0:T(8,128)(2,1)S(1)}, bf16[448,128]{1,0:T(8,128)(2,1)S(1)}, u32[]{:S(2)}, u32[]{:S(2)}) collective-permute-start(bf16[448,128]{1,0:T(8,128)(2,1)S(1)} %slice.37), channel_id=1, source_target_pairs={{0,8},{8,16},{16,24},{24,28},{28,20},{20,12},{12,4},{4,0},{1,9},{9... | collective-permute-start | bytes 344072 | tf_op jit(solution)/shard_map/ppermute | solution.py:358
  110.8 1.6 %collective-permute-start.22 = (bf16[448,128]{1,0:T(8,128)(2,1)S(1)}, bf16[448,128]{1,0:T(8,128)(2,1)S(1)}, u32[]{:S(2)}, u32[]{:S(2)}) collective-permute-start(bf16[448,128]{1,0:T(8,128)(2,1)S(1)} %slice.34), channel_id=1, source_target_pairs={{0,8},{8,16},{16,24},{24,28},{28,20},{20,12},{12,4},{4,0},{1,9},{9... | collective-permute-start | bytes 344072 | tf_op jit(solution)/shard_map/ppermute | solution.py:358
  112.4 0.5 collective-permute-start.48
  113.0 2.4 %write_update.7.refs_4_ = bf16[1024,7168]{1,0:T(8,128)(2,1)} custom-call(s32[1]{0:T(128)} %bitcast.here_ref, bf16[1024,256]{1,0:T(8,128)(2,1)S(1)} %copy-done, bf16[896,128]{1,0:T(8,128)(2,1)S(1)} %collective-permute-done.20.refs_0_, bf16[896,128]{1,0:T(8,128)(2,1)S(1)} %collective-permute-done.42.refs_1_, ...), custom_call_target="tpu_custom_call", output_to_operand_aliasing={{}: (6, {})} | custom-call | flops 939524096 | bytes 3670016 | tf_op jit(solution)/shard_map/write_update/pallas_call | solution.py:327
  115.4 2.4 %write_update.8.refs_4_ = bf16[1024,7168]{1,0:T(8,128)(2,1)} custom-call(s32[1]{0:T(128)} %bitcast.here_ref, bf16[1024,256]{1,0:T(8,128)(2,1)S(1)} %copy-done, bf16[896,128]{1,0:T(8,128)(2,1)S(1)} %collective-permute-done.21.refs_0_, bf16[896,128]{1,0:T(8,128)(2,1)S(1)} %collective-permute-done.43.refs_1_, ...), custom_call_target="tpu_custom_call", output_to_operand_aliasing={{}: (6, {})} | custom-call | flops 939524096 | bytes 3670016 | tf_op jit(solution)/shard_map/write_update/pallas_call | solution.py:327
  117.9 1.7 %write_update.9 = bf16[1024,7168]{1,0:T(8,128)(2,1)} custom-call(s32[1]{0:T(128)} %bitcast.here_ref, bf16[1024,256]{1,0:T(8,128)(2,1)S(1)} %copy-done, bf16[448,128]{1,0:T(8,128)(2,1)S(1)} %collective-permute-done.22.refs_0_, bf16[448,128]{1,0:T(8,128)(2,1)S(1)} %collective-permute-done.44.refs_1_, ...), custom_call_target="tpu_custom_call", output_to_operand_aliasing={{}: (6, {})} | custom-call | flops 469762048 | bytes 1835008 | tf_op jit(solution)/shard_map/write_update/pallas_call | solution.py:327
  (91 shorter events, 15.1 us)
Async XLA Ops:
  0.6 40.2 %slice-start = ((s8[7340032]{0:T(1024)(128)(4,1)}), s8[3145728]{0:T(1024)(128)(4,1)S(1)}, s32[]{:S(2)}) async-start(s8[7340032]{0:T(1024)(128)(4,1)} %bitcast.2), calls=%async_computation | async-start | bytes 6291456
  2.6 22.7 %collective-permute-start = (bf16[128,4096]{1,0:T(8,128)(2,1)S(1)}, bf16[128,4096]{1,0:T(8,128)(2,1)S(1)}, u32[]{:S(2)}, u32[]{:S(2)}) collective-permute-start(bf16[128,4096]{1,0:T(8,128)(2,1)S(1)} %get-tuple-element.28), channel_id=1, source_target_pairs={{0,1},{1,0},{2,3},{3,2},{4,5},{5,4},{6,7},{7,6},{8,9},{9,8},{10,11... | collective-permute-start | bytes 3145736 | tf_op jit(solution)/shard_map/ppermute | solution.py:376
  4.1 6.9 %collective-permute-start.23 = (bf16[512,128]{1,0:T(8,128)(2,1)S(1)}, bf16[512,128]{1,0:T(8,128)(2,1)S(1)}, u32[]{:S(2)}, u32[]{:S(2)}) collective-permute-start(bf16[512,128]{1,0:T(8,128)(2,1)S(1)} %get-tuple-element.34.refs_2_), channel_id=1, source_target_pairs={{0,8},{8,16},{16,24},{24,28},{28,20},{20,12},{12,4},{4,0},{1,9},{9... | collective-permute-start | bytes 393224 | tf_op jit(solution)/shard_map/ppermute | solution.py:358
  6.7 6.4 %collective-permute-start.24 = (bf16[512,128]{1,0:T(8,128)(2,1)S(1)}, bf16[512,128]{1,0:T(8,128)(2,1)S(1)}, u32[]{:S(2)}, u32[]{:S(2)}) collective-permute-start(bf16[512,128]{1,0:T(8,128)(2,1)S(1)} %get-tuple-element.34.refs_2_), channel_id=1, source_target_pairs={{8,0},{16,8},{24,16},{28,24},{20,28},{12,20},{4,12},{0,4},{9,1},{1... | collective-permute-start | bytes 393224 | tf_op jit(solution)/shard_map/ppermute | solution.py:358
  6.7 7.1 %collective-permute-start.1 = (bf16[512,128]{1,0:T(8,128)(2,1)S(1)}, bf16[512,128]{1,0:T(8,128)(2,1)S(1)}, u32[]{:S(2)}, u32[]{:S(2)}) collective-permute-start(bf16[512,128]{1,0:T(8,128)(2,1)S(1)} %get-tuple-element.29.refs_2_), channel_id=1, source_target_pairs={{0,8},{8,16},{16,24},{24,28},{28,20},{20,12},{12,4},{4,0},{1,9},{9... | collective-permute-start | bytes 393224 | tf_op jit(solution)/shard_map/ppermute | solution.py:358
  8.8 7.2 %collective-permute-start.2 = (bf16[512,128]{1,0:T(8,128)(2,1)S(1)}, bf16[512,128]{1,0:T(8,128)(2,1)S(1)}, u32[]{:S(2)}, u32[]{:S(2)}) collective-permute-start(bf16[512,128]{1,0:T(8,128)(2,1)S(1)} %get-tuple-element.29.refs_2_), channel_id=1, source_target_pairs={{8,0},{16,8},{24,16},{28,24},{20,28},{12,20},{4,12},{0,4},{9,1},{1... | collective-permute-start | bytes 393224 | tf_op jit(solution)/shard_map/ppermute | solution.py:358
  11.0 5.7 %collective-permute-start.25 = (bf16[512,128]{1,0:T(8,128)(2,1)S(1)}, bf16[512,128]{1,0:T(8,128)(2,1)S(1)}, u32[]{:S(2)}, u32[]{:S(2)}) collective-permute-start(bf16[512,128]{1,0:T(8,128)(2,1)S(1)} %collective-permute-done.23.refs_3_), channel_id=1, source_target_pairs={{0,8},{8,16},{16,24},{24,28},{28,20},{20,12},{12,4},{4,0},{1,9},{9... | collective-permute-start | bytes 393224 | tf_op jit(solution)/shard_map/ppermute | solution.py:358
  13.1 5.7 %collective-permute-start.26 = (bf16[512,128]{1,0:T(8,128)(2,1)S(1)}, bf16[512,128]{1,0:T(8,128)(2,1)S(1)}, u32[]{:S(2)}, u32[]{:S(2)}) collective-permute-start(bf16[512,128]{1,0:T(8,128)(2,1)S(1)} %collective-permute-done.24.refs_4_), channel_id=1, source_target_pairs={{8,0},{16,8},{24,16},{28,24},{20,28},{12,20},{4,12},{0,4},{9,1},{1... | collective-permute-start | bytes 393224 | tf_op jit(solution)/shard_map/ppermute | solution.py:358
  13.8 6.4 %collective-permute-start.3 = (bf16[512,128]{1,0:T(8,128)(2,1)S(1)}, bf16[512,128]{1,0:T(8,128)(2,1)S(1)}, u32[]{:S(2)}, u32[]{:S(2)}) collective-permute-start(bf16[512,128]{1,0:T(8,128)(2,1)S(1)} %collective-permute-done.1.refs_3_), channel_id=1, source_target_pairs={{0,8},{8,16},{16,24},{24,28},{28,20},{20,12},{12,4},{4,0},{1,9},{9... | collective-permute-start | bytes 393224 | tf_op jit(solution)/shard_map/ppermute | solution.py:358
  15.9 6.4 %collective-permute-start.4 = (bf16[512,128]{1,0:T(8,128)(2,1)S(1)}, bf16[512,128]{1,0:T(8,128)(2,1)S(1)}, u32[]{:S(2)}, u32[]{:S(2)}) collective-permute-start(bf16[512,128]{1,0:T(8,128)(2,1)S(1)} %collective-permute-done.2.refs_4_), channel_id=1, source_target_pairs={{8,0},{16,8},{24,16},{28,24},{20,28},{12,20},{4,12},{0,4},{9,1},{1... | collective-permute-start | bytes 393224 | tf_op jit(solution)/shard_map/ppermute | solution.py:358
  16.7 6.4 %collective-permute-start.27 = (bf16[512,128]{1,0:T(8,128)(2,1)S(1)}, bf16[512,128]{1,0:T(8,128)(2,1)S(1)}, u32[]{:S(2)}, u32[]{:S(2)}) collective-permute-start(bf16[512,128]{1,0:T(8,128)(2,1)S(1)} %collective-permute-done.25.refs_5_), channel_id=1, source_target_pairs={{0,8},{8,16},{16,24},{24,28},{28,20},{20,12},{12,4},{4,0},{1,9},{9... | collective-permute-start | bytes 393224 | tf_op jit(solution)/shard_map/ppermute | solution.py:358
  18.8 6.4 %collective-permute-start.28 = (bf16[512,128]{1,0:T(8,128)(2,1)S(1)}, bf16[512,128]{1,0:T(8,128)(2,1)S(1)}, u32[]{:S(2)}, u32[]{:S(2)}) collective-permute-start(bf16[512,128]{1,0:T(8,128)(2,1)S(1)} %collective-permute-done.26.refs_6_), channel_id=1, source_target_pairs={{8,0},{16,8},{24,16},{28,24},{20,28},{12,20},{4,12},{0,4},{9,1},{1... | collective-permute-start | bytes 393224 | tf_op jit(solution)/shard_map/ppermute | solution.py:358
  20.2 9.6 %collective-permute-start.5 = (bf16[512,128]{1,0:T(8,128)(2,1)S(1)}, bf16[512,128]{1,0:T(8,128)(2,1)S(1)}, u32[]{:S(2)}, u32[]{:S(2)}) collective-permute-start(bf16[512,128]{1,0:T(8,128)(2,1)S(1)} %collective-permute-done.3.refs_5_), channel_id=1, source_target_pairs={{0,8},{8,16},{16,24},{24,28},{28,20},{20,12},{12,4},{4,0},{1,9},{9... | collective-permute-start | bytes 393224 | tf_op jit(solution)/shard_map/ppermute | solution.py:358
  22.3 9.2 %collective-permute-start.6 = (bf16[512,128]{1,0:T(8,128)(2,1)S(1)}, bf16[512,128]{1,0:T(8,128)(2,1)S(1)}, u32[]{:S(2)}, u32[]{:S(2)}) collective-permute-start(bf16[512,128]{1,0:T(8,128)(2,1)S(1)} %collective-permute-done.4.refs_6_), channel_id=1, source_target_pairs={{8,0},{16,8},{24,16},{28,24},{20,28},{12,20},{4,12},{0,4},{9,1},{1... | collective-permute-start | bytes 393224 | tf_op jit(solution)/shard_map/ppermute | solution.py:358
  23.1 4.3 %collective-permute-start.29 = (bf16[256,128]{1,0:T(8,128)(2,1)S(1)}, bf16[256,128]{1,0:T(8,128)(2,1)S(1)}, u32[]{:S(2)}, u32[]{:S(2)}) collective-permute-start(bf16[256,128]{1,0:T(8,128)(2,1)S(1)} %slice.35), channel_id=1, source_target_pairs={{0,8},{8,16},{16,24},{24,28},{28,20},{20,12},{12,4},{4,0},{1,9},{9... | collective-permute-start | bytes 196616 | tf_op jit(solution)/shard_map/ppermute | solution.py:358
  25.2 4.3 %collective-permute-start.30 = (bf16[256,128]{1,0:T(8,128)(2,1)S(1)}, bf16[256,128]{1,0:T(8,128)(2,1)S(1)}, u32[]{:S(2)}, u32[]{:S(2)}) collective-permute-start(bf16[256,128]{1,0:T(8,128)(2,1)S(1)} %slice.36), channel_id=1, source_target_pairs={{8,0},{16,8},{24,16},{28,24},{20,28},{12,20},{4,12},{0,4},{9,1},{1... | collective-permute-start | bytes 196616 | tf_op jit(solution)/shard_map/ppermute | solution.py:358
  25.9 14.9 %slice-start.1 = ((s8[7340032]{0:T(1024)(128)(4,1)}), s8[4194304]{0:T(1024)(128)(4,1)S(1)}, s32[]{:S(2)}) async-start(s8[7340032]{0:T(1024)(128)(4,1)} %bitcast.2), calls=%async_computation.1 | async-start | bytes 8388608
  29.8 6.4 %collective-permute-start.31 = (f32[256,128]{1,0:T(8,128)S(1)}, f32[256,128]{1,0:T(8,128)S(1)}, u32[]{:S(2)}, u32[]{:S(2)}) collective-permute-start(f32[256,128]{1,0:T(8,128)S(1)} %add_coords.7), channel_id=1, source_target_pairs={{0,1},{1,0},{2,3},{3,2},{4,5},{5,4},{6,7},{7,6},{8,9},{9,8},{10,11... | collective-permute-start | bytes 393224 | tf_op jit(solution)/shard_map/ppermute | solution.py:393
  29.9 4.5 %collective-permute-start.7 = (bf16[256,128]{1,0:T(8,128)(2,1)S(1)}, bf16[256,128]{1,0:T(8,128)(2,1)S(1)}, u32[]{:S(2)}, u32[]{:S(2)}) collective-permute-start(bf16[256,128]{1,0:T(8,128)(2,1)S(1)} %slice.32), channel_id=1, source_target_pairs={{0,8},{8,16},{16,24},{24,28},{28,20},{20,12},{12,4},{4,0},{1,9},{9... | collective-permute-start | bytes 196616 | tf_op jit(solution)/shard_map/ppermute | solution.py:358
  31.5 4.3 %collective-permute-start.8 = (bf16[256,128]{1,0:T(8,128)(2,1)S(1)}, bf16[256,128]{1,0:T(8,128)(2,1)S(1)}, u32[]{:S(2)}, u32[]{:S(2)}) collective-permute-start(bf16[256,128]{1,0:T(8,128)(2,1)S(1)} %slice.33), channel_id=1, source_target_pairs={{8,0},{16,8},{24,16},{28,24},{20,28},{12,20},{4,12},{0,4},{9,1},{1... | collective-permute-start | bytes 196616 | tf_op jit(solution)/shard_map/ppermute | solution.py:358
  36.0 1.7 %collective-permute-start.9 = (f32[256,128]{1,0:T(8,128)S(1)}, f32[256,128]{1,0:T(8,128)S(1)}, u32[]{:S(2)}, u32[]{:S(2)}) collective-permute-start(f32[256,128]{1,0:T(8,128)S(1)} %add_coords.5), channel_id=1, source_target_pairs={{0,1},{1,0},{2,3},{3,2},{4,5},{5,4},{6,7},{7,6},{8,9},{9,8},{10,11... | collective-permute-start | bytes 393224 | tf_op jit(solution)/shard_map/ppermute | solution.py:393
  36.1 4.6 %collective-permute-start.32 = (bf16[256,128]{1,0:T(8,128)(2,1)S(1)}, bf16[256,128]{1,0:T(8,128)(2,1)S(1)}, u32[]{:S(2)}, u32[]{:S(2)}) collective-permute-start(bf16[256,128]{1,0:T(8,128)(2,1)S(1)} %add_convert_fusion.refs_0_), channel_id=1, source_target_pairs={{0,2},{1,3},{2,0},{3,1},{4,6},{5,7},{6,4},{7,5},{8,10},{9,11},{10,... | collective-permute-start | bytes 196616 | tf_op jit(solution)/shard_map/ppermute | solution.py:395
  37.7 5.7 %collective-permute-start.10 = (bf16[256,128]{1,0:T(8,128)(2,1)S(1)}, bf16[256,128]{1,0:T(8,128)(2,1)S(1)}, u32[]{:S(2)}, u32[]{:S(2)}) collective-permute-start(bf16[256,128]{1,0:T(8,128)(2,1)S(1)} %add_convert_fusion.1.refs_0_), channel_id=1, source_target_pairs={{0,2},{1,3},{2,0},{3,1},{4,6},{5,7},{6,4},{7,5},{8,10},{9,11},{10,... | collective-permute-start | bytes 196616 | tf_op jit(solution)/shard_map/ppermute | solution.py:395
  41.3 5.5 %collective-permute-start.37 = (bf16[448,128]{1,0:T(8,128)(2,1)S(1)}, bf16[448,128]{1,0:T(8,128)(2,1)S(1)}, u32[]{:S(2)}, u32[]{:S(2)}) collective-permute-start(bf16[448,128]{1,0:T(8,128)(2,1)S(1)} %get-tuple-element.37), channel_id=1, source_target_pairs={{8,0},{16,8},{24,16},{28,24},{20,28},{12,20},{4,12},{0,4},{9,1},{1... | collective-permute-start | bytes 344072 | tf_op jit(solution)/shard_map/ppermute | solution.py:358
  41.8 6.0 %collective-permute-start.33 = (bf16[448,128]{1,0:T(8,128)(2,1)S(1)}, bf16[448,128]{1,0:T(8,128)(2,1)S(1)}, u32[]{:S(2)}, u32[]{:S(2)}) collective-permute-start(bf16[448,128]{1,0:T(8,128)(2,1)S(1)} %get-tuple-element.36), channel_id=1, source_target_pairs={{0,8},{8,16},{16,24},{24,28},{28,20},{20,12},{12,4},{4,0},{1,9},{9... | collective-permute-start | bytes 344072 | tf_op jit(solution)/shard_map/ppermute | solution.py:358
  43.9 6.0 %collective-permute-start.15 = (bf16[448,128]{1,0:T(8,128)(2,1)S(1)}, bf16[448,128]{1,0:T(8,128)(2,1)S(1)}, u32[]{:S(2)}, u32[]{:S(2)}) collective-permute-start(bf16[448,128]{1,0:T(8,128)(2,1)S(1)} %get-tuple-element.32), channel_id=1, source_target_pairs={{8,0},{16,8},{24,16},{28,24},{20,28},{12,20},{4,12},{0,4},{9,1},{1... | collective-permute-start | bytes 344072 | tf_op jit(solution)/shard_map/ppermute | solution.py:358
  44.4 6.6 %collective-permute-start.11 = (bf16[448,128]{1,0:T(8,128)(2,1)S(1)}, bf16[448,128]{1,0:T(8,128)(2,1)S(1)}, u32[]{:S(2)}, u32[]{:S(2)}) collective-permute-start(bf16[448,128]{1,0:T(8,128)(2,1)S(1)} %get-tuple-element.31), channel_id=1, source_target_pairs={{0,8},{8,16},{16,24},{24,28},{28,20},{20,12},{12,4},{4,0},{1,9},{9... | collective-permute-start | bytes 344072 | tf_op jit(solution)/shard_map/ppermute | solution.py:358
  47.3 8.5 %collective-permute-start.38 = (bf16[896,128]{1,0:T(8,128)(2,1)S(1)}, bf16[896,128]{1,0:T(8,128)(2,1)S(1)}, u32[]{:S(2)}, u32[]{:S(2)}) collective-permute-start(bf16[896,128]{1,0:T(8,128)(2,1)S(1)} %next_partials.21), channel_id=1, source_target_pairs={{8,0},{16,8},{24,16},{28,24},{20,28},{12,20},{4,12},{0,4},{9,1},{1... | collective-permute-start | bytes 688136 | tf_op jit(solution)/shard_map/ppermute | solution.py:358
  48.3 8.5 %collective-permute-start.34 = (bf16[896,128]{1,0:T(8,128)(2,1)S(1)}, bf16[896,128]{1,0:T(8,128)(2,1)S(1)}, u32[]{:S(2)}, u32[]{:S(2)}) collective-permute-start(bf16[896,128]{1,0:T(8,128)(2,1)S(1)} %next_partials.18), channel_id=1, source_target_pairs={{0,8},{8,16},{16,24},{24,28},{28,20},{20,12},{12,4},{4,0},{1,9},{9... | collective-permute-start | bytes 688136 | tf_op jit(solution)/shard_map/ppermute | solution.py:358
  50.4 10.3 %collective-permute-start.16 = (bf16[896,128]{1,0:T(8,128)(2,1)S(1)}, bf16[896,128]{1,0:T(8,128)(2,1)S(1)}, u32[]{:S(2)}, u32[]{:S(2)}) collective-permute-start(bf16[896,128]{1,0:T(8,128)(2,1)S(1)} %next_partials.15), channel_id=1, source_target_pairs={{8,0},{16,8},{24,16},{28,24},{20,28},{12,20},{4,12},{0,4},{9,1},{1... | collective-permute-start | bytes 688136 | tf_op jit(solution)/shard_map/ppermute | solution.py:358
  51.5 10.3 %collective-permute-start.12 = (bf16[896,128]{1,0:T(8,128)(2,1)S(1)}, bf16[896,128]{1,0:T(8,128)(2,1)S(1)}, u32[]{:S(2)}, u32[]{:S(2)}) collective-permute-start(bf16[896,128]{1,0:T(8,128)(2,1)S(1)} %next_partials.12), channel_id=1, source_target_pairs={{0,8},{8,16},{16,24},{24,28},{28,20},{20,12},{12,4},{4,0},{1,9},{9... | collective-permute-start | bytes 688136 | tf_op jit(solution)/shard_map/ppermute | solution.py:358
  56.3 9.4 %collective-permute-start.39 = (bf16[896,128]{1,0:T(8,128)(2,1)S(1)}, bf16[896,128]{1,0:T(8,128)(2,1)S(1)}, u32[]{:S(2)}, u32[]{:S(2)}) collective-permute-start(bf16[896,128]{1,0:T(8,128)(2,1)S(1)} %next_partials.22), channel_id=1, source_target_pairs={{8,0},{16,8},{24,16},{28,24},{20,28},{12,20},{4,12},{0,4},{9,1},{1... | collective-permute-start | bytes 688136 | tf_op jit(solution)/shard_map/ppermute | solution.py:358
  57.3 9.4 %collective-permute-start.35 = (bf16[896,128]{1,0:T(8,128)(2,1)S(1)}, bf16[896,128]{1,0:T(8,128)(2,1)S(1)}, u32[]{:S(2)}, u32[]{:S(2)}) collective-permute-start(bf16[896,128]{1,0:T(8,128)(2,1)S(1)} %next_partials.19), channel_id=1, source_target_pairs={{0,8},{8,16},{16,24},{24,28},{28,20},{20,12},{12,4},{4,0},{1,9},{9... | collective-permute-start | bytes 688136 | tf_op jit(solution)/shard_map/ppermute | solution.py:358
  61.2 9.4 %collective-permute-start.17 = (bf16[896,128]{1,0:T(8,128)(2,1)S(1)}, bf16[896,128]{1,0:T(8,128)(2,1)S(1)}, u32[]{:S(2)}, u32[]{:S(2)}) collective-permute-start(bf16[896,128]{1,0:T(8,128)(2,1)S(1)} %next_partials.16), channel_id=1, source_target_pairs={{8,0},{16,8},{24,16},{28,24},{20,28},{12,20},{4,12},{0,4},{9,1},{1... | collective-permute-start | bytes 688136 | tf_op jit(solution)/shard_map/ppermute | solution.py:358
  62.2 14.3 %copy-start.1 = (f32[896,256]{1,0:T(8,128)S(1)}, f32[896,256]{1,0:T(8,128)}, u32[]{:S(2)}) copy-start(f32[896,256]{1,0:T(8,128)} %refs_2_.1) | copy-start | bytes 2752516
  62.2 14.3 %copy-start.2 = (f32[896,256]{1,0:T(8,128)S(1)}, f32[896,256]{1,0:T(8,128)}, u32[]{:S(2)}) copy-start(f32[896,256]{1,0:T(8,128)} %refs_3_.1) | copy-start | bytes 2752516
  62.2 9.3 %collective-permute-start.13 = (bf16[896,128]{1,0:T(8,128)(2,1)S(1)}, bf16[896,128]{1,0:T(8,128)(2,1)S(1)}, u32[]{:S(2)}, u32[]{:S(2)}) collective-permute-start(bf16[896,128]{1,0:T(8,128)(2,1)S(1)} %next_partials.13), channel_id=1, source_target_pairs={{0,8},{8,16},{16,24},{24,28},{28,20},{20,12},{12,4},{4,0},{1,9},{9... | collective-permute-start | bytes 688136 | tf_op jit(solution)/shard_map/ppermute | solution.py:358
  66.1 9.4 %collective-permute-start.40 = (bf16[896,128]{1,0:T(8,128)(2,1)S(1)}, bf16[896,128]{1,0:T(8,128)(2,1)S(1)}, u32[]{:S(2)}, u32[]{:S(2)}) collective-permute-start(bf16[896,128]{1,0:T(8,128)(2,1)S(1)} %next_partials.23), channel_id=1, source_target_pairs={{8,0},{16,8},{24,16},{28,24},{20,28},{12,20},{4,12},{0,4},{9,1},{1... | collective-permute-start | bytes 688136 | tf_op jit(solution)/shard_map/ppermute | solution.py:358
  67.1 9.4 %collective-permute-start.36 = (bf16[896,128]{1,0:T(8,128)(2,1)S(1)}, bf16[896,128]{1,0:T(8,128)(2,1)S(1)}, u32[]{:S(2)}, u32[]{:S(2)}) collective-permute-start(bf16[896,128]{1,0:T(8,128)(2,1)S(1)} %next_partials.20), channel_id=1, source_target_pairs={{0,8},{8,16},{16,24},{24,28},{28,20},{20,12},{12,4},{4,0},{1,9},{9... | collective-permute-start | bytes 688136 | tf_op jit(solution)/shard_map/ppermute | solution.py:358
  71.0 33.4 %copy-start = (bf16[1024,256]{1,0:T(8,128)(2,1)S(1)}, bf16[1024,256]{1,0:T(8,128)(2,1)}, u32[]{:S(2)}) copy-start(bf16[1024,256]{1,0:T(8,128)(2,1)} %base.4) | copy-start | bytes 1572868
  71.0 9.4 %collective-permute-start.18 = (bf16[896,128]{1,0:T(8,128)(2,1)S(1)}, bf16[896,128]{1,0:T(8,128)(2,1)S(1)}, u32[]{:S(2)}, u32[]{:S(2)}) collective-permute-start(bf16[896,128]{1,0:T(8,128)(2,1)S(1)} %next_partials.17), channel_id=1, source_target_pairs={{8,0},{16,8},{24,16},{28,24},{20,28},{12,20},{4,12},{0,4},{9,1},{1... | collective-permute-start | bytes 688136 | tf_op jit(solution)/shard_map/ppermute | solution.py:358
  72.1 9.4 %collective-permute-start.14 = (bf16[896,128]{1,0:T(8,128)(2,1)S(1)}, bf16[896,128]{1,0:T(8,128)(2,1)S(1)}, u32[]{:S(2)}, u32[]{:S(2)}) collective-permute-start(bf16[896,128]{1,0:T(8,128)(2,1)S(1)} %next_partials.14), channel_id=1, source_target_pairs={{0,8},{8,16},{16,24},{24,28},{28,20},{20,12},{12,4},{4,0},{1,9},{9... | collective-permute-start | bytes 688136 | tf_op jit(solution)/shard_map/ppermute | solution.py:358
  77.2 9.2 %collective-permute-start.41 = (bf16[896,128]{1,0:T(8,128)(2,1)S(1)}, bf16[896,128]{1,0:T(8,128)(2,1)S(1)}, u32[]{:S(2)}, u32[]{:S(2)}) collective-permute-start(bf16[896,128]{1,0:T(8,128)(2,1)S(1)} %get-tuple-element.38.refs_1_), channel_id=1, source_target_pairs={{0,8},{8,16},{16,24},{24,28},{28,20},{20,12},{12,4},{4,0},{1,9},{9... | collective-permute-start | bytes 688136 | tf_op jit(solution)/shard_map/ppermute | solution.py:358
  78.8 9.1 %collective-permute-start.49 = (bf16[896,128]{1,0:T(8,128)(2,1)S(1)}, bf16[896,128]{1,0:T(8,128)(2,1)S(1)}, u32[]{:S(2)}, u32[]{:S(2)}) collective-permute-start(bf16[896,128]{1,0:T(8,128)(2,1)S(1)} %get-tuple-element.38.refs_1_), channel_id=1, source_target_pairs={{8,0},{16,8},{24,16},{28,24},{20,28},{12,20},{4,12},{0,4},{9,1},{1... | collective-permute-start | bytes 688136 | tf_op jit(solution)/shard_map/ppermute | solution.py:358
  82.1 9.2 %collective-permute-start.19 = (bf16[896,128]{1,0:T(8,128)(2,1)S(1)}, bf16[896,128]{1,0:T(8,128)(2,1)S(1)}, u32[]{:S(2)}, u32[]{:S(2)}) collective-permute-start(bf16[896,128]{1,0:T(8,128)(2,1)S(1)} %get-tuple-element.33.refs_0_), channel_id=1, source_target_pairs={{0,8},{8,16},{16,24},{24,28},{28,20},{20,12},{12,4},{4,0},{1,9},{9... | collective-permute-start | bytes 688136 | tf_op jit(solution)/shard_map/ppermute | solution.py:358
  83.7 9.1 %collective-permute-start.45 = (bf16[896,128]{1,0:T(8,128)(2,1)S(1)}, bf16[896,128]{1,0:T(8,128)(2,1)S(1)}, u32[]{:S(2)}, u32[]{:S(2)}) collective-permute-start(bf16[896,128]{1,0:T(8,128)(2,1)S(1)} %get-tuple-element.33.refs_0_), channel_id=1, source_target_pairs={{8,0},{16,8},{24,16},{28,24},{20,28},{12,20},{4,12},{0,4},{9,1},{1... | collective-permute-start | bytes 688136 | tf_op jit(solution)/shard_map/ppermute | solution.py:358
  86.3 9.8 %collective-permute-start.42 = (bf16[896,128]{1,0:T(8,128)(2,1)S(1)}, bf16[896,128]{1,0:T(8,128)(2,1)S(1)}, u32[]{:S(2)}, u32[]{:S(2)}) collective-permute-start(bf16[896,128]{1,0:T(8,128)(2,1)S(1)} %collective-permute-done.41.refs_1_), channel_id=1, source_target_pairs={{0,8},{8,16},{16,24},{24,28},{28,20},{20,12},{12,4},{4,0},{1,9},{9... | collective-permute-start | bytes 688136 | tf_op jit(solution)/shard_map/ppermute | solution.py:358
  87.9 9.8 %collective-permute-start.50 = (bf16[896,128]{1,0:T(8,128)(2,1)S(1)}, bf16[896,128]{1,0:T(8,128)(2,1)S(1)}, u32[]{:S(2)}, u32[]{:S(2)}) collective-permute-start(bf16[896,128]{1,0:T(8,128)(2,1)S(1)} %collective-permute-done.49.refs_3_), channel_id=1, source_target_pairs={{8,0},{16,8},{24,16},{28,24},{20,28},{12,20},{4,12},{0,4},{9,1},{1... | collective-permute-start | bytes 688136 | tf_op jit(solution)/shard_map/ppermute | solution.py:358
  91.2 9.8 %collective-permute-start.20 = (bf16[896,128]{1,0:T(8,128)(2,1)S(1)}, bf16[896,128]{1,0:T(8,128)(2,1)S(1)}, u32[]{:S(2)}, u32[]{:S(2)}) collective-permute-start(bf16[896,128]{1,0:T(8,128)(2,1)S(1)} %collective-permute-done.19.refs_0_), channel_id=1, source_target_pairs={{0,8},{8,16},{16,24},{24,28},{28,20},{20,12},{12,4},{4,0},{1,9},{9... | collective-permute-start | bytes 688136 | tf_op jit(solution)/shard_map/ppermute | solution.py:358
  92.8 9.8 %collective-permute-start.46 = (bf16[896,128]{1,0:T(8,128)(2,1)S(1)}, bf16[896,128]{1,0:T(8,128)(2,1)S(1)}, u32[]{:S(2)}, u32[]{:S(2)}) collective-permute-start(bf16[896,128]{1,0:T(8,128)(2,1)S(1)} %collective-permute-done.45.refs_2_), channel_id=1, source_target_pairs={{8,0},{16,8},{24,16},{28,24},{20,28},{12,20},{4,12},{0,4},{9,1},{1... | collective-permute-start | bytes 688136 | tf_op jit(solution)/shard_map/ppermute | solution.py:358
  96.2 12.5 %collective-permute-start.43 = (bf16[896,128]{1,0:T(8,128)(2,1)S(1)}, bf16[896,128]{1,0:T(8,128)(2,1)S(1)}, u32[]{:S(2)}, u32[]{:S(2)}) collective-permute-start(bf16[896,128]{1,0:T(8,128)(2,1)S(1)} %collective-permute-done.42.refs_1_), channel_id=1, source_target_pairs={{0,8},{8,16},{16,24},{24,28},{28,20},{20,12},{12,4},{4,0},{1,9},{9... | collective-permute-start | bytes 688136 | tf_op jit(solution)/shard_map/ppermute | solution.py:358
  97.7 12.5 %collective-permute-start.51 = (bf16[896,128]{1,0:T(8,128)(2,1)S(1)}, bf16[896,128]{1,0:T(8,128)(2,1)S(1)}, u32[]{:S(2)}, u32[]{:S(2)}) collective-permute-start(bf16[896,128]{1,0:T(8,128)(2,1)S(1)} %collective-permute-done.50.refs_3_), channel_id=1, source_target_pairs={{8,0},{16,8},{24,16},{28,24},{20,28},{12,20},{4,12},{0,4},{9,1},{1... | collective-permute-start | bytes 688136 | tf_op jit(solution)/shard_map/ppermute | solution.py:358
  101.1 9.7 %collective-permute-start.21 = (bf16[896,128]{1,0:T(8,128)(2,1)S(1)}, bf16[896,128]{1,0:T(8,128)(2,1)S(1)}, u32[]{:S(2)}, u32[]{:S(2)}) collective-permute-start(bf16[896,128]{1,0:T(8,128)(2,1)S(1)} %collective-permute-done.20.refs_0_), channel_id=1, source_target_pairs={{0,8},{8,16},{16,24},{24,28},{28,20},{20,12},{12,4},{4,0},{1,9},{9... | collective-permute-start | bytes 688136 | tf_op jit(solution)/shard_map/ppermute | solution.py:358
  102.6 9.8 %collective-permute-start.47 = (bf16[896,128]{1,0:T(8,128)(2,1)S(1)}, bf16[896,128]{1,0:T(8,128)(2,1)S(1)}, u32[]{:S(2)}, u32[]{:S(2)}) collective-permute-start(bf16[896,128]{1,0:T(8,128)(2,1)S(1)} %collective-permute-done.46.refs_2_), channel_id=1, source_target_pairs={{8,0},{16,8},{24,16},{28,24},{20,28},{12,20},{4,12},{0,4},{9,1},{1... | collective-permute-start | bytes 688136 | tf_op jit(solution)/shard_map/ppermute | solution.py:358
  108.7 9.2 %collective-permute-start.44 = (bf16[448,128]{1,0:T(8,128)(2,1)S(1)}, bf16[448,128]{1,0:T(8,128)(2,1)S(1)}, u32[]{:S(2)}, u32[]{:S(2)}) collective-permute-start(bf16[448,128]{1,0:T(8,128)(2,1)S(1)} %slice.37), channel_id=1, source_target_pairs={{0,8},{8,16},{16,24},{24,28},{28,20},{20,12},{12,4},{4,0},{1,9},{9... | collective-permute-start | bytes 344072 | tf_op jit(solution)/shard_map/ppermute | solution.py:358
  110.3 7.6 %collective-permute-start.52 = (bf16[448,128]{1,0:T(8,128)(2,1)S(1)}, bf16[448,128]{1,0:T(8,128)(2,1)S(1)}, u32[]{:S(2)}, u32[]{:S(2)}) collective-permute-start(bf16[448,128]{1,0:T(8,128)(2,1)S(1)} %slice.39), channel_id=1, source_target_pairs={{8,0},{16,8},{24,16},{28,24},{20,28},{12,20},{4,12},{0,4},{9,1},{1... | collective-permute-start | bytes 344072 | tf_op jit(solution)/shard_map/ppermute | solution.py:358
  110.8 7.0 %collective-permute-start.22 = (bf16[448,128]{1,0:T(8,128)(2,1)S(1)}, bf16[448,128]{1,0:T(8,128)(2,1)S(1)}, u32[]{:S(2)}, u32[]{:S(2)}) collective-permute-start(bf16[448,128]{1,0:T(8,128)(2,1)S(1)} %slice.34), channel_id=1, source_target_pairs={{0,8},{8,16},{16,24},{24,28},{28,20},{20,12},{12,4},{4,0},{1,9},{9... | collective-permute-start | bytes 344072 | tf_op jit(solution)/shard_map/ppermute | solution.py:358
  112.4 5.4 %collective-permute-start.48 = (bf16[448,128]{1,0:T(8,128)(2,1)S(1)}, bf16[448,128]{1,0:T(8,128)(2,1)S(1)}, u32[]{:S(2)}, u32[]{:S(2)}) collective-permute-start(bf16[448,128]{1,0:T(8,128)(2,1)S(1)} %slice.38), channel_id=1, source_target_pairs={{8,0},{16,8},{24,16},{28,24},{20,28},{12,20},{4,12},{0,4},{9,1},{1... | collective-permute-start | bytes 344072 | tf_op jit(solution)/shard_map/ppermute | solution.py:358

commit v5 on v4

--- a/solution.py
+++ b/solution.py
@@ -81,47 +81,52 @@
     return [pltpu.with_memory_space_constraint(a, pltpu.VMEM) for a in arrays]
 
 
-def split_columns(me, activations, n):
+def split_columns(here, me, activations, n):
     tokens, features = activations.shape
-    part = features // n // 2
-    half = pltpu.VMEM((tokens, features // 2), activations.dtype)
-
-    def kernel(me_ref, source, kept, sent, sems):
-        side = lax.bitwise_and(me_ref[0], 1)
+    depth = features // n
+    part = depth // 2
+    near = pltpu.VMEM((tokens, part + (n // 2 - 1) * depth), activations.dtype)
+    far = pltpu.VMEM((tokens, depth), activations.dtype)
+
+    def kernel(here_ref, me_ref, source, kept, sent, farthest, sems):
+        mine = lax.bitwise_and(me_ref[0], 1)
         copies = []
-        for way, (out, which) in enumerate(((sent, 1 - side), (kept, side))):
-            for j in range(n):
-                columns = pl.ds(pl.multiple_of((2 * j + which) * part, 128), part)
-                copies.append(
-                    pltpu.make_async_copy(
-                        source.at[:, columns], out.at[:, pl.ds(j * part, part)], sems.at[way, j]
-                    )
-                )
-        for copy in copies:
-            copy.start()
-        for copy in copies:
-            copy.wait()
-
-    return pl.pallas_call(
-        kernel,
-        out_shape=(half, half),
-        in_specs=[scalars(), pl.BlockSpec(memory_space=pltpu.HBM)],
-        out_specs=(on_chip(),) * 2,
-        scratch_shapes=[pltpu.SemaphoreType.DMA((2, n))],
+
+        def copy(start, size, out, low):
+            columns = pl.ds(pl.multiple_of(start, 128), size)
+            copies.append(
+                pltpu.make_async_copy(source.at[:, columns], out.at[:, pl.ds(low, size)], sems.at[len(copies)])
+            )
+
+        copy(chunk_at(here_ref, n // 2, n) * depth, depth, farthest, 0)
+        for out, side in ((sent, 1 - mine), (kept, mine)):
+            copy(here_ref[0] * depth + side * part, part, out, 0)
+            for k in range(1, n // 2):
+                block = chunk_at(here_ref, lax.select(side == 0, n - k, k), n)
+                copy(block * depth, depth, out, part + (k - 1) * depth)
+        for one in copies:
+            one.start()
+        for one in copies:
+            one.wait()
+
+    return pl.pallas_call(
+        kernel,
+        out_shape=(near, near, far),
+        in_specs=[scalars(), scalars(), pl.BlockSpec(memory_space=pltpu.HBM)],
+        out_specs=(on_chip(),) * 3,
+        scratch_shapes=[pltpu.SemaphoreType.DMA((n + 1,))],
         compiler_params=pltpu.CompilerParams(vmem_limit_bytes=SCRATCH_BYTES),
         name="split_columns",
-    )(me, left_in_hbm(activations))
-
-
-def own_pieces(me, basis):
+    )(here, me, left_in_hbm(activations))
+
+
+def own_pieces(basis):
     depth, rank = basis.shape
-    piece = pltpu.VMEM((depth // 2, rank // STREAMS), basis.dtype)
-
-    def kernel(me_ref, source, *refs):
-        rows = pl.ds(pl.multiple_of(lax.bitwise_and(me_ref[0], 1) * (depth // 2), depth // 2), depth // 2)
-        width = rank // STREAMS
+    width = rank // STREAMS
+
+    def kernel(source, *refs):
         copies = [
-            pltpu.make_async_copy(source.at[rows, pl.ds(s * width, width)], refs[s], refs[-1].at[s])
+            pltpu.make_async_copy(source.at[:, pl.ds(s * width, width)], refs[s], refs[-1].at[s])
             for s in range(STREAMS)
         ]
         for copy in copies:
@@ -131,79 +136,106 @@
 
     return pl.pallas_call(
         kernel,
-        out_shape=(piece,) * STREAMS,
-        in_specs=[scalars(), pl.BlockSpec(memory_space=pltpu.HBM)],
+        out_shape=(pltpu.VMEM((depth, width), basis.dtype),) * STREAMS,
+        in_specs=[pl.BlockSpec(memory_space=pltpu.HBM)],
         out_specs=(on_chip(),) * STREAMS,
         scratch_shapes=[pltpu.SemaphoreType.DMA((STREAMS,))],
         compiler_params=pltpu.CompilerParams(vmem_limit_bytes=SCRATCH_BYTES),
         name="own_pieces",
-    )(me, left_in_hbm(basis))
-
-
-def add_coords(here, me, kept, came, total, pieces, depth, n):
+    )(left_in_hbm(basis))
+
+
+def half_rows(me, block):
+    part = block.shape[0] // 2
+
+    def kernel(me_ref, source, out):
+        out[...] = source[pl.ds(pl.multiple_of(lax.bitwise_and(me_ref[0], 1) * part, part), part)]
+
+    return pl.pallas_call(
+        kernel,
+        out_shape=pltpu.VMEM((part, block.shape[1]), block.dtype),
+        in_specs=[scalars(), on_chip()],
+        out_specs=on_chip(),
+        compiler_params=pltpu.CompilerParams(vmem_limit_bytes=SCRATCH_BYTES),
+        name="half_rows",
+    )(me, *kept_on_chip([block]))
+
+
+def add_coords(me, kept, came, total, pieces):
     tokens, width = kept.shape[0], pieces[0][0].shape[1]
     held = () if total is None else (total,)
     arrays = [piece for piece, _, _ in pieces]
 
-    def kernel(here_ref, me_ref, *refs):
+    def kernel(me_ref, *refs):
         out = refs[-1]
         side = lax.bitwise_and(me_ref[0], 1)
         refs_of = refs[2 + len(held) : -1]
         for act, place in ((refs[0], side), (refs[1], 1 - side)):
             rows = pl.ds(pl.multiple_of(place * tokens, tokens), tokens)
             acc = refs[2][rows] if held else jnp.zeros((tokens, width), jnp.float32)
-            for ref, (_, away, low) in zip(refs_of, pieces, strict=True):
-                start = pl.multiple_of(chunk_at(here_ref, away, n) * depth + low, 128)
-                acc += jnp.dot(
-                    act[:, pl.ds(start, ref.shape[0])], ref[...], preferred_element_type=jnp.float32
-                )
+            for ref, (_, low, size) in zip(refs_of, pieces, strict=True):
+                own = pl.ds(pl.multiple_of(side * size, size), size) if size < ref.shape[0] else slice(None)
+                acc += jnp.dot(act[:, low : low + size], ref[own], preferred_element_type=jnp.float32)
             out[rows] = acc
 
     return pl.pallas_call(
         kernel,
         out_shape=pltpu.VMEM((2 * tokens, width), jnp.float32),
-        in_specs=[scalars(), scalars(), *[on_chip()] * (2 + len(held) + len(arrays))],
+        in_specs=[scalars(), *[on_chip()] * (2 + len(held) + len(arrays))],
         out_specs=on_chip(),
         cost_estimate=pl.CostEstimate(
-            flops=4 * tokens * width * sum(a.shape[0] for a in arrays), transcendentals=0, bytes_accessed=4 << 20
+            flops=4 * tokens * width * sum(size for _, _, size in pieces), transcendentals=0, bytes_accessed=4 << 20
         ),
         compiler_params=pltpu.CompilerParams(vmem_limit_bytes=SCRATCH_BYTES),
         name="add_coords",
-    )(here, me, *kept_on_chip([kept, came, *held, *arrays]))
+    )(me, *kept_on_chip([kept, came, *held, *arrays]))
 
 
 def contract_tokens(grad, coords):
     return lax.dot_general(grad, coords, (((0,), (0,)), ((), ())), preferred_element_type=jnp.float32)
 
 
-def first_partials(here, me, grad_out, parts, n):
-    group, width = parts[0].shape
+def first_partials(here, me, grad_out, sums, fars, lasts, n, m):
+    group, width = sums[0].shape
     tokens, all_columns = grad_out.shape
+    own_tokens = group // 2
     cols = all_columns // n
-    groups = tokens // group
+    part = lasts[0].shape[0]
 
     def kernel(here_ref, me_ref, grad, *refs):
-        coords, top, bottom = refs[len(parts) :]
-        for k, ref in enumerate(refs[: len(parts)]):
-            at = lax.rem(lax.shift_right_logical(me_ref[0], 1) + groups - k, groups)
-            coords[pl.ds(pl.multiple_of(at * group, group), group)] = ref[...]
+        coords, top, bottom = refs[-3:]
+        own_last, other_last = refs[-5:-3]
+        side = lax.bitwise_and(me_ref[0], 1)
+        own_columns = pl.ds(pl.multiple_of(side * part, part), part)
+        other_columns = pl.ds(pl.multiple_of((1 - side) * part, part), part)
+        for k, pair in enumerate(refs[: len(sums)]):
+            first = lax.rem(lax.bitwise_and(me_ref[0], ~1) + m - 2 * k, m)
+            for place, far in zip((side, 1 - side), refs[len(sums) + 2 * k :][:2], strict=True):
+                total = (
+                    pair[pl.ds(pl.multiple_of(place * own_tokens, own_tokens), own_tokens)]
+                    + jnp.dot(far[:, own_columns], own_last[...], preferred_element_type=jnp.float32)
+                    + jnp.dot(far[:, other_columns], other_last[...], preferred_element_type=jnp.float32)
+                )
+                low = pl.multiple_of((first + place) * own_tokens, own_tokens)
+                coords[pl.ds(low, own_tokens)] = total.astype(jnp.bfloat16)
         column = pl.multiple_of(chunk_at(here_ref, n // 2, n) * cols, 128)
-        part = contract_tokens(grad[:, pl.ds(column, cols)], coords[...]).astype(jnp.bfloat16)
-        top[...] = part[: cols // 2]
-        bottom[...] = part[cols // 2 :]
+        sent = contract_tokens(grad[:, pl.ds(column, cols)], coords[...]).astype(jnp.bfloat16)
+        top[...] = sent[: cols // 2]
+        bottom[...] = sent[cols // 2 :]
 
     half = pltpu.VMEM((cols // 2, width), jnp.bfloat16)
+    arrays = [grad_out, *sums, *fars, *lasts]
     return pl.pallas_call(
         kernel,
         out_shape=(pltpu.VMEM((tokens, width), jnp.bfloat16), half, half),
-        in_specs=[scalars(), scalars(), *[on_chip()] * (1 + len(parts))],
+        in_specs=[scalars(), scalars(), *[on_chip()] * len(arrays)],
         out_specs=(on_chip(),) * 3,
         cost_estimate=pl.CostEstimate(
-            flops=2 * tokens * cols * width, transcendentals=0, bytes_accessed=4 << 20
+            flops=2 * tokens * (cols + 2 * part) * width, transcendentals=0, bytes_accessed=4 << 20
         ),
         compiler_params=pltpu.CompilerParams(vmem_limit_bytes=SCRATCH_BYTES),
         name="first_partials",
-    )(here, me, *kept_on_chip([grad_out, *parts]))
+    )(here, me, *kept_on_chip(arrays))
 
 
 def next_partials(here, grad_out, coords, came, n, away, upward):
@@ -368,35 +400,36 @@
     half = n // 2
     streams = range(STREAMS)
 
+    apart = [
+        (a * m + k, b * m + k) for k in range(m) for a, b in (downward if k % 2 else upward)
+    ]
     part = depth // 2
-    own = own_pieces(me, basis)
-    ups, downs = list(own), list(own)
-    pieces = [[(own[s], 0, 0)] for s in streams]
-    kept, sent = split_columns(me, activations, n)
+    passing = list(own_pieces(basis))
+    pieces = [[(passing[s], 0, part)] for s in streams]
+    kept, sent, far = split_columns(here, me, activations, n)
     swapped = lax.ppermute(sent, "mp", partners)
+    fars = [far, lax.ppermute(far, "mp", partners)]
+    for k in range(2, m, 2):
+        far = lax.ppermute(fars[0], "mp", [(a, (a + k) % m) for a in range(m)])
+        fars += [far, lax.ppermute(far, "mp", partners)]
     total = [None] * STREAMS
-    for k in range(1, half + 1):
+    for k in range(1, half):
         for s in streams:
-            low = 0
-            if k == half:
-                low = part // 2
-                ups[s], downs[s] = ups[s][:low], downs[s][low:]
-                total[s] = add_coords(here, me, kept, swapped, None, pieces[s], part, n)
+            if k == half - 1:
+                total[s] = add_coords(me, kept, swapped, None, pieces[s])
                 pieces[s] = []
-            ups[s], downs[s] = hop(ups[s], downs[s])
-            pieces[s] += [(ups[s], n - k, 0), (downs[s], k, low)]
+            passing[s] = lax.ppermute(passing[s], ("dp", "mp"), apart)
+            pieces[s].append((passing[s], part + (k - 1) * depth, depth))
+
+    coords, ups, downs = [None] * STREAMS, [None] * STREAMS, [None] * STREAMS
     for s in streams:
-        total[s] = add_coords(here, me, kept, swapped, total[s], pieces[s], part, n)
-
-    parts = [None] * STREAMS
-    for s in streams:
-        other = lax.ppermute(total[s], "mp", partners)
-        pair = (total[s] + other).astype(jnp.bfloat16)
-        parts[s] = [pair] + [lax.ppermute(pair, "mp", [(a, (a + k) % m) for a in range(m)]) for k in range(2, m, 2)]
-
-    coords = [None] * STREAMS
-    for s in streams:
-        coords[s], ups[s], downs[s] = first_partials(here, me, grad_out, parts[s], n)
+        near = add_coords(me, kept, swapped, total[s], pieces[s])
+        sums = [near + lax.ppermute(near, "mp", partners)]
+        sums += [lax.ppermute(sums[0], "mp", [(a, (a + k) % m) for a in range(m)]) for k in range(2, m, 2)]
+        last = half_rows(me, passing[s])
+        last = lax.ppermute(last, ("dp", "mp"), apart)
+        lasts = [last, lax.ppermute(last, "mp", partners)]
+        coords[s], ups[s], downs[s] = first_partials(here, me, grad_out, sums, fars, lasts, n, m)
         ups[s], downs[s] = hop(ups[s], downs[s])
     for k in range(2, half + 1):
         for s in streams:
@@ -427,7 +460,7 @@
 
 def solution(mesh):
     n, m = mesh.shape["dp"], mesh.shape["mp"]
-    ring = 4 <= n <= LONGEST_RING and n % 2 == 0 and m % 2 == 0
+    ring = 6 <= n <= LONGEST_RING and n % 2 == 0 and m % 2 == 0
     placed = (
         P(("dp", "mp"), None),
         P("dp", "mp"),

time: 120 us -> 118 us (0.983)
  waiting for transfers between devices: 39.4 us -> 37.1 us
    ppermute x24 -> x16, starting transfers between devices: 42.3 us -> 7.49 us  [hop(): lax.ppermute(to_up, 'dp', upward)]
    ppermute x24 -> x16, starting transfers between devices: 8.59 us -> 26.1 us  [hop(): lax.ppermute(to_down, 'dp', downward)]
    ppermute x4 -> x17, starting transfers between devices: 3 us -> 20.2 us  [the longest x6 12 us: on_ring(): passing[s] = lax.ppermute(passing[s], ('dp', 'mp'), apart)]
    ppermute x4 -> x17, waiting for transfers between devices: 1.78 us -> 11.9 us  [the longest x6 6.16 us: on_ring(): passing[s] = lax.ppermute(passing[s], ('dp', 'mp'), apart)]
    ppermute x24 -> x16, waiting for transfers between devices: 22.3 us -> 15.4 us  [hop(): lax.ppermute(to_up, 'dp', upward)]
    ppermute x24 -> x16, waiting for transfers between devices: 15.4 us -> 9.8 us  [hop(): lax.ppermute(to_down, 'dp', downward)]
    pallas_call x2 -> x4, Pallas kernels: 2.88 us -> 2.84 us  [the longest x1 1.77 us: split_columns(): pl.pallas_call(kernel, out_shape=(near, near, far), in_specs=[scalars(),...]
  transfers between devices with their start and end apart: 53 -> 50, of which waited for: 23 -> 22; matrix products, arithmetic and copies ran while one was open for 0% -> 0% of each run, Pallas kernels for 18% -> 18%
where the time goes in v5:
time: 118 us
  starting transfers between devices  54.4 us (46%)
  waiting for transfers between devices  37.1 us (31%)
  Pallas kernels  25.1 us (21%)
    ppermute x16, starting transfers between devices, hop(): lax.ppermute(to_down, 'dp', downward)  26.1 us
    ppermute x16, waiting for transfers between devices, hop(): lax.ppermute(to_up, 'dp', upward)  15.4 us
    ppermute x6, starting transfers between devices, on_ring(): passing[s] = lax.ppermute(passing[s], ('dp', 'mp'), apart)  12 us
    pallas_call x5, Pallas kernels, write_update(): pl.pallas_call(kernel, out_shape=jax.ShapeDtypeStruct((depth, all_columns...  10.7 us
    ppermute x16, waiting for transfers between devices, hop(): lax.ppermute(to_down, 'dp', downward)  9.8 us
    ppermute x16, starting transfers between devices, hop(): lax.ppermute(to_up, 'dp', upward)  7.49 us
    ppermute x6, waiting for transfers between devices, on_ring(): passing[s] = lax.ppermute(passing[s], ('dp', 'mp'), apart)  6.16 us
    pallas_call x12, Pallas kernels, next_partials(): pl.pallas_call(kernel, out_shape=pltpu.VMEM((cols, width), jnp.bfloat16),...  5.68 us
  transfers between devices with their start and end apart: 50, of which 22 were waited for; matrix products, arithmetic and copies ran while one was open for 0% of the time, Pallas kernels for 18%

profile of v5, /device:TPU:0, one launch (start us, length us, event | category | flops | bytes accessed | tf_op | source)
XLA Modules:
  0.0 117.8 jit_solution(3779857832098605615)
XLA Ops:
  0.6 1.8 %split_columns.1 = (bf16[128,3584]{1,0:T(8,128)(2,1)S(1)}, bf16[128,3584]{1,0:T(8,128)(2,1)S(1)}, bf16[128,1024]{1,0:T(8,128)(2,1)S(1)}) custom-call(s32[1]{0:T(128)} %bitcast.here_ref, s32[1]{0:T(128)} %bitcast.1.me_ref, bf16[128,8192]{1,0:T(8,128)(2,1)} %source), custom_call_target="tpu_custom_call" | custom-call | tf_op jit(solution)/shard_map/split_columns/pallas_call | solution.py:112
  2.4 0.6 collective-permute-start
  3.0 1.0 own_pieces.1
  4.0 2.6 %collective-permute-start.23 = (bf16[1024,128]{1,0:T(8,128)(2,1)S(1)}, bf16[1024,128]{1,0:T(8,128)(2,1)S(1)}, u32[]{:S(2)}, u32[]{:S(2)}) collective-permute-start(bf16[1024,128]{1,0:T(8,128)(2,1)S(1)} %get-tuple-element.36.refs_2_), channel_id=1, source_target_pairs={{0,8},{8,16},{16,24},{24,28},{28,20},{20,12},{12,4},{4,0},{9,1},{1... | collective-permute-start | bytes 786440 | tf_op jit(solution)/shard_map/ppermute | solution.py:421
  6.7 1.6 %collective-permute-start.1 = (bf16[1024,128]{1,0:T(8,128)(2,1)S(1)}, bf16[1024,128]{1,0:T(8,128)(2,1)S(1)}, u32[]{:S(2)}, u32[]{:S(2)}) collective-permute-start(bf16[1024,128]{1,0:T(8,128)(2,1)S(1)} %get-tuple-element.30.refs_2_), channel_id=1, source_target_pairs={{0,8},{8,16},{16,24},{24,28},{28,20},{20,12},{12,4},{4,0},{9,1},{1... | collective-permute-start | bytes 786440 | tf_op jit(solution)/shard_map/ppermute | solution.py:421
  8.2 2.7 %collective-permute-done.23.refs_3_ = bf16[1024,128]{1,0:T(8,128)(2,1)S(1)} collective-permute-done((bf16[1024,128]{1,0:T(8,128)(2,1)S(1)}, bf16[1024,128]{1,0:T(8,128)(2,1)S(1)}, u32[]{:S(2)}, u32[]{:S(2)}) %collective-permute-start.23) | collective-permute-done | bytes 262176 | tf_op jit(solution)/shard_map/ppermute | solution.py:421
  11.0 2.1 %collective-permute-start.24 = (bf16[1024,128]{1,0:T(8,128)(2,1)S(1)}, bf16[1024,128]{1,0:T(8,128)(2,1)S(1)}, u32[]{:S(2)}, u32[]{:S(2)}) collective-permute-start(bf16[1024,128]{1,0:T(8,128)(2,1)S(1)} %collective-permute-done.23.refs_3_), channel_id=1, source_target_pairs={{0,8},{8,16},{16,24},{24,28},{28,20},{20,12},{12,4},{4,0},{9,1},{1... | collective-permute-start | bytes 786440 | tf_op jit(solution)/shard_map/ppermute | solution.py:421
  13.0 0.7 collective-permute-done.1.refs_3_
  13.8 2.1 %collective-permute-start.2 = (bf16[1024,128]{1,0:T(8,128)(2,1)S(1)}, bf16[1024,128]{1,0:T(8,128)(2,1)S(1)}, u32[]{:S(2)}, u32[]{:S(2)}) collective-permute-start(bf16[1024,128]{1,0:T(8,128)(2,1)S(1)} %collective-permute-done.1.refs_3_), channel_id=1, source_target_pairs={{0,8},{8,16},{16,24},{24,28},{28,20},{20,12},{12,4},{4,0},{9,1},{1... | collective-permute-start | bytes 786440 | tf_op jit(solution)/shard_map/ppermute | solution.py:421
  15.9 1.5 %collective-permute-done.24.refs_4_ = bf16[1024,128]{1,0:T(8,128)(2,1)S(1)} collective-permute-done((bf16[1024,128]{1,0:T(8,128)(2,1)S(1)}, bf16[1024,128]{1,0:T(8,128)(2,1)S(1)}, u32[]{:S(2)}, u32[]{:S(2)}) %collective-permute-start.24) | collective-permute-done | bytes 262176 | tf_op jit(solution)/shard_map/ppermute | solution.py:421
  17.3 2.1 %collective-permute-start.25 = (bf16[1024,128]{1,0:T(8,128)(2,1)S(1)}, bf16[1024,128]{1,0:T(8,128)(2,1)S(1)}, u32[]{:S(2)}, u32[]{:S(2)}) collective-permute-start(bf16[1024,128]{1,0:T(8,128)(2,1)S(1)} %collective-permute-done.24.refs_4_), channel_id=1, source_target_pairs={{0,8},{8,16},{16,24},{24,28},{28,20},{20,12},{12,4},{4,0},{9,1},{1... | collective-permute-start | bytes 786440 | tf_op jit(solution)/shard_map/ppermute | solution.py:421
  19.4 1.5 %collective-permute-start.7 = (bf16[128,1024]{1,0:T(8,128)(2,1)S(1)}, bf16[128,1024]{1,0:T(8,128)(2,1)S(1)}, u32[]{:S(2)}, u32[]{:S(2)}) collective-permute-start(bf16[128,1024]{1,0:T(8,128)(2,1)S(1)} %get-tuple-element.31.refs_2_), channel_id=1, source_target_pairs={{0,2},{1,3},{2,0},{3,1},{4,6},{5,7},{6,4},{7,5},{8,10},{9,11},{10,... | collective-permute-start | bytes 786440 | tf_op jit(solution)/shard_map/ppermute | solution.py:413
  20.9 1.6 %collective-permute-start.3 = (bf16[1024,128]{1,0:T(8,128)(2,1)S(1)}, bf16[1024,128]{1,0:T(8,128)(2,1)S(1)}, u32[]{:S(2)}, u32[]{:S(2)}) collective-permute-start(bf16[1024,128]{1,0:T(8,128)(2,1)S(1)} %collective-permute-done.2.refs_4_), channel_id=1, source_target_pairs={{0,8},{8,16},{16,24},{24,28},{28,20},{20,12},{12,4},{4,0},{9,1},{1... | collective-permute-start | bytes 786440 | tf_op jit(solution)/shard_map/ppermute | solution.py:421
  22.5 1.2 %collective-permute-done.25.refs_3_.source = bf16[1024,128]{1,0:T(8,128)(2,1)S(1)} collective-permute-done((bf16[1024,128]{1,0:T(8,128)(2,1)S(1)}, bf16[1024,128]{1,0:T(8,128)(2,1)S(1)}, u32[]{:S(2)}, u32[]{:S(2)}) %collective-permute-start.25) | collective-permute-done | bytes 262176 | tf_op jit(solution)/shard_map/ppermute | solution.py:421
  23.7 2.1 %collective-permute-start.28 = (bf16[512,128]{1,0:T(8,128)(2,1)S(1)}, bf16[512,128]{1,0:T(8,128)(2,1)S(1)}, u32[]{:S(2)}, u32[]{:S(2)}) collective-permute-start(bf16[512,128]{1,0:T(8,128)(2,1)S(1)} %half_rows.3), channel_id=1, source_target_pairs={{0,8},{8,16},{16,24},{24,28},{28,20},{20,12},{12,4},{4,0},{9,1},{1... | collective-permute-start | bytes 393224 | tf_op jit(solution)/shard_map/ppermute | solution.py:430
  26.4 0.5 add_coords.6.refs_2_
  27.6 1.4 %collective-permute-start.9 = (bf16[512,128]{1,0:T(8,128)(2,1)S(1)}, bf16[512,128]{1,0:T(8,128)(2,1)S(1)}, u32[]{:S(2)}, u32[]{:S(2)}) collective-permute-start(bf16[512,128]{1,0:T(8,128)(2,1)S(1)} %half_rows.2), channel_id=1, source_target_pairs={{0,8},{8,16},{16,24},{24,28},{28,20},{20,12},{12,4},{4,0},{9,1},{1... | collective-permute-start | bytes 393224 | tf_op jit(solution)/shard_map/ppermute | solution.py:430
  28.9 0.5 add_coords.4.refs_2_
  30.3 2.3 %collective-permute-done.9.refs_6_ = bf16[512,128]{1,0:T(8,128)(2,1)S(1)} collective-permute-done((bf16[512,128]{1,0:T(8,128)(2,1)S(1)}, bf16[512,128]{1,0:T(8,128)(2,1)S(1)}, u32[]{:S(2)}, u32[]{:S(2)}) %collective-permute-start.9) | collective-permute-done | bytes 131104 | tf_op jit(solution)/shard_map/ppermute | solution.py:430
  32.6 1.5 %collective-permute-start.27 = (f32[256,128]{1,0:T(8,128)S(1)}, f32[256,128]{1,0:T(8,128)S(1)}, u32[]{:S(2)}, u32[]{:S(2)}) collective-permute-start(f32[256,128]{1,0:T(8,128)S(1)} %add.7.refs_0_), channel_id=1, source_target_pairs={{0,2},{1,3},{2,0},{3,1},{4,6},{5,7},{6,4},{7,5},{8,10},{9,11},{10,... | collective-permute-start | bytes 393224 | tf_op jit(solution)/shard_map/ppermute | solution.py:428
  34.1 0.6 collective-permute-start.5
  34.7 3.1 %collective-permute-done.27.refs_1_ = f32[256,128]{1,0:T(8,128)S(1)} collective-permute-done((f32[256,128]{1,0:T(8,128)S(1)}, f32[256,128]{1,0:T(8,128)S(1)}, u32[]{:S(2)}, u32[]{:S(2)}) %collective-permute-start.27) | collective-permute-done | bytes 131104 | tf_op jit(solution)/shard_map/ppermute | solution.py:428
  37.8 0.8 first_partials.3
  38.7 1.6 %collective-permute-start.34 = (bf16[448,128]{1,0:T(8,128)(2,1)S(1)}, bf16[448,128]{1,0:T(8,128)(2,1)S(1)}, u32[]{:S(2)}, u32[]{:S(2)}) collective-permute-start(bf16[448,128]{1,0:T(8,128)(2,1)S(1)} %get-tuple-element.39), channel_id=1, source_target_pairs={{8,0},{16,8},{24,16},{28,24},{20,28},{12,20},{4,12},{0,4},{9,1},{1... | collective-permute-start | bytes 344072 | tf_op jit(solution)/shard_map/ppermute | solution.py:390
  40.8 0.8 first_partials.2
  41.6 1.6 %collective-permute-start.15 = (bf16[448,128]{1,0:T(8,128)(2,1)S(1)}, bf16[448,128]{1,0:T(8,128)(2,1)S(1)}, u32[]{:S(2)}, u32[]{:S(2)}) collective-permute-start(bf16[448,128]{1,0:T(8,128)(2,1)S(1)} %get-tuple-element.34), channel_id=1, source_target_pairs={{8,0},{16,8},{24,16},{28,24},{20,28},{12,20},{4,12},{0,4},{9,1},{1... | collective-permute-start | bytes 344072 | tf_op jit(solution)/shard_map/ppermute | solution.py:390
  43.7 0.5 next_partials.21
  44.2 1.6 %collective-permute-start.35 = (bf16[896,128]{1,0:T(8,128)(2,1)S(1)}, bf16[896,128]{1,0:T(8,128)(2,1)S(1)}, u32[]{:S(2)}, u32[]{:S(2)}) collective-permute-start(bf16[896,128]{1,0:T(8,128)(2,1)S(1)} %next_partials.21), channel_id=1, source_target_pairs={{8,0},{16,8},{24,16},{28,24},{20,28},{12,20},{4,12},{0,4},{9,1},{1... | collective-permute-start | bytes 688136 | tf_op jit(solution)/shard_map/ppermute | solution.py:390
  45.8 0.5 next_partials.18
  47.2 0.5 next_partials.15
  47.7 1.6 %collective-permute-start.16 = (bf16[896,128]{1,0:T(8,128)(2,1)S(1)}, bf16[896,128]{1,0:T(8,128)(2,1)S(1)}, u32[]{:S(2)}, u32[]{:S(2)}) collective-permute-start(bf16[896,128]{1,0:T(8,128)(2,1)S(1)} %next_partials.15), channel_id=1, source_target_pairs={{8,0},{16,8},{24,16},{28,24},{20,28},{12,20},{4,12},{0,4},{9,1},{1... | collective-permute-start | bytes 688136 | tf_op jit(solution)/shard_map/ppermute | solution.py:390
  49.3 0.5 next_partials.12
  50.3 2.4 %collective-permute-done.35.arrived = bf16[896,128]{1,0:T(8,128)(2,1)S(1)} collective-permute-done((bf16[896,128]{1,0:T(8,128)(2,1)S(1)}, bf16[896,128]{1,0:T(8,128)(2,1)S(1)}, u32[]{:S(2)}, u32[]{:S(2)}) %collective-permute-start.35) | collective-permute-done | bytes 229408 | tf_op jit(solution)/shard_map/ppermute | solution.py:390
  53.2 1.6 %collective-permute-start.36 = (bf16[896,128]{1,0:T(8,128)(2,1)S(1)}, bf16[896,128]{1,0:T(8,128)(2,1)S(1)}, u32[]{:S(2)}, u32[]{:S(2)}) collective-permute-start(bf16[896,128]{1,0:T(8,128)(2,1)S(1)} %next_partials.22), channel_id=1, source_target_pairs={{8,0},{16,8},{24,16},{28,24},{20,28},{12,20},{4,12},{0,4},{9,1},{1... | collective-permute-start | bytes 688136 | tf_op jit(solution)/shard_map/ppermute | solution.py:390
  55.8 1.8 %collective-permute-done.16.arrived = bf16[896,128]{1,0:T(8,128)(2,1)S(1)} collective-permute-done((bf16[896,128]{1,0:T(8,128)(2,1)S(1)}, bf16[896,128]{1,0:T(8,128)(2,1)S(1)}, u32[]{:S(2)}, u32[]{:S(2)}) %collective-permute-start.16) | collective-permute-done | bytes 229408 | tf_op jit(solution)/shard_map/ppermute | solution.py:390
  58.1 1.6 %collective-permute-start.17 = (bf16[896,128]{1,0:T(8,128)(2,1)S(1)}, bf16[896,128]{1,0:T(8,128)(2,1)S(1)}, u32[]{:S(2)}, u32[]{:S(2)}) collective-permute-start(bf16[896,128]{1,0:T(8,128)(2,1)S(1)} %next_partials.16), channel_id=1, source_target_pairs={{8,0},{16,8},{24,16},{28,24},{20,28},{12,20},{4,12},{0,4},{9,1},{1... | collective-permute-start | bytes 688136 | tf_op jit(solution)/shard_map/ppermute | solution.py:390
  60.8 1.8 %collective-permute-done.36.arrived = bf16[896,128]{1,0:T(8,128)(2,1)S(1)} collective-permute-done((bf16[896,128]{1,0:T(8,128)(2,1)S(1)}, bf16[896,128]{1,0:T(8,128)(2,1)S(1)}, u32[]{:S(2)}, u32[]{:S(2)}) %collective-permute-start.36) | collective-permute-done | bytes 229408 | tf_op jit(solution)/shard_map/ppermute | solution.py:390
  63.0 1.6 %collective-permute-start.37 = (bf16[896,128]{1,0:T(8,128)(2,1)S(1)}, bf16[896,128]{1,0:T(8,128)(2,1)S(1)}, u32[]{:S(2)}, u32[]{:S(2)}) collective-permute-start(bf16[896,128]{1,0:T(8,128)(2,1)S(1)} %next_partials.23), channel_id=1, source_target_pairs={{8,0},{16,8},{24,16},{28,24},{20,28},{12,20},{4,12},{0,4},{9,1},{1... | collective-permute-start | bytes 688136 | tf_op jit(solution)/shard_map/ppermute | solution.py:390
  65.7 1.8 %collective-permute-done.17.arrived = bf16[896,128]{1,0:T(8,128)(2,1)S(1)} collective-permute-done((bf16[896,128]{1,0:T(8,128)(2,1)S(1)}, bf16[896,128]{1,0:T(8,128)(2,1)S(1)}, u32[]{:S(2)}, u32[]{:S(2)}) %collective-permute-start.17) | collective-permute-done | bytes 229408 | tf_op jit(solution)/shard_map/ppermute | solution.py:390
  67.9 1.6 %collective-permute-start.18 = (bf16[896,128]{1,0:T(8,128)(2,1)S(1)}, bf16[896,128]{1,0:T(8,128)(2,1)S(1)}, u32[]{:S(2)}, u32[]{:S(2)}) collective-permute-start(bf16[896,128]{1,0:T(8,128)(2,1)S(1)} %next_partials.17), channel_id=1, source_target_pairs={{8,0},{16,8},{24,16},{28,24},{20,28},{12,20},{4,12},{0,4},{9,1},{1... | collective-permute-start | bytes 688136 | tf_op jit(solution)/shard_map/ppermute | solution.py:390
  70.1 0.6 collective-permute-start.14
  70.8 1.6 %collective-permute-done.37.in_down = bf16[896,128]{1,0:T(8,128)(2,1)S(1)} collective-permute-done((bf16[896,128]{1,0:T(8,128)(2,1)S(1)}, bf16[896,128]{1,0:T(8,128)(2,1)S(1)}, u32[]{:S(2)}, u32[]{:S(2)}) %collective-permute-start.37) | collective-permute-done | bytes 229408 | tf_op jit(solution)/shard_map/ppermute | solution.py:390
  72.4 2.2 %collective-permute-done.33.in_up = bf16[896,128]{1,0:T(8,128)(2,1)S(1)} collective-permute-done((bf16[896,128]{1,0:T(8,128)(2,1)S(1)}, bf16[896,128]{1,0:T(8,128)(2,1)S(1)}, u32[]{:S(2)}, u32[]{:S(2)}) %collective-permute-start.33) | collective-permute-done | bytes 229408 | tf_op jit(solution)/shard_map/ppermute | solution.py:390
  74.6 0.7 own_direction.3
  75.7 1.6 %collective-permute-start.46 = (bf16[896,128]{1,0:T(8,128)(2,1)S(1)}, bf16[896,128]{1,0:T(8,128)(2,1)S(1)}, u32[]{:S(2)}, u32[]{:S(2)}) collective-permute-start(bf16[896,128]{1,0:T(8,128)(2,1)S(1)} %get-tuple-element.40.refs_1_), channel_id=1, source_target_pairs={{8,0},{16,8},{24,16},{28,24},{20,28},{12,20},{4,12},{0,4},{9,1},{1... | collective-permute-start | bytes 688136 | tf_op jit(solution)/shard_map/ppermute | solution.py:390
  77.3 2.2 %collective-permute-done.14.in_up = bf16[896,128]{1,0:T(8,128)(2,1)S(1)} collective-permute-done((bf16[896,128]{1,0:T(8,128)(2,1)S(1)}, bf16[896,128]{1,0:T(8,128)(2,1)S(1)}, u32[]{:S(2)}, u32[]{:S(2)}) %collective-permute-start.14) | collective-permute-done | bytes 229408 | tf_op jit(solution)/shard_map/ppermute | solution.py:390
  79.5 0.6 own_direction.2
  80.6 1.6 %collective-permute-start.42 = (bf16[896,128]{1,0:T(8,128)(2,1)S(1)}, bf16[896,128]{1,0:T(8,128)(2,1)S(1)}, u32[]{:S(2)}, u32[]{:S(2)}) collective-permute-start(bf16[896,128]{1,0:T(8,128)(2,1)S(1)} %get-tuple-element.35.refs_0_), channel_id=1, source_target_pairs={{8,0},{16,8},{24,16},{28,24},{20,28},{12,20},{4,12},{0,4},{9,1},{1... | collective-permute-start | bytes 688136 | tf_op jit(solution)/shard_map/ppermute | solution.py:390
  82.2 2.2 %collective-permute-done.38.refs_1_ = bf16[896,128]{1,0:T(8,128)(2,1)S(1)} collective-permute-done((bf16[896,128]{1,0:T(8,128)(2,1)S(1)}, bf16[896,128]{1,0:T(8,128)(2,1)S(1)}, u32[]{:S(2)}, u32[]{:S(2)}) %collective-permute-start.38) | collective-permute-done | bytes 229408 | tf_op jit(solution)/shard_map/ppermute | solution.py:390
  84.8 1.6 %collective-permute-start.47 = (bf16[896,128]{1,0:T(8,128)(2,1)S(1)}, bf16[896,128]{1,0:T(8,128)(2,1)S(1)}, u32[]{:S(2)}, u32[]{:S(2)}) collective-permute-start(bf16[896,128]{1,0:T(8,128)(2,1)S(1)} %collective-permute-done.46.refs_3_), channel_id=1, source_target_pairs={{8,0},{16,8},{24,16},{28,24},{20,28},{12,20},{4,12},{0,4},{9,1},{1... | collective-permute-start | bytes 688136 | tf_op jit(solution)/shard_map/ppermute | solution.py:390
  86.4 2.9 %collective-permute-done.19.refs_0_ = bf16[896,128]{1,0:T(8,128)(2,1)S(1)} collective-permute-done((bf16[896,128]{1,0:T(8,128)(2,1)S(1)}, bf16[896,128]{1,0:T(8,128)(2,1)S(1)}, u32[]{:S(2)}, u32[]{:S(2)}) %collective-permute-start.19) | collective-permute-done | bytes 229408 | tf_op jit(solution)/shard_map/ppermute | solution.py:390
  89.7 1.6 %collective-permute-start.43 = (bf16[896,128]{1,0:T(8,128)(2,1)S(1)}, bf16[896,128]{1,0:T(8,128)(2,1)S(1)}, u32[]{:S(2)}, u32[]{:S(2)}) collective-permute-start(bf16[896,128]{1,0:T(8,128)(2,1)S(1)} %collective-permute-done.42.refs_2_), channel_id=1, source_target_pairs={{8,0},{16,8},{24,16},{28,24},{20,28},{12,20},{4,12},{0,4},{9,1},{1... | collective-permute-start | bytes 688136 | tf_op jit(solution)/shard_map/ppermute | solution.py:390
  91.3 2.9 %collective-permute-done.39.refs_1_ = bf16[896,128]{1,0:T(8,128)(2,1)S(1)} collective-permute-done((bf16[896,128]{1,0:T(8,128)(2,1)S(1)}, bf16[896,128]{1,0:T(8,128)(2,1)S(1)}, u32[]{:S(2)}, u32[]{:S(2)}) %collective-permute-start.39) | collective-permute-done | bytes 229408 | tf_op jit(solution)/shard_map/ppermute | solution.py:390
  94.6 1.6 %collective-permute-start.48 = (bf16[896,128]{1,0:T(8,128)(2,1)S(1)}, bf16[896,128]{1,0:T(8,128)(2,1)S(1)}, u32[]{:S(2)}, u32[]{:S(2)}) collective-permute-start(bf16[896,128]{1,0:T(8,128)(2,1)S(1)} %collective-permute-done.47.refs_3_), channel_id=1, source_target_pairs={{8,0},{16,8},{24,16},{28,24},{20,28},{12,20},{4,12},{0,4},{9,1},{1... | collective-permute-start | bytes 688136 | tf_op jit(solution)/shard_map/ppermute | solution.py:390
  96.2 2.9 %collective-permute-done.20.refs_0_ = bf16[896,128]{1,0:T(8,128)(2,1)S(1)} collective-permute-done((bf16[896,128]{1,0:T(8,128)(2,1)S(1)}, bf16[896,128]{1,0:T(8,128)(2,1)S(1)}, u32[]{:S(2)}, u32[]{:S(2)}) %collective-permute-start.20) | collective-permute-done | bytes 229408 | tf_op jit(solution)/shard_map/ppermute | solution.py:390
  99.6 1.6 %collective-permute-start.44 = (bf16[896,128]{1,0:T(8,128)(2,1)S(1)}, bf16[896,128]{1,0:T(8,128)(2,1)S(1)}, u32[]{:S(2)}, u32[]{:S(2)}) collective-permute-start(bf16[896,128]{1,0:T(8,128)(2,1)S(1)} %collective-permute-done.43.refs_2_), channel_id=1, source_target_pairs={{8,0},{16,8},{24,16},{28,24},{20,28},{12,20},{4,12},{0,4},{9,1},{1... | collective-permute-start | bytes 688136 | tf_op jit(solution)/shard_map/ppermute | solution.py:390
  101.2 1.4 %new_moments.1 = (f32[896,256]{1,0:T(8,128)}, f32[896,256]{1,0:T(8,128)}) custom-call(f32[896,128]{1,0:T(8,128)S(1)} %get-tuple-element.41.refs_0_, f32[896,128]{1,0:T(8,128)S(1)} %get-tuple-element.42.refs_1_, f32[896,256]{1,0:T(8,128)S(1)} %copy-done.1, f32[896,256]{1,0:T(8,128)S(1)} %copy-done.2), custom_call_target="tpu_custom_call" | custom-call | bytes 6291456 | tf_op jit(solution)/shard_map/new_moments/pallas_call | solution.py:312
  102.5 1.7 %write_update.5.refs_4_ = bf16[1024,7168]{1,0:T(8,128)(2,1)} custom-call(s32[1]{0:T(128)} %bitcast.here_ref, bf16[1024,256]{1,0:T(8,128)(2,1)S(1)} %copy-done, bf16[896,128]{1,0:T(8,128)(2,1)S(1)} %get-tuple-element.35.refs_0_, bf16[896,128]{1,0:T(8,128)(2,1)S(1)} %get-tuple-element.40.refs_1_), custom_call_target="tpu_custom_call" | custom-call | flops 469762048 | bytes 1835008 | tf_op jit(solution)/shard_map/write_update/pallas_call | solution.py:359
  104.3 2.4 %write_update.6.refs_4_ = bf16[1024,7168]{1,0:T(8,128)(2,1)} custom-call(s32[1]{0:T(128)} %bitcast.here_ref, bf16[1024,256]{1,0:T(8,128)(2,1)S(1)} %copy-done, bf16[896,128]{1,0:T(8,128)(2,1)S(1)} %collective-permute-done.19.refs_0_, bf16[896,128]{1,0:T(8,128)(2,1)S(1)} %collective-permute-done.38.refs_1_, ...), custom_call_target="tpu_custom_call", output_to_operand_aliasing={{}: (6, {})} | custom-call | flops 939524096 | bytes 3670016 | tf_op jit(solution)/shard_map/write_update/pallas_call | solution.py:359
  107.2 1.7 %collective-permute-start.49 = (bf16[448,128]{1,0:T(8,128)(2,1)S(1)}, bf16[448,128]{1,0:T(8,128)(2,1)S(1)}, u32[]{:S(2)}, u32[]{:S(2)}) collective-permute-start(bf16[448,128]{1,0:T(8,128)(2,1)S(1)} %slice.19), channel_id=1, source_target_pairs={{8,0},{16,8},{24,16},{28,24},{20,28},{12,20},{4,12},{0,4},{9,1},{1... | collective-permute-start | bytes 344072 | tf_op jit(solution)/shard_map/ppermute | solution.py:390
  109.4 1.7 %collective-permute-start.45 = (bf16[448,128]{1,0:T(8,128)(2,1)S(1)}, bf16[448,128]{1,0:T(8,128)(2,1)S(1)}, u32[]{:S(2)}, u32[]{:S(2)}) collective-permute-start(bf16[448,128]{1,0:T(8,128)(2,1)S(1)} %slice.18), channel_id=1, source_target_pairs={{8,0},{16,8},{24,16},{28,24},{20,28},{12,20},{4,12},{0,4},{9,1},{1... | collective-permute-start | bytes 344072 | tf_op jit(solution)/shard_map/ppermute | solution.py:390
  111.0 2.4 %write_update.7.refs_4_ = bf16[1024,7168]{1,0:T(8,128)(2,1)} custom-call(s32[1]{0:T(128)} %bitcast.here_ref, bf16[1024,256]{1,0:T(8,128)(2,1)S(1)} %copy-done, bf16[896,128]{1,0:T(8,128)(2,1)S(1)} %collective-permute-done.20.refs_0_, bf16[896,128]{1,0:T(8,128)(2,1)S(1)} %collective-permute-done.39.refs_1_, ...), custom_call_target="tpu_custom_call", output_to_operand_aliasing={{}: (6, {})} | custom-call | flops 939524096 | bytes 3670016 | tf_op jit(solution)/shard_map/write_update/pallas_call | solution.py:359
  113.4 2.4 %write_update.8.refs_4_ = bf16[1024,7168]{1,0:T(8,128)(2,1)} custom-call(s32[1]{0:T(128)} %bitcast.here_ref, bf16[1024,256]{1,0:T(8,128)(2,1)S(1)} %copy-done, bf16[896,128]{1,0:T(8,128)(2,1)S(1)} %collective-permute-done.21.refs_0_, bf16[896,128]{1,0:T(8,128)(2,1)S(1)} %collective-permute-done.40.refs_1_, ...), custom_call_target="tpu_custom_call", output_to_operand_aliasing={{}: (6, {})} | custom-call | flops 939524096 | bytes 3670016 | tf_op jit(solution)/shard_map/write_update/pallas_call | solution.py:359
  115.9 1.7 %write_update.9 = bf16[1024,7168]{1,0:T(8,128)(2,1)} custom-call(s32[1]{0:T(128)} %bitcast.here_ref, bf16[1024,256]{1,0:T(8,128)(2,1)S(1)} %copy-done, bf16[448,128]{1,0:T(8,128)(2,1)S(1)} %collective-permute-done.22.refs_0_, bf16[448,128]{1,0:T(8,128)(2,1)S(1)} %collective-permute-done.41.refs_1_, ...), custom_call_target="tpu_custom_call", output_to_operand_aliasing={{}: (6, {})} | custom-call | flops 469762048 | bytes 1835008 | tf_op jit(solution)/shard_map/write_update/pallas_call | solution.py:359
  (83 shorter events, 13.3 us)
Async XLA Ops:
  0.6 37.2 %slice-start = ((s8[7340032]{0:T(1024)(128)(4,1)}), s8[3145728]{0:T(1024)(128)(4,1)S(1)}, s32[]{:S(2)}) async-start(s8[7340032]{0:T(1024)(128)(4,1)} %bitcast.2), calls=%async_computation | async-start | bytes 6291456
  2.4 23.9 %collective-permute-start = (bf16[128,3584]{1,0:T(8,128)(2,1)S(1)}, bf16[128,3584]{1,0:T(8,128)(2,1)S(1)}, u32[]{:S(2)}, u32[]{:S(2)}) collective-permute-start(bf16[128,3584]{1,0:T(8,128)(2,1)S(1)} %get-tuple-element.29), channel_id=1, source_target_pairs={{0,1},{1,0},{2,3},{3,2},{4,5},{5,4},{6,7},{7,6},{8,9},{9,8},{10,11... | collective-permute-start | bytes 2752520 | tf_op jit(solution)/shard_map/ppermute | solution.py:410
  4.0 6.9 %collective-permute-start.23 = (bf16[1024,128]{1,0:T(8,128)(2,1)S(1)}, bf16[1024,128]{1,0:T(8,128)(2,1)S(1)}, u32[]{:S(2)}, u32[]{:S(2)}) collective-permute-start(bf16[1024,128]{1,0:T(8,128)(2,1)S(1)} %get-tuple-element.36.refs_2_), channel_id=1, source_target_pairs={{0,8},{8,16},{16,24},{24,28},{28,20},{20,12},{12,4},{4,0},{9,1},{1... | collective-permute-start | bytes 786440 | tf_op jit(solution)/shard_map/ppermute | solution.py:421
  6.7 7.1 %collective-permute-start.1 = (bf16[1024,128]{1,0:T(8,128)(2,1)S(1)}, bf16[1024,128]{1,0:T(8,128)(2,1)S(1)}, u32[]{:S(2)}, u32[]{:S(2)}) collective-permute-start(bf16[1024,128]{1,0:T(8,128)(2,1)S(1)} %get-tuple-element.30.refs_2_), channel_id=1, source_target_pairs={{0,8},{8,16},{16,24},{24,28},{28,20},{20,12},{12,4},{4,0},{9,1},{1... | collective-permute-start | bytes 786440 | tf_op jit(solution)/shard_map/ppermute | solution.py:421
  11.0 6.4 %collective-permute-start.24 = (bf16[1024,128]{1,0:T(8,128)(2,1)S(1)}, bf16[1024,128]{1,0:T(8,128)(2,1)S(1)}, u32[]{:S(2)}, u32[]{:S(2)}) collective-permute-start(bf16[1024,128]{1,0:T(8,128)(2,1)S(1)} %collective-permute-done.23.refs_3_), channel_id=1, source_target_pairs={{0,8},{8,16},{16,24},{24,28},{28,20},{20,12},{12,4},{4,0},{9,1},{1... | collective-permute-start | bytes 786440 | tf_op jit(solution)/shard_map/ppermute | solution.py:421
  13.8 7.1 %collective-permute-start.2 = (bf16[1024,128]{1,0:T(8,128)(2,1)S(1)}, bf16[1024,128]{1,0:T(8,128)(2,1)S(1)}, u32[]{:S(2)}, u32[]{:S(2)}) collective-permute-start(bf16[1024,128]{1,0:T(8,128)(2,1)S(1)} %collective-permute-done.1.refs_3_), channel_id=1, source_target_pairs={{0,8},{8,16},{16,24},{24,28},{28,20},{20,12},{12,4},{4,0},{9,1},{1... | collective-permute-start | bytes 786440 | tf_op jit(solution)/shard_map/ppermute | solution.py:421
  17.3 6.4 %collective-permute-start.25 = (bf16[1024,128]{1,0:T(8,128)(2,1)S(1)}, bf16[1024,128]{1,0:T(8,128)(2,1)S(1)}, u32[]{:S(2)}, u32[]{:S(2)}) collective-permute-start(bf16[1024,128]{1,0:T(8,128)(2,1)S(1)} %collective-permute-done.24.refs_4_), channel_id=1, source_target_pairs={{0,8},{8,16},{16,24},{24,28},{28,20},{20,12},{12,4},{4,0},{9,1},{1... | collective-permute-start | bytes 786440 | tf_op jit(solution)/shard_map/ppermute | solution.py:421
  19.4 6.8 %collective-permute-start.7 = (bf16[128,1024]{1,0:T(8,128)(2,1)S(1)}, bf16[128,1024]{1,0:T(8,128)(2,1)S(1)}, u32[]{:S(2)}, u32[]{:S(2)}) collective-permute-start(bf16[128,1024]{1,0:T(8,128)(2,1)S(1)} %get-tuple-element.31.refs_2_), channel_id=1, source_target_pairs={{0,2},{1,3},{2,0},{3,1},{4,6},{5,7},{6,4},{7,5},{8,10},{9,11},{10,... | collective-permute-start | bytes 786440 | tf_op jit(solution)/shard_map/ppermute | solution.py:413
  20.9 6.6 %collective-permute-start.3 = (bf16[1024,128]{1,0:T(8,128)(2,1)S(1)}, bf16[1024,128]{1,0:T(8,128)(2,1)S(1)}, u32[]{:S(2)}, u32[]{:S(2)}) collective-permute-start(bf16[1024,128]{1,0:T(8,128)(2,1)S(1)} %collective-permute-done.2.refs_4_), channel_id=1, source_target_pairs={{0,8},{8,16},{16,24},{24,28},{28,20},{20,12},{12,4},{4,0},{9,1},{1... | collective-permute-start | bytes 786440 | tf_op jit(solution)/shard_map/ppermute | solution.py:421
  23.7 6.0 %collective-permute-start.28 = (bf16[512,128]{1,0:T(8,128)(2,1)S(1)}, bf16[512,128]{1,0:T(8,128)(2,1)S(1)}, u32[]{:S(2)}, u32[]{:S(2)}) collective-permute-start(bf16[512,128]{1,0:T(8,128)(2,1)S(1)} %half_rows.3), channel_id=1, source_target_pairs={{0,8},{8,16},{16,24},{24,28},{28,20},{20,12},{12,4},{4,0},{9,1},{1... | collective-permute-start | bytes 393224 | tf_op jit(solution)/shard_map/ppermute | solution.py:430
  25.9 8.3 %collective-permute-start.6 = (bf16[128,1024]{1,0:T(8,128)(2,1)S(1)}, bf16[128,1024]{1,0:T(8,128)(2,1)S(1)}, u32[]{:S(2)}, u32[]{:S(2)}) collective-permute-start(bf16[128,1024]{1,0:T(8,128)(2,1)S(1)} %get-tuple-element.31.refs_2_), channel_id=1, source_target_pairs={{0,1},{1,0},{2,3},{3,2},{4,5},{5,4},{6,7},{7,6},{8,9},{9,8},{10,11... | collective-permute-start | bytes 786440 | tf_op jit(solution)/shard_map/ppermute | solution.py:411
  26.2 8.6 %collective-permute-start.8 = (bf16[128,1024]{1,0:T(8,128)(2,1)S(1)}, bf16[128,1024]{1,0:T(8,128)(2,1)S(1)}, u32[]{:S(2)}, u32[]{:S(2)}) collective-permute-start(bf16[128,1024]{1,0:T(8,128)(2,1)S(1)} %collective-permute-done.7.refs_4_), channel_id=1, source_target_pairs={{0,1},{1,0},{2,3},{3,2},{4,5},{5,4},{6,7},{7,6},{8,9},{9,8},{10,11... | collective-permute-start | bytes 786440 | tf_op jit(solution)/shard_map/ppermute | solution.py:414
  26.9 11.0 %slice-start.1 = ((s8[7340032]{0:T(1024)(128)(4,1)}), s8[4194304]{0:T(1024)(128)(4,1)S(1)}, s32[]{:S(2)}) async-start(s8[7340032]{0:T(1024)(128)(4,1)} %bitcast.2), calls=%async_computation.1 | async-start | bytes 8388608
  27.2 2.7 %collective-permute-start.26 = (f32[256,128]{1,0:T(8,128)S(1)}, f32[256,128]{1,0:T(8,128)S(1)}, u32[]{:S(2)}, u32[]{:S(2)}) collective-permute-start(f32[256,128]{1,0:T(8,128)S(1)} %add_coords.7), channel_id=1, source_target_pairs={{0,1},{1,0},{2,3},{3,2},{4,5},{5,4},{6,7},{7,6},{8,9},{9,8},{10,11... | collective-permute-start | bytes 393224 | tf_op jit(solution)/shard_map/ppermute | solution.py:427
  27.6 5.0 %collective-permute-start.9 = (bf16[512,128]{1,0:T(8,128)(2,1)S(1)}, bf16[512,128]{1,0:T(8,128)(2,1)S(1)}, u32[]{:S(2)}, u32[]{:S(2)}) collective-permute-start(bf16[512,128]{1,0:T(8,128)(2,1)S(1)} %half_rows.2), channel_id=1, source_target_pairs={{0,8},{8,16},{16,24},{24,28},{28,20},{20,12},{12,4},{4,0},{9,1},{1... | collective-permute-start | bytes 393224 | tf_op jit(solution)/shard_map/ppermute | solution.py:430
  29.7 4.3 %collective-permute-start.4 = (f32[256,128]{1,0:T(8,128)S(1)}, f32[256,128]{1,0:T(8,128)S(1)}, u32[]{:S(2)}, u32[]{:S(2)}) collective-permute-start(f32[256,128]{1,0:T(8,128)S(1)} %add_coords.5), channel_id=1, source_target_pairs={{0,1},{1,0},{2,3},{3,2},{4,5},{5,4},{6,7},{7,6},{8,9},{9,8},{10,11... | collective-permute-start | bytes 393224 | tf_op jit(solution)/shard_map/ppermute | solution.py:427
  29.8 4.9 %collective-permute-start.29 = (bf16[512,128]{1,0:T(8,128)(2,1)S(1)}, bf16[512,128]{1,0:T(8,128)(2,1)S(1)}, u32[]{:S(2)}, u32[]{:S(2)}) collective-permute-start(bf16[512,128]{1,0:T(8,128)(2,1)S(1)} %collective-permute-done.28.refs_6_), channel_id=1, source_target_pairs={{0,1},{1,0},{2,3},{3,2},{4,5},{5,4},{6,7},{7,6},{8,9},{9,8},{10,11... | collective-permute-start | bytes 393224 | tf_op jit(solution)/shard_map/ppermute | solution.py:431
  32.6 5.2 %collective-permute-start.27 = (f32[256,128]{1,0:T(8,128)S(1)}, f32[256,128]{1,0:T(8,128)S(1)}, u32[]{:S(2)}, u32[]{:S(2)}) collective-permute-start(f32[256,128]{1,0:T(8,128)S(1)} %add.7.refs_0_), channel_id=1, source_target_pairs={{0,2},{1,3},{2,0},{3,1},{4,6},{5,7},{6,4},{7,5},{8,10},{9,11},{10,... | collective-permute-start | bytes 393224 | tf_op jit(solution)/shard_map/ppermute | solution.py:428
  34.1 6.7 %collective-permute-start.10 = (bf16[512,128]{1,0:T(8,128)(2,1)S(1)}, bf16[512,128]{1,0:T(8,128)(2,1)S(1)}, u32[]{:S(2)}, u32[]{:S(2)}) collective-permute-start(bf16[512,128]{1,0:T(8,128)(2,1)S(1)} %collective-permute-done.9.refs_6_), channel_id=1, source_target_pairs={{0,1},{1,0},{2,3},{3,2},{4,5},{5,4},{6,7},{7,6},{8,9},{9,8},{10,11... | collective-permute-start | bytes 393224 | tf_op jit(solution)/shard_map/ppermute | solution.py:431
  34.1 6.7 %collective-permute-start.5 = (f32[256,128]{1,0:T(8,128)S(1)}, f32[256,128]{1,0:T(8,128)S(1)}, u32[]{:S(2)}, u32[]{:S(2)}) collective-permute-start(f32[256,128]{1,0:T(8,128)S(1)} %add.6.refs_0_), channel_id=1, source_target_pairs={{0,2},{1,3},{2,0},{3,1},{4,6},{5,7},{6,4},{7,5},{8,10},{9,11},{10,... | collective-permute-start | bytes 393224 | tf_op jit(solution)/shard_map/ppermute | solution.py:428
  38.7 5.0 %collective-permute-start.34 = (bf16[448,128]{1,0:T(8,128)(2,1)S(1)}, bf16[448,128]{1,0:T(8,128)(2,1)S(1)}, u32[]{:S(2)}, u32[]{:S(2)}) collective-permute-start(bf16[448,128]{1,0:T(8,128)(2,1)S(1)} %get-tuple-element.39), channel_id=1, source_target_pairs={{8,0},{16,8},{24,16},{28,24},{20,28},{12,20},{4,12},{0,4},{9,1},{1... | collective-permute-start | bytes 344072 | tf_op jit(solution)/shard_map/ppermute | solution.py:390
  40.3 5.5 %collective-permute-start.30 = (bf16[448,128]{1,0:T(8,128)(2,1)S(1)}, bf16[448,128]{1,0:T(8,128)(2,1)S(1)}, u32[]{:S(2)}, u32[]{:S(2)}) collective-permute-start(bf16[448,128]{1,0:T(8,128)(2,1)S(1)} %get-tuple-element.38), channel_id=1, source_target_pairs={{0,8},{8,16},{16,24},{24,28},{28,20},{20,12},{12,4},{4,0},{1,9},{9... | collective-permute-start | bytes 344072 | tf_op jit(solution)/shard_map/ppermute | solution.py:390
  41.6 5.6 %collective-permute-start.15 = (bf16[448,128]{1,0:T(8,128)(2,1)S(1)}, bf16[448,128]{1,0:T(8,128)(2,1)S(1)}, u32[]{:S(2)}, u32[]{:S(2)}) collective-permute-start(bf16[448,128]{1,0:T(8,128)(2,1)S(1)} %get-tuple-element.34), channel_id=1, source_target_pairs={{8,0},{16,8},{24,16},{28,24},{20,28},{12,20},{4,12},{0,4},{9,1},{1... | collective-permute-start | bytes 344072 | tf_op jit(solution)/shard_map/ppermute | solution.py:390
  43.3 6.1 %collective-permute-start.11 = (bf16[448,128]{1,0:T(8,128)(2,1)S(1)}, bf16[448,128]{1,0:T(8,128)(2,1)S(1)}, u32[]{:S(2)}, u32[]{:S(2)}) collective-permute-start(bf16[448,128]{1,0:T(8,128)(2,1)S(1)} %get-tuple-element.33), channel_id=1, source_target_pairs={{0,8},{8,16},{16,24},{24,28},{28,20},{20,12},{12,4},{4,0},{1,9},{9... | collective-permute-start | bytes 344072 | tf_op jit(solution)/shard_map/ppermute | solution.py:390
  44.2 8.5 %collective-permute-start.35 = (bf16[896,128]{1,0:T(8,128)(2,1)S(1)}, bf16[896,128]{1,0:T(8,128)(2,1)S(1)}, u32[]{:S(2)}, u32[]{:S(2)}) collective-permute-start(bf16[896,128]{1,0:T(8,128)(2,1)S(1)} %next_partials.21), channel_id=1, source_target_pairs={{8,0},{16,8},{24,16},{28,24},{20,28},{12,20},{4,12},{0,4},{9,1},{1... | collective-permute-start | bytes 688136 | tf_op jit(solution)/shard_map/ppermute | solution.py:390
  46.4 8.5 %collective-permute-start.31 = (bf16[896,128]{1,0:T(8,128)(2,1)S(1)}, bf16[896,128]{1,0:T(8,128)(2,1)S(1)}, u32[]{:S(2)}, u32[]{:S(2)}) collective-permute-start(bf16[896,128]{1,0:T(8,128)(2,1)S(1)} %next_partials.18), channel_id=1, source_target_pairs={{0,8},{8,16},{16,24},{24,28},{28,20},{20,12},{12,4},{4,0},{1,9},{9... | collective-permute-start | bytes 688136 | tf_op jit(solution)/shard_map/ppermute | solution.py:390
  47.7 9.9 %collective-permute-start.16 = (bf16[896,128]{1,0:T(8,128)(2,1)S(1)}, bf16[896,128]{1,0:T(8,128)(2,1)S(1)}, u32[]{:S(2)}, u32[]{:S(2)}) collective-permute-start(bf16[896,128]{1,0:T(8,128)(2,1)S(1)} %next_partials.15), channel_id=1, source_target_pairs={{8,0},{16,8},{24,16},{28,24},{20,28},{12,20},{4,12},{0,4},{9,1},{1... | collective-permute-start | bytes 688136 | tf_op jit(solution)/shard_map/ppermute | solution.py:390
  49.9 10.0 %collective-permute-start.12 = (bf16[896,128]{1,0:T(8,128)(2,1)S(1)}, bf16[896,128]{1,0:T(8,128)(2,1)S(1)}, u32[]{:S(2)}, u32[]{:S(2)}) collective-permute-start(bf16[896,128]{1,0:T(8,128)(2,1)S(1)} %next_partials.12), channel_id=1, source_target_pairs={{0,8},{8,16},{16,24},{24,28},{28,20},{20,12},{12,4},{4,0},{1,9},{9... | collective-permute-start | bytes 688136 | tf_op jit(solution)/shard_map/ppermute | solution.py:390
  53.2 9.4 %collective-permute-start.36 = (bf16[896,128]{1,0:T(8,128)(2,1)S(1)}, bf16[896,128]{1,0:T(8,128)(2,1)S(1)}, u32[]{:S(2)}, u32[]{:S(2)}) collective-permute-start(bf16[896,128]{1,0:T(8,128)(2,1)S(1)} %next_partials.22), channel_id=1, source_target_pairs={{8,0},{16,8},{24,16},{28,24},{20,28},{12,20},{4,12},{0,4},{9,1},{1... | collective-permute-start | bytes 688136 | tf_op jit(solution)/shard_map/ppermute | solution.py:390
  55.4 9.4 %collective-permute-start.32 = (bf16[896,128]{1,0:T(8,128)(2,1)S(1)}, bf16[896,128]{1,0:T(8,128)(2,1)S(1)}, u32[]{:S(2)}, u32[]{:S(2)}) collective-permute-start(bf16[896,128]{1,0:T(8,128)(2,1)S(1)} %next_partials.19), channel_id=1, source_target_pairs={{0,8},{8,16},{16,24},{24,28},{28,20},{20,12},{12,4},{4,0},{1,9},{9... | collective-permute-start | bytes 688136 | tf_op jit(solution)/shard_map/ppermute | solution.py:390
  58.1 9.4 %collective-permute-start.17 = (bf16[896,128]{1,0:T(8,128)(2,1)S(1)}, bf16[896,128]{1,0:T(8,128)(2,1)S(1)}, u32[]{:S(2)}, u32[]{:S(2)}) collective-permute-start(bf16[896,128]{1,0:T(8,128)(2,1)S(1)} %next_partials.16), channel_id=1, source_target_pairs={{8,0},{16,8},{24,16},{28,24},{20,28},{12,20},{4,12},{0,4},{9,1},{1... | collective-permute-start | bytes 688136 | tf_op jit(solution)/shard_map/ppermute | solution.py:390
  60.3 14.3 %copy-start.1 = (f32[896,256]{1,0:T(8,128)S(1)}, f32[896,256]{1,0:T(8,128)}, u32[]{:S(2)}) copy-start(f32[896,256]{1,0:T(8,128)} %refs_2_.1) | copy-start | bytes 2752516
  60.3 14.3 %copy-start.2 = (f32[896,256]{1,0:T(8,128)S(1)}, f32[896,256]{1,0:T(8,128)}, u32[]{:S(2)}) copy-start(f32[896,256]{1,0:T(8,128)} %refs_3_.1) | copy-start | bytes 2752516
  60.3 9.3 %collective-permute-start.13 = (bf16[896,128]{1,0:T(8,128)(2,1)S(1)}, bf16[896,128]{1,0:T(8,128)(2,1)S(1)}, u32[]{:S(2)}, u32[]{:S(2)}) collective-permute-start(bf16[896,128]{1,0:T(8,128)(2,1)S(1)} %next_partials.13), channel_id=1, source_target_pairs={{0,8},{8,16},{16,24},{24,28},{28,20},{20,12},{12,4},{4,0},{1,9},{9... | collective-permute-start | bytes 688136 | tf_op jit(solution)/shard_map/ppermute | solution.py:390
  63.0 9.4 %collective-permute-start.37 = (bf16[896,128]{1,0:T(8,128)(2,1)S(1)}, bf16[896,128]{1,0:T(8,128)(2,1)S(1)}, u32[]{:S(2)}, u32[]{:S(2)}) collective-permute-start(bf16[896,128]{1,0:T(8,128)(2,1)S(1)} %next_partials.23), channel_id=1, source_target_pairs={{8,0},{16,8},{24,16},{28,24},{20,28},{12,20},{4,12},{0,4},{9,1},{1... | collective-permute-start | bytes 688136 | tf_op jit(solution)/shard_map/ppermute | solution.py:390
  65.2 9.4 %collective-permute-start.33 = (bf16[896,128]{1,0:T(8,128)(2,1)S(1)}, bf16[896,128]{1,0:T(8,128)(2,1)S(1)}, u32[]{:S(2)}, u32[]{:S(2)}) collective-permute-start(bf16[896,128]{1,0:T(8,128)(2,1)S(1)} %next_partials.20), channel_id=1, source_target_pairs={{0,8},{8,16},{16,24},{24,28},{28,20},{20,12},{12,4},{4,0},{1,9},{9... | collective-permute-start | bytes 688136 | tf_op jit(solution)/shard_map/ppermute | solution.py:390
  67.9 34.6 %copy-start = (bf16[1024,256]{1,0:T(8,128)(2,1)S(1)}, bf16[1024,256]{1,0:T(8,128)(2,1)}, u32[]{:S(2)}) copy-start(bf16[1024,256]{1,0:T(8,128)(2,1)} %base.4) | copy-start | bytes 1572868
  67.9 9.4 %collective-permute-start.18 = (bf16[896,128]{1,0:T(8,128)(2,1)S(1)}, bf16[896,128]{1,0:T(8,128)(2,1)S(1)}, u32[]{:S(2)}, u32[]{:S(2)}) collective-permute-start(bf16[896,128]{1,0:T(8,128)(2,1)S(1)} %next_partials.17), channel_id=1, source_target_pairs={{8,0},{16,8},{24,16},{28,24},{20,28},{12,20},{4,12},{0,4},{9,1},{1... | collective-permute-start | bytes 688136 | tf_op jit(solution)/shard_map/ppermute | solution.py:390
  70.1 9.4 %collective-permute-start.14 = (bf16[896,128]{1,0:T(8,128)(2,1)S(1)}, bf16[896,128]{1,0:T(8,128)(2,1)S(1)}, u32[]{:S(2)}, u32[]{:S(2)}) collective-permute-start(bf16[896,128]{1,0:T(8,128)(2,1)S(1)} %next_partials.14), channel_id=1, source_target_pairs={{0,8},{8,16},{16,24},{24,28},{28,20},{20,12},{12,4},{4,0},{1,9},{9... | collective-permute-start | bytes 688136 | tf_op jit(solution)/shard_map/ppermute | solution.py:390
  75.2 9.2 %collective-permute-start.38 = (bf16[896,128]{1,0:T(8,128)(2,1)S(1)}, bf16[896,128]{1,0:T(8,128)(2,1)S(1)}, u32[]{:S(2)}, u32[]{:S(2)}) collective-permute-start(bf16[896,128]{1,0:T(8,128)(2,1)S(1)} %get-tuple-element.40.refs_1_), channel_id=1, source_target_pairs={{0,8},{8,16},{16,24},{24,28},{28,20},{20,12},{12,4},{4,0},{1,9},{9... | collective-permute-start | bytes 688136 | tf_op jit(solution)/shard_map/ppermute | solution.py:390
  75.7 9.1 %collective-permute-start.46 = (bf16[896,128]{1,0:T(8,128)(2,1)S(1)}, bf16[896,128]{1,0:T(8,128)(2,1)S(1)}, u32[]{:S(2)}, u32[]{:S(2)}) collective-permute-start(bf16[896,128]{1,0:T(8,128)(2,1)S(1)} %get-tuple-element.40.refs_1_), channel_id=1, source_target_pairs={{8,0},{16,8},{24,16},{28,24},{20,28},{12,20},{4,12},{0,4},{9,1},{1... | collective-permute-start | bytes 688136 | tf_op jit(solution)/shard_map/ppermute | solution.py:390
  80.1 9.2 %collective-permute-start.19 = (bf16[896,128]{1,0:T(8,128)(2,1)S(1)}, bf16[896,128]{1,0:T(8,128)(2,1)S(1)}, u32[]{:S(2)}, u32[]{:S(2)}) collective-permute-start(bf16[896,128]{1,0:T(8,128)(2,1)S(1)} %get-tuple-element.35.refs_0_), channel_id=1, source_target_pairs={{0,8},{8,16},{16,24},{24,28},{28,20},{20,12},{12,4},{4,0},{1,9},{9... | collective-permute-start | bytes 688136 | tf_op jit(solution)/shard_map/ppermute | solution.py:390
  80.6 9.1 %collective-permute-start.42 = (bf16[896,128]{1,0:T(8,128)(2,1)S(1)}, bf16[896,128]{1,0:T(8,128)(2,1)S(1)}, u32[]{:S(2)}, u32[]{:S(2)}) collective-permute-start(bf16[896,128]{1,0:T(8,128)(2,1)S(1)} %get-tuple-element.35.refs_0_), channel_id=1, source_target_pairs={{8,0},{16,8},{24,16},{28,24},{20,28},{12,20},{4,12},{0,4},{9,1},{1... | collective-permute-start | bytes 688136 | tf_op jit(solution)/shard_map/ppermute | solution.py:390
  84.4 9.8 %collective-permute-start.39 = (bf16[896,128]{1,0:T(8,128)(2,1)S(1)}, bf16[896,128]{1,0:T(8,128)(2,1)S(1)}, u32[]{:S(2)}, u32[]{:S(2)}) collective-permute-start(bf16[896,128]{1,0:T(8,128)(2,1)S(1)} %collective-permute-done.38.refs_1_), channel_id=1, source_target_pairs={{0,8},{8,16},{16,24},{24,28},{28,20},{20,12},{12,4},{4,0},{1,9},{9... | collective-permute-start | bytes 688136 | tf_op jit(solution)/shard_map/ppermute | solution.py:390
  84.8 9.8 %collective-permute-start.47 = (bf16[896,128]{1,0:T(8,128)(2,1)S(1)}, bf16[896,128]{1,0:T(8,128)(2,1)S(1)}, u32[]{:S(2)}, u32[]{:S(2)}) collective-permute-start(bf16[896,128]{1,0:T(8,128)(2,1)S(1)} %collective-permute-done.46.refs_3_), channel_id=1, source_target_pairs={{8,0},{16,8},{24,16},{28,24},{20,28},{12,20},{4,12},{0,4},{9,1},{1... | collective-permute-start | bytes 688136 | tf_op jit(solution)/shard_map/ppermute | solution.py:390
  89.3 9.8 %collective-permute-start.20 = (bf16[896,128]{1,0:T(8,128)(2,1)S(1)}, bf16[896,128]{1,0:T(8,128)(2,1)S(1)}, u32[]{:S(2)}, u32[]{:S(2)}) collective-permute-start(bf16[896,128]{1,0:T(8,128)(2,1)S(1)} %collective-permute-done.19.refs_0_), channel_id=1, source_target_pairs={{0,8},{8,16},{16,24},{24,28},{28,20},{20,12},{12,4},{4,0},{1,9},{9... | collective-permute-start | bytes 688136 | tf_op jit(solution)/shard_map/ppermute | solution.py:390
  89.7 9.8 %collective-permute-start.43 = (bf16[896,128]{1,0:T(8,128)(2,1)S(1)}, bf16[896,128]{1,0:T(8,128)(2,1)S(1)}, u32[]{:S(2)}, u32[]{:S(2)}) collective-permute-start(bf16[896,128]{1,0:T(8,128)(2,1)S(1)} %collective-permute-done.42.refs_2_), channel_id=1, source_target_pairs={{8,0},{16,8},{24,16},{28,24},{20,28},{12,20},{4,12},{0,4},{9,1},{1... | collective-permute-start | bytes 688136 | tf_op jit(solution)/shard_map/ppermute | solution.py:390
  94.2 12.5 %collective-permute-start.40 = (bf16[896,128]{1,0:T(8,128)(2,1)S(1)}, bf16[896,128]{1,0:T(8,128)(2,1)S(1)}, u32[]{:S(2)}, u32[]{:S(2)}) collective-permute-start(bf16[896,128]{1,0:T(8,128)(2,1)S(1)} %collective-permute-done.39.refs_1_), channel_id=1, source_target_pairs={{0,8},{8,16},{16,24},{24,28},{28,20},{20,12},{12,4},{4,0},{1,9},{9... | collective-permute-start | bytes 688136 | tf_op jit(solution)/shard_map/ppermute | solution.py:390
  94.6 12.5 %collective-permute-start.48 = (bf16[896,128]{1,0:T(8,128)(2,1)S(1)}, bf16[896,128]{1,0:T(8,128)(2,1)S(1)}, u32[]{:S(2)}, u32[]{:S(2)}) collective-permute-start(bf16[896,128]{1,0:T(8,128)(2,1)S(1)} %collective-permute-done.47.refs_3_), channel_id=1, source_target_pairs={{8,0},{16,8},{24,16},{28,24},{20,28},{12,20},{4,12},{0,4},{9,1},{1... | collective-permute-start | bytes 688136 | tf_op jit(solution)/shard_map/ppermute | solution.py:390
  99.1 9.7 %collective-permute-start.21 = (bf16[896,128]{1,0:T(8,128)(2,1)S(1)}, bf16[896,128]{1,0:T(8,128)(2,1)S(1)}, u32[]{:S(2)}, u32[]{:S(2)}) collective-permute-start(bf16[896,128]{1,0:T(8,128)(2,1)S(1)} %collective-permute-done.20.refs_0_), channel_id=1, source_target_pairs={{0,8},{8,16},{16,24},{24,28},{28,20},{20,12},{12,4},{4,0},{1,9},{9... | collective-permute-start | bytes 688136 | tf_op jit(solution)/shard_map/ppermute | solution.py:390
  99.6 9.8 %collective-permute-start.44 = (bf16[896,128]{1,0:T(8,128)(2,1)S(1)}, bf16[896,128]{1,0:T(8,128)(2,1)S(1)}, u32[]{:S(2)}, u32[]{:S(2)}) collective-permute-start(bf16[896,128]{1,0:T(8,128)(2,1)S(1)} %collective-permute-done.43.refs_2_), channel_id=1, source_target_pairs={{8,0},{16,8},{24,16},{28,24},{20,28},{12,20},{4,12},{0,4},{9,1},{1... | collective-permute-start | bytes 688136 | tf_op jit(solution)/shard_map/ppermute | solution.py:390
  106.7 9.2 %collective-permute-start.41 = (bf16[448,128]{1,0:T(8,128)(2,1)S(1)}, bf16[448,128]{1,0:T(8,128)(2,1)S(1)}, u32[]{:S(2)}, u32[]{:S(2)}) collective-permute-start(bf16[448,128]{1,0:T(8,128)(2,1)S(1)} %slice.17), channel_id=1, source_target_pairs={{0,8},{8,16},{16,24},{24,28},{28,20},{20,12},{12,4},{4,0},{1,9},{9... | collective-permute-start | bytes 344072 | tf_op jit(solution)/shard_map/ppermute | solution.py:390
  107.2 8.7 %collective-permute-start.49 = (bf16[448,128]{1,0:T(8,128)(2,1)S(1)}, bf16[448,128]{1,0:T(8,128)(2,1)S(1)}, u32[]{:S(2)}, u32[]{:S(2)}) collective-permute-start(bf16[448,128]{1,0:T(8,128)(2,1)S(1)} %slice.19), channel_id=1, source_target_pairs={{8,0},{16,8},{24,16},{28,24},{20,28},{12,20},{4,12},{0,4},{9,1},{1... | collective-permute-start | bytes 344072 | tf_op jit(solution)/shard_map/ppermute | solution.py:390
  108.9 7.0 %collective-permute-start.22 = (bf16[448,128]{1,0:T(8,128)(2,1)S(1)}, bf16[448,128]{1,0:T(8,128)(2,1)S(1)}, u32[]{:S(2)}, u32[]{:S(2)}) collective-permute-start(bf16[448,128]{1,0:T(8,128)(2,1)S(1)} %slice.16), channel_id=1, source_target_pairs={{0,8},{8,16},{16,24},{24,28},{28,20},{20,12},{12,4},{4,0},{1,9},{9... | collective-permute-start | bytes 344072 | tf_op jit(solution)/shard_map/ppermute | solution.py:390
  109.4 6.5 %collective-permute-start.45 = (bf16[448,128]{1,0:T(8,128)(2,1)S(1)}, bf16[448,128]{1,0:T(8,128)(2,1)S(1)}, u32[]{:S(2)}, u32[]{:S(2)}) collective-permute-start(bf16[448,128]{1,0:T(8,128)(2,1)S(1)} %slice.18), channel_id=1, source_target_pairs={{8,0},{16,8},{24,16},{28,24},{20,28},{12,20},{4,12},{0,4},{9,1},{1... | collective-permute-start | bytes 344072 | tf_op jit(solution)/shard_map/ppermute | solution.py:390

commit v6 on v5

--- a/solution.py
+++ b/solution.py
@@ -15,6 +15,7 @@
 adam_eps = 1e-08
 
 STREAMS = 2
+WAYS = ("up", "down")
 LONGEST_RING = 16
 SCRATCH_BYTES = 12 << 20
 
@@ -69,11 +70,15 @@
     return [*range(0, n, 2), *range(n - 1, 0, -2)]
 
 
+def own_at(here, n):
+    return lax.rem(here[0], n)
+
+
 def chunk_at(here, away, n):
-    index = here[0]
+    index = own_at(here, n)
     step = lax.shift_right_logical(index, 1)
     place = lax.select(lax.bitwise_and(index, 1) == 0, step, n - 1 - step)
-    there = lax.rem(place + away, n)
+    there = lax.rem(place + lax.select(here[0] < n, away, n - away), n)
     return lax.select(there < n // 2, 2 * there, 2 * (n - 1 - there) + 1)
 
 
@@ -81,15 +86,15 @@
     return [pltpu.with_memory_space_constraint(a, pltpu.VMEM) for a in arrays]
 
 
-def split_columns(here, me, activations, n):
+def nearer_columns(here, me, activations, n, own, with_farthest):
     tokens, features = activations.shape
     depth = features // n
     part = depth // 2
-    near = pltpu.VMEM((tokens, part + (n // 2 - 1) * depth), activations.dtype)
-    far = pltpu.VMEM((tokens, depth), activations.dtype)
-
-    def kernel(here_ref, me_ref, source, kept, sent, farthest, sems):
-        mine = lax.bitwise_and(me_ref[0], 1)
+    shapes = [part + (n // 2 - 1) * depth] + [depth] * with_farthest
+
+    def kernel(here_ref, me_ref, source, *refs):
+        out, sems = refs[0], refs[-1]
+        side = lax.bitwise_xor(lax.bitwise_and(me_ref[0], 1), 0 if own else 1)
         copies = []
 
         def copy(start, size, out, low):
@@ -98,12 +103,11 @@
                 pltpu.make_async_copy(source.at[:, columns], out.at[:, pl.ds(low, size)], sems.at[len(copies)])
             )
 
-        copy(chunk_at(here_ref, n // 2, n) * depth, depth, farthest, 0)
-        for out, side in ((sent, 1 - mine), (kept, mine)):
-            copy(here_ref[0] * depth + side * part, part, out, 0)
-            for k in range(1, n // 2):
-                block = chunk_at(here_ref, lax.select(side == 0, n - k, k), n)
-                copy(block * depth, depth, out, part + (k - 1) * depth)
+        copy(own_at(here_ref, n) * depth + side * part, part, out, 0)
+        for k in range(1, n // 2):
+            copy(chunk_at(here_ref, n - k if own else k, n) * depth, depth, out, part + (k - 1) * depth)
+        if with_farthest:
+            copy(chunk_at(here_ref, n // 2, n) * depth, depth, refs[1], 0)
         for one in copies:
             one.start()
         for one in copies:
@@ -111,37 +115,30 @@
 
     return pl.pallas_call(
         kernel,
-        out_shape=(near, near, far),
+        out_shape=tuple(pltpu.VMEM((tokens, size), activations.dtype) for size in shapes),
         in_specs=[scalars(), scalars(), pl.BlockSpec(memory_space=pltpu.HBM)],
-        out_specs=(on_chip(),) * 3,
-        scratch_shapes=[pltpu.SemaphoreType.DMA((n + 1,))],
-        compiler_params=pltpu.CompilerParams(vmem_limit_bytes=SCRATCH_BYTES),
-        name="split_columns",
+        out_specs=(on_chip(),) * len(shapes),
+        scratch_shapes=[pltpu.SemaphoreType.DMA((n // 2 + with_farthest,))],
+        compiler_params=pltpu.CompilerParams(vmem_limit_bytes=SCRATCH_BYTES),
     )(here, me, left_in_hbm(activations))
 
 
-def own_pieces(basis):
+def own_piece(basis, s):
     depth, rank = basis.shape
     width = rank // STREAMS
 
-    def kernel(source, *refs):
-        copies = [
-            pltpu.make_async_copy(source.at[:, pl.ds(s * width, width)], refs[s], refs[-1].at[s])
-            for s in range(STREAMS)
-        ]
-        for copy in copies:
-            copy.start()
-        for copy in copies:
-            copy.wait()
-
-    return pl.pallas_call(
-        kernel,
-        out_shape=(pltpu.VMEM((depth, width), basis.dtype),) * STREAMS,
+    def kernel(source, out, sem):
+        copy = pltpu.make_async_copy(source.at[:, pl.ds(s * width, width)], out, sem)
+        copy.start()
+        copy.wait()
+
+    return pl.pallas_call(
+        kernel,
+        out_shape=pltpu.VMEM((depth, width), basis.dtype),
         in_specs=[pl.BlockSpec(memory_space=pltpu.HBM)],
-        out_specs=(on_chip(),) * STREAMS,
-        scratch_shapes=[pltpu.SemaphoreType.DMA((STREAMS,))],
-        compiler_params=pltpu.CompilerParams(vmem_limit_bytes=SCRATCH_BYTES),
-        name="own_pieces",
+        out_specs=on_chip(),
+        scratch_shapes=[pltpu.SemaphoreType.DMA],
+        compiler_params=pltpu.CompilerParams(vmem_limit_bytes=SCRATCH_BYTES),
     )(left_in_hbm(basis))
 
 
@@ -157,7 +154,6 @@
         in_specs=[scalars(), on_chip()],
         out_specs=on_chip(),
         compiler_params=pltpu.CompilerParams(vmem_limit_bytes=SCRATCH_BYTES),
-        name="half_rows",
     )(me, *kept_on_chip([block]))
 
 
@@ -187,7 +183,6 @@
             flops=4 * tokens * width * sum(size for _, _, size in pieces), transcendentals=0, bytes_accessed=4 << 20
         ),
         compiler_params=pltpu.CompilerParams(vmem_limit_bytes=SCRATCH_BYTES),
-        name="add_coords",
     )(me, *kept_on_chip([kept, came, *held, *arrays]))
 
 
@@ -234,7 +229,6 @@
             flops=2 * tokens * (cols + 2 * part) * width, transcendentals=0, bytes_accessed=4 << 20
         ),
         compiler_params=pltpu.CompilerParams(vmem_limit_bytes=SCRATCH_BYTES),
-        name="first_partials",
     )(here, me, *kept_on_chip(arrays))
 
 
@@ -261,7 +255,6 @@
             flops=2 * tokens * cols * width, transcendentals=0, bytes_accessed=2 << 20
         ),
         compiler_params=pltpu.CompilerParams(vmem_limit_bytes=SCRATCH_BYTES),
-        name="next_partials",
     )(here, *kept_on_chip([grad_out, coords, came]))
 
 
@@ -270,7 +263,7 @@
     cols = grad_out.shape[1] // n
 
     def kernel(here_ref, grad, coord, in_up, in_down, first, second, projected, direction):
-        column = pl.multiple_of(here_ref[0] * cols, 128)
+        column = pl.multiple_of(own_at(here_ref, n) * cols, 128)
         total = (
             contract_tokens(grad[:, pl.ds(column, cols)], coord[...])
             + in_up[...].astype(jnp.float32)
@@ -292,7 +285,6 @@
             flops=2 * tokens * cols * width, transcendentals=0, bytes_accessed=4 << 20
         ),
         compiler_params=pltpu.CompilerParams(vmem_limit_bytes=SCRATCH_BYTES),
-        name="own_direction",
     )(here, *kept_on_chip([grad_out, coords, came_up, came_down, first_moment, second_moment]))
 
 
@@ -317,7 +309,6 @@
         out_specs=(block, block),
         cost_estimate=pl.CostEstimate(flops=0, transcendentals=0, bytes_accessed=6 << 20),
         compiler_params=pltpu.CompilerParams(vmem_limit_bytes=SCRATCH_BYTES),
-        name="new_moments",
     )(*kept_on_chip([*projected, first_moment, second_moment]))
 
 
@@ -376,22 +367,22 @@
             bytes_accessed=2 * depth * cols * len(chunks),
         ),
         compiler_params=pltpu.CompilerParams(vmem_limit_bytes=SCRATCH_BYTES),
-        name="write_update",
     )(here, *kept_on_chip([basis, *flat]), *held)
 
 
 def on_ring(n, m, activations, grad_out, basis, first_moment, second_moment):
     order = ring_order(n)
-    upward = [(order[k], order[(k + 1) % n]) for k in range(n)]
+    ring = [(order[k], order[(k + 1) % n]) for k in range(n)]
+    upward = [(b * m + k, a * m + k) if k % 2 else (a * m + k, b * m + k) for k in range(m) for a, b in ring]
     downward = [(b, a) for a, b in upward]
     partners = [(k, k ^ 1) for k in range(m)]
 
     def hop(to_up, to_down):
-        return (lax.ppermute(to_up, "dp", upward), lax.ppermute(to_down, "dp", downward))
+        return (lax.ppermute(to_up, ("dp", "mp"), upward), lax.ppermute(to_down, ("dp", "mp"), downward))
 
     me = lax.axis_index("mp")
     here, me, activations, basis = lax.optimization_barrier(
-        (lax.axis_index("dp").reshape(1), me.reshape(1), activations, basis)
+        ((lax.axis_index("dp") + n * lax.bitwise_and(me, 1)).reshape(1), me.reshape(1), activations, basis)
     )
 
     depth, _ = basis.shape
@@ -400,13 +391,11 @@
     half = n // 2
     streams = range(STREAMS)
 
-    apart = [
-        (a * m + k, b * m + k) for k in range(m) for a, b in (downward if k % 2 else upward)
-    ]
     part = depth // 2
-    passing = list(own_pieces(basis))
+    passing = [own_piece(basis, s) for s in streams]
     pieces = [[(passing[s], 0, part)] for s in streams]
-    kept, sent, far = split_columns(here, me, activations, n)
+    (kept,) = nearer_columns(here, me, activations, n, True, False)
+    sent, far = nearer_columns(here, me, activations, n, False, True)
     swapped = lax.ppermute(sent, "mp", partners)
     fars = [far, lax.ppermute(far, "mp", partners)]
     for k in range(2, m, 2):
@@ -418,7 +407,7 @@
             if k == half - 1:
                 total[s] = add_coords(me, kept, swapped, None, pieces[s])
                 pieces[s] = []
-            passing[s] = lax.ppermute(passing[s], ("dp", "mp"), apart)
+            passing[s] = lax.ppermute(passing[s], ("dp", "mp"), upward)
             pieces[s].append((passing[s], part + (k - 1) * depth, depth))
 
     coords, ups, downs = [None] * STREAMS, [None] * STREAMS, [None] * STREAMS
@@ -427,15 +416,15 @@
         sums = [near + lax.ppermute(near, "mp", partners)]
         sums += [lax.ppermute(sums[0], "mp", [(a, (a + k) % m) for a in range(m)]) for k in range(2, m, 2)]
         last = half_rows(me, passing[s])
-        last = lax.ppermute(last, ("dp", "mp"), apart)
+        last = lax.ppermute(last, ("dp", "mp"), upward)
         lasts = [last, lax.ppermute(last, "mp", partners)]
         coords[s], ups[s], downs[s] = first_partials(here, me, grad_out, sums, fars, lasts, n, m)
         ups[s], downs[s] = hop(ups[s], downs[s])
     for k in range(2, half + 1):
         for s in streams:
             ups[s], downs[s] = [
-                next_partials(here, grad_out, coords[s], came, n, half + 1 - k, way == "up")
-                for way, came in (("up", ups[s]), ("down", downs[s]))
+                next_partials(here, grad_out, coords[s], came, n, half + 1 - k, way == WAYS[0])
+                for way, came in zip(WAYS, (ups[s], downs[s]), strict=True)
             ]
             ups[s], downs[s] = hop(ups[s], downs[s])
     projected = [None] * STREAMS

time: 118 us -> 117 us (level)
  waiting for transfers between devices: 37.1 us -> 34.1 us
  Pallas kernels: 25.1 us -> 26.9 us
    ppermute x40, waiting for transfers between devices: 33.6 us -> 30.8 us  [the longest x16 12.4 us: hop(): lax.ppermute(to_up, ('dp', 'mp'), upward)]
    pallas_call x2 -> x4, Pallas kernels: 2.82 us -> 4.58 us  [the longest x2 2.67 us: nearer_columns(): pl.pallas_call(kernel, out_shape=tuple((pltpu.VMEM((tokens, size), activa...]
  transfers between devices with their start and end apart: 50 -> 50, of which waited for: 22 -> 23; matrix products, arithmetic and copies ran while one was open for 0% -> 0% of each run, Pallas kernels for 18% -> 20%
where the time goes in v6:
time: 117 us
  starting transfers between devices  54.3 us (46%)
  waiting for transfers between devices  34.1 us (29%)
  Pallas kernels  26.9 us (23%)
  between operations  1.17 us (1%)
    ppermute x16, starting transfers between devices, hop(): lax.ppermute(to_up, ('dp', 'mp'), upward)  26 us
    ppermute x16, waiting for transfers between devices, hop(): lax.ppermute(to_up, ('dp', 'mp'), upward)  12.4 us
    ppermute x6, starting transfers between devices, on_ring(): passing[s] = lax.ppermute(passing[s], ('dp', 'mp'), upward)  11.8 us
    ppermute x16, waiting for transfers between devices, hop(): lax.ppermute(to_down, ('dp', 'mp'), downward)  11 us
    pallas_call x5, Pallas kernels, write_update(): pl.pallas_call(kernel, out_shape=jax.ShapeDtypeStruct((depth, all_columns...  10.7 us
    ppermute x16, starting transfers between devices, hop(): lax.ppermute(to_down, ('dp', 'mp'), downward)  7.42 us
    pallas_call x12, Pallas kernels, next_partials(): pl.pallas_call(kernel, out_shape=pltpu.VMEM((cols, width), jnp.bfloat16),...  5.66 us
    ppermute x6, waiting for transfers between devices, on_ring(): passing[s] = lax.ppermute(passing[s], ('dp', 'mp'), upward)  5.43 us
  transfers between devices with their start and end apart: 50, of which 23 were waited for; matrix products, arithmetic and copies ran while one was open for 0% of the time, Pallas kernels for 20%

profile of v6, /device:TPU:0, one launch (start us, length us, event | category | flops | bytes accessed | tf_op | source)
XLA Modules:
  0.0 116.5 jit_solution(4734815292019357434)
XLA Ops:
  0.7 1.5 %shard_map.77 = (bf16[128,3584]{1,0:T(8,128)(2,1)S(1)}, bf16[128,1024]{1,0:T(8,128)(2,1)S(1)}) custom-call(s32[1]{0:T(128)} %bitcast.here_ref, s32[1]{0:T(128)} %bitcast.1.me_ref, bf16[128,8192]{1,0:T(8,128)(2,1)} %source.1), custom_call_target="tpu_custom_call" | custom-call | tf_op jit(solution)/shard_map/pallas_call | solution.py:116
  2.1 0.6 collective-permute-start
  2.7 1.0 shard_map.90.refs_2_
  3.6 2.6 %collective-permute-start.23 = (bf16[1024,128]{1,0:T(8,128)(2,1)S(1)}, bf16[1024,128]{1,0:T(8,128)(2,1)S(1)}, u32[]{:S(2)}, u32[]{:S(2)}) collective-permute-start(bf16[1024,128]{1,0:T(8,128)(2,1)S(1)} %shard_map.90.refs_2_), channel_id=1, source_target_pairs={{0,8},{8,16},{16,24},{24,28},{28,20},{20,12},{12,4},{4,0},{9,1},{1... | collective-permute-start | bytes 786440 | tf_op jit(solution)/shard_map/ppermute | solution.py:410
  6.3 1.0 shard_map.78.refs_2_
  7.2 1.6 %collective-permute-start.1 = (bf16[1024,128]{1,0:T(8,128)(2,1)S(1)}, bf16[1024,128]{1,0:T(8,128)(2,1)S(1)}, u32[]{:S(2)}, u32[]{:S(2)}) collective-permute-start(bf16[1024,128]{1,0:T(8,128)(2,1)S(1)} %shard_map.78.refs_2_), channel_id=1, source_target_pairs={{0,8},{8,16},{16,24},{24,28},{28,20},{20,12},{12,4},{4,0},{9,1},{1... | collective-permute-start | bytes 786440 | tf_op jit(solution)/shard_map/ppermute | solution.py:410
  8.9 1.7 %collective-permute-done.23.refs_3_ = bf16[1024,128]{1,0:T(8,128)(2,1)S(1)} collective-permute-done((bf16[1024,128]{1,0:T(8,128)(2,1)S(1)}, bf16[1024,128]{1,0:T(8,128)(2,1)S(1)}, u32[]{:S(2)}, u32[]{:S(2)}) %collective-permute-start.23) | collective-permute-done | bytes 262176 | tf_op jit(solution)/shard_map/ppermute | solution.py:410
  10.6 2.1 %collective-permute-start.24 = (bf16[1024,128]{1,0:T(8,128)(2,1)S(1)}, bf16[1024,128]{1,0:T(8,128)(2,1)S(1)}, u32[]{:S(2)}, u32[]{:S(2)}) collective-permute-start(bf16[1024,128]{1,0:T(8,128)(2,1)S(1)} %collective-permute-done.23.refs_3_), channel_id=1, source_target_pairs={{0,8},{8,16},{16,24},{24,28},{28,20},{20,12},{12,4},{4,0},{9,1},{1... | collective-permute-start | bytes 786440 | tf_op jit(solution)/shard_map/ppermute | solution.py:410
  12.6 1.0 collective-permute-done.1.refs_3_
  13.7 1.8 %collective-permute-start.2 = (bf16[1024,128]{1,0:T(8,128)(2,1)S(1)}, bf16[1024,128]{1,0:T(8,128)(2,1)S(1)}, u32[]{:S(2)}, u32[]{:S(2)}) collective-permute-start(bf16[1024,128]{1,0:T(8,128)(2,1)S(1)} %collective-permute-done.1.refs_3_), channel_id=1, source_target_pairs={{0,8},{8,16},{16,24},{24,28},{28,20},{20,12},{12,4},{4,0},{9,1},{1... | collective-permute-start | bytes 786440 | tf_op jit(solution)/shard_map/ppermute | solution.py:410
  15.4 1.5 %collective-permute-done.24.refs_4_ = bf16[1024,128]{1,0:T(8,128)(2,1)S(1)} collective-permute-done((bf16[1024,128]{1,0:T(8,128)(2,1)S(1)}, bf16[1024,128]{1,0:T(8,128)(2,1)S(1)}, u32[]{:S(2)}, u32[]{:S(2)}) %collective-permute-start.24) | collective-permute-done | bytes 262176 | tf_op jit(solution)/shard_map/ppermute | solution.py:410
  16.9 2.1 %collective-permute-start.25 = (bf16[1024,128]{1,0:T(8,128)(2,1)S(1)}, bf16[1024,128]{1,0:T(8,128)(2,1)S(1)}, u32[]{:S(2)}, u32[]{:S(2)}) collective-permute-start(bf16[1024,128]{1,0:T(8,128)(2,1)S(1)} %collective-permute-done.24.refs_4_), channel_id=1, source_target_pairs={{0,8},{8,16},{16,24},{24,28},{28,20},{20,12},{12,4},{4,0},{9,1},{1... | collective-permute-start | bytes 786440 | tf_op jit(solution)/shard_map/ppermute | solution.py:410
  19.0 1.5 %collective-permute-start.7 = (bf16[128,1024]{1,0:T(8,128)(2,1)S(1)}, bf16[128,1024]{1,0:T(8,128)(2,1)S(1)}, u32[]{:S(2)}, u32[]{:S(2)}) collective-permute-start(bf16[128,1024]{1,0:T(8,128)(2,1)S(1)} %get-tuple-element.26.refs_2_), channel_id=1, source_target_pairs={{0,2},{1,3},{2,0},{3,1},{4,6},{5,7},{6,4},{7,5},{8,10},{9,11},{10,... | collective-permute-start | bytes 786440 | tf_op jit(solution)/shard_map/ppermute | solution.py:402
  20.5 1.6 %collective-permute-start.3 = (bf16[1024,128]{1,0:T(8,128)(2,1)S(1)}, bf16[1024,128]{1,0:T(8,128)(2,1)S(1)}, u32[]{:S(2)}, u32[]{:S(2)}) collective-permute-start(bf16[1024,128]{1,0:T(8,128)(2,1)S(1)} %collective-permute-done.2.refs_4_), channel_id=1, source_target_pairs={{0,8},{8,16},{16,24},{24,28},{28,20},{20,12},{12,4},{4,0},{9,1},{1... | collective-permute-start | bytes 786440 | tf_op jit(solution)/shard_map/ppermute | solution.py:410
  22.1 1.2 %collective-permute-done.25.refs_3_.source = bf16[1024,128]{1,0:T(8,128)(2,1)S(1)} collective-permute-done((bf16[1024,128]{1,0:T(8,128)(2,1)S(1)}, bf16[1024,128]{1,0:T(8,128)(2,1)S(1)}, u32[]{:S(2)}, u32[]{:S(2)}) %collective-permute-start.25) | collective-permute-done | bytes 262176 | tf_op jit(solution)/shard_map/ppermute | solution.py:410
  23.3 2.1 %collective-permute-start.28 = (bf16[512,128]{1,0:T(8,128)(2,1)S(1)}, bf16[512,128]{1,0:T(8,128)(2,1)S(1)}, u32[]{:S(2)}, u32[]{:S(2)}) collective-permute-start(bf16[512,128]{1,0:T(8,128)(2,1)S(1)} %shard_map.93), channel_id=1, source_target_pairs={{0,8},{8,16},{16,24},{24,28},{28,20},{20,12},{12,4},{4,0},{9,1},{1... | collective-permute-start | bytes 393224 | tf_op jit(solution)/shard_map/ppermute | solution.py:419
  25.5 1.2 %shard_map.76.refs_0_ = bf16[128,3584]{1,0:T(8,128)(2,1)S(1)} custom-call(s32[1]{0:T(128)} %bitcast.here_ref, s32[1]{0:T(128)} %bitcast.1.me_ref, bf16[128,8192]{1,0:T(8,128)(2,1)} %source.1), custom_call_target="tpu_custom_call" | custom-call | tf_op jit(solution)/shard_map/pallas_call | solution.py:116
  26.7 0.6 collective-permute-start.8
  27.3 0.5 shard_map.91.refs_2_
  28.2 1.6 %collective-permute-start.9 = (bf16[512,128]{1,0:T(8,128)(2,1)S(1)}, bf16[512,128]{1,0:T(8,128)(2,1)S(1)}, u32[]{:S(2)}, u32[]{:S(2)}) collective-permute-start(bf16[512,128]{1,0:T(8,128)(2,1)S(1)} %shard_map.81), channel_id=1, source_target_pairs={{0,8},{8,16},{16,24},{24,28},{28,20},{20,12},{12,4},{4,0},{9,1},{1... | collective-permute-start | bytes 393224 | tf_op jit(solution)/shard_map/ppermute | solution.py:419
  31.2 2.0 %collective-permute-done.9.refs_6_ = bf16[512,128]{1,0:T(8,128)(2,1)S(1)} collective-permute-done((bf16[512,128]{1,0:T(8,128)(2,1)S(1)}, bf16[512,128]{1,0:T(8,128)(2,1)S(1)}, u32[]{:S(2)}, u32[]{:S(2)}) %collective-permute-start.9) | collective-permute-done | bytes 131104 | tf_op jit(solution)/shard_map/ppermute | solution.py:419
  33.2 1.5 %collective-permute-start.27 = (f32[256,128]{1,0:T(8,128)S(1)}, f32[256,128]{1,0:T(8,128)S(1)}, u32[]{:S(2)}, u32[]{:S(2)}) collective-permute-start(f32[256,128]{1,0:T(8,128)S(1)} %add.11.refs_0_), channel_id=1, source_target_pairs={{0,2},{1,3},{2,0},{3,1},{4,6},{5,7},{6,4},{7,5},{8,10},{9,11},{10,... | collective-permute-start | bytes 393224 | tf_op jit(solution)/shard_map/ppermute | solution.py:417
  34.7 0.6 collective-permute-start.5
  35.3 3.2 %collective-permute-done.27.refs_1_ = f32[256,128]{1,0:T(8,128)S(1)} collective-permute-done((f32[256,128]{1,0:T(8,128)S(1)}, f32[256,128]{1,0:T(8,128)S(1)}, u32[]{:S(2)}, u32[]{:S(2)}) %collective-permute-start.27) | collective-permute-done | bytes 131104 | tf_op jit(solution)/shard_map/ppermute | solution.py:417
  38.6 0.8 shard_map.94
  39.9 1.6 %collective-permute-start.30 = (bf16[448,128]{1,0:T(8,128)(2,1)S(1)}, bf16[448,128]{1,0:T(8,128)(2,1)S(1)}, u32[]{:S(2)}, u32[]{:S(2)}) collective-permute-start(bf16[448,128]{1,0:T(8,128)(2,1)S(1)} %get-tuple-element.32), channel_id=1, source_target_pairs={{0,8},{8,16},{16,24},{24,28},{28,20},{20,12},{12,4},{4,0},{9,1},{1... | collective-permute-start | bytes 344072 | tf_op jit(solution)/shard_map/ppermute | solution.py:381
  41.5 0.8 shard_map.82
  42.8 1.6 %collective-permute-start.11 = (bf16[448,128]{1,0:T(8,128)(2,1)S(1)}, bf16[448,128]{1,0:T(8,128)(2,1)S(1)}, u32[]{:S(2)}, u32[]{:S(2)}) collective-permute-start(bf16[448,128]{1,0:T(8,128)(2,1)S(1)} %get-tuple-element.28), channel_id=1, source_target_pairs={{0,8},{8,16},{16,24},{24,28},{28,20},{20,12},{12,4},{4,0},{9,1},{1... | collective-permute-start | bytes 344072 | tf_op jit(solution)/shard_map/ppermute | solution.py:381
  44.4 0.5 shard_map.98
  45.9 1.6 %collective-permute-start.31 = (bf16[896,128]{1,0:T(8,128)(2,1)S(1)}, bf16[896,128]{1,0:T(8,128)(2,1)S(1)}, u32[]{:S(2)}, u32[]{:S(2)}) collective-permute-start(bf16[896,128]{1,0:T(8,128)(2,1)S(1)} %shard_map.95), channel_id=1, source_target_pairs={{0,8},{8,16},{16,24},{24,28},{28,20},{20,12},{12,4},{4,0},{9,1},{1... | collective-permute-start | bytes 688136 | tf_op jit(solution)/shard_map/ppermute | solution.py:381
  47.6 0.5 collective-permute-done.15.arrived
  48.1 0.5 shard_map.86
  49.6 1.6 %collective-permute-start.12 = (bf16[896,128]{1,0:T(8,128)(2,1)S(1)}, bf16[896,128]{1,0:T(8,128)(2,1)S(1)}, u32[]{:S(2)}, u32[]{:S(2)}) collective-permute-start(bf16[896,128]{1,0:T(8,128)(2,1)S(1)} %shard_map.83), channel_id=1, source_target_pairs={{0,8},{8,16},{16,24},{24,28},{28,20},{20,12},{12,4},{4,0},{9,1},{1... | collective-permute-start | bytes 688136 | tf_op jit(solution)/shard_map/ppermute | solution.py:381
  51.2 2.3 %collective-permute-done.35.arrived = bf16[896,128]{1,0:T(8,128)(2,1)S(1)} collective-permute-done((bf16[896,128]{1,0:T(8,128)(2,1)S(1)}, bf16[896,128]{1,0:T(8,128)(2,1)S(1)}, u32[]{:S(2)}, u32[]{:S(2)}) %collective-permute-start.35) | collective-permute-done | bytes 229408 | tf_op jit(solution)/shard_map/ppermute | solution.py:381
  55.0 1.6 %collective-permute-start.32 = (bf16[896,128]{1,0:T(8,128)(2,1)S(1)}, bf16[896,128]{1,0:T(8,128)(2,1)S(1)}, u32[]{:S(2)}, u32[]{:S(2)}) collective-permute-start(bf16[896,128]{1,0:T(8,128)(2,1)S(1)} %shard_map.96), channel_id=1, source_target_pairs={{0,8},{8,16},{16,24},{24,28},{28,20},{20,12},{12,4},{4,0},{9,1},{1... | collective-permute-start | bytes 688136 | tf_op jit(solution)/shard_map/ppermute | solution.py:381
  56.6 1.8 %collective-permute-done.16.arrived = bf16[896,128]{1,0:T(8,128)(2,1)S(1)} collective-permute-done((bf16[896,128]{1,0:T(8,128)(2,1)S(1)}, bf16[896,128]{1,0:T(8,128)(2,1)S(1)}, u32[]{:S(2)}, u32[]{:S(2)}) %collective-permute-start.16) | collective-permute-done | bytes 229408 | tf_op jit(solution)/shard_map/ppermute | solution.py:381
  59.9 1.6 %collective-permute-start.13 = (bf16[896,128]{1,0:T(8,128)(2,1)S(1)}, bf16[896,128]{1,0:T(8,128)(2,1)S(1)}, u32[]{:S(2)}, u32[]{:S(2)}) collective-permute-start(bf16[896,128]{1,0:T(8,128)(2,1)S(1)} %shard_map.84), channel_id=1, source_target_pairs={{0,8},{8,16},{16,24},{24,28},{28,20},{20,12},{12,4},{4,0},{9,1},{1... | collective-permute-start | bytes 688136 | tf_op jit(solution)/shard_map/ppermute | solution.py:381
  61.5 1.8 %collective-permute-done.36.arrived = bf16[896,128]{1,0:T(8,128)(2,1)S(1)} collective-permute-done((bf16[896,128]{1,0:T(8,128)(2,1)S(1)}, bf16[896,128]{1,0:T(8,128)(2,1)S(1)}, u32[]{:S(2)}, u32[]{:S(2)}) %collective-permute-start.36) | collective-permute-done | bytes 229408 | tf_op jit(solution)/shard_map/ppermute | solution.py:381
  64.8 1.6 %collective-permute-start.33 = (bf16[896,128]{1,0:T(8,128)(2,1)S(1)}, bf16[896,128]{1,0:T(8,128)(2,1)S(1)}, u32[]{:S(2)}, u32[]{:S(2)}) collective-permute-start(bf16[896,128]{1,0:T(8,128)(2,1)S(1)} %shard_map.97), channel_id=1, source_target_pairs={{0,8},{8,16},{16,24},{24,28},{28,20},{20,12},{12,4},{4,0},{9,1},{1... | collective-permute-start | bytes 688136 | tf_op jit(solution)/shard_map/ppermute | solution.py:381
  66.4 1.8 %collective-permute-done.17.arrived = bf16[896,128]{1,0:T(8,128)(2,1)S(1)} collective-permute-done((bf16[896,128]{1,0:T(8,128)(2,1)S(1)}, bf16[896,128]{1,0:T(8,128)(2,1)S(1)}, u32[]{:S(2)}, u32[]{:S(2)}) %collective-permute-start.17) | collective-permute-done | bytes 229408 | tf_op jit(solution)/shard_map/ppermute | solution.py:381
  69.7 1.8 %collective-permute-start.14 = (bf16[896,128]{1,0:T(8,128)(2,1)S(1)}, bf16[896,128]{1,0:T(8,128)(2,1)S(1)}, u32[]{:S(2)}, u32[]{:S(2)}) collective-permute-start(bf16[896,128]{1,0:T(8,128)(2,1)S(1)} %shard_map.85), channel_id=1, source_target_pairs={{0,8},{8,16},{16,24},{24,28},{28,20},{20,12},{12,4},{4,0},{9,1},{1... | collective-permute-start | bytes 688136 | tf_op jit(solution)/shard_map/ppermute | solution.py:381
  71.5 1.6 %collective-permute-done.37.in_down = bf16[896,128]{1,0:T(8,128)(2,1)S(1)} collective-permute-done((bf16[896,128]{1,0:T(8,128)(2,1)S(1)}, bf16[896,128]{1,0:T(8,128)(2,1)S(1)}, u32[]{:S(2)}, u32[]{:S(2)}) %collective-permute-start.37) | collective-permute-done | bytes 229408 | tf_op jit(solution)/shard_map/ppermute | solution.py:381
  73.1 1.0 collective-permute-done.33.in_up
  74.2 0.7 shard_map.101
  74.8 1.6 %collective-permute-start.38 = (bf16[896,128]{1,0:T(8,128)(2,1)S(1)}, bf16[896,128]{1,0:T(8,128)(2,1)S(1)}, u32[]{:S(2)}, u32[]{:S(2)}) collective-permute-start(bf16[896,128]{1,0:T(8,128)(2,1)S(1)} %get-tuple-element.34.refs_1_), channel_id=1, source_target_pairs={{0,8},{8,16},{16,24},{24,28},{28,20},{20,12},{12,4},{4,0},{9,1},{1... | collective-permute-start | bytes 688136 | tf_op jit(solution)/shard_map/ppermute | solution.py:381
  76.9 1.1 collective-permute-done.18.in_down
  78.1 0.6 shard_map.89
  78.7 1.7 %collective-permute-start.19 = (bf16[896,128]{1,0:T(8,128)(2,1)S(1)}, bf16[896,128]{1,0:T(8,128)(2,1)S(1)}, u32[]{:S(2)}, u32[]{:S(2)}) collective-permute-start(bf16[896,128]{1,0:T(8,128)(2,1)S(1)} %get-tuple-element.30.refs_0_), channel_id=1, source_target_pairs={{0,8},{8,16},{16,24},{24,28},{28,20},{20,12},{12,4},{4,0},{9,1},{1... | collective-permute-start | bytes 688136 | tf_op jit(solution)/shard_map/ppermute | solution.py:381
  80.8 2.2 %collective-permute-done.38.refs_1_ = bf16[896,128]{1,0:T(8,128)(2,1)S(1)} collective-permute-done((bf16[896,128]{1,0:T(8,128)(2,1)S(1)}, bf16[896,128]{1,0:T(8,128)(2,1)S(1)}, u32[]{:S(2)}, u32[]{:S(2)}) %collective-permute-start.38) | collective-permute-done | bytes 229408 | tf_op jit(solution)/shard_map/ppermute | solution.py:381
  83.0 1.6 %collective-permute-start.39 = (bf16[896,128]{1,0:T(8,128)(2,1)S(1)}, bf16[896,128]{1,0:T(8,128)(2,1)S(1)}, u32[]{:S(2)}, u32[]{:S(2)}) collective-permute-start(bf16[896,128]{1,0:T(8,128)(2,1)S(1)} %collective-permute-done.38.refs_1_), channel_id=1, source_target_pairs={{0,8},{8,16},{16,24},{24,28},{28,20},{20,12},{12,4},{4,0},{9,1},{1... | collective-permute-start | bytes 688136 | tf_op jit(solution)/shard_map/ppermute | solution.py:381
  85.1 2.9 %collective-permute-done.19.refs_0_ = bf16[896,128]{1,0:T(8,128)(2,1)S(1)} collective-permute-done((bf16[896,128]{1,0:T(8,128)(2,1)S(1)}, bf16[896,128]{1,0:T(8,128)(2,1)S(1)}, u32[]{:S(2)}, u32[]{:S(2)}) %collective-permute-start.19) | collective-permute-done | bytes 229408 | tf_op jit(solution)/shard_map/ppermute | solution.py:381
  87.9 1.6 %collective-permute-start.20 = (bf16[896,128]{1,0:T(8,128)(2,1)S(1)}, bf16[896,128]{1,0:T(8,128)(2,1)S(1)}, u32[]{:S(2)}, u32[]{:S(2)}) collective-permute-start(bf16[896,128]{1,0:T(8,128)(2,1)S(1)} %collective-permute-done.19.refs_0_), channel_id=1, source_target_pairs={{0,8},{8,16},{16,24},{24,28},{28,20},{20,12},{12,4},{4,0},{9,1},{1... | collective-permute-start | bytes 688136 | tf_op jit(solution)/shard_map/ppermute | solution.py:381
  90.0 2.9 %collective-permute-done.39.refs_1_ = bf16[896,128]{1,0:T(8,128)(2,1)S(1)} collective-permute-done((bf16[896,128]{1,0:T(8,128)(2,1)S(1)}, bf16[896,128]{1,0:T(8,128)(2,1)S(1)}, u32[]{:S(2)}, u32[]{:S(2)}) %collective-permute-start.39) | collective-permute-done | bytes 229408 | tf_op jit(solution)/shard_map/ppermute | solution.py:381
  92.9 1.6 %collective-permute-start.40 = (bf16[896,128]{1,0:T(8,128)(2,1)S(1)}, bf16[896,128]{1,0:T(8,128)(2,1)S(1)}, u32[]{:S(2)}, u32[]{:S(2)}) collective-permute-start(bf16[896,128]{1,0:T(8,128)(2,1)S(1)} %collective-permute-done.39.refs_1_), channel_id=1, source_target_pairs={{0,8},{8,16},{16,24},{24,28},{28,20},{20,12},{12,4},{4,0},{9,1},{1... | collective-permute-start | bytes 688136 | tf_op jit(solution)/shard_map/ppermute | solution.py:381
  94.9 2.9 %collective-permute-done.20.refs_0_ = bf16[896,128]{1,0:T(8,128)(2,1)S(1)} collective-permute-done((bf16[896,128]{1,0:T(8,128)(2,1)S(1)}, bf16[896,128]{1,0:T(8,128)(2,1)S(1)}, u32[]{:S(2)}, u32[]{:S(2)}) %collective-permute-start.20) | collective-permute-done | bytes 229408 | tf_op jit(solution)/shard_map/ppermute | solution.py:381
  97.8 1.6 %collective-permute-start.21 = (bf16[896,128]{1,0:T(8,128)(2,1)S(1)}, bf16[896,128]{1,0:T(8,128)(2,1)S(1)}, u32[]{:S(2)}, u32[]{:S(2)}) collective-permute-start(bf16[896,128]{1,0:T(8,128)(2,1)S(1)} %collective-permute-done.20.refs_0_), channel_id=1, source_target_pairs={{0,8},{8,16},{16,24},{24,28},{28,20},{20,12},{12,4},{4,0},{9,1},{1... | collective-permute-start | bytes 688136 | tf_op jit(solution)/shard_map/ppermute | solution.py:381
  99.8 1.4 %shard_map.107 = (f32[896,256]{1,0:T(8,128)}, f32[896,256]{1,0:T(8,128)}) custom-call(f32[896,128]{1,0:T(8,128)S(1)} %get-tuple-element.35.refs_0_, f32[896,128]{1,0:T(8,128)S(1)} %get-tuple-element.36.refs_1_, f32[896,256]{1,0:T(8,128)S(1)} %copy-done.1, f32[896,256]{1,0:T(8,128)S(1)} %copy-done.2), custom_call_target="tpu_custom_call" | custom-call | bytes 6291456 | tf_op jit(solution)/shard_map/pallas_call | solution.py:304
  101.2 1.7 %shard_map.102.refs_4_ = bf16[1024,7168]{1,0:T(8,128)(2,1)} custom-call(s32[1]{0:T(128)} %bitcast.here_ref, bf16[1024,256]{1,0:T(8,128)(2,1)S(1)} %copy-done, bf16[896,128]{1,0:T(8,128)(2,1)S(1)} %get-tuple-element.30.refs_0_, bf16[896,128]{1,0:T(8,128)(2,1)S(1)} %get-tuple-element.34.refs_1_), custom_call_target="tpu_custom_call" | custom-call | flops 469762048 | bytes 1835008 | tf_op jit(solution)/shard_map/pallas_call | solution.py:350
  102.9 2.4 %shard_map.103.refs_4_ = bf16[1024,7168]{1,0:T(8,128)(2,1)} custom-call(s32[1]{0:T(128)} %bitcast.here_ref, bf16[1024,256]{1,0:T(8,128)(2,1)S(1)} %copy-done, bf16[896,128]{1,0:T(8,128)(2,1)S(1)} %collective-permute-done.19.refs_0_, bf16[896,128]{1,0:T(8,128)(2,1)S(1)} %collective-permute-done.38.refs_1_, ...), custom_call_target="tpu_custom_call", output_to_operand_aliasing={{}: (6, {})} | custom-call | flops 939524096 | bytes 3670016 | tf_op jit(solution)/shard_map/pallas_call | solution.py:350
  105.3 1.6 %collective-permute-start.41 = (bf16[448,128]{1,0:T(8,128)(2,1)S(1)}, bf16[448,128]{1,0:T(8,128)(2,1)S(1)}, u32[]{:S(2)}, u32[]{:S(2)}) collective-permute-start(bf16[448,128]{1,0:T(8,128)(2,1)S(1)} %slice.17), channel_id=1, source_target_pairs={{0,8},{8,16},{16,24},{24,28},{28,20},{20,12},{12,4},{4,0},{9,1},{1... | collective-permute-start | bytes 344072 | tf_op jit(solution)/shard_map/ppermute | solution.py:381
  107.6 1.6 %collective-permute-start.22 = (bf16[448,128]{1,0:T(8,128)(2,1)S(1)}, bf16[448,128]{1,0:T(8,128)(2,1)S(1)}, u32[]{:S(2)}, u32[]{:S(2)}) collective-permute-start(bf16[448,128]{1,0:T(8,128)(2,1)S(1)} %slice.16), channel_id=1, source_target_pairs={{0,8},{8,16},{16,24},{24,28},{28,20},{20,12},{12,4},{4,0},{9,1},{1... | collective-permute-start | bytes 344072 | tf_op jit(solution)/shard_map/ppermute | solution.py:381
  109.8 2.4 %shard_map.104.refs_4_ = bf16[1024,7168]{1,0:T(8,128)(2,1)} custom-call(s32[1]{0:T(128)} %bitcast.here_ref, bf16[1024,256]{1,0:T(8,128)(2,1)S(1)} %copy-done, bf16[896,128]{1,0:T(8,128)(2,1)S(1)} %collective-permute-done.20.refs_0_, bf16[896,128]{1,0:T(8,128)(2,1)S(1)} %collective-permute-done.39.refs_1_, ...), custom_call_target="tpu_custom_call", output_to_operand_aliasing={{}: (6, {})} | custom-call | flops 939524096 | bytes 3670016 | tf_op jit(solution)/shard_map/pallas_call | solution.py:350
  112.2 2.4 %shard_map.105.refs_4_ = bf16[1024,7168]{1,0:T(8,128)(2,1)} custom-call(s32[1]{0:T(128)} %bitcast.here_ref, bf16[1024,256]{1,0:T(8,128)(2,1)S(1)} %copy-done, bf16[896,128]{1,0:T(8,128)(2,1)S(1)} %collective-permute-done.21.refs_0_, bf16[896,128]{1,0:T(8,128)(2,1)S(1)} %collective-permute-done.40.refs_1_, ...), custom_call_target="tpu_custom_call", output_to_operand_aliasing={{}: (6, {})} | custom-call | flops 939524096 | bytes 3670016 | tf_op jit(solution)/shard_map/pallas_call | solution.py:350
  114.7 1.7 %shard_map.106 = bf16[1024,7168]{1,0:T(8,128)(2,1)} custom-call(s32[1]{0:T(128)} %bitcast.here_ref, bf16[1024,256]{1,0:T(8,128)(2,1)S(1)} %copy-done, bf16[448,128]{1,0:T(8,128)(2,1)S(1)} %collective-permute-done.22.refs_0_, bf16[448,128]{1,0:T(8,128)(2,1)S(1)} %collective-permute-done.41.refs_1_, ...), custom_call_target="tpu_custom_call", output_to_operand_aliasing={{}: (6, {})} | custom-call | flops 469762048 | bytes 1835008 | tf_op jit(solution)/shard_map/pallas_call | solution.py:350
  (85 shorter events, 14.5 us)
Async XLA Ops:
  0.6 37.9 %slice-start = ((s8[7340032]{0:T(1024)(128)(4,1)}), s8[3145728]{0:T(1024)(128)(4,1)S(1)}, s32[]{:S(2)}) async-start(s8[7340032]{0:T(1024)(128)(4,1)} %bitcast.2), calls=%async_computation | async-start | bytes 6291456
  2.1 25.2 %collective-permute-start = (bf16[128,3584]{1,0:T(8,128)(2,1)S(1)}, bf16[128,3584]{1,0:T(8,128)(2,1)S(1)}, u32[]{:S(2)}, u32[]{:S(2)}) collective-permute-start(bf16[128,3584]{1,0:T(8,128)(2,1)S(1)} %get-tuple-element.25), channel_id=1, source_target_pairs={{0,1},{1,0},{2,3},{3,2},{4,5},{5,4},{6,7},{7,6},{8,9},{9,8},{10,11... | collective-permute-start | bytes 2752520 | tf_op jit(solution)/shard_map/ppermute | solution.py:399
  3.6 6.9 %collective-permute-start.23 = (bf16[1024,128]{1,0:T(8,128)(2,1)S(1)}, bf16[1024,128]{1,0:T(8,128)(2,1)S(1)}, u32[]{:S(2)}, u32[]{:S(2)}) collective-permute-start(bf16[1024,128]{1,0:T(8,128)(2,1)S(1)} %shard_map.90.refs_2_), channel_id=1, source_target_pairs={{0,8},{8,16},{16,24},{24,28},{28,20},{20,12},{12,4},{4,0},{9,1},{1... | collective-permute-start | bytes 786440 | tf_op jit(solution)/shard_map/ppermute | solution.py:410
  7.2 6.4 %collective-permute-start.1 = (bf16[1024,128]{1,0:T(8,128)(2,1)S(1)}, bf16[1024,128]{1,0:T(8,128)(2,1)S(1)}, u32[]{:S(2)}, u32[]{:S(2)}) collective-permute-start(bf16[1024,128]{1,0:T(8,128)(2,1)S(1)} %shard_map.78.refs_2_), channel_id=1, source_target_pairs={{0,8},{8,16},{16,24},{24,28},{28,20},{20,12},{12,4},{4,0},{9,1},{1... | collective-permute-start | bytes 786440 | tf_op jit(solution)/shard_map/ppermute | solution.py:410
  10.6 6.4 %collective-permute-start.24 = (bf16[1024,128]{1,0:T(8,128)(2,1)S(1)}, bf16[1024,128]{1,0:T(8,128)(2,1)S(1)}, u32[]{:S(2)}, u32[]{:S(2)}) collective-permute-start(bf16[1024,128]{1,0:T(8,128)(2,1)S(1)} %collective-permute-done.23.refs_3_), channel_id=1, source_target_pairs={{0,8},{8,16},{16,24},{24,28},{28,20},{20,12},{12,4},{4,0},{9,1},{1... | collective-permute-start | bytes 786440 | tf_op jit(solution)/shard_map/ppermute | solution.py:410
  13.7 6.8 %collective-permute-start.2 = (bf16[1024,128]{1,0:T(8,128)(2,1)S(1)}, bf16[1024,128]{1,0:T(8,128)(2,1)S(1)}, u32[]{:S(2)}, u32[]{:S(2)}) collective-permute-start(bf16[1024,128]{1,0:T(8,128)(2,1)S(1)} %collective-permute-done.1.refs_3_), channel_id=1, source_target_pairs={{0,8},{8,16},{16,24},{24,28},{28,20},{20,12},{12,4},{4,0},{9,1},{1... | collective-permute-start | bytes 786440 | tf_op jit(solution)/shard_map/ppermute | solution.py:410
  16.9 6.4 %collective-permute-start.25 = (bf16[1024,128]{1,0:T(8,128)(2,1)S(1)}, bf16[1024,128]{1,0:T(8,128)(2,1)S(1)}, u32[]{:S(2)}, u32[]{:S(2)}) collective-permute-start(bf16[1024,128]{1,0:T(8,128)(2,1)S(1)} %collective-permute-done.24.refs_4_), channel_id=1, source_target_pairs={{0,8},{8,16},{16,24},{24,28},{28,20},{20,12},{12,4},{4,0},{9,1},{1... | collective-permute-start | bytes 786440 | tf_op jit(solution)/shard_map/ppermute | solution.py:410
  19.0 7.7 %collective-permute-start.7 = (bf16[128,1024]{1,0:T(8,128)(2,1)S(1)}, bf16[128,1024]{1,0:T(8,128)(2,1)S(1)}, u32[]{:S(2)}, u32[]{:S(2)}) collective-permute-start(bf16[128,1024]{1,0:T(8,128)(2,1)S(1)} %get-tuple-element.26.refs_2_), channel_id=1, source_target_pairs={{0,2},{1,3},{2,0},{3,1},{4,6},{5,7},{6,4},{7,5},{8,10},{9,11},{10,... | collective-permute-start | bytes 786440 | tf_op jit(solution)/shard_map/ppermute | solution.py:402
  20.5 7.7 %collective-permute-start.3 = (bf16[1024,128]{1,0:T(8,128)(2,1)S(1)}, bf16[1024,128]{1,0:T(8,128)(2,1)S(1)}, u32[]{:S(2)}, u32[]{:S(2)}) collective-permute-start(bf16[1024,128]{1,0:T(8,128)(2,1)S(1)} %collective-permute-done.2.refs_4_), channel_id=1, source_target_pairs={{0,8},{8,16},{16,24},{24,28},{28,20},{20,12},{12,4},{4,0},{9,1},{1... | collective-permute-start | bytes 786440 | tf_op jit(solution)/shard_map/ppermute | solution.py:410
  23.3 7.3 %collective-permute-start.28 = (bf16[512,128]{1,0:T(8,128)(2,1)S(1)}, bf16[512,128]{1,0:T(8,128)(2,1)S(1)}, u32[]{:S(2)}, u32[]{:S(2)}) collective-permute-start(bf16[512,128]{1,0:T(8,128)(2,1)S(1)} %shard_map.93), channel_id=1, source_target_pairs={{0,8},{8,16},{16,24},{24,28},{28,20},{20,12},{12,4},{4,0},{9,1},{1... | collective-permute-start | bytes 393224 | tf_op jit(solution)/shard_map/ppermute | solution.py:419
  25.4 9.3 %collective-permute-start.6 = (bf16[128,1024]{1,0:T(8,128)(2,1)S(1)}, bf16[128,1024]{1,0:T(8,128)(2,1)S(1)}, u32[]{:S(2)}, u32[]{:S(2)}) collective-permute-start(bf16[128,1024]{1,0:T(8,128)(2,1)S(1)} %get-tuple-element.26.refs_2_), channel_id=1, source_target_pairs={{0,1},{1,0},{2,3},{3,2},{4,5},{5,4},{6,7},{7,6},{8,9},{9,8},{10,11... | collective-permute-start | bytes 786440 | tf_op jit(solution)/shard_map/ppermute | solution.py:400
  26.7 11.9 %slice-start.1 = ((s8[7340032]{0:T(1024)(128)(4,1)}), s8[4194304]{0:T(1024)(128)(4,1)S(1)}, s32[]{:S(2)}) async-start(s8[7340032]{0:T(1024)(128)(4,1)} %bitcast.2), calls=%async_computation.1 | async-start | bytes 8388608
  26.7 8.6 %collective-permute-start.8 = (bf16[128,1024]{1,0:T(8,128)(2,1)S(1)}, bf16[128,1024]{1,0:T(8,128)(2,1)S(1)}, u32[]{:S(2)}, u32[]{:S(2)}) collective-permute-start(bf16[128,1024]{1,0:T(8,128)(2,1)S(1)} %collective-permute-done.7.refs_4_), channel_id=1, source_target_pairs={{0,1},{1,0},{2,3},{3,2},{4,5},{5,4},{6,7},{7,6},{8,9},{9,8},{10,11... | collective-permute-start | bytes 786440 | tf_op jit(solution)/shard_map/ppermute | solution.py:403
  28.1 2.6 %collective-permute-start.26 = (f32[256,128]{1,0:T(8,128)S(1)}, f32[256,128]{1,0:T(8,128)S(1)}, u32[]{:S(2)}, u32[]{:S(2)}) collective-permute-start(f32[256,128]{1,0:T(8,128)S(1)} %shard_map.92), channel_id=1, source_target_pairs={{0,1},{1,0},{2,3},{3,2},{4,5},{5,4},{6,7},{7,6},{8,9},{9,8},{10,11... | collective-permute-start | bytes 393224 | tf_op jit(solution)/shard_map/ppermute | solution.py:416
  28.2 5.0 %collective-permute-start.9 = (bf16[512,128]{1,0:T(8,128)(2,1)S(1)}, bf16[512,128]{1,0:T(8,128)(2,1)S(1)}, u32[]{:S(2)}, u32[]{:S(2)}) collective-permute-start(bf16[512,128]{1,0:T(8,128)(2,1)S(1)} %shard_map.81), channel_id=1, source_target_pairs={{0,8},{8,16},{16,24},{24,28},{28,20},{20,12},{12,4},{4,0},{9,1},{1... | collective-permute-start | bytes 393224 | tf_op jit(solution)/shard_map/ppermute | solution.py:419
  30.6 4.1 %collective-permute-start.4 = (f32[256,128]{1,0:T(8,128)S(1)}, f32[256,128]{1,0:T(8,128)S(1)}, u32[]{:S(2)}, u32[]{:S(2)}) collective-permute-start(f32[256,128]{1,0:T(8,128)S(1)} %shard_map.80), channel_id=1, source_target_pairs={{0,1},{1,0},{2,3},{3,2},{4,5},{5,4},{6,7},{7,6},{8,9},{9,8},{10,11... | collective-permute-start | bytes 393224 | tf_op jit(solution)/shard_map/ppermute | solution.py:416
  30.7 4.6 %collective-permute-start.29 = (bf16[512,128]{1,0:T(8,128)(2,1)S(1)}, bf16[512,128]{1,0:T(8,128)(2,1)S(1)}, u32[]{:S(2)}, u32[]{:S(2)}) collective-permute-start(bf16[512,128]{1,0:T(8,128)(2,1)S(1)} %collective-permute-done.28.refs_6_), channel_id=1, source_target_pairs={{0,1},{1,0},{2,3},{3,2},{4,5},{5,4},{6,7},{7,6},{8,9},{9,8},{10,11... | collective-permute-start | bytes 393224 | tf_op jit(solution)/shard_map/ppermute | solution.py:420
  33.2 5.4 %collective-permute-start.27 = (f32[256,128]{1,0:T(8,128)S(1)}, f32[256,128]{1,0:T(8,128)S(1)}, u32[]{:S(2)}, u32[]{:S(2)}) collective-permute-start(f32[256,128]{1,0:T(8,128)S(1)} %add.11.refs_0_), channel_id=1, source_target_pairs={{0,2},{1,3},{2,0},{3,1},{4,6},{5,7},{6,4},{7,5},{8,10},{9,11},{10,... | collective-permute-start | bytes 393224 | tf_op jit(solution)/shard_map/ppermute | solution.py:417
  34.7 6.8 %collective-permute-start.10 = (bf16[512,128]{1,0:T(8,128)(2,1)S(1)}, bf16[512,128]{1,0:T(8,128)(2,1)S(1)}, u32[]{:S(2)}, u32[]{:S(2)}) collective-permute-start(bf16[512,128]{1,0:T(8,128)(2,1)S(1)} %collective-permute-done.9.refs_6_), channel_id=1, source_target_pairs={{0,1},{1,0},{2,3},{3,2},{4,5},{5,4},{6,7},{7,6},{8,9},{9,8},{10,11... | collective-permute-start | bytes 393224 | tf_op jit(solution)/shard_map/ppermute | solution.py:420
  34.7 6.8 %collective-permute-start.5 = (f32[256,128]{1,0:T(8,128)S(1)}, f32[256,128]{1,0:T(8,128)S(1)}, u32[]{:S(2)}, u32[]{:S(2)}) collective-permute-start(f32[256,128]{1,0:T(8,128)S(1)} %add.10.refs_0_), channel_id=1, source_target_pairs={{0,2},{1,3},{2,0},{3,1},{4,6},{5,7},{6,4},{7,5},{8,10},{9,11},{10,... | collective-permute-start | bytes 393224 | tf_op jit(solution)/shard_map/ppermute | solution.py:417
  39.4 5.0 %collective-permute-start.34 = (bf16[448,128]{1,0:T(8,128)(2,1)S(1)}, bf16[448,128]{1,0:T(8,128)(2,1)S(1)}, u32[]{:S(2)}, u32[]{:S(2)}) collective-permute-start(bf16[448,128]{1,0:T(8,128)(2,1)S(1)} %get-tuple-element.33), channel_id=1, source_target_pairs={{8,0},{16,8},{24,16},{28,24},{20,28},{12,20},{4,12},{0,4},{1,9},{9... | collective-permute-start | bytes 344072 | tf_op jit(solution)/shard_map/ppermute | solution.py:381
  39.9 5.5 %collective-permute-start.30 = (bf16[448,128]{1,0:T(8,128)(2,1)S(1)}, bf16[448,128]{1,0:T(8,128)(2,1)S(1)}, u32[]{:S(2)}, u32[]{:S(2)}) collective-permute-start(bf16[448,128]{1,0:T(8,128)(2,1)S(1)} %get-tuple-element.32), channel_id=1, source_target_pairs={{0,8},{8,16},{16,24},{24,28},{28,20},{20,12},{12,4},{4,0},{9,1},{1... | collective-permute-start | bytes 344072 | tf_op jit(solution)/shard_map/ppermute | solution.py:381
  42.4 5.7 %collective-permute-start.15 = (bf16[448,128]{1,0:T(8,128)(2,1)S(1)}, bf16[448,128]{1,0:T(8,128)(2,1)S(1)}, u32[]{:S(2)}, u32[]{:S(2)}) collective-permute-start(bf16[448,128]{1,0:T(8,128)(2,1)S(1)} %get-tuple-element.29), channel_id=1, source_target_pairs={{8,0},{16,8},{24,16},{28,24},{20,28},{12,20},{4,12},{0,4},{1,9},{9... | collective-permute-start | bytes 344072 | tf_op jit(solution)/shard_map/ppermute | solution.py:381
  42.8 6.2 %collective-permute-start.11 = (bf16[448,128]{1,0:T(8,128)(2,1)S(1)}, bf16[448,128]{1,0:T(8,128)(2,1)S(1)}, u32[]{:S(2)}, u32[]{:S(2)}) collective-permute-start(bf16[448,128]{1,0:T(8,128)(2,1)S(1)} %get-tuple-element.28), channel_id=1, source_target_pairs={{0,8},{8,16},{16,24},{24,28},{28,20},{20,12},{12,4},{4,0},{9,1},{1... | collective-permute-start | bytes 344072 | tf_op jit(solution)/shard_map/ppermute | solution.py:381
  44.9 8.5 %collective-permute-start.35 = (bf16[896,128]{1,0:T(8,128)(2,1)S(1)}, bf16[896,128]{1,0:T(8,128)(2,1)S(1)}, u32[]{:S(2)}, u32[]{:S(2)}) collective-permute-start(bf16[896,128]{1,0:T(8,128)(2,1)S(1)} %shard_map.98), channel_id=1, source_target_pairs={{8,0},{16,8},{24,16},{28,24},{20,28},{12,20},{4,12},{0,4},{1,9},{9... | collective-permute-start | bytes 688136 | tf_op jit(solution)/shard_map/ppermute | solution.py:381
  45.9 8.6 %collective-permute-start.31 = (bf16[896,128]{1,0:T(8,128)(2,1)S(1)}, bf16[896,128]{1,0:T(8,128)(2,1)S(1)}, u32[]{:S(2)}, u32[]{:S(2)}) collective-permute-start(bf16[896,128]{1,0:T(8,128)(2,1)S(1)} %shard_map.95), channel_id=1, source_target_pairs={{0,8},{8,16},{16,24},{24,28},{28,20},{20,12},{12,4},{4,0},{9,1},{1... | collective-permute-start | bytes 688136 | tf_op jit(solution)/shard_map/ppermute | solution.py:381
  48.6 9.8 %collective-permute-start.16 = (bf16[896,128]{1,0:T(8,128)(2,1)S(1)}, bf16[896,128]{1,0:T(8,128)(2,1)S(1)}, u32[]{:S(2)}, u32[]{:S(2)}) collective-permute-start(bf16[896,128]{1,0:T(8,128)(2,1)S(1)} %shard_map.86), channel_id=1, source_target_pairs={{8,0},{16,8},{24,16},{28,24},{20,28},{12,20},{4,12},{0,4},{1,9},{9... | collective-permute-start | bytes 688136 | tf_op jit(solution)/shard_map/ppermute | solution.py:381
  49.6 9.9 %collective-permute-start.12 = (bf16[896,128]{1,0:T(8,128)(2,1)S(1)}, bf16[896,128]{1,0:T(8,128)(2,1)S(1)}, u32[]{:S(2)}, u32[]{:S(2)}) collective-permute-start(bf16[896,128]{1,0:T(8,128)(2,1)S(1)} %shard_map.83), channel_id=1, source_target_pairs={{0,8},{8,16},{16,24},{24,28},{28,20},{20,12},{12,4},{4,0},{9,1},{1... | collective-permute-start | bytes 688136 | tf_op jit(solution)/shard_map/ppermute | solution.py:381
  53.9 9.4 %collective-permute-start.36 = (bf16[896,128]{1,0:T(8,128)(2,1)S(1)}, bf16[896,128]{1,0:T(8,128)(2,1)S(1)}, u32[]{:S(2)}, u32[]{:S(2)}) collective-permute-start(bf16[896,128]{1,0:T(8,128)(2,1)S(1)} %shard_map.99), channel_id=1, source_target_pairs={{8,0},{16,8},{24,16},{28,24},{20,28},{12,20},{4,12},{0,4},{1,9},{9... | collective-permute-start | bytes 688136 | tf_op jit(solution)/shard_map/ppermute | solution.py:381
  55.0 9.4 %collective-permute-start.32 = (bf16[896,128]{1,0:T(8,128)(2,1)S(1)}, bf16[896,128]{1,0:T(8,128)(2,1)S(1)}, u32[]{:S(2)}, u32[]{:S(2)}) collective-permute-start(bf16[896,128]{1,0:T(8,128)(2,1)S(1)} %shard_map.96), channel_id=1, source_target_pairs={{0,8},{8,16},{16,24},{24,28},{28,20},{20,12},{12,4},{4,0},{9,1},{1... | collective-permute-start | bytes 688136 | tf_op jit(solution)/shard_map/ppermute | solution.py:381
  58.8 9.4 %collective-permute-start.17 = (bf16[896,128]{1,0:T(8,128)(2,1)S(1)}, bf16[896,128]{1,0:T(8,128)(2,1)S(1)}, u32[]{:S(2)}, u32[]{:S(2)}) collective-permute-start(bf16[896,128]{1,0:T(8,128)(2,1)S(1)} %shard_map.87), channel_id=1, source_target_pairs={{8,0},{16,8},{24,16},{28,24},{20,28},{12,20},{4,12},{0,4},{1,9},{9... | collective-permute-start | bytes 688136 | tf_op jit(solution)/shard_map/ppermute | solution.py:381
  59.9 14.3 %copy-start.1 = (f32[896,256]{1,0:T(8,128)S(1)}, f32[896,256]{1,0:T(8,128)}, u32[]{:S(2)}) copy-start(f32[896,256]{1,0:T(8,128)} %refs_2_.1) | copy-start | bytes 2752516
  59.9 14.3 %copy-start.2 = (f32[896,256]{1,0:T(8,128)S(1)}, f32[896,256]{1,0:T(8,128)}, u32[]{:S(2)}) copy-start(f32[896,256]{1,0:T(8,128)} %refs_3_.1) | copy-start | bytes 2752516
  59.9 9.3 %collective-permute-start.13 = (bf16[896,128]{1,0:T(8,128)(2,1)S(1)}, bf16[896,128]{1,0:T(8,128)(2,1)S(1)}, u32[]{:S(2)}, u32[]{:S(2)}) collective-permute-start(bf16[896,128]{1,0:T(8,128)(2,1)S(1)} %shard_map.84), channel_id=1, source_target_pairs={{0,8},{8,16},{16,24},{24,28},{28,20},{20,12},{12,4},{4,0},{9,1},{1... | collective-permute-start | bytes 688136 | tf_op jit(solution)/shard_map/ppermute | solution.py:381
  63.8 9.4 %collective-permute-start.37 = (bf16[896,128]{1,0:T(8,128)(2,1)S(1)}, bf16[896,128]{1,0:T(8,128)(2,1)S(1)}, u32[]{:S(2)}, u32[]{:S(2)}) collective-permute-start(bf16[896,128]{1,0:T(8,128)(2,1)S(1)} %shard_map.100), channel_id=1, source_target_pairs={{8,0},{16,8},{24,16},{28,24},{20,28},{12,20},{4,12},{0,4},{1,9},{9... | collective-permute-start | bytes 688136 | tf_op jit(solution)/shard_map/ppermute | solution.py:381
  64.8 9.4 %collective-permute-start.33 = (bf16[896,128]{1,0:T(8,128)(2,1)S(1)}, bf16[896,128]{1,0:T(8,128)(2,1)S(1)}, u32[]{:S(2)}, u32[]{:S(2)}) collective-permute-start(bf16[896,128]{1,0:T(8,128)(2,1)S(1)} %shard_map.97), channel_id=1, source_target_pairs={{0,8},{8,16},{16,24},{24,28},{28,20},{20,12},{12,4},{4,0},{9,1},{1... | collective-permute-start | bytes 688136 | tf_op jit(solution)/shard_map/ppermute | solution.py:381
  68.7 32.5 %copy-start = (bf16[1024,256]{1,0:T(8,128)(2,1)S(1)}, bf16[1024,256]{1,0:T(8,128)(2,1)}, u32[]{:S(2)}) copy-start(bf16[1024,256]{1,0:T(8,128)(2,1)} %base.4) | copy-start | bytes 1572868
  68.7 9.4 %collective-permute-start.18 = (bf16[896,128]{1,0:T(8,128)(2,1)S(1)}, bf16[896,128]{1,0:T(8,128)(2,1)S(1)}, u32[]{:S(2)}, u32[]{:S(2)}) collective-permute-start(bf16[896,128]{1,0:T(8,128)(2,1)S(1)} %shard_map.88), channel_id=1, source_target_pairs={{8,0},{16,8},{24,16},{28,24},{20,28},{12,20},{4,12},{0,4},{1,9},{9... | collective-permute-start | bytes 688136 | tf_op jit(solution)/shard_map/ppermute | solution.py:381
  69.7 8.4 %collective-permute-start.14 = (bf16[896,128]{1,0:T(8,128)(2,1)S(1)}, bf16[896,128]{1,0:T(8,128)(2,1)S(1)}, u32[]{:S(2)}, u32[]{:S(2)}) collective-permute-start(bf16[896,128]{1,0:T(8,128)(2,1)S(1)} %shard_map.85), channel_id=1, source_target_pairs={{0,8},{8,16},{16,24},{24,28},{28,20},{20,12},{12,4},{4,0},{9,1},{1... | collective-permute-start | bytes 688136 | tf_op jit(solution)/shard_map/ppermute | solution.py:381
  74.8 8.2 %collective-permute-start.38 = (bf16[896,128]{1,0:T(8,128)(2,1)S(1)}, bf16[896,128]{1,0:T(8,128)(2,1)S(1)}, u32[]{:S(2)}, u32[]{:S(2)}) collective-permute-start(bf16[896,128]{1,0:T(8,128)(2,1)S(1)} %get-tuple-element.34.refs_1_), channel_id=1, source_target_pairs={{0,8},{8,16},{16,24},{24,28},{28,20},{20,12},{12,4},{4,0},{9,1},{1... | collective-permute-start | bytes 688136 | tf_op jit(solution)/shard_map/ppermute | solution.py:381
  76.4 8.2 %collective-permute-start.46 = (bf16[896,128]{1,0:T(8,128)(2,1)S(1)}, bf16[896,128]{1,0:T(8,128)(2,1)S(1)}, u32[]{:S(2)}, u32[]{:S(2)}) collective-permute-start(bf16[896,128]{1,0:T(8,128)(2,1)S(1)} %get-tuple-element.34.refs_1_), channel_id=1, source_target_pairs={{8,0},{16,8},{24,16},{28,24},{20,28},{12,20},{4,12},{0,4},{1,9},{9... | collective-permute-start | bytes 688136 | tf_op jit(solution)/shard_map/ppermute | solution.py:381
  78.7 9.2 %collective-permute-start.19 = (bf16[896,128]{1,0:T(8,128)(2,1)S(1)}, bf16[896,128]{1,0:T(8,128)(2,1)S(1)}, u32[]{:S(2)}, u32[]{:S(2)}) collective-permute-start(bf16[896,128]{1,0:T(8,128)(2,1)S(1)} %get-tuple-element.30.refs_0_), channel_id=1, source_target_pairs={{0,8},{8,16},{16,24},{24,28},{28,20},{20,12},{12,4},{4,0},{9,1},{1... | collective-permute-start | bytes 688136 | tf_op jit(solution)/shard_map/ppermute | solution.py:381
  80.4 9.1 %collective-permute-start.42 = (bf16[896,128]{1,0:T(8,128)(2,1)S(1)}, bf16[896,128]{1,0:T(8,128)(2,1)S(1)}, u32[]{:S(2)}, u32[]{:S(2)}) collective-permute-start(bf16[896,128]{1,0:T(8,128)(2,1)S(1)} %get-tuple-element.30.refs_0_), channel_id=1, source_target_pairs={{8,0},{16,8},{24,16},{28,24},{20,28},{12,20},{4,12},{0,4},{1,9},{9... | collective-permute-start | bytes 688136 | tf_op jit(solution)/shard_map/ppermute | solution.py:381
  83.0 9.8 %collective-permute-start.39 = (bf16[896,128]{1,0:T(8,128)(2,1)S(1)}, bf16[896,128]{1,0:T(8,128)(2,1)S(1)}, u32[]{:S(2)}, u32[]{:S(2)}) collective-permute-start(bf16[896,128]{1,0:T(8,128)(2,1)S(1)} %collective-permute-done.38.refs_1_), channel_id=1, source_target_pairs={{0,8},{8,16},{16,24},{24,28},{28,20},{20,12},{12,4},{4,0},{9,1},{1... | collective-permute-start | bytes 688136 | tf_op jit(solution)/shard_map/ppermute | solution.py:381
  84.6 9.8 %collective-permute-start.47 = (bf16[896,128]{1,0:T(8,128)(2,1)S(1)}, bf16[896,128]{1,0:T(8,128)(2,1)S(1)}, u32[]{:S(2)}, u32[]{:S(2)}) collective-permute-start(bf16[896,128]{1,0:T(8,128)(2,1)S(1)} %collective-permute-done.46.refs_3_), channel_id=1, source_target_pairs={{8,0},{16,8},{24,16},{28,24},{20,28},{12,20},{4,12},{0,4},{1,9},{9... | collective-permute-start | bytes 688136 | tf_op jit(solution)/shard_map/ppermute | solution.py:381
  87.9 9.8 %collective-permute-start.20 = (bf16[896,128]{1,0:T(8,128)(2,1)S(1)}, bf16[896,128]{1,0:T(8,128)(2,1)S(1)}, u32[]{:S(2)}, u32[]{:S(2)}) collective-permute-start(bf16[896,128]{1,0:T(8,128)(2,1)S(1)} %collective-permute-done.19.refs_0_), channel_id=1, source_target_pairs={{0,8},{8,16},{16,24},{24,28},{28,20},{20,12},{12,4},{4,0},{9,1},{1... | collective-permute-start | bytes 688136 | tf_op jit(solution)/shard_map/ppermute | solution.py:381
  89.5 9.8 %collective-permute-start.43 = (bf16[896,128]{1,0:T(8,128)(2,1)S(1)}, bf16[896,128]{1,0:T(8,128)(2,1)S(1)}, u32[]{:S(2)}, u32[]{:S(2)}) collective-permute-start(bf16[896,128]{1,0:T(8,128)(2,1)S(1)} %collective-permute-done.42.refs_2_), channel_id=1, source_target_pairs={{8,0},{16,8},{24,16},{28,24},{20,28},{12,20},{4,12},{0,4},{1,9},{9... | collective-permute-start | bytes 688136 | tf_op jit(solution)/shard_map/ppermute | solution.py:381
  92.9 12.5 %collective-permute-start.40 = (bf16[896,128]{1,0:T(8,128)(2,1)S(1)}, bf16[896,128]{1,0:T(8,128)(2,1)S(1)}, u32[]{:S(2)}, u32[]{:S(2)}) collective-permute-start(bf16[896,128]{1,0:T(8,128)(2,1)S(1)} %collective-permute-done.39.refs_1_), channel_id=1, source_target_pairs={{0,8},{8,16},{16,24},{24,28},{28,20},{20,12},{12,4},{4,0},{9,1},{1... | collective-permute-start | bytes 688136 | tf_op jit(solution)/shard_map/ppermute | solution.py:381
  94.5 12.5 %collective-permute-start.48 = (bf16[896,128]{1,0:T(8,128)(2,1)S(1)}, bf16[896,128]{1,0:T(8,128)(2,1)S(1)}, u32[]{:S(2)}, u32[]{:S(2)}) collective-permute-start(bf16[896,128]{1,0:T(8,128)(2,1)S(1)} %collective-permute-done.47.refs_3_), channel_id=1, source_target_pairs={{8,0},{16,8},{24,16},{28,24},{20,28},{12,20},{4,12},{0,4},{1,9},{9... | collective-permute-start | bytes 688136 | tf_op jit(solution)/shard_map/ppermute | solution.py:381
  97.8 9.8 %collective-permute-start.21 = (bf16[896,128]{1,0:T(8,128)(2,1)S(1)}, bf16[896,128]{1,0:T(8,128)(2,1)S(1)}, u32[]{:S(2)}, u32[]{:S(2)}) collective-permute-start(bf16[896,128]{1,0:T(8,128)(2,1)S(1)} %collective-permute-done.20.refs_0_), channel_id=1, source_target_pairs={{0,8},{8,16},{16,24},{24,28},{28,20},{20,12},{12,4},{4,0},{9,1},{1... | collective-permute-start | bytes 688136 | tf_op jit(solution)/shard_map/ppermute | solution.py:381
  99.4 9.9 %collective-permute-start.44 = (bf16[896,128]{1,0:T(8,128)(2,1)S(1)}, bf16[896,128]{1,0:T(8,128)(2,1)S(1)}, u32[]{:S(2)}, u32[]{:S(2)}) collective-permute-start(bf16[896,128]{1,0:T(8,128)(2,1)S(1)} %collective-permute-done.43.refs_2_), channel_id=1, source_target_pairs={{8,0},{16,8},{24,16},{28,24},{20,28},{12,20},{4,12},{0,4},{1,9},{9... | collective-permute-start | bytes 688136 | tf_op jit(solution)/shard_map/ppermute | solution.py:381
  105.3 9.3 %collective-permute-start.41 = (bf16[448,128]{1,0:T(8,128)(2,1)S(1)}, bf16[448,128]{1,0:T(8,128)(2,1)S(1)}, u32[]{:S(2)}, u32[]{:S(2)}) collective-permute-start(bf16[448,128]{1,0:T(8,128)(2,1)S(1)} %slice.17), channel_id=1, source_target_pairs={{0,8},{8,16},{16,24},{24,28},{28,20},{20,12},{12,4},{4,0},{9,1},{1... | collective-permute-start | bytes 344072 | tf_op jit(solution)/shard_map/ppermute | solution.py:381
  107.0 7.6 %collective-permute-start.49 = (bf16[448,128]{1,0:T(8,128)(2,1)S(1)}, bf16[448,128]{1,0:T(8,128)(2,1)S(1)}, u32[]{:S(2)}, u32[]{:S(2)}) collective-permute-start(bf16[448,128]{1,0:T(8,128)(2,1)S(1)} %slice.19), channel_id=1, source_target_pairs={{8,0},{16,8},{24,16},{28,24},{20,28},{12,20},{4,12},{0,4},{1,9},{9... | collective-permute-start | bytes 344072 | tf_op jit(solution)/shard_map/ppermute | solution.py:381
  107.6 7.0 %collective-permute-start.22 = (bf16[448,128]{1,0:T(8,128)(2,1)S(1)}, bf16[448,128]{1,0:T(8,128)(2,1)S(1)}, u32[]{:S(2)}, u32[]{:S(2)}) collective-permute-start(bf16[448,128]{1,0:T(8,128)(2,1)S(1)} %slice.16), channel_id=1, source_target_pairs={{0,8},{8,16},{16,24},{24,28},{28,20},{20,12},{12,4},{4,0},{9,1},{1... | collective-permute-start | bytes 344072 | tf_op jit(solution)/shard_map/ppermute | solution.py:381
  109.3 5.4 %collective-permute-start.45 = (bf16[448,128]{1,0:T(8,128)(2,1)S(1)}, bf16[448,128]{1,0:T(8,128)(2,1)S(1)}, u32[]{:S(2)}, u32[]{:S(2)}) collective-permute-start(bf16[448,128]{1,0:T(8,128)(2,1)S(1)} %slice.18), channel_id=1, source_target_pairs={{8,0},{16,8},{24,16},{28,24},{20,28},{12,20},{4,12},{0,4},{1,9},{9... | collective-permute-start | bytes 344072 | tf_op jit(solution)/shard_map/ppermute | solution.py:381
